TPU v7x, 32 devices: a whole 2x2x4 slice. The times are simulated.
32 devices in a mesh: mem: 8 (over y, x, core), band: 4 (over z).
Axes of the slice: x: 2, y: 2, z: 4, core: 2. Of those that a mesh axis runs over, the one named last changes fastest.
Arguments:
- ensemble: bfloat16 [256, 3, 240, 160], P('mem', None, 'band'), may hold values from -8 to 8, as said below
- layer_depth: float32 [240, 160], P('band'), may hold values from 0.5 to 2
- observed_cell: int32 [8, 8, 512], P('mem', 'band'), may hold values from 0 to 1799
- observed_value: float32 [8, 8, 512], P('mem', 'band'), may hold values from -6 to 6
- error_variance: float32 [8, 8, 512], P('mem', 'band'), may hold values from 4 to 64
- observed_count: int32 [8, 8], P('mem', 'band'), may hold values from 256 to 512, as said below
Outputs:
- analysis: bfloat16 [256, 3, 240, 160], P('mem', None, 'band')
Inputs may be any that keep to these rules, and one draw needn't show every extreme that they name: `ensemble`: the forecast members scatter around a common state. `observed_count`: some tile holds 512 observations; the slots from the count on are unused.
All inputs are finite; a program needn't handle non-finite values.
Results may differ from a plain program's by a relative error of at most 0.0051.
The roundings to bfloat16 on the way count: a program that leaves them out, or rounds other values in their place, can miss the bound.
Values may be sent and summed in bfloat16 or wider, within the bound.
No kernel may reach another device: no remote copies, remote signals or barrier semaphores. Data moves between devices by JAX's collectives and lax.ppermute only.
A program may use at most 128 MiB of HBM per device.

v0:
```python
import math

import jax
import jax.numpy as jnp
from jax import lax
from jax.sharding import PartitionSpec as P

SWEEPS = 5


half_step = 0.1
coriolis_scale = 0.3
neighbour_weight = 0.75


def padded_2(cells, sides, width):
    for axis, dim in sides:
        count = lax.axis_size(axis)
        head = lax.slice_in_dim(cells, 0, width, axis=dim)
        tail = lax.slice_in_dim(cells, cells.shape[dim] - width, cells.shape[dim], axis=dim)
        cells = jnp.concatenate(
            [
                lax.ppermute(tail, axis, [(i, (i + 1) % count) for i in range(count)]),
                cells,
                lax.ppermute(head, axis, [((i + 1) % count, i) for i in range(count)]),
            ],
            axis=dim,
        )
    return cells


def north_south(source):
    widths = [(0, 0)] * (source.ndim - 1) + [(1, 1)]
    padded = jnp.pad(source, widths)
    return padded[..., 2:] - padded[..., :-2]


def coriolis(latitudes):
    position = jnp.arange(latitudes, dtype=jnp.float32)
    return coriolis_scale * jnp.sin(math.pi * ((position + 0.5) / latitudes - 0.5))


def newton_schulz(starting):
    identity = jnp.eye(starting.shape[-1], dtype=starting.dtype)
    root_part = starting
    inverse_root = jnp.broadcast_to(identity, starting.shape)
    for sweep_index in range(SWEEPS):
        product = jnp.einsum(
            "tij,tjk->tik", inverse_root, root_part, precision=lax.Precision.HIGHEST
        )
        middle = 1.5 * identity - 0.5 * product
        root_part = jnp.einsum("tij,tjk->tik", root_part, middle, precision=lax.Precision.HIGHEST)
        inverse_root = jnp.einsum(
            "tij,tjk->tik", middle, inverse_root, precision=lax.Precision.HIGHEST
        )
    return inverse_root


def on_device(ensemble, layer_depth, observed_cell, observed_value, error_variance, observed_count):
    block_members = ensemble.shape[0]
    columns = ensemble.shape[2]
    latitudes = ensemble.shape[3]
    strips = lax.axis_size("mem")
    members = block_members * strips
    strip_rows = latitudes // strips
    tile_count = observed_cell.shape[1]
    tile_columns = columns // tile_count
    slot_count = observed_cell.shape[2]
    tile_cells = 3 * tile_columns * strip_rows
    height = ensemble[:, 0].astype(jnp.float32)
    eastward = ensemble[:, 1].astype(jnp.float32)
    northward = ensemble[:, 2].astype(jnp.float32)
    turning = coriolis(latitudes)
    flux_east = (layer_depth * eastward).astype(jnp.bfloat16)
    flux_north = (layer_depth * northward).astype(jnp.bfloat16)
    east_margin = padded_2(flux_east, (("band", 1),), 1)
    east_west = east_margin[:, 2:].astype(jnp.float32) - east_margin[:, :-2].astype(jnp.float32)
    north_local = lax.optimization_barrier(flux_north).astype(jnp.float32)
    raised = height - half_step * (east_west + north_south(north_local))
    surface_elevation_cast = raised.astype(jnp.bfloat16)
    height_margin = padded_2(surface_elevation_cast, (("band", 1),), 1)
    margin_wide = height_margin.astype(jnp.float32)
    height_inner = margin_wide[:, 1:-1]
    revised_zonal_velocity = (
        eastward + turning * northward - half_step * (margin_wide[:, 2:] - margin_wide[:, :-2])
    )
    revised_meridional_velocity = (
        northward - turning * eastward - half_step * north_south(height_inner)
    )
    advance_dynamics = jnp.stack(
        [
            surface_elevation_cast,
            revised_zonal_velocity.astype(jnp.bfloat16),
            revised_meridional_velocity.astype(jnp.bfloat16),
        ],
        axis=1,
    )
    reordered = advance_dynamics.reshape(
        block_members, 3, tile_count, tile_columns, strips, strip_rows
    )
    reordered = jnp.transpose(reordered, (4, 2, 0, 1, 3, 5)).reshape(
        strips, tile_count, block_members, tile_cells
    )
    tile_block = lax.all_to_all(reordered, "mem", split_axis=0, concat_axis=2, tiled=True)[0]
    cells_here = observed_cell[0]
    values = jnp.take_along_axis(tile_block, cells_here[:, None, :], axis=2)
    observed_mean = jnp.sum(values, axis=1, dtype=jnp.float32) / members
    slot_index = jnp.arange(slot_count, dtype=jnp.int32)[None, :]
    live_slots = slot_index < observed_count[0][:, None]
    root_weight = jnp.sqrt(jnp.where(live_slots, 1.0 / error_variance[0], 0.0))
    spread = (
        root_weight[:, None, :] * (values.astype(jnp.float32) - observed_mean[:, None, :])
    ).astype(jnp.bfloat16)
    misfit = (root_weight * (observed_value[0] - observed_mean)).astype(jnp.bfloat16)
    spread_margin, misfit_margin = (
        padded_2(spread[None], (("mem", 0), ("band", 1)), 1),
        padded_2(misfit[None], (("mem", 0), ("band", 1)), 1),
    )
    gram_margin = jnp.einsum(
        "atko,atlo->atkl", spread_margin, spread_margin, preferred_element_type=jnp.float32
    )
    pull_margin = jnp.einsum(
        "atko,ato->atk", spread_margin, misfit_margin, preferred_element_type=jnp.float32
    )
    strip_here = lax.axis_index("mem")
    lower_valid = (strip_here > 0).astype(jnp.float32)
    upper_valid = (strip_here < strips - 1).astype(jnp.float32)
    strip_mask = (lower_valid, 1.0, upper_valid)
    total_gram = jnp.zeros((tile_count, members, members), jnp.float32)
    total_pull = jnp.zeros((tile_count, members), jnp.float32)
    for offset_lat in range(3):
        for offset_lon in range(3):
            factor = (
                neighbour_weight ** (abs(offset_lat - 1) + abs(offset_lon - 1))
                * strip_mask[offset_lat]
            )
            total_gram = (
                total_gram + factor * gram_margin[offset_lat, offset_lon : offset_lon + tile_count]
            )
            total_pull = (
                total_pull + factor * pull_margin[offset_lat, offset_lon : offset_lon + tile_count]
            )
    system = (members - 1) * jnp.eye(members, dtype=jnp.float32)[None] + total_gram
    frobenius = jnp.sqrt(jnp.sum(system * system, axis=(1, 2)))
    inverse_root = newton_schulz(system / frobenius[:, None, None])
    spread_map = inverse_root * (math.sqrt(members - 1) / jnp.sqrt(frobenius))[:, None, None]
    half_pull = jnp.einsum("tij,tj->ti", inverse_root, total_pull, precision=lax.Precision.HIGHEST)
    shift_weights = (
        jnp.einsum("tij,tj->ti", inverse_root, half_pull, precision=lax.Precision.HIGHEST)
        / frobenius[:, None]
    )
    weights = (spread_map + shift_weights[:, :, None]).astype(jnp.bfloat16)
    state_mean = jnp.sum(tile_block, axis=1, dtype=jnp.float32) / members
    anomaly = (tile_block.astype(jnp.float32) - state_mean[:, None, :]).astype(jnp.bfloat16)
    update = jnp.einsum("tjk,tjc->tkc", weights, anomaly, preferred_element_type=jnp.float32)
    analysed = (state_mean[:, None, :] + update).astype(jnp.bfloat16)
    returned = lax.all_to_all(analysed[None], "mem", split_axis=2, concat_axis=0, tiled=True)
    returned = returned.reshape(strips, tile_count, block_members, 3, tile_columns, strip_rows)
    return jnp.transpose(returned, (2, 3, 1, 4, 0, 5)).reshape(block_members, 3, columns, latitudes)


def solution(mesh):
    in_specs = (
        P("mem", None, "band", None),
        P("band", None),
        P("mem", "band", None),
        P("mem", "band", None),
        P("mem", "band", None),
        P("mem", "band"),
    )
    out_specs = P("mem", None, "band", None)
    return jax.shard_map(
        on_device, mesh=mesh, in_specs=in_specs, out_specs=out_specs, check_vma=False
    )
```

profile of v0, /device:TPU:0, one launch (start us, length us, event | category | flops | bytes accessed | tf_op | source)
XLA Modules:
  0.0 279.9 jit_solution(7164611219929606275)
XLA Ops:
  2.1 5.1 %collective-permute-start = (bf16[32,1,160]{2,0,1:T(8,128)(2,1)S(1)}, bf16[32,1,160]{2,0,1:T(8,128)(2,1)S(1)}, u32[]{:S(2)}, u32[]{:S(2)}) collective-permute-start(bf16[32,1,160]{2,0,1:T(8,128)(2,1)S(1)} %get-tuple-element.15), channel_id=1, source_target_pairs={{1,0},{2,1},{3,2},{0,3},{5,4},{6,5},{7,6},{4,7},{9,8},{10,9},{11,1... | collective-permute-start | bytes 30728 | tf_op jit(solution)/shard_map/ppermute | solution.py:25
  8.6 4.1 %collective-permute-done.1 = bf16[32,1,160]{2,0,1:T(8,128)(2,1)S(1)} collective-permute-done((bf16[32,1,160]{2,0,1:T(8,128)(2,1)S(1)}, bf16[32,1,160]{2,0,1:T(8,128)(2,1)S(1)}, u32[]{:S(2)}, u32[]{:S(2)}) %collective-permute-start.1) | collective-permute-done | bytes 10272 | tf_op jit(solution)/shard_map/ppermute | solution.py:23
  14.9 3.8 %collective-permute-start.3 = (bf16[32,1,160]{2,0,1:T(8,128)(2,1)S(1)}, bf16[32,1,160]{2,0,1:T(8,128)(2,1)S(1)}, u32[]{:S(2)}, u32[]{:S(2)}) collective-permute-start(bf16[32,1,160]{2,0,1:T(8,128)(2,1)S(1)} %get-tuple-element.14), channel_id=1, source_target_pairs={{1,0},{2,1},{3,2},{0,3},{5,4},{6,5},{7,6},{4,7},{9,8},{10,9},{11,1... | collective-permute-start | bytes 30728 | tf_op jit(solution)/shard_map/ppermute | solution.py:25
  20.9 4.6 %stack.12 = bf16[32,1,2,30,8,20]{3,2,5,4,0,1:T(2,128)(2,1)S(1)} reshape(bf16[32,60,160]{1,2,0:T(8,128)(2,1)} %copy.30) | data formatting | bytes 1228800 | tf_op jit(solution)/shard_map/stack | solution.py:90
  31.4 3.0 %copy.31 = bf16[32,60,160]{1,2,0:T(8,128)(2,1)} copy(bf16[32,60,160]{2,0,1:T(8,128)(2,1)} %get-tuple-element.9) | data formatting | bytes 1228800 | tf_op jit(solution)/shard_map/convert_element_type | solution.py:93
  34.4 5.6 %stack.13 = bf16[32,1,2,30,8,20]{3,2,5,4,0,1:T(2,128)(2,1)} reshape(bf16[32,60,160]{1,2,0:T(8,128)(2,1)} %copy.31) | data formatting | bytes 1228800 | tf_op jit(solution)/shard_map/stack | solution.py:90
  40.0 3.1 %copy.32 = bf16[32,60,160]{1,2,0:T(8,128)(2,1)} copy(bf16[32,60,160]{2,0,1:T(8,128)(2,1)} %get-tuple-element.10) | data formatting | bytes 1228800 | tf_op jit(solution)/shard_map/convert_element_type | solution.py:94
  43.1 5.6 %stack.14 = bf16[32,1,2,30,8,20]{3,2,5,4,0,1:T(2,128)(2,1)} reshape(bf16[32,60,160]{1,2,0:T(8,128)(2,1)} %copy.32) | data formatting | bytes 1228800 | tf_op jit(solution)/shard_map/stack | solution.py:90
  48.7 17.0 %maximum_bitcast_fusion = bf16[8,2,32,3,30,20]{4,1,5,0,2,3:T(2,128)(2,1)} fusion(bf16[32,1,2,30,8,20]{3,2,5,4,0,1:T(2,128)(2,1)} %stack.14, bf16[32,1,2,30,8,20]{3,2,5,4,0,1:T(2,128)(2,1)} %stack.13, bf16[32,1,2,30,8,20]{3,2,5,4,0,1:T(2,128)(2,1)S(1)} %stack.12), kind=kLoop, calls=%fused_computation.1 | loop fusion | flops 1843200 | bytes 3686400 | tf_op jit(solution)/shard_map/transpose | solution.py:101
  65.7 24.9 %copy.33 = bf16[8,2,32,3,30,20]{2,0,5,4,3,1:T(8,128)(2,1)} copy(bf16[8,2,32,3,30,20]{4,1,5,0,2,3:T(2,128)(2,1)} %maximum_bitcast_fusion) | data formatting | bytes 3686400 | tf_op jit(solution)/shard_map/transpose | solution.py:101
  90.6 9.1 %copy.34 = bf16[8,2,32,1800]{3,2,1,0:T(8,128)(2,1)} copy(bf16[8,2,32,1800]{2,0,3,1:T(8,128)(2,1)} %bitcast.114) | data formatting | bytes 3686400 | tf_op jit(solution)/shard_map/reshape | solution.py:101
  99.7 4.0 %all-to-all-start = ((bf16[8,2,32,1800]{3,2,1,0:T(8,128)(2,1)}), bf16[8,2,32,1800]{3,2,1,0:T(8,128)(2,1)S(1)}, u32[]{:S(2)}, u32[]{:S(2)}) async-start(bf16[8,2,32,1800]{3,2,1,0:T(8,128)(2,1)} %copy.34), calls=%async_computation | async-start | bytes 3932160 | tf_op jit(solution)/shard_map/all_to_all | solution.py:104
  103.8 25.0 %all-to-all-done = bf16[8,2,32,1800]{3,2,1,0:T(8,128)(2,1)S(1)} async-done(((bf16[8,2,32,1800]{3,2,1,0:T(8,128)(2,1)}), bf16[8,2,32,1800]{3,2,1,0:T(8,128)(2,1)S(1)}, u32[]{:S(2)}, u32[]{:S(2)}) %all-to-all-start) | async-done | bytes 1843232 | tf_op jit(solution)/shard_map/all_to_all | solution.py:104
  130.8 2.8 %copy.36 = bf16[2,256,1800]{1,2,0:T(8,128)(2,1)S(1)} copy(bf16[2,256,1800]{2,1,0:T(8,128)(2,1)} %bitcast.118) | data formatting | bytes 3686400 | tf_op jit(solution)/shard_map/squeeze | solution.py:104
  133.6 5.8 %gather_fusion = bf16[1024,256]{1,0:T(8,128)(2,1)S(1)} fusion(bf16[2,256,1800]{1,2,0:T(8,128)(2,1)S(1)} %copy.36, s32[1024]{0:T(1024)S(1)} %bitcast.113), kind=kCustom, calls=%fused_computation | custom fusion | bytes 1056768 | tf_op jit(solution)/shard_map/jit(take_along_axis)/gather | solution.py:106
  144.9 7.6 %collective-permute-done.5 = bf16[1,2,256,512]{3,2,1,0:T(8,128)(2,1)S(1)} collective-permute-done((bf16[1,2,256,512]{3,2,1,0:T(8,128)(2,1)S(1)}, bf16[1,2,256,512]{3,2,1,0:T(8,128)(2,1)S(1)}, u32[]{:S(2)}, u32[]{:S(2)}) %collective-permute-start.5) | collective-permute-done | bytes 524320 | tf_op jit(solution)/shard_map/ppermute | solution.py:25
  153.9 3.8 %collective-permute-start.7 = (bf16[3,1,256,512]{3,2,1,0:T(8,128)(2,1)S(1)}, bf16[3,1,256,512]{3,2,1,0:T(8,128)(2,1)S(1)}, u32[]{:S(2)}, u32[]{:S(2)}) collective-permute-start(bf16[3,1,256,512]{3,2,1,0:T(8,128)(2,1)S(1)} %get-tuple-element.12), channel_id=1, source_target_pairs={{1,0},{2,1},{3,2},{0,3},{5,4},{6,5},{7,6},{4,7},{9,8},{10,9},{11,1... | collective-permute-start | bytes 2359304 | tf_op jit(solution)/shard_map/ppermute | solution.py:25
  157.9 3.8 %collective-permute-start.11 = (bf16[3,1,512]{2,1,0:T(2,128)(2,1)S(1)}, bf16[3,1,512]{2,1,0:T(2,128)(2,1)S(1)}, u32[]{:S(2)}, u32[]{:S(2)}) collective-permute-start(bf16[3,1,512]{2,1,0:T(2,128)(2,1)S(1)} %get-tuple-element.18), channel_id=1, source_target_pairs={{1,0},{2,1},{3,2},{0,3},{5,4},{6,5},{7,6},{4,7},{9,8},{10,9},{11,1... | collective-permute-start | bytes 9224 | tf_op jit(solution)/shard_map/ppermute | solution.py:25
  161.7 29.6 %collective-permute-done.10 = bf16[3,1,512]{2,1,0:T(2,128)(2,1)S(1)} collective-permute-done((bf16[3,1,512]{2,1,0:T(2,128)(2,1)S(1)}, bf16[3,1,512]{2,1,0:T(2,128)(2,1)S(1)}, u32[]{:S(2)}, u32[]{:S(2)}) %collective-permute-start.10) | collective-permute-done | bytes 3104 | tf_op jit(solution)/shard_map/ppermute | solution.py:23
  207.2 5.1 %copy.39 = bf16[1,2,256,1800]{3,1,0,2:T(2,128)(2,1)S(1)} copy(bf16[1,2,256,1800]{2,3,1,0:T(8,128)(2,1)} %fusion) | data formatting | bytes 3686400 | tf_op jit(solution)/shard_map/broadcast_in_dim | solution.py:157
  212.3 28.6 %all_to_all.30 = bf16[1,2,256,1800]{3,1,0,2:T(2,128)(2,1)S(1)} all-to-all(bf16[1,2,256,1800]{3,1,0,2:T(2,128)(2,1)S(1)} %copy.39), channel_id=1, replica_groups=mesh['mem'=8,'band'=4] {'mem'}, dimensions={2} | all-to-all | bytes 3686400 | tf_op jit(solution)/shard_map/all_to_all | solution.py:157
  241.1 7.6 %copy.41 = bf16[8,1,2,32,1800]{3,0,4,2,1:T(8,128)(2,1)} copy(bf16[8,1,2,32,1800]{4,3,0,2,1:T(8,128)(2,1)S(1)} %bitcast.117) | data formatting | bytes 3686400 | tf_op jit(solution)/shard_map/all_to_all | solution.py:157
  248.6 16.8 %copy.50 = bf16[32,3,2,30,8,20]{5,4,0,3,2,1:T(8,128)(2,1)} copy(bf16[32,3,2,30,8,20]{0,4,5,3,1,2:T(8,128)(2,1)} %bitcast.115) | data formatting | bytes 3686400 | tf_op jit(solution)/shard_map/reshape | solution.py:159
  265.4 14.5 %reshape.287 = bf16[32,3,60,160]{3,0,2,1:T(8,128)(2,1)} reshape(bf16[32,3,2,30,8,20]{5,4,0,3,2,1:T(8,128)(2,1)} %copy.50) | data formatting | bytes 3686400 | tf_op jit(solution)/shard_map/reshape | solution.py:159
  (86 shorter events, 38.7 us)
Async XLA Ops:
  2.1 6.5 %collective-permute-start = (bf16[32,1,160]{2,0,1:T(8,128)(2,1)S(1)}, bf16[32,1,160]{2,0,1:T(8,128)(2,1)S(1)}, u32[]{:S(2)}, u32[]{:S(2)}) collective-permute-start(bf16[32,1,160]{2,0,1:T(8,128)(2,1)S(1)} %get-tuple-element.15), channel_id=1, source_target_pairs={{1,0},{2,1},{3,2},{0,3},{5,4},{6,5},{7,6},{4,7},{9,8},{10,9},{11,1... | collective-permute-start | bytes 30728 | tf_op jit(solution)/shard_map/ppermute | solution.py:25
  7.2 5.5 %collective-permute-start.1 = (bf16[32,1,160]{2,0,1:T(8,128)(2,1)S(1)}, bf16[32,1,160]{2,0,1:T(8,128)(2,1)S(1)}, u32[]{:S(2)}, u32[]{:S(2)}) collective-permute-start(bf16[32,1,160]{2,0,1:T(8,128)(2,1)S(1)} %get-tuple-element.16), channel_id=1, source_target_pairs={{0,1},{1,2},{2,3},{3,0},{4,5},{5,6},{6,7},{7,4},{8,9},{9,10},{10,1... | collective-permute-start | bytes 30728 | tf_op jit(solution)/shard_map/ppermute | solution.py:23
  14.8 4.0 %copy-start.1 = (bf16[32,60,160]{2,0,1:T(8,128)(2,1)}, bf16[32,60,160]{2,0,1:T(8,128)(2,1)S(1)}, u32[]{:S(2)}) copy-start(bf16[32,60,160]{2,0,1:T(8,128)(2,1)S(1)} %fusion.11) | copy-start | bytes 1843204
  14.8 10.6 %collective-permute-start.2 = (bf16[32,1,160]{2,0,1:T(8,128)(2,1)S(1)}, bf16[32,1,160]{2,0,1:T(8,128)(2,1)S(1)}, u32[]{:S(2)}, u32[]{:S(2)}) collective-permute-start(bf16[32,1,160]{2,0,1:T(8,128)(2,1)S(1)} %get-tuple-element.13), channel_id=1, source_target_pairs={{0,1},{1,2},{2,3},{3,0},{4,5},{5,6},{6,7},{7,4},{8,9},{9,10},{10,1... | collective-permute-start | bytes 30728 | tf_op jit(solution)/shard_map/ppermute | solution.py:23
  14.9 10.5 %collective-permute-start.3 = (bf16[32,1,160]{2,0,1:T(8,128)(2,1)S(1)}, bf16[32,1,160]{2,0,1:T(8,128)(2,1)S(1)}, u32[]{:S(2)}, u32[]{:S(2)}) collective-permute-start(bf16[32,1,160]{2,0,1:T(8,128)(2,1)S(1)} %get-tuple-element.14), channel_id=1, source_target_pairs={{1,0},{2,1},{3,2},{0,3},{5,4},{6,5},{7,6},{4,7},{9,8},{10,9},{11,1... | collective-permute-start | bytes 30728 | tf_op jit(solution)/shard_map/ppermute | solution.py:25
  26.9 1.8 copy-start.2
  99.7 4.0 %copy-start.3 = (s32[1,2,512]{2,1,0:T(2,128)S(1)}, s32[1,2,512]{2,1,0:T(2,128)}, u32[]{:S(2)}) copy-start(s32[1,2,512]{2,1,0:T(2,128)} %param.8) | copy-start | bytes 12292
  99.7 29.1 %all-to-all-start = ((bf16[8,2,32,1800]{3,2,1,0:T(8,128)(2,1)}), bf16[8,2,32,1800]{3,2,1,0:T(8,128)(2,1)S(1)}, u32[]{:S(2)}, u32[]{:S(2)}) async-start(bf16[8,2,32,1800]{3,2,1,0:T(8,128)(2,1)} %copy.34), calls=%async_computation | async-start | bytes 3932160 | tf_op jit(solution)/shard_map/all_to_all | solution.py:104
  128.8 2.0 copy-start
  133.6 6.2 %copy-start.4 = (f32[1,2,512]{2,1,0:T(2,128)S(1)}, f32[1,2,512]{2,1,0:T(2,128)}, u32[]{:S(2)}) copy-start(f32[1,2,512]{2,1,0:T(2,128)} %param.10) | copy-start | bytes 12292
  133.6 6.2 %copy-start.6 = (s32[1,2]{1,0:T(1,128)S(1)}, s32[1,2]{1,0:T(1,128)}, u32[]{:S(2)}) copy-start(s32[1,2]{1,0:T(1,128)} %param.11) | copy-start | bytes 28
  139.5 1.2 copy-start.5
  140.1 12.4 %collective-permute-start.5 = (bf16[1,2,256,512]{3,2,1,0:T(8,128)(2,1)S(1)}, bf16[1,2,256,512]{3,2,1,0:T(8,128)(2,1)S(1)}, u32[]{:S(2)}, u32[]{:S(2)}) collective-permute-start(bf16[1,2,256,512]{3,2,1,0:T(8,128)(2,1)S(1)} %multiply_convert_fusion), channel_id=1, source_target_pairs={{4,0},{8,4},{12,8},{16,12},{20,16},{24,20},{28,24},{0,28},{5,1},{9... | collective-permute-start | bytes 1572872 | tf_op jit(solution)/shard_map/ppermute | solution.py:25
  140.1 13.4 %collective-permute-start.4 = (bf16[1,2,256,512]{3,2,1,0:T(8,128)(2,1)S(1)}, bf16[1,2,256,512]{3,2,1,0:T(8,128)(2,1)S(1)}, u32[]{:S(2)}, u32[]{:S(2)}) collective-permute-start(bf16[1,2,256,512]{3,2,1,0:T(8,128)(2,1)S(1)} %multiply_convert_fusion), channel_id=1, source_target_pairs={{0,4},{4,8},{8,12},{12,16},{16,20},{20,24},{24,28},{28,0},{1,5},{5... | collective-permute-start | bytes 1572872 | tf_op jit(solution)/shard_map/ppermute | solution.py:23
  140.8 17.0 %collective-permute-start.9 = (bf16[1,2,512]{2,1,0:T(2,128)(2,1)S(1)}, bf16[1,2,512]{2,1,0:T(2,128)(2,1)S(1)}, u32[]{:S(2)}, u32[]{:S(2)}) collective-permute-start(bf16[1,2,512]{2,1,0:T(2,128)(2,1)S(1)} %fusion.45), channel_id=1, source_target_pairs={{4,0},{8,4},{12,8},{16,12},{20,16},{24,20},{28,24},{0,28},{5,1},{9... | collective-permute-start | bytes 6152 | tf_op jit(solution)/shard_map/ppermute | solution.py:25
  143.0 14.7 %collective-permute-start.8 = (bf16[1,2,512]{2,1,0:T(2,128)(2,1)S(1)}, bf16[1,2,512]{2,1,0:T(2,128)(2,1)S(1)}, u32[]{:S(2)}, u32[]{:S(2)}) collective-permute-start(bf16[1,2,512]{2,1,0:T(2,128)(2,1)S(1)} %fusion.45), channel_id=1, source_target_pairs={{0,4},{4,8},{8,12},{12,16},{16,20},{20,24},{24,28},{28,0},{1,5},{5... | collective-permute-start | bytes 6152 | tf_op jit(solution)/shard_map/ppermute | solution.py:23
  153.9 37.5 %collective-permute-start.6 = (bf16[3,1,256,512]{3,2,1,0:T(8,128)(2,1)S(1)}, bf16[3,1,256,512]{3,2,1,0:T(8,128)(2,1)S(1)}, u32[]{:S(2)}, u32[]{:S(2)}) collective-permute-start(bf16[3,1,256,512]{3,2,1,0:T(8,128)(2,1)S(1)} %get-tuple-element.11), channel_id=1, source_target_pairs={{0,1},{1,2},{2,3},{3,0},{4,5},{5,6},{6,7},{7,4},{8,9},{9,10},{10,1... | collective-permute-start | bytes 2359304 | tf_op jit(solution)/shard_map/ppermute | solution.py:23
  153.9 37.4 %collective-permute-start.7 = (bf16[3,1,256,512]{3,2,1,0:T(8,128)(2,1)S(1)}, bf16[3,1,256,512]{3,2,1,0:T(8,128)(2,1)S(1)}, u32[]{:S(2)}, u32[]{:S(2)}) collective-permute-start(bf16[3,1,256,512]{3,2,1,0:T(8,128)(2,1)S(1)} %get-tuple-element.12), channel_id=1, source_target_pairs={{1,0},{2,1},{3,2},{0,3},{5,4},{6,5},{7,6},{4,7},{9,8},{10,9},{11,1... | collective-permute-start | bytes 2359304 | tf_op jit(solution)/shard_map/ppermute | solution.py:25
  157.8 33.5 %collective-permute-start.10 = (bf16[3,1,512]{2,1,0:T(2,128)(2,1)S(1)}, bf16[3,1,512]{2,1,0:T(2,128)(2,1)S(1)}, u32[]{:S(2)}, u32[]{:S(2)}) collective-permute-start(bf16[3,1,512]{2,1,0:T(2,128)(2,1)S(1)} %get-tuple-element.17), channel_id=1, source_target_pairs={{0,1},{1,2},{2,3},{3,0},{4,5},{5,6},{6,7},{7,4},{8,9},{9,10},{10,1... | collective-permute-start | bytes 9224 | tf_op jit(solution)/shard_map/ppermute | solution.py:23
  157.9 33.4 %collective-permute-start.11 = (bf16[3,1,512]{2,1,0:T(2,128)(2,1)S(1)}, bf16[3,1,512]{2,1,0:T(2,128)(2,1)S(1)}, u32[]{:S(2)}, u32[]{:S(2)}) collective-permute-start(bf16[3,1,512]{2,1,0:T(2,128)(2,1)S(1)} %get-tuple-element.18), channel_id=1, source_target_pairs={{1,0},{2,1},{3,2},{0,3},{5,4},{6,5},{7,6},{4,7},{9,8},{10,9},{11,1... | collective-permute-start | bytes 9224 | tf_op jit(solution)/shard_map/ppermute | solution.py:25
where the time goes:
time: 282 us; the launch traced here: 280 us
  local copies, waits for them, and re-layouts  115 us (41%)
  waiting for transfers between devices  68.4 us (24%)
  other arithmetic  28.9 us (10%)
  blocking collectives  28.6 us (10%)
  starting transfers between devices  23.5 us (8%)
  matrix products  15.1 us (5%)
    ppermute x6, waiting for transfers between devices, padded_2(): lax.ppermute(tail, axis, [(i, (i + 1) % count) for i in range(count)])  34.8 us
    reshape x2, local copies, waits for them, and re-layouts, on_device(): jnp.transpose(returned, (2, 3, 1, 4, 0, 5))  31.3 us
    all_to_all x1, blocking collectives, on_device(): lax.all_to_all(analysed[None], 'mem', split_axis=2, concat_axis=0, tiled=...  28.6 us
    all_to_all x1, waiting for transfers between devices, on_device(): lax.all_to_all(reordered, 'mem', split_axis=0, concat_axis=2, tiled=True)[0]  25 us
    transpose x1, local copies, waits for them, and re-layouts, on_device(): jnp.transpose(reordered, (4, 2, 0, 1, 3, 5))  24.9 us
    ppermute x6, starting transfers between devices, padded_2(): lax.ppermute(head, axis, [((i + 1) % count, i) for i in range(count)])  18.8 us
    transpose x1, other arithmetic, on_device(): jnp.transpose(reordered, (4, 2, 0, 1, 3, 5))  17 us
    another operation x3, local copies, waits for them, and re-layouts, on_device(): jnp.stack([surface_elevation_cast, revised_zonal_velocity.astype(jnp.bflo...  15.8 us
  transfers between devices with their start and end apart: 13, of which 6 were waited for; matrix products, arithmetic and copies ran while one was open for 3% of the time, Pallas kernels for 0%

commit v1 on v0

--- a/solution.py
+++ b/solution.py
@@ -3,6 +3,8 @@
 import jax
 import jax.numpy as jnp
 from jax import lax
+from jax.experimental import pallas as pl
+from jax.experimental.pallas import tpu as pltpu
 from jax.sharding import PartitionSpec as P
 
 SWEEPS = 5
@@ -159,6 +161,372 @@
     return jnp.transpose(returned, (2, 3, 1, 4, 0, 5)).reshape(block_members, 3, columns, latitudes)
 
 
+LANES = 128
+PAIRS = 8
+GROUPS = 23
+F32 = jnp.float32
+BF16 = jnp.bfloat16
+VMEM_BYTES = 56 * 1024 * 1024
+
+
+def params():
+    return pltpu.CompilerParams(vmem_limit_bytes=VMEM_BYTES)
+
+
+def identity(size, dtype):
+    row = lax.broadcasted_iota(jnp.int32, (size, size), 0)
+    column = lax.broadcasted_iota(jnp.int32, (size, size), 1)
+    return (row == column).astype(F32).astype(dtype)
+
+
+def dot_nt(left, right):
+    return lax.dot_general(left, right, (((1,), (1,)), ((), ())), preferred_element_type=F32)
+
+
+def dot_nn(left, right):
+    return lax.dot_general(left, right, (((1,), (0,)), ((), ())), preferred_element_type=F32)
+
+
+def split(value):
+    high = value.astype(BF16)
+    return high, (value - high.astype(F32)).astype(BF16)
+
+
+def dot_3(left, right):
+    return dot_nn(left[0], right[0]) + (dot_nn(left[0], right[1]) + dot_nn(left[1], right[0]))
+
+
+def exchange_lanes(blocks, lane):
+    blocks = list(blocks)
+    for bit in range(3):
+        step = 1 << bit
+        odd = (lane & step) != 0
+        for q in range(8):
+            if q & step:
+                continue
+            low, high = blocks[q], blocks[q | step]
+            blocks[q] = jnp.where(odd, pltpu.roll(high, step, 1), low)
+            blocks[q | step] = jnp.where(odd, high, pltpu.roll(low, LANES - step, 1))
+    return blocks
+
+
+def group_of(variable, index):
+    return variable * 7 + index
+
+
+def forecast_kernel(
+    ens, left, right, depth, turn, out, wide, flux, height, deep, fields, staged
+):
+    members = ens.shape[0]
+    batch = wide.shape[0]
+    latitudes = ens.shape[3]
+    rows = latitudes // 8
+    wide[...] = jnp.zeros(wide.shape, F32)
+    flux[...] = jnp.zeros(flux.shape, F32)
+    height[...] = jnp.zeros(height.shape, F32)
+    deep[...] = jnp.zeros(deep.shape, F32)
+    deep[8:68, :] = depth[...]
+    deep[6:8, :] = (left[96].astype(F32) + left[97].astype(F32)) + left[98].astype(F32)
+    deep[68:70, :] = (right[96].astype(F32) + right[97].astype(F32)) + right[98].astype(F32)
+    source = lax.broadcasted_iota(jnp.int32, (latitudes, latitudes), 0)
+    target = lax.broadcasted_iota(jnp.int32, (latitudes, latitudes), 1)
+    shift = (source == target + 1).astype(F32) - (source == target - 1).astype(F32)
+    shift = shift.astype(BF16)
+    turning = turn[0:1, :][None]
+
+    def rows_apart(value):
+        flat = value.reshape(batch * 80, latitudes)
+        return dot_nn(flat, shift).reshape(batch, 80, latitudes)
+
+    def step(index, carry):
+        first = index * batch
+        for k in range(batch):
+            for v in range(3):
+                wide[k, v, 8:68, :] = ens[first + k, v].astype(F32)
+                wide[k, v, 6:8, :] = left[(first + k) * 3 + v].astype(F32)
+                wide[k, v, 68:70, :] = right[(first + k) * 3 + v].astype(F32)
+        depths = deep[...][None]
+        flux[:, 8:88, :] = (depths * wide[:, 1]).astype(BF16).astype(F32)
+        flux_north = (depths * wide[:, 2]).astype(BF16)
+        east_west = flux[:, 9:89, :] - flux[:, 7:87, :]
+        raised = wide[:, 0] - half_step * (east_west + rows_apart(flux_north))
+        rounded = raised.astype(BF16)
+        height[:, 8:88, :] = rounded.astype(F32)
+        steps_north = rows_apart(rounded)[:, 8:72]
+        steps_east = height[:, 17:81, :] - height[:, 15:79, :]
+        east = wide[:, 1, 8:72, :]
+        north = wide[:, 2, 8:72, :]
+        new_east = east + turning * north - half_step * steps_east
+        new_north = north - turning * east - half_step * steps_north
+        here = pl.ds(first, batch)
+        fields[0, here] = height[:, 16:80, :]
+        fields[1, here] = new_east
+        fields[2, here] = new_north
+        fields[0, here, 60:64, :] = new_east[:, 56:60]
+        fields[2, here, 60:64, :] = jnp.zeros((batch, 4, latitudes), F32)
+        return carry
+
+    lax.fori_loop(0, members // batch, step, 0)
+    eye = identity(latitudes, BF16)
+    staged[:, 460:464, :] = jnp.zeros((8, 4, 256), F32)
+
+    def turn_group(v, first, g):
+        block = fields[v, :, first : first + 8, :].reshape(256, latitudes).astype(BF16)
+        turned = dot_nt(eye, block)
+        for s in range(8):
+            staged[s, rows * g : rows * (g + 1), :] = turned[rows * s : rows * (s + 1)]
+
+    for v in range(3):
+        for index in range(7):
+            turn_group(v, 8 * index, group_of(v, index))
+    turn_group(0, 56, 21)
+    turn_group(2, 56, 22)
+    out[...] = staged[...].astype(BF16)
+
+
+def observe_kernel(cells, got, weight, target, held, gram, wide, seen):
+    lane = lax.broadcasted_iota(jnp.int32, (16, LANES), 1)
+
+    def spread_out(index, carry):
+        here = pl.ds(pl.multiple_of(index * 16, 16), 16)
+        for h in range(2):
+            span = slice(h * LANES, (h + 1) * LANES)
+            blocks = exchange_lanes([got[q, here, span].astype(F32) for q in range(8)], lane)
+            for q in range(8):
+                to = pl.ds(pl.multiple_of(q * 464 + index * 16, 16), 16)
+                wide[h, to, :] = blocks[q]
+                held[q, here, span] = blocks[q].astype(BF16)
+        return carry
+
+    lax.fori_loop(0, 29, spread_out, 0)
+    ones = jnp.full((256, 256), 1.0, BF16)
+    eye = identity(256, BF16)
+    slots = seen.shape[2]
+    unroll = 8
+
+    def pick(index, carry):
+        for t in range(2):
+            for k in range(unroll):
+                slot = index * unroll + k
+                row = cells[t, slot]
+                for h in range(2):
+                    seen[t, h, pl.ds(slot, 1), :] = wide[h, pl.ds(row, 1), :]
+        return carry
+
+    lax.fori_loop(0, slots // unroll, pick, 0)
+    for t in range(2):
+        values = jnp.concatenate([seen[t, 0], seen[t, 1]], axis=1)
+        mean = dot_nn(values.astype(BF16), ones) * (1.0 / 256)
+        root = jnp.concatenate([weight[t], weight[t]], axis=1)
+        goal = jnp.concatenate([target[t], target[t]], axis=1)
+        spread = (root * (values - mean)).astype(BF16)
+        misfit = (root * (goal - mean)).astype(BF16).astype(F32)
+        pull = jnp.sum(spread.astype(F32) * misfit, axis=0, keepdims=True)
+        turned = dot_nt(eye, spread).astype(BF16)
+        gram[t, 0:256, :] = dot_nt(turned, turned)
+        gram[t, 256:264, :] = jnp.broadcast_to(pull, (8, 256))
+        gram[t, 264:272, :] = jnp.zeros((8, 256), F32)
+
+
+def analyse_kernel(held, here, below, above, out, results):
+    size = 256
+    eye = identity(size, F32)
+    maps = []
+    for t in range(2):
+        total = here[t] + neighbour_weight * (below[t].astype(F32) + above[t].astype(F32))
+        system = (size - 1) * eye + total[0:256]
+        pull = total[256:264]
+        square = jnp.sum(jnp.sum(system * system, axis=0, keepdims=True), axis=1, keepdims=True)
+        frobenius = jnp.sqrt(square)
+        root_part = system / frobenius
+        inverse_root = None
+        for sweep in range(SWEEPS):
+            if sweep == 0:
+                middle = 1.5 * eye - 0.5 * root_part
+                inverse_root = middle
+                root_part = dot_3(split(root_part), split(middle))
+            else:
+                inverse_parts, root_parts = split(inverse_root), split(root_part)
+                middle = 1.5 * eye - 0.5 * dot_3(inverse_parts, root_parts)
+                middle_parts = split(middle)
+                if sweep < SWEEPS - 1:
+                    root_part = dot_3(root_parts, middle_parts)
+                inverse_root = dot_3(middle_parts, inverse_parts)
+        inverse_parts = split(inverse_root)
+        half_pull = dot_3(split(pull), inverse_parts)
+        shift = dot_3(split(half_pull), inverse_parts) / frobenius
+        scale = math.sqrt(size - 1) / jnp.sqrt(frobenius)
+        maps.append((inverse_root * scale + shift[0:1]).astype(BF16))
+    average = jnp.full((size, size), 1.0 / size, BF16)
+    row = lax.broadcasted_iota(jnp.int32, (464, size), 0)
+    group = row // 20
+    for q in range(8):
+        cells = held[q]
+        mean = dot_nn(cells, average)
+        anomaly = (cells.astype(F32) - mean).astype(BF16)
+        first = dot_nt(anomaly, maps[0])
+        second = dot_nt(anomaly, maps[1])
+        position = group - (group // 7) * 7
+        is_first = (position < (4 if q < 6 else 3)) & (group < 21)
+        results[q] = mean + jnp.where(is_first, first, second)
+    lane = lax.broadcasted_iota(jnp.int32, (16, LANES), 1)
+
+    def gather_in(index, carry):
+        span16 = pl.ds(pl.multiple_of(index * 16, 16), 16)
+        for h in range(2):
+            span = slice(h * LANES, (h + 1) * LANES)
+            blocks = exchange_lanes([results[q, span16, span] for q in range(8)], lane)
+            for q in range(8):
+                out[q, span16, span] = blocks[q].astype(BF16)
+        return carry
+
+    lax.fori_loop(0, 29, gather_in, 0)
+
+
+def return_kernel(got, out, wide, turned):
+    members = out.shape[0]
+    latitudes = out.shape[3]
+    rows = latitudes // 8
+    wide[...] = got[...].astype(F32)
+    eye = identity(256, BF16)
+
+    def turn_group(g):
+        for s in range(8):
+            turned[g, rows * s : rows * (s + 1), :] = wide[s, rows * g : rows * (g + 1), :]
+        block = dot_nt(eye, turned[g].astype(BF16))
+        return block.reshape(members, 8, latitudes)
+
+    mixed = turn_group(21)
+    last = (mixed[:, 0:4], mixed[:, 4:8], turn_group(22)[:, 0:4])
+    for v in range(3):
+        for index in range(3):
+            pair = [turn_group(group_of(v, 2 * index + k)) for k in range(2)]
+            both = jnp.concatenate(pair, axis=1).astype(BF16)
+            out[:, v, 16 * index : 16 * (index + 1), :] = both
+        both = jnp.concatenate([turn_group(group_of(v, 6)), last[v]], axis=1).astype(BF16)
+        out[:, v, 48:60, :] = both
+
+
+def edges(ensemble, depth, first):
+    part = lax.slice_in_dim(ensemble, first, first + 2, axis=2)
+    part = part.reshape(-1, 2, ensemble.shape[3])
+    deep = lax.slice_in_dim(depth, first, first + 2, axis=0)
+    pieces = []
+    for _ in range(3):
+        piece = lax.reduce_precision(deep, 8, 7)
+        pieces.append(piece.astype(BF16))
+        deep = deep - piece
+    return jnp.concatenate([part, jnp.stack(pieces)], axis=0)
+
+
+def around(value, axis, step):
+    count = lax.axis_size(axis)
+    return lax.ppermute(value, axis, [(i, (i + step) % count) for i in range(count)])
+
+
+def along(value, axis, step):
+    count = lax.axis_size(axis)
+    pairs = [(i, i + step) for i in range(count) if 0 <= i + step < count]
+    return lax.ppermute(value, axis, pairs)
+
+
+def swap(value):
+    return lax.all_to_all(value, "mem", split_axis=0, concat_axis=0, tiled=True)
+
+
+def on_device_fast(
+    ensemble, layer_depth, observed_cell, observed_value, error_variance, observed_count
+):
+    members, _, columns, latitudes = ensemble.shape
+    slots = observed_cell.shape[2]
+    left = around(edges(ensemble, layer_depth, columns - 2), "band", 1)
+    right = around(edges(ensemble, layer_depth, 0), "band", -1)
+    turning = jnp.broadcast_to(coriolis(latitudes)[None], (8, latitudes))
+    sent = pl.pallas_call(
+        forecast_kernel,
+        out_shape=jax.ShapeDtypeStruct((8, 464, 256), BF16),
+        scratch_shapes=[
+            pltpu.VMEM((4, 3, 80, latitudes), F32),
+            pltpu.VMEM((4, 96, latitudes), F32),
+            pltpu.VMEM((4, 96, latitudes), F32),
+            pltpu.VMEM((80, latitudes), F32),
+            pltpu.VMEM((3, members, 64, latitudes), F32),
+            pltpu.VMEM((8, 464, 256), F32),
+        ],
+        compiler_params=params(),
+        name="forecast",
+    )(ensemble, left, right, layer_depth, turning)
+    got = swap(sent)
+
+    cell = observed_cell[0]
+    variable = cell // 600
+    tile = jnp.arange(2, dtype=jnp.int32)[:, None]
+    column = tile * 30 + cell // 20 % 30
+    group = variable * 7 + column // 8
+    place = column % 8
+    is_last = column >= 56
+    group = jnp.where(is_last, 21 + variable // 2, group)
+    place = jnp.where(is_last, column - 56 + 4 * (variable % 2), place)
+    rows = place * 464 + group * 20 + cell % 20
+    live = jnp.arange(slots, dtype=jnp.int32)[None, :] < observed_count[0][:, None]
+    root = jnp.sqrt(jnp.where(live, 1.0 / error_variance[0], 0.0))
+    root = jnp.broadcast_to(root[:, :, None], (2, slots, LANES))
+    goal = jnp.broadcast_to(observed_value[0][:, :, None], (2, slots, LANES))
+    vmem = pl.BlockSpec(memory_space=pltpu.VMEM)
+    held, gram = pl.pallas_call(
+        observe_kernel,
+        out_shape=(
+            jax.ShapeDtypeStruct((8, 464, 256), BF16),
+            jax.ShapeDtypeStruct((2, 272, 256), F32),
+        ),
+        in_specs=[pl.BlockSpec(memory_space=pltpu.SMEM), vmem, vmem, vmem],
+        scratch_shapes=[
+            pltpu.VMEM((2, 8 * 464, LANES), F32),
+            pltpu.VMEM((2, 2, slots, LANES), F32),
+        ],
+        compiler_params=params(),
+        name="observe",
+    )(rows, got, root, goal)
+
+    short = gram.astype(BF16)
+    west = around(short[1], "band", 1).astype(F32)
+    east = around(short[0], "band", -1).astype(F32)
+    across = jnp.stack(
+        [
+            gram[0] + neighbour_weight * (west + gram[1]),
+            gram[1] + neighbour_weight * (gram[0] + east),
+        ]
+    )
+    short = across.astype(BF16)
+    below = along(short, "mem", 1)
+    above = along(short, "mem", -1)
+    back = pl.pallas_call(
+        analyse_kernel,
+        out_shape=jax.ShapeDtypeStruct((8, 464, 256), BF16),
+        scratch_shapes=[pltpu.VMEM((8, 464, 256), F32)],
+        compiler_params=params(),
+        name="analyse",
+    )(held, across, below, above)
+    returned = swap(back)
+    return pl.pallas_call(
+        return_kernel,
+        out_shape=jax.ShapeDtypeStruct(ensemble.shape, BF16),
+        scratch_shapes=[
+            pltpu.VMEM((8, 464, 256), F32),
+            pltpu.VMEM((GROUPS, latitudes, 256), F32),
+        ],
+        compiler_params=params(),
+        name="come_back",
+    )(returned)
+
+
+def choose(ensemble, layer_depth, observed_cell, *rest):
+    shape = (lax.axis_size("mem"), ensemble.shape, observed_cell.shape[1])
+    fits = shape == (8, (32, 3, 60, 160), 2) and observed_cell.shape[2] % 16 == 0
+    chosen = on_device_fast if fits else on_device
+    return chosen(ensemble, layer_depth, observed_cell, *rest)
+
+
 def solution(mesh):
     in_specs = (
         P("mem", None, "band", None),
@@ -170,5 +538,5 @@
     )
     out_specs = P("mem", None, "band", None)
     return jax.shard_map(
-        on_device, mesh=mesh, in_specs=in_specs, out_specs=out_specs, check_vma=False
-    )
+        choose, mesh=mesh, in_specs=in_specs, out_specs=out_specs, check_vma=False
+    )

time: 282 us -> 141 us (0.50)
  local copies, waits for them, and re-layouts: 115 us -> 15.1 us
  Pallas kernels: 0 us -> 43.1 us
  waiting for transfers between devices: 68.4 us -> 30.5 us
  other arithmetic: 28.9 us -> 4.98 us
  matrix products: 15.1 us -> 0 us
  starting transfers between devices: 23.5 us -> 15.9 us
    pallas_call x0 -> x4, Pallas kernels: none -> 43.1 us  [the longest x1 18.4 us: on_device_fast(): pl.pallas_call(analyse_kernel, out_shape=jax.ShapeDtypeStruct((8, 464, 25...]
    reshape x3 -> x0, local copies, waits for them, and re-layouts: 40.3 us -> none  [the longest x2 31.3 us: on_device(): jnp.transpose(returned, (2, 3, 1, 4, 0, 5))]
    ppermute x12 -> x6, waiting for transfers between devices: 43.4 us -> 6.73 us  [the longest x2 3.59 us: along(): return lax.ppermute(value, axis, pairs)]
    transpose x1 -> x0, local copies, waits for them, and re-layouts: 24.9 us -> none  [on_device(): jnp.transpose(reordered, (4, 2, 0, 1, 3, 5))]
    transpose x1 -> x0, other arithmetic: 17 us -> none  [on_device(): jnp.transpose(reordered, (4, 2, 0, 1, 3, 5))]
    another operation x3 -> x0, local copies, waits for them, and re-layouts: 15.8 us -> none  [on_device(): jnp.stack([surface_elevation_cast, revised_zonal_velocity.astype(jnp.bflo...]
    dot_general x19 -> x0, matrix products: 15.1 us -> none  [the longest x5 3.37 us: newton_schulz(): jnp.einsum('tij,tjk->tik', inverse_root, root_part, precision=lax.Precisi...]
    all_to_all x3 -> x0, local copies, waits for them, and re-layouts: 9.28 us -> none  [the longest x2 7.75 us: on_device(): lax.all_to_all(analysed[None], 'mem', split_axis=2, concat_axis=0, tiled=...]
  transfers between devices with their start and end apart: 13 -> 7, of which waited for: 6 -> 3; matrix products, arithmetic and copies ran while one was open for 3% -> 5% of each run, Pallas kernels for 0% -> 0%
where the time goes in v1:
time: 141 us
  Pallas kernels  43.1 us (31%)
  blocking collectives  31.1 us (22%)
  waiting for transfers between devices  30.5 us (22%)
  starting transfers between devices  15.9 us (11%)
  local copies, waits for them, and re-layouts  15.1 us (11%)
  other arithmetic  4.98 us (4%)
    all_to_all x1, blocking collectives, swap(): return lax.all_to_all(value, 'mem', split_axis=0, concat_axis=0, tiled=True)  31.1 us
    all_to_all x1, waiting for transfers between devices, swap(): return lax.all_to_all(value, 'mem', split_axis=0, concat_axis=0, tiled=True)  23.7 us
    pallas_call x1, Pallas kernels, on_device_fast(): pl.pallas_call(analyse_kernel, out_shape=jax.ShapeDtypeStruct((8, 464, 25...  18.4 us
    pallas_call x1, Pallas kernels, on_device_fast(): pl.pallas_call(observe_kernel, out_shape=(jax.ShapeDtypeStruct((8, 464, 2...  12.4 us
    ppermute x4, starting transfers between devices, around(): lax.ppermute(value, axis, [(i, (i + step) % count) for i in range(count)])  9.04 us
    pallas_call x1, Pallas kernels, on_device_fast(): pl.pallas_call(forecast_kernel, out_shape=jax.ShapeDtypeStruct((8, 464, 2...  8.07 us
    unnamed x19, local copies, waits for them, and re-layouts  5.92 us
    pallas_call x1, local copies, waits for them, and re-layouts, on_device_fast(): pl.pallas_call(return_kernel, out_shape=jax.ShapeDtypeStruct(ensemble.sha...  5.16 us
  transfers between devices with their start and end apart: 7, of which 3 were waited for; matrix products, arithmetic and copies ran while one was open for 5% of the time, Pallas kernels for 0%

profile of v1, /device:TPU:0, one launch (start us, length us, event | category | flops | bytes accessed | tf_op | source)
XLA Modules:
  0.0 140.8 jit_solution(13488827925971664820)
XLA Ops:
  0.0 0.7 fusion.22
  0.7 1.0 fusion.27
  2.0 3.1 %collective-permute-start = (bf16[99,2,160]{2,1,0:T(2,128)(2,1)S(1)}, bf16[99,2,160]{2,1,0:T(2,128)(2,1)S(1)}, u32[]{:S(2)}, u32[]{:S(2)}) collective-permute-start(bf16[99,2,160]{2,1,0:T(2,128)(2,1)S(1)} %pad_maximum_fusion.1), channel_id=1, source_target_pairs={{0,1},{1,2},{2,3},{3,0},{4,5},{5,6},{6,7},{7,4},{8,9},{9,10},{10,1... | collective-permute-start | bytes 190088 | tf_op jit(solution)/shard_map/ppermute | solution.py:424
  5.4 2.1 %collective-permute-start.1 = (bf16[99,2,160]{2,1,0:T(2,128)(2,1)S(1)}, bf16[99,2,160]{2,1,0:T(2,128)(2,1)S(1)}, u32[]{:S(2)}, u32[]{:S(2)}) collective-permute-start(bf16[99,2,160]{2,1,0:T(2,128)(2,1)S(1)} %pad_maximum_fusion.2), channel_id=1, source_target_pairs={{0,3},{1,0},{2,1},{3,2},{4,7},{5,4},{6,5},{7,6},{8,11},{9,8},{10,9... | collective-permute-start | bytes 190088 | tf_op jit(solution)/shard_map/ppermute | solution.py:424
  7.4 5.2 %copy.9.ens = bf16[32,3,60,160]{3,2,1,0:T(8,128)(2,1)} copy(bf16[32,3,60,160]{3,0,2,1:T(8,128)(2,1)} %param.6) | data formatting | bytes 3686400 | tf_op args[0]
  13.3 8.1 %forecast.1 = bf16[8,464,256]{2,1,0:T(8,128)(2,1)} custom-call(bf16[32,3,60,160]{3,2,1,0:T(8,128)(2,1)} %copy.9.ens, bf16[99,2,160]{2,1,0:T(2,128)(2,1)} %copy-done.3, bf16[99,2,160]{2,1,0:T(2,128)(2,1)} %copy-done.4, f32[60,160]{1,0:T(8,128)} %depth.1, f32[8,160]{1,0:T(8,128)} %broadcast_in_dim.12.turn), custom_call_target="tpu_custom_call" | custom-call | tf_op jit(solution)/shard_map/forecast/pallas_call | solution.py:445
  21.4 4.1 %all-to-all-start = ((bf16[8,464,256]{2,1,0:T(8,128)(2,1)}), bf16[8,464,256]{2,1,0:T(8,128)(2,1)S(1)}, u32[]{:S(2)}, u32[]{:S(2)}) async-start(bf16[8,464,256]{2,1,0:T(8,128)(2,1)} %forecast.1), calls=%async_computation | async-start | bytes 3801088 | tf_op jit(solution)/shard_map/all_to_all | solution.py:434
  26.3 23.7 %all-to-all-done.got = bf16[8,464,256]{2,1,0:T(8,128)(2,1)S(1)} async-done(((bf16[8,464,256]{2,1,0:T(8,128)(2,1)}), bf16[8,464,256]{2,1,0:T(8,128)(2,1)S(1)}, u32[]{:S(2)}, u32[]{:S(2)}) %all-to-all-start) | async-done | bytes 1900576 | tf_op jit(solution)/shard_map/all_to_all | solution.py:434
  50.0 1.2 broadcast_in_dim.14.weight
  51.2 1.0 broadcast_in_dim.29.target
  52.3 12.4 %observe.1 = (bf16[8,464,256]{2,1,0:T(8,128)(2,1)}, f32[2,272,256]{2,1,0:T(8,128)}) custom-call(s32[2,512]{1,0:T(2,128)} %fusion.13.cells, bf16[8,464,256]{2,1,0:T(8,128)(2,1)} %copy-done, f32[2,512,128]{2,1,0:T(8,128)} %broadcast_in_dim.14.weight, f32[2,512,128]{2,1,0:T(8,128)} %broadcast_in_dim.29.target), custom_call_target="tpu_custom_call" | custom-call | tf_op jit(solution)/shard_map/observe/pallas_call | solution.py:476
  64.7 1.1 convert_element_type.36
  65.8 3.8 %collective-permute-start.3 = (bf16[272,256]{1,0:T(8,128)(2,1)S(1)}, bf16[272,256]{1,0:T(8,128)(2,1)S(1)}, u32[]{:S(2)}, u32[]{:S(2)}) collective-permute-start(bf16[272,256]{1,0:T(8,128)(2,1)S(1)} %get-tuple-element.14), channel_id=1, source_target_pairs={{0,3},{1,0},{2,1},{3,2},{4,7},{5,4},{6,5},{7,6},{8,11},{9,8},{10,9... | collective-permute-start | bytes 417800 | tf_op jit(solution)/shard_map/ppermute | solution.py:424
  69.7 3.1 %collective-permute-done.2 = bf16[272,256]{1,0:T(8,128)(2,1)S(1)} collective-permute-done((bf16[272,256]{1,0:T(8,128)(2,1)S(1)}, bf16[272,256]{1,0:T(8,128)(2,1)S(1)}, u32[]{:S(2)}, u32[]{:S(2)}) %collective-permute-start.2) | collective-permute-done | bytes 139296 | tf_op jit(solution)/shard_map/ppermute | solution.py:424
  72.8 1.1 fusion.2
  74.0 1.3 collective-permute-start.4
  75.3 1.5 %collective-permute-start.5 = (bf16[2,272,256]{2,1,0:T(8,128)(2,1)S(1)}, bf16[2,272,256]{2,1,0:T(8,128)(2,1)S(1)}, u32[]{:S(2)}, u32[]{:S(2)}) collective-permute-start(bf16[2,272,256]{2,1,0:T(8,128)(2,1)S(1)} %fusion.26), channel_id=1, source_target_pairs={{4,0},{8,4},{12,8},{16,12},{20,16},{24,20},{28,24},{5,1},{9,5},{13... | collective-permute-start | bytes 835592 | tf_op jit(solution)/shard_map/ppermute | solution.py:430
  76.8 0.8 pad_maximum_fusion.here
  77.6 3.6 %collective-permute-done.5.above = bf16[2,272,256]{2,1,0:T(8,128)(2,1)S(1)} collective-permute-done((bf16[2,272,256]{2,1,0:T(8,128)(2,1)S(1)}, bf16[2,272,256]{2,1,0:T(8,128)(2,1)S(1)}, u32[]{:S(2)}, u32[]{:S(2)}) %collective-permute-start.5) | collective-permute-done | bytes 278560 | tf_op jit(solution)/shard_map/ppermute | solution.py:430
  81.2 0.7 copy-done.2
  81.9 18.4 %analyse.1 = bf16[8,464,256]{2,1,0:T(8,128)(2,1)} custom-call(bf16[8,464,256]{2,1,0:T(8,128)(2,1)} %get-tuple-element.7.held, f32[2,272,256]{2,1,0:T(8,128)} %pad_maximum_fusion.here, bf16[2,272,256]{2,1,0:T(8,128)(2,1)} %copy-done.1, bf16[2,272,256]{2,1,0:T(8,128)(2,1)} %copy-done.2), custom_call_target="tpu_custom_call" | custom-call | tf_op jit(solution)/shard_map/analyse/pallas_call | solution.py:503
  100.3 31.1 %all_to_all.10.got = bf16[8,464,256]{2,1,0:T(8,128)(2,1)} all-to-all(bf16[8,464,256]{2,1,0:T(8,128)(2,1)} %analyse.1), channel_id=1, replica_groups=mesh['mem'=8,'band'=4] {'mem'}, dimensions={0} | all-to-all | bytes 3801088 | tf_op jit(solution)/shard_map/all_to_all | solution.py:434
  131.4 4.2 %come_back.1 = bf16[32,3,60,160]{3,2,1,0:T(8,128)(2,1)} custom-call(bf16[8,464,256]{2,1,0:T(8,128)(2,1)} %all_to_all.10.got), custom_call_target="tpu_custom_call" | custom-call | tf_op jit(solution)/shard_map/come_back/pallas_call | solution.py:511
  135.6 5.2 %copy.10 = bf16[32,3,60,160]{3,0,2,1:T(8,128)(2,1)} copy(bf16[32,3,60,160]{3,2,1,0:T(8,128)(2,1)} %come_back.1) | data formatting | bytes 3686400 | tf_op jit(solution)/shard_map/come_back/pallas_call | solution.py:511
  (33 shorter events, 2.2 us)
Async XLA Ops:
  2.0 10.7 %collective-permute-start = (bf16[99,2,160]{2,1,0:T(2,128)(2,1)S(1)}, bf16[99,2,160]{2,1,0:T(2,128)(2,1)S(1)}, u32[]{:S(2)}, u32[]{:S(2)}) collective-permute-start(bf16[99,2,160]{2,1,0:T(2,128)(2,1)S(1)} %pad_maximum_fusion.1), channel_id=1, source_target_pairs={{0,1},{1,2},{2,3},{3,0},{4,5},{5,6},{6,7},{7,4},{8,9},{9,10},{10,1... | collective-permute-start | bytes 190088 | tf_op jit(solution)/shard_map/ppermute | solution.py:424
  5.4 7.3 %collective-permute-start.1 = (bf16[99,2,160]{2,1,0:T(2,128)(2,1)S(1)}, bf16[99,2,160]{2,1,0:T(2,128)(2,1)S(1)}, u32[]{:S(2)}, u32[]{:S(2)}) collective-permute-start(bf16[99,2,160]{2,1,0:T(2,128)(2,1)S(1)} %pad_maximum_fusion.2), channel_id=1, source_target_pairs={{0,3},{1,0},{2,1},{3,2},{4,7},{5,4},{6,5},{7,6},{8,11},{9,8},{10,9... | collective-permute-start | bytes 190088 | tf_op jit(solution)/shard_map/ppermute | solution.py:424
  12.7 0.7 copy-start.3
  12.7 0.7 copy-start.4
  21.4 4.1 %copy-start.6 = (f32[1,2,512]{2,1,0:T(2,128)S(1)}, f32[1,2,512]{2,1,0:T(2,128)}, u32[]{:S(2)}) copy-start(f32[1,2,512]{2,1,0:T(2,128)} %param.10) | copy-start | bytes 12292
  21.4 4.1 %copy-start.8 = (s32[1,2]{1,0:T(1,128)S(1)}, s32[1,2]{1,0:T(1,128)}, u32[]{:S(2)}) copy-start(s32[1,2]{1,0:T(1,128)} %param.11) | copy-start | bytes 28
  21.4 4.2 %copy-start.7 = (s32[1,2,512]{2,1,0:T(2,128)S(1)}, s32[1,2,512]{2,1,0:T(2,128)}, u32[]{:S(2)}) copy-start(s32[1,2,512]{2,1,0:T(2,128)} %param.8) | copy-start | bytes 12292
  21.4 29.8 %copy-start.5 = (f32[1,2,512]{2,1,0:T(2,128)S(1)}, f32[1,2,512]{2,1,0:T(2,128)}, u32[]{:S(2)}) copy-start(f32[1,2,512]{2,1,0:T(2,128)} %param.9) | copy-start | bytes 12292
  21.4 28.6 %all-to-all-start = ((bf16[8,464,256]{2,1,0:T(8,128)(2,1)}), bf16[8,464,256]{2,1,0:T(8,128)(2,1)S(1)}, u32[]{:S(2)}, u32[]{:S(2)}) async-start(bf16[8,464,256]{2,1,0:T(8,128)(2,1)} %forecast.1), calls=%async_computation | async-start | bytes 3801088 | tf_op jit(solution)/shard_map/all_to_all | solution.py:434
  50.0 2.2 %copy-start = (bf16[8,464,256]{2,1,0:T(8,128)(2,1)}, bf16[8,464,256]{2,1,0:T(8,128)(2,1)S(1)}, u32[]{:S(2)}) copy-start(bf16[8,464,256]{2,1,0:T(8,128)(2,1)S(1)} %all-to-all-done.got) | copy-start | bytes 5701636
  65.8 7.0 %collective-permute-start.2 = (bf16[272,256]{1,0:T(8,128)(2,1)S(1)}, bf16[272,256]{1,0:T(8,128)(2,1)S(1)}, u32[]{:S(2)}, u32[]{:S(2)}) collective-permute-start(bf16[272,256]{1,0:T(8,128)(2,1)S(1)} %get-tuple-element.13), channel_id=1, source_target_pairs={{0,1},{1,2},{2,3},{3,0},{4,5},{5,6},{6,7},{7,4},{8,9},{9,10},{10,1... | collective-permute-start | bytes 417800 | tf_op jit(solution)/shard_map/ppermute | solution.py:424
  65.8 7.0 %collective-permute-start.3 = (bf16[272,256]{1,0:T(8,128)(2,1)S(1)}, bf16[272,256]{1,0:T(8,128)(2,1)S(1)}, u32[]{:S(2)}, u32[]{:S(2)}) collective-permute-start(bf16[272,256]{1,0:T(8,128)(2,1)S(1)} %get-tuple-element.14), channel_id=1, source_target_pairs={{0,3},{1,0},{2,1},{3,2},{4,7},{5,4},{6,5},{7,6},{8,11},{9,8},{10,9... | collective-permute-start | bytes 417800 | tf_op jit(solution)/shard_map/ppermute | solution.py:424
  74.0 3.6 %collective-permute-start.4 = (bf16[2,272,256]{2,1,0:T(8,128)(2,1)S(1)}, bf16[2,272,256]{2,1,0:T(8,128)(2,1)S(1)}, u32[]{:S(2)}, u32[]{:S(2)}) collective-permute-start(bf16[2,272,256]{2,1,0:T(8,128)(2,1)S(1)} %fusion.26), channel_id=1, source_target_pairs={{0,4},{4,8},{8,12},{12,16},{16,20},{20,24},{24,28},{1,5},{5,9},{9,... | collective-permute-start | bytes 835592 | tf_op jit(solution)/shard_map/ppermute | solution.py:430
  75.3 5.9 %collective-permute-start.5 = (bf16[2,272,256]{2,1,0:T(8,128)(2,1)S(1)}, bf16[2,272,256]{2,1,0:T(8,128)(2,1)S(1)}, u32[]{:S(2)}, u32[]{:S(2)}) collective-permute-start(bf16[2,272,256]{2,1,0:T(8,128)(2,1)S(1)} %fusion.26), channel_id=1, source_target_pairs={{4,0},{8,4},{12,8},{16,12},{20,16},{24,20},{28,24},{5,1},{9,5},{13... | collective-permute-start | bytes 835592 | tf_op jit(solution)/shard_map/ppermute | solution.py:430
  77.6 3.6 %copy-start.1 = (bf16[2,272,256]{2,1,0:T(8,128)(2,1)}, bf16[2,272,256]{2,1,0:T(8,128)(2,1)S(1)}, u32[]{:S(2)}) copy-start(bf16[2,272,256]{2,1,0:T(8,128)(2,1)S(1)} %collective-permute-done.4.below) | copy-start | bytes 835588
  81.2 0.7 copy-start.2

commit v2 on v0

--- a/solution.py
+++ b/solution.py
@@ -3,6 +3,8 @@
 import jax
 import jax.numpy as jnp
 from jax import lax
+from jax.experimental import pallas as pl
+from jax.experimental.pallas import tpu as pltpu
 from jax.sharding import PartitionSpec as P
 
 SWEEPS = 5
@@ -159,6 +161,396 @@
     return jnp.transpose(returned, (2, 3, 1, 4, 0, 5)).reshape(block_members, 3, columns, latitudes)
 
 
+LANES = 128
+GROUPS = 23
+CELLS = 464
+F32 = jnp.float32
+BF16 = jnp.bfloat16
+VMEM_BYTES = 56 * 1024 * 1024
+
+
+def params():
+    return pltpu.CompilerParams(vmem_limit_bytes=VMEM_BYTES)
+
+
+def identity(size, dtype):
+    row = lax.broadcasted_iota(jnp.int32, (size, size), 0)
+    column = lax.broadcasted_iota(jnp.int32, (size, size), 1)
+    return (row == column).astype(F32).astype(dtype)
+
+
+def dot_nt(left, right):
+    return lax.dot_general(left, right, (((1,), (1,)), ((), ())), preferred_element_type=F32)
+
+
+def dot_nn(left, right):
+    return lax.dot_general(left, right, (((1,), (0,)), ((), ())), preferred_element_type=F32)
+
+
+def split(value):
+    high = value.astype(BF16)
+    return high, (value - high.astype(F32)).astype(BF16)
+
+
+def dot_3(left, right):
+    return dot_nn(left[0], right[0]) + (dot_nn(left[0], right[1]) + dot_nn(left[1], right[0]))
+
+
+def exchange_lanes(blocks, lane):
+    blocks = [list(pair) for pair in blocks]
+    for q in range(4):
+        low, high = blocks[q], blocks[q + 4]
+        blocks[q], blocks[q + 4] = [low[0], high[0]], [low[1], high[1]]
+    for bit in range(2):
+        step = 32 << bit
+        odd = (lane & step) != 0
+        for q in range(8):
+            if q & (1 << bit):
+                continue
+            for h in range(2):
+                low, high = blocks[q][h], blocks[q | (1 << bit)][h]
+                blocks[q][h] = jnp.where(odd, pltpu.roll(high, step, 1), low)
+                blocks[q | (1 << bit)][h] = jnp.where(odd, high, pltpu.roll(low, LANES - step, 1))
+    return blocks
+
+
+def group_of(variable, index):
+    if index < 3:
+        return variable * 3 + index
+    return 9 + variable if index == 3 else 12 + variable * 3 + index - 4
+
+
+def edge_kernel(first, last, depth, to_west, to_east):
+    for out, block, columns, near in ((to_west, first, (0, 1), 0), (to_east, last, (58, 59), 1)):
+        far = 1 - near
+        out[0] = block[0, near]
+        for plane, v, k in ((1, 2, near), (2, 1, near), (3, 1, far)):
+            deep = depth[columns[k] : columns[k] + 1, :]
+            out[plane] = (deep * block[v, k].astype(F32)).astype(BF16)
+
+
+def forecast_kernel(ens, left, right, depth, turn, out, deep, flux, height, staged):
+    columns, members, latitudes = ens.shape[1:]
+    rows = latitudes // 8
+    source = lax.broadcasted_iota(jnp.int32, (latitudes, latitudes), 0)
+    target = lax.broadcasted_iota(jnp.int32, (latitudes, latitudes), 1)
+    shift = (source == target + 1).astype(F32) - (source == target - 1).astype(F32)
+    shift = shift.astype(BF16)
+    turning = turn[0:1, :][None]
+
+    def rows_apart(value):
+        flat = value.reshape(-1, latitudes)
+        return dot_nn(flat, shift).reshape(value.shape)
+
+    for c in range(columns):
+        deep[c] = jnp.broadcast_to(depth[c : c + 1, :], (members, latitudes))
+    flux[0] = left[3].astype(F32)
+    flux[1] = left[2].astype(F32)
+    flux[columns + 2] = right[2].astype(F32)
+    flux[columns + 3] = right[3].astype(F32)
+    batch = 12
+
+    def fluxes(index, carry):
+        first = index * batch
+        east = ens[1, pl.ds(first, batch)].astype(F32)
+        flux[pl.ds(first + 2, batch)] = (deep[pl.ds(first, batch)] * east).astype(BF16).astype(F32)
+        return carry
+
+    lax.fori_loop(0, columns // batch, fluxes, 0)
+
+    def heights(index, carry):
+        first = index * batch
+        here = pl.ds(first, batch)
+        flux_north = (deep[here] * ens[2, here].astype(F32)).astype(BF16)
+        east_west = flux[pl.ds(first + 3, batch)] - flux[pl.ds(first + 1, batch)]
+        raised = ens[0, here].astype(F32) - half_step * (east_west + rows_apart(flux_north))
+        height[pl.ds(first + 1, batch)] = raised.astype(BF16)
+        return carry
+
+    lax.fori_loop(0, columns // batch, heights, 0)
+    for edge, at in ((left, 0), (right, columns + 1)):
+        east_west = flux[at + 2] - flux[at]
+        raised = edge[0].astype(F32) - half_step * (east_west + rows_apart(edge[1]))
+        height[at] = raised.astype(BF16)
+
+    eye = identity(latitudes, BF16)
+    staged[:, 460:464, :] = jnp.zeros((8, 4, 256), F32)
+
+    def put(block, g):
+        turned = dot_nt(eye, block.reshape(256, latitudes))
+        for s in range(8):
+            staged[s, rows * g : rows * (g + 1), :] = turned[rows * s : rows * (s + 1)]
+
+    def new_fields(first, count):
+        here = slice(first, first + count)
+        new_height = height[first + 1 : first + 1 + count]
+        east = ens[1, here].astype(F32)
+        north = ens[2, here].astype(F32)
+        ahead = height[first + 2 : first + 2 + count].astype(F32)
+        behind = height[first : first + count].astype(F32)
+        new_east = east + turning * north - half_step * (ahead - behind)
+        new_north = north - turning * east - half_step * rows_apart(new_height)
+        return new_height, new_east.astype(BF16), new_north.astype(BF16)
+
+    for index in range(7):
+        for v, field in enumerate(new_fields(8 * index, 8)):
+            put(field, group_of(v, index))
+    ends = new_fields(56, 4)
+    put(jnp.concatenate([ends[0], ends[1]], axis=0), 21)
+    put(jnp.concatenate([ends[2], jnp.zeros_like(ends[2])], axis=0), 22)
+    out[...] = staged[...].astype(BF16)
+
+
+def observe_kernel(cells, got, weight, target, held, gram, short, wide, seen):
+    lane = lax.broadcasted_iota(jnp.int32, (16, LANES), 1)
+
+    def spread_out(index, carry):
+        here = pl.ds(pl.multiple_of(index * 16, 16), 16)
+        spans = [slice(h * LANES, (h + 1) * LANES) for h in range(2)]
+        blocks = [[got[q, here, span].astype(F32) for span in spans] for q in range(8)]
+        blocks = exchange_lanes(blocks, lane)
+        for q in range(8):
+            to = pl.ds(pl.multiple_of(q * CELLS + index * 16, 16), 16)
+            for h in range(2):
+                wide[h, to, :] = blocks[q][h]
+                held[q, here, spans[h]] = blocks[q][h].astype(BF16)
+        return carry
+
+    lax.fori_loop(0, CELLS // 16, spread_out, 0)
+    slots = seen.shape[2]
+    unroll = 16
+
+    def pick(index, carry):
+        for t in range(2):
+            for k in range(unroll):
+                slot = index * unroll + k
+                row = cells[t, slot]
+                for h in range(2):
+                    seen[t, h, pl.ds(slot, 1), :] = wide[h, pl.ds(row, 1), :]
+        return carry
+
+    lax.fori_loop(0, slots // unroll, pick, 0)
+    eye = identity(256, BF16)
+    for t in range(2):
+        values = jnp.concatenate([seen[t, 0], seen[t, 1]], axis=1).astype(BF16)
+        turned = dot_nt(eye, values)
+        mean = jnp.sum(turned, axis=0, keepdims=True) * (1.0 / 256)
+        root = weight[t : t + 1, :]
+        spread = (root * (turned - mean)).astype(BF16)
+        misfit = (root * (target[t : t + 1, :] - mean)).astype(BF16)
+        block = dot_nt(spread, spread)
+        pull = dot_nt(jnp.broadcast_to(misfit, (16, slots)), spread)
+        gram[t, 0:256, :] = block
+        gram[t, 256:272, :] = pull
+        short[t, 0:256, :] = block.astype(BF16)
+        short[t, 256:272, :] = pull.astype(BF16)
+
+
+def analyse_kernel(held, gram, west, east, below, above, out, results):
+    size = 256
+    eye = identity(size, F32)
+    maps = []
+    for t in range(2):
+        beside = west[...].astype(F32) + gram[1] if t == 0 else gram[0] + east[...].astype(F32)
+        total = gram[t] + neighbour_weight * beside
+        total = total + neighbour_weight * (below[t].astype(F32) + above[t].astype(F32))
+        system = (size - 1) * eye + total[0:256]
+        pull = total[256:272]
+        square = jnp.sum(jnp.sum(system * system, axis=0, keepdims=True), axis=1, keepdims=True)
+        frobenius = jnp.sqrt(square)
+        root_part = system / frobenius
+        inverse_root = None
+        for sweep in range(SWEEPS):
+            if sweep == 0:
+                middle = 1.5 * eye - 0.5 * root_part
+                inverse_root = middle
+                root_part = dot_3(split(root_part), split(middle))
+            else:
+                inverse_parts, root_parts = split(inverse_root), split(root_part)
+                middle = 1.5 * eye - 0.5 * dot_3(inverse_parts, root_parts)
+                middle_parts = split(middle)
+                if sweep < SWEEPS - 1:
+                    root_part = dot_3(root_parts, middle_parts)
+                inverse_root = dot_3(middle_parts, inverse_parts)
+        inverse_parts = split(inverse_root)
+        half_pull = dot_3(split(pull), inverse_parts)
+        shift = dot_3(split(half_pull), inverse_parts) / frobenius
+        scale = math.sqrt(size - 1) / jnp.sqrt(frobenius)
+        maps.append((inverse_root * scale + shift[0:1]).astype(BF16))
+    average = jnp.full((size, size), 1.0 / size, BF16)
+    near = lax.broadcasted_iota(jnp.int32, (16, size), 0) < 4
+
+    for q in range(8):
+        cells = held[q]
+        mean = dot_nn(cells, average)
+        anomaly = (cells.astype(F32) - mean).astype(BF16)
+        if q < 6:
+            results[q, 0:240] = mean[0:240] + dot_nt(anomaly[0:240], maps[0])
+            results[q, 240:464] = mean[240:464] + dot_nt(anomaly[240:464], maps[1])
+        else:
+            first = dot_nt(anomaly[0:192], maps[0])
+            second = dot_nt(anomaly[176:464], maps[1])
+            results[q, 0:176] = mean[0:176] + first[0:176]
+            results[q, 176:192] = mean[176:192] + jnp.where(near, first[176:192], second[0:16])
+            results[q, 192:464] = mean[192:464] + second[16:288]
+    lane = lax.broadcasted_iota(jnp.int32, (16, LANES), 1)
+
+    def gather_in(index, carry):
+        here = pl.ds(pl.multiple_of(index * 16, 16), 16)
+        spans = [slice(h * LANES, (h + 1) * LANES) for h in range(2)]
+        blocks = [[results[q, here, span] for span in spans] for q in range(8)]
+        blocks = exchange_lanes(blocks, lane)
+        for q in range(8):
+            for h in range(2):
+                out[q, here, spans[h]] = blocks[q][h].astype(BF16)
+        return carry
+
+    lax.fori_loop(0, CELLS // 16, gather_in, 0)
+
+
+def return_kernel(got, out, wide, turned):
+    members, latitudes = out.shape[2:]
+    rows = latitudes // 8
+    wide[...] = got[...].astype(F32)
+    eye = identity(256, BF16)
+
+    def take(g):
+        for s in range(8):
+            turned[g, rows * s : rows * (s + 1), :] = wide[s, rows * g : rows * (g + 1), :]
+        block = dot_nt(eye, turned[g].astype(BF16)).astype(BF16)
+        return block.reshape(8, members, latitudes)
+
+    for v in range(3):
+        for index in range(7):
+            out[v, 8 * index : 8 * index + 8] = take(group_of(v, index))
+    mixed = take(21)
+    out[0, 56:60] = mixed[0:4]
+    out[1, 56:60] = mixed[4:8]
+    out[2, 56:60] = take(22)[0:4]
+
+
+def around(value, axis, step):
+    count = lax.axis_size(axis)
+    return lax.ppermute(value, axis, [(i, (i + step) % count) for i in range(count)])
+
+
+def along(value, axis, step):
+    count = lax.axis_size(axis)
+    pairs = [(i, i + step) for i in range(count) if 0 <= i + step < count]
+    return lax.ppermute(value, axis, pairs)
+
+
+def swap(value):
+    return lax.all_to_all(value, "mem", split_axis=0, concat_axis=0, tiled=True)
+
+
+def cell_rows(cell):
+    variable = cell // 600
+    tile = jnp.arange(2, dtype=jnp.int32)[:, None]
+    column = tile * 30 + cell // 20 % 30
+    index = column // 8
+    place = column % 8
+    group = jnp.where(index < 3, variable * 3 + index, 8 + variable * 3 + index)
+    group = jnp.where(index == 3, 9 + variable, group)
+    is_last = column >= 56
+    group = jnp.where(is_last, 21 + variable // 2, group)
+    place = jnp.where(is_last, column - 56 + 4 * (variable % 2), place)
+    return place * CELLS + group * 20 + cell % 20
+
+
+def on_device_fast(
+    ensemble, layer_depth, observed_cell, observed_value, error_variance, observed_count
+):
+    members, _, columns, latitudes = ensemble.shape
+    slots = observed_cell.shape[2]
+    planes = jnp.transpose(ensemble, (1, 2, 0, 3))
+    edge = jax.ShapeDtypeStruct((4, members, latitudes), BF16)
+    pair = (3, 2, members, latitudes)
+    whole = pl.BlockSpec((4, members, latitudes), lambda i: (0, 0, 0))
+    to_west, to_east = pl.pallas_call(
+        edge_kernel,
+        grid=(1,),
+        out_shape=(edge, edge),
+        in_specs=[
+            pl.BlockSpec(pair, lambda i: (0, 0, 0, 0)),
+            pl.BlockSpec(pair, lambda i: (0, columns // 2 - 1, 0, 0)),
+            pl.BlockSpec((columns, latitudes), lambda i: (0, 0)),
+        ],
+        out_specs=(whole, whole),
+        compiler_params=params(),
+        name="edges",
+    )(planes, planes, layer_depth)
+    left = around(to_east, "band", 1)
+    right = around(to_west, "band", -1)
+    turning = jnp.broadcast_to(coriolis(latitudes)[None], (8, latitudes))
+    sent = pl.pallas_call(
+        forecast_kernel,
+        out_shape=jax.ShapeDtypeStruct((8, CELLS, 256), BF16),
+        scratch_shapes=[
+            pltpu.VMEM((columns, members, latitudes), F32),
+            pltpu.VMEM((columns + 4, members, latitudes), F32),
+            pltpu.VMEM((columns + 2, members, latitudes), BF16),
+            pltpu.VMEM((8, CELLS, 256), F32),
+        ],
+        compiler_params=params(),
+        name="forecast",
+    )(planes, left, right, layer_depth, turning)
+    got = swap(sent)
+
+    rows = cell_rows(observed_cell[0])
+    live = jnp.arange(slots, dtype=jnp.int32)[None, :] < observed_count[0][:, None]
+    root = jnp.sqrt(jnp.where(live, 1.0 / error_variance[0], 0.0))
+    vmem = pl.BlockSpec(memory_space=pltpu.VMEM)
+    held, gram, short = pl.pallas_call(
+        observe_kernel,
+        out_shape=(
+            jax.ShapeDtypeStruct((8, CELLS, 256), BF16),
+            jax.ShapeDtypeStruct((2, 272, 256), F32),
+            jax.ShapeDtypeStruct((2, 272, 256), BF16),
+        ),
+        in_specs=[pl.BlockSpec(memory_space=pltpu.SMEM), vmem, vmem, vmem],
+        scratch_shapes=[
+            pltpu.VMEM((2, 8 * CELLS, LANES), F32),
+            pltpu.VMEM((2, 2, slots, LANES), F32),
+        ],
+        compiler_params=params(),
+        name="observe",
+    )(rows, got, root, observed_value[0])
+
+    west = around(short[1], "band", 1)
+    east = around(short[0], "band", -1)
+    beside = jnp.stack([west.astype(F32) + gram[1], gram[0] + east.astype(F32)])
+    short = (gram + neighbour_weight * beside).astype(BF16)
+    below = along(short, "mem", 1)
+    above = along(short, "mem", -1)
+    back = pl.pallas_call(
+        analyse_kernel,
+        out_shape=jax.ShapeDtypeStruct((8, CELLS, 256), BF16),
+        scratch_shapes=[pltpu.VMEM((8, CELLS, 256), F32)],
+        compiler_params=params(),
+        name="analyse",
+    )(held, gram, west, east, below, above)
+    returned = swap(back)
+    planes = pl.pallas_call(
+        return_kernel,
+        out_shape=jax.ShapeDtypeStruct(planes.shape, BF16),
+        scratch_shapes=[
+            pltpu.VMEM((8, CELLS, 256), F32),
+            pltpu.VMEM((GROUPS, latitudes, 256), F32),
+        ],
+        compiler_params=params(),
+        name="come_back",
+    )(returned)
+    return jnp.transpose(planes, (2, 0, 1, 3))
+
+
+def choose(ensemble, layer_depth, observed_cell, *rest):
+    shape = (lax.axis_size("mem"), ensemble.shape, observed_cell.shape[1])
+    fits = shape == (8, (32, 3, 60, 160), 2) and observed_cell.shape[2] % 16 == 0
+    chosen = on_device_fast if fits else on_device
+    return chosen(ensemble, layer_depth, observed_cell, *rest)
+
+
 def solution(mesh):
     in_specs = (
         P("mem", None, "band", None),
@@ -170,5 +562,5 @@
     )
     out_specs = P("mem", None, "band", None)
     return jax.shard_map(
-        on_device, mesh=mesh, in_specs=in_specs, out_specs=out_specs, check_vma=False
-    )
+        choose, mesh=mesh, in_specs=in_specs, out_specs=out_specs, check_vma=False
+    )

time: 282 us -> 128 us (0.45)
  local copies, waits for them, and re-layouts: 115 us -> 3.67 us
  Pallas kernels: 0 us -> 38.4 us
  waiting for transfers between devices: 68.4 us -> 34.2 us
  other arithmetic: 28.9 us -> 2.65 us
  matrix products: 15.1 us -> 0 us
  starting transfers between devices: 23.5 us -> 16.7 us
  blocking collectives: 28.6 us -> 32.1 us
    reshape x3 -> x0, local copies, waits for them, and re-layouts: 40.3 us -> none  [the longest x2 31.3 us: on_device(): jnp.transpose(returned, (2, 3, 1, 4, 0, 5))]
    pallas_call x0 -> x5, Pallas kernels: none -> 38.4 us  [the longest x1 15.8 us: on_device_fast(): pl.pallas_call(analyse_kernel, out_shape=jax.ShapeDtypeStruct((8, CELLS,...]
    ppermute x12 -> x6, waiting for transfers between devices: 43.4 us -> 11.1 us  [the longest x4 9.95 us: around(): lax.ppermute(value, axis, [(i, (i + step) % count) for i in range(count)])]
    transpose x1 -> x0, local copies, waits for them, and re-layouts: 24.9 us -> none  [on_device(): jnp.transpose(reordered, (4, 2, 0, 1, 3, 5))]
    transpose x1 -> x0, other arithmetic: 17 us -> none  [on_device(): jnp.transpose(reordered, (4, 2, 0, 1, 3, 5))]
    another operation x3 -> x0, local copies, waits for them, and re-layouts: 15.8 us -> none  [on_device(): jnp.stack([surface_elevation_cast, revised_zonal_velocity.astype(jnp.bflo...]
    dot_general x19 -> x0, matrix products: 15.1 us -> none  [the longest x5 3.37 us: newton_schulz(): jnp.einsum('tij,tjk->tik', inverse_root, root_part, precision=lax.Precisi...]
    all_to_all x3 -> x0, local copies, waits for them, and re-layouts: 9.28 us -> none  [the longest x2 7.75 us: on_device(): lax.all_to_all(analysed[None], 'mem', split_axis=2, concat_axis=0, tiled=...]
  transfers between devices with their start and end apart: 13 -> 7, of which waited for: 6 -> 6; matrix products, arithmetic and copies ran while one was open for 3% -> 1% of each run, Pallas kernels for 0% -> 0%
where the time goes in v2:
time: 128 us
  Pallas kernels  38.4 us (30%)
  waiting for transfers between devices  34.2 us (27%)
  blocking collectives  32.1 us (25%)
  starting transfers between devices  16.7 us (13%)
  local copies, waits for them, and re-layouts  3.67 us (3%)
  other arithmetic  2.65 us (2%)
    all_to_all x1, blocking collectives, swap(): return lax.all_to_all(value, 'mem', split_axis=0, concat_axis=0, tiled=True)  32.1 us
    all_to_all x1, waiting for transfers between devices, swap(): return lax.all_to_all(value, 'mem', split_axis=0, concat_axis=0, tiled=True)  23.2 us
    pallas_call x1, Pallas kernels, on_device_fast(): pl.pallas_call(analyse_kernel, out_shape=jax.ShapeDtypeStruct((8, CELLS,...  15.8 us
    pallas_call x1, Pallas kernels, on_device_fast(): pl.pallas_call(observe_kernel, out_shape=(jax.ShapeDtypeStruct((8, CELLS,...  10.4 us
    ppermute x4, waiting for transfers between devices, around(): lax.ppermute(value, axis, [(i, (i + step) % count) for i in range(count)])  9.95 us
    ppermute x4, starting transfers between devices, around(): lax.ppermute(value, axis, [(i, (i + step) % count) for i in range(count)])  8.45 us
    pallas_call x1, Pallas kernels, on_device_fast(): pl.pallas_call(forecast_kernel, out_shape=jax.ShapeDtypeStruct((8, CELLS,...  6.42 us
    ppermute x2, starting transfers between devices, along(): return lax.ppermute(value, axis, pairs)  4.34 us
  transfers between devices with their start and end apart: 7, of which 6 were waited for; matrix products, arithmetic and copies ran while one was open for 1% of the time, Pallas kernels for 0%

profile of v2, /device:TPU:0, one launch (start us, length us, event | category | flops | bytes accessed | tf_op | source)
XLA Modules:
  0.0 127.8 jit_solution(13695575528003869321)
XLA Ops:
  0.0 1.6 %edges.1 = (bf16[4,32,160]{2,1,0:T(8,128)(2,1)}, bf16[4,32,160]{2,1,0:T(8,128)(2,1)}) custom-call(bf16[3,60,32,160]{3,2,1,0:T(8,128)(2,1)} %bitcast.58, bf16[3,60,32,160]{3,2,1,0:T(8,128)(2,1)} %bitcast.59, f32[60,160]{1,0:T(8,128)} %depth.3), custom_call_target="tpu_custom_call" | custom-call | tf_op jit(solution)/shard_map/edges/pallas_call | solution.py:470
  1.6 3.0 %collective-permute-start = (bf16[4,32,160]{2,1,0:T(8,128)(2,1)}, bf16[4,32,160]{2,1,0:T(8,128)(2,1)S(1)}, u32[]{:S(2)}, u32[]{:S(2)}) collective-permute-start(bf16[4,32,160]{2,1,0:T(8,128)(2,1)} %get-tuple-element.10), channel_id=1, source_target_pairs={{0,1},{1,2},{2,3},{3,0},{4,5},{5,6},{6,7},{7,4},{8,9},{9,10},{10,1... | collective-permute-start | bytes 122888 | tf_op jit(solution)/shard_map/ppermute | solution.py:434
  4.6 2.0 %collective-permute-start.1 = (bf16[4,32,160]{2,1,0:T(8,128)(2,1)}, bf16[4,32,160]{2,1,0:T(8,128)(2,1)S(1)}, u32[]{:S(2)}, u32[]{:S(2)}) collective-permute-start(bf16[4,32,160]{2,1,0:T(8,128)(2,1)} %get-tuple-element.11), channel_id=1, source_target_pairs={{0,3},{1,0},{2,1},{3,2},{4,7},{5,4},{6,5},{7,6},{8,11},{9,8},{10,9... | collective-permute-start | bytes 122888 | tf_op jit(solution)/shard_map/ppermute | solution.py:434
  6.7 2.6 %collective-permute-done.left = bf16[4,32,160]{2,1,0:T(8,128)(2,1)S(1)} collective-permute-done((bf16[4,32,160]{2,1,0:T(8,128)(2,1)}, bf16[4,32,160]{2,1,0:T(8,128)(2,1)S(1)}, u32[]{:S(2)}, u32[]{:S(2)}) %collective-permute-start) | collective-permute-done | bytes 40992 | tf_op jit(solution)/shard_map/ppermute | solution.py:434
  9.8 0.6 broadcast_in_dim.5.turn
  10.4 6.4 %forecast.1 = bf16[8,464,256]{2,1,0:T(8,128)(2,1)} custom-call(bf16[3,60,32,160]{3,2,1,0:T(8,128)(2,1)} %bitcast.60, bf16[4,32,160]{2,1,0:T(8,128)(2,1)} %copy-done.6, bf16[4,32,160]{2,1,0:T(8,128)(2,1)} %copy-done.7, f32[60,160]{1,0:T(8,128)} %depth.3, f32[8,160]{1,0:T(8,128)} %broadcast_in_dim.5.turn), custom_call_target="tpu_custom_call" | custom-call | tf_op jit(solution)/shard_map/forecast/pallas_call | solution.py:486
  16.9 3.9 %all-to-all-start = ((bf16[8,464,256]{2,1,0:T(8,128)(2,1)}), bf16[8,464,256]{2,1,0:T(8,128)(2,1)S(1)}, u32[]{:S(2)}, u32[]{:S(2)}) async-start(bf16[8,464,256]{2,1,0:T(8,128)(2,1)} %forecast.1), calls=%async_computation | async-start | bytes 3801088 | tf_op jit(solution)/shard_map/all_to_all | solution.py:444
  20.7 0.7 fusion.13.cells
  21.4 0.7 fusion.14.weight
  22.1 23.2 %all-to-all-done.got = bf16[8,464,256]{2,1,0:T(8,128)(2,1)S(1)} async-done(((bf16[8,464,256]{2,1,0:T(8,128)(2,1)}), bf16[8,464,256]{2,1,0:T(8,128)(2,1)S(1)}, u32[]{:S(2)}, u32[]{:S(2)}) %all-to-all-start) | async-done | bytes 1900576 | tf_op jit(solution)/shard_map/all_to_all | solution.py:444
  45.3 1.2 copy-done
  46.5 10.4 %observe.1 = (bf16[8,464,256]{2,1,0:T(8,128)(2,1)}, f32[2,272,256]{2,1,0:T(8,128)}, bf16[2,272,256]{2,1,0:T(8,128)(2,1)}) custom-call(s32[2,512]{1,0:T(2,128)} %fusion.13.cells, bf16[8,464,256]{2,1,0:T(8,128)(2,1)} %copy-done, f32[2,512]{1,0:T(2,128)} %fusion.14.weight, f32[2,512]{1,0:T(2,128)} %bitcast.61), custom_call_target="tpu_custom_call" | custom-call | tf_op jit(solution)/shard_map/observe/pallas_call | solution.py:504
  56.9 1.1 slice_bitcast_fusion
  58.0 3.4 %collective-permute-start.3 = (bf16[272,256]{1,0:T(8,128)(2,1)S(1)}, bf16[272,256]{1,0:T(8,128)(2,1)S(1)}, u32[]{:S(2)}, u32[]{:S(2)}) collective-permute-start(bf16[272,256]{1,0:T(8,128)(2,1)S(1)} %get-tuple-element.17), channel_id=1, source_target_pairs={{0,3},{1,0},{2,1},{3,2},{4,7},{5,4},{6,5},{7,6},{8,11},{9,8},{10,9... | collective-permute-start | bytes 417800 | tf_op jit(solution)/shard_map/ppermute | solution.py:434
  61.4 2.6 %collective-permute-done.3.east = bf16[272,256]{1,0:T(8,128)(2,1)S(1)} collective-permute-done((bf16[272,256]{1,0:T(8,128)(2,1)S(1)}, bf16[272,256]{1,0:T(8,128)(2,1)S(1)}, u32[]{:S(2)}, u32[]{:S(2)}) %collective-permute-start.3) | collective-permute-done | bytes 139296 | tf_op jit(solution)/shard_map/ppermute | solution.py:434
  64.0 4.3 %collective-permute-done.2.west = bf16[272,256]{1,0:T(8,128)(2,1)S(1)} collective-permute-done((bf16[272,256]{1,0:T(8,128)(2,1)S(1)}, bf16[272,256]{1,0:T(8,128)(2,1)S(1)}, u32[]{:S(2)}, u32[]{:S(2)}) %collective-permute-start.2) | collective-permute-done | bytes 139296 | tf_op jit(solution)/shard_map/ppermute | solution.py:434
  68.2 1.2 fusion.3
  69.5 1.3 %collective-permute-start.5 = (bf16[2,272,256]{2,1,0:T(8,128)(2,1)S(1)}, bf16[2,272,256]{2,1,0:T(8,128)(2,1)S(1)}, u32[]{:S(2)}, u32[]{:S(2)}) collective-permute-start(bf16[2,272,256]{2,1,0:T(8,128)(2,1)S(1)} %fusion.1), channel_id=1, source_target_pairs={{4,0},{8,4},{12,8},{16,12},{20,16},{24,20},{28,24},{5,1},{9,5},{13... | collective-permute-start | bytes 835592 | tf_op jit(solution)/shard_map/ppermute | solution.py:440
  70.8 3.0 %collective-permute-start.4 = (bf16[2,272,256]{2,1,0:T(8,128)(2,1)S(1)}, bf16[2,272,256]{2,1,0:T(8,128)(2,1)S(1)}, u32[]{:S(2)}, u32[]{:S(2)}) collective-permute-start(bf16[2,272,256]{2,1,0:T(8,128)(2,1)S(1)} %fusion.1), channel_id=1, source_target_pairs={{0,4},{4,8},{8,12},{12,16},{16,20},{20,24},{24,28},{1,5},{5,9},{9,... | collective-permute-start | bytes 835592 | tf_op jit(solution)/shard_map/ppermute | solution.py:440
  73.9 1.1 collective-permute-done.4.below
  75.0 0.7 copy-done.5
  75.7 15.8 %analyse.1 = bf16[8,464,256]{2,1,0:T(8,128)(2,1)} custom-call(bf16[8,464,256]{2,1,0:T(8,128)(2,1)} %get-tuple-element.12.held, f32[2,272,256]{2,1,0:T(8,128)} %get-tuple-element.13.gram, bf16[272,256]{1,0:T(8,128)(2,1)} %copy-done.3, bf16[272,256]{1,0:T(8,128)(2,1)} %copy-done.2, bf16[2,272,256]{2,1,0:T(8,128)(2,1)} %copy-done.5, bf16[2,272,256]{2,1,0:T(8,128)(2,1)} %copy-done.4), custom_call_target="tpu_custom_call" | custom-call | tf_op jit(solution)/shard_map/analyse/pallas_call | solution.py:526
  91.5 32.1 %all_to_all.10.got = bf16[8,464,256]{2,1,0:T(8,128)(2,1)} all-to-all(bf16[8,464,256]{2,1,0:T(8,128)(2,1)} %analyse.1), channel_id=1, replica_groups=mesh['mem'=8,'band'=4] {'mem'}, dimensions={0} | all-to-all | bytes 3801088 | tf_op jit(solution)/shard_map/all_to_all | solution.py:444
  123.6 4.2 %come_back.1 = bf16[3,60,32,160]{3,2,1,0:T(8,128)(2,1)} custom-call(bf16[8,464,256]{2,1,0:T(8,128)(2,1)} %all_to_all.10.got), custom_call_target="tpu_custom_call" | custom-call | tf_op jit(solution)/shard_map/come_back/pallas_call | solution.py:534
  (26 shorter events, 0.7 us)
Async XLA Ops:
  1.6 7.7 %collective-permute-start = (bf16[4,32,160]{2,1,0:T(8,128)(2,1)}, bf16[4,32,160]{2,1,0:T(8,128)(2,1)S(1)}, u32[]{:S(2)}, u32[]{:S(2)}) collective-permute-start(bf16[4,32,160]{2,1,0:T(8,128)(2,1)} %get-tuple-element.10), channel_id=1, source_target_pairs={{0,1},{1,2},{2,3},{3,0},{4,5},{5,6},{6,7},{7,4},{8,9},{9,10},{10,1... | collective-permute-start | bytes 122888 | tf_op jit(solution)/shard_map/ppermute | solution.py:434
  4.6 5.2 %collective-permute-start.1 = (bf16[4,32,160]{2,1,0:T(8,128)(2,1)}, bf16[4,32,160]{2,1,0:T(8,128)(2,1)S(1)}, u32[]{:S(2)}, u32[]{:S(2)}) collective-permute-start(bf16[4,32,160]{2,1,0:T(8,128)(2,1)} %get-tuple-element.11), channel_id=1, source_target_pairs={{0,3},{1,0},{2,1},{3,2},{4,7},{5,4},{6,5},{7,6},{8,11},{9,8},{10,9... | collective-permute-start | bytes 122888 | tf_op jit(solution)/shard_map/ppermute | solution.py:434
  9.3 1.2 copy-start.6
  9.8 0.6 copy-start.7
  16.9 3.9 %copy-start.8 = (s32[1,2,512]{2,1,0:T(2,128)S(1)}, s32[1,2,512]{2,1,0:T(2,128)}, u32[]{:S(2)}) copy-start(s32[1,2,512]{2,1,0:T(2,128)} %param.8) | copy-start | bytes 12292
  16.9 4.6 %copy-start.9 = (f32[1,2,512]{2,1,0:T(2,128)S(1)}, f32[1,2,512]{2,1,0:T(2,128)}, u32[]{:S(2)}) copy-start(f32[1,2,512]{2,1,0:T(2,128)} %param.10) | copy-start | bytes 12292
  16.9 4.6 %copy-start.10 = (s32[1,2]{1,0:T(1,128)S(1)}, s32[1,2]{1,0:T(1,128)}, u32[]{:S(2)}) copy-start(s32[1,2]{1,0:T(1,128)} %param.11) | copy-start | bytes 28
  16.9 28.4 %all-to-all-start = ((bf16[8,464,256]{2,1,0:T(8,128)(2,1)}), bf16[8,464,256]{2,1,0:T(8,128)(2,1)S(1)}, u32[]{:S(2)}, u32[]{:S(2)}) async-start(bf16[8,464,256]{2,1,0:T(8,128)(2,1)} %forecast.1), calls=%async_computation | async-start | bytes 3801088 | tf_op jit(solution)/shard_map/all_to_all | solution.py:444
  45.3 1.2 copy-start
  56.9 12.5 %copy-start.1 = (f32[2,272,256]{2,1,0:T(8,128)S(1)}, f32[2,272,256]{2,1,0:T(8,128)}, u32[]{:S(2)}) copy-start(f32[2,272,256]{2,1,0:T(8,128)} %get-tuple-element.13.gram) | copy-start | bytes 1671172
  58.0 6.0 %collective-permute-start.3 = (bf16[272,256]{1,0:T(8,128)(2,1)S(1)}, bf16[272,256]{1,0:T(8,128)(2,1)S(1)}, u32[]{:S(2)}, u32[]{:S(2)}) collective-permute-start(bf16[272,256]{1,0:T(8,128)(2,1)S(1)} %get-tuple-element.17), channel_id=1, source_target_pairs={{0,3},{1,0},{2,1},{3,2},{4,7},{5,4},{6,5},{7,6},{8,11},{9,8},{10,9... | collective-permute-start | bytes 417800 | tf_op jit(solution)/shard_map/ppermute | solution.py:434
  61.4 6.9 %collective-permute-start.2 = (bf16[272,256]{1,0:T(8,128)(2,1)S(1)}, bf16[272,256]{1,0:T(8,128)(2,1)S(1)}, u32[]{:S(2)}, u32[]{:S(2)}) collective-permute-start(bf16[272,256]{1,0:T(8,128)(2,1)S(1)} %get-tuple-element.18), channel_id=1, source_target_pairs={{0,1},{1,2},{2,3},{3,0},{4,5},{5,6},{6,7},{7,4},{8,9},{9,10},{10,1... | collective-permute-start | bytes 417800 | tf_op jit(solution)/shard_map/ppermute | solution.py:434
  64.0 11.0 %copy-start.2 = (bf16[272,256]{1,0:T(8,128)(2,1)}, bf16[272,256]{1,0:T(8,128)(2,1)S(1)}, u32[]{:S(2)}) copy-start(bf16[272,256]{1,0:T(8,128)(2,1)S(1)} %collective-permute-done.3.east) | copy-start | bytes 417796
  68.2 6.8 %copy-start.3 = (bf16[272,256]{1,0:T(8,128)(2,1)}, bf16[272,256]{1,0:T(8,128)(2,1)S(1)}, u32[]{:S(2)}) copy-start(bf16[272,256]{1,0:T(8,128)(2,1)S(1)} %collective-permute-done.2.west) | copy-start | bytes 417796
  69.5 4.4 %collective-permute-start.5 = (bf16[2,272,256]{2,1,0:T(8,128)(2,1)S(1)}, bf16[2,272,256]{2,1,0:T(8,128)(2,1)S(1)}, u32[]{:S(2)}, u32[]{:S(2)}) collective-permute-start(bf16[2,272,256]{2,1,0:T(8,128)(2,1)S(1)} %fusion.1), channel_id=1, source_target_pairs={{4,0},{8,4},{12,8},{16,12},{20,16},{24,20},{28,24},{5,1},{9,5},{13... | collective-permute-start | bytes 835592 | tf_op jit(solution)/shard_map/ppermute | solution.py:440
  70.8 4.2 %collective-permute-start.4 = (bf16[2,272,256]{2,1,0:T(8,128)(2,1)S(1)}, bf16[2,272,256]{2,1,0:T(8,128)(2,1)S(1)}, u32[]{:S(2)}, u32[]{:S(2)}) collective-permute-start(bf16[2,272,256]{2,1,0:T(8,128)(2,1)S(1)} %fusion.1), channel_id=1, source_target_pairs={{0,4},{4,8},{8,12},{12,16},{16,20},{20,24},{24,28},{1,5},{5,9},{9,... | collective-permute-start | bytes 835592 | tf_op jit(solution)/shard_map/ppermute | solution.py:440
  73.8 1.1 copy-start.4
  75.0 0.7 copy-start.5

commit v3 on v2

--- a/solution.py
+++ b/solution.py
@@ -2,6 +2,7 @@
 
 import jax
 import jax.numpy as jnp
+import numpy as np
 from jax import lax
 from jax.experimental import pallas as pl
 from jax.experimental.pallas import tpu as pltpu
@@ -166,11 +167,12 @@
 CELLS = 464
 F32 = jnp.float32
 BF16 = jnp.bfloat16
-VMEM_BYTES = 56 * 1024 * 1024
-
-
-def params():
-    return pltpu.CompilerParams(vmem_limit_bytes=VMEM_BYTES)
+PACKED = 144
+MIB = 1024 * 1024
+
+
+def params(size):
+    return pltpu.CompilerParams(vmem_limit_bytes=size * MIB)
 
 
 def identity(size, dtype):
@@ -192,8 +194,39 @@
     return high, (value - high.astype(F32)).astype(BF16)
 
 
-def dot_3(left, right):
-    return dot_nn(left[0], right[0]) + (dot_nn(left[0], right[1]) + dot_nn(left[1], right[0]))
+def left_3(parts):
+    return jnp.concatenate([parts[0], parts[0], parts[1]], axis=1)
+
+
+def right_3(parts):
+    return jnp.concatenate([parts[0], parts[1], parts[0]], axis=0)
+
+
+def triangle(size):
+    row = lax.broadcasted_iota(jnp.int32, (size, size), 0)
+    column = lax.broadcasted_iota(jnp.int32, (size, size), 1)
+    return row, column
+
+
+def packed(block, pull):
+    row, column = triangle(128)
+    last = block[128:256, 128:256]
+    corner = jnp.where(row >= column, block[0:128, 0:128], last)
+    middle = jnp.sum(jnp.where(row == column, last, 0.0), axis=0, keepdims=True)
+    middle = jnp.concatenate([jnp.zeros_like(middle), middle], axis=1)
+    top = jnp.concatenate([block[128:256, 0:128], corner], axis=1)
+    return jnp.concatenate([top, pull, jnp.broadcast_to(middle, (8, 256))], axis=0)
+
+
+def unpacked(value):
+    row, column = triangle(128)
+    low, corner = value[0:128, 0:128], value[0:128, 128:256]
+    other = jnp.transpose(corner)
+    first = jnp.where(row >= column, corner, other)
+    last = jnp.where(row < column, corner, other)
+    last = jnp.where(row == column, value[136:137, 128:256], last)
+    top = jnp.concatenate([first, jnp.transpose(low)], axis=1)
+    return jnp.concatenate([top, jnp.concatenate([low, last], axis=1)], axis=0), value[128:136]
 
 
 def exchange_lanes(blocks, lane):
@@ -307,16 +340,16 @@
     def spread_out(index, carry):
         here = pl.ds(pl.multiple_of(index * 16, 16), 16)
         spans = [slice(h * LANES, (h + 1) * LANES) for h in range(2)]
-        blocks = [[got[q, here, span].astype(F32) for span in spans] for q in range(8)]
+        blocks = [[got[q, here, span] for span in spans] for q in range(8)]
         blocks = exchange_lanes(blocks, lane)
         for q in range(8):
             to = pl.ds(pl.multiple_of(q * CELLS + index * 16, 16), 16)
             for h in range(2):
-                wide[h, to, :] = blocks[q][h]
-                held[q, here, spans[h]] = blocks[q][h].astype(BF16)
+                wide[h, to, :] = blocks[q][h].astype(F32)
+                held[q, here, spans[h]] = blocks[q][h]
         return carry
 
-    lax.fori_loop(0, CELLS // 16, spread_out, 0)
+    lax.fori_loop(0, CELLS // 16, spread_out, 0, unroll=4)
     slots = seen.shape[2]
     unroll = 16
 
@@ -340,43 +373,50 @@
         misfit = (root * (target[t : t + 1, :] - mean)).astype(BF16)
         block = dot_nt(spread, spread)
         pull = dot_nt(jnp.broadcast_to(misfit, (16, slots)), spread)
-        gram[t, 0:256, :] = block
-        gram[t, 256:272, :] = pull
-        short[t, 0:256, :] = block.astype(BF16)
-        short[t, 256:272, :] = pull.astype(BF16)
-
-
-def analyse_kernel(held, gram, west, east, below, above, out, results):
+        whole = packed(block, pull[0:8])
+        gram[t] = whole
+        short[t] = whole.astype(BF16)
+
+
+def combine_kernel(gram, below, above, column, to_west, to_east):
+    total = gram[...] + neighbour_weight * (below[...].astype(F32) + above[...].astype(F32))
+    column[...] = total
+    to_west[...] = total[0].astype(BF16)
+    to_east[...] = total[1].astype(BF16)
+
+
+def analyse_kernel(held, column, west, east, out, results):
     size = 256
     eye = identity(size, F32)
+    beside = (west[...].astype(F32) + column[1], column[0] + east[...].astype(F32))
+    norms, pulls, roots, inverses = [], [], [], []
+    for t in range(2):
+        block, pull = unpacked(column[t] + neighbour_weight * beside[t])
+        system = (size - 1) * eye + block
+        square = jnp.sum(jnp.sum(system * system, axis=0, keepdims=True), axis=1, keepdims=True)
+        norms.append(jnp.sqrt(square))
+        pulls.append(pull)
+        roots.append(system / norms[t])
+    for sweep in range(SWEEPS):
+        rights = [right_3(split(root)) for root in roots]
+        if sweep == 0:
+            inverses = [1.5 * eye - 0.5 * root for root in roots]
+            lefts = [left_3(split(inverse)) for inverse in inverses]
+            roots = [dot_nn(left, right) for left, right in zip(lefts, rights)]
+            continue
+        parts = [split(inverse) for inverse in inverses]
+        products = [dot_nn(left_3(part), right) for part, right in zip(parts, rights)]
+        middles = [left_3(split(1.5 * eye - 0.5 * product)) for product in products]
+        if sweep < SWEEPS - 1:
+            roots = [dot_nn(middle, right) for middle, right in zip(middles, rights)]
+        inverses = [dot_nn(middle, right_3(part)) for middle, part in zip(middles, parts)]
     maps = []
     for t in range(2):
-        beside = west[...].astype(F32) + gram[1] if t == 0 else gram[0] + east[...].astype(F32)
-        total = gram[t] + neighbour_weight * beside
-        total = total + neighbour_weight * (below[t].astype(F32) + above[t].astype(F32))
-        system = (size - 1) * eye + total[0:256]
-        pull = total[256:272]
-        square = jnp.sum(jnp.sum(system * system, axis=0, keepdims=True), axis=1, keepdims=True)
-        frobenius = jnp.sqrt(square)
-        root_part = system / frobenius
-        inverse_root = None
-        for sweep in range(SWEEPS):
-            if sweep == 0:
-                middle = 1.5 * eye - 0.5 * root_part
-                inverse_root = middle
-                root_part = dot_3(split(root_part), split(middle))
-            else:
-                inverse_parts, root_parts = split(inverse_root), split(root_part)
-                middle = 1.5 * eye - 0.5 * dot_3(inverse_parts, root_parts)
-                middle_parts = split(middle)
-                if sweep < SWEEPS - 1:
-                    root_part = dot_3(root_parts, middle_parts)
-                inverse_root = dot_3(middle_parts, inverse_parts)
-        inverse_parts = split(inverse_root)
-        half_pull = dot_3(split(pull), inverse_parts)
-        shift = dot_3(split(half_pull), inverse_parts) / frobenius
-        scale = math.sqrt(size - 1) / jnp.sqrt(frobenius)
-        maps.append((inverse_root * scale + shift[0:1]).astype(BF16))
+        right = right_3(split(inverses[t]))
+        half_pull = dot_nn(left_3(split(pulls[t])), right)
+        shift = dot_nn(left_3(split(half_pull)), right) / norms[t]
+        scale = math.sqrt(size - 1) / jnp.sqrt(norms[t])
+        maps.append((inverses[t] * scale + shift[0:1]).astype(BF16))
     average = jnp.full((size, size), 1.0 / size, BF16)
     near = lax.broadcasted_iota(jnp.int32, (16, size), 0) < 4
 
@@ -385,14 +425,16 @@
         mean = dot_nn(cells, average)
         anomaly = (cells.astype(F32) - mean).astype(BF16)
         if q < 6:
-            results[q, 0:240] = mean[0:240] + dot_nt(anomaly[0:240], maps[0])
-            results[q, 240:464] = mean[240:464] + dot_nt(anomaly[240:464], maps[1])
+            first = mean[0:240] + dot_nt(anomaly[0:240], maps[0])
+            second = mean[240:464] + dot_nt(anomaly[240:464], maps[1])
+            results[q, 0:240] = first.astype(BF16)
+            results[q, 240:464] = second.astype(BF16)
         else:
-            first = dot_nt(anomaly[0:192], maps[0])
-            second = dot_nt(anomaly[176:464], maps[1])
-            results[q, 0:176] = mean[0:176] + first[0:176]
-            results[q, 176:192] = mean[176:192] + jnp.where(near, first[176:192], second[0:16])
-            results[q, 192:464] = mean[192:464] + second[16:288]
+            first = mean[0:192] + dot_nt(anomaly[0:192], maps[0])
+            second = mean[176:464] + dot_nt(anomaly[176:464], maps[1])
+            results[q, 0:176] = first[0:176].astype(BF16)
+            results[q, 176:192] = jnp.where(near, first[176:192], second[0:16]).astype(BF16)
+            results[q, 192:464] = second[16:288].astype(BF16)
     lane = lax.broadcasted_iota(jnp.int32, (16, LANES), 1)
 
     def gather_in(index, carry):
@@ -402,10 +444,10 @@
         blocks = exchange_lanes(blocks, lane)
         for q in range(8):
             for h in range(2):
-                out[q, here, spans[h]] = blocks[q][h].astype(BF16)
+                out[q, here, spans[h]] = blocks[q][h]
         return carry
 
-    lax.fori_loop(0, CELLS // 16, gather_in, 0)
+    lax.fori_loop(0, CELLS // 16, gather_in, 0, unroll=4)
 
 
 def return_kernel(got, out, wide, turned):
@@ -477,12 +519,14 @@
             pl.BlockSpec((columns, latitudes), lambda i: (0, 0)),
         ],
         out_specs=(whole, whole),
-        compiler_params=params(),
+        compiler_params=params(8),
         name="edges",
     )(planes, planes, layer_depth)
     left = around(to_east, "band", 1)
     right = around(to_west, "band", -1)
-    turning = jnp.broadcast_to(coriolis(latitudes)[None], (8, latitudes))
+    position = (np.arange(latitudes) + 0.5) / latitudes - 0.5
+    turning = coriolis_scale * np.sin(math.pi * position)
+    turning = jnp.asarray(np.broadcast_to(turning.astype(np.float32), (8, latitudes)))
     sent = pl.pallas_call(
         forecast_kernel,
         out_shape=jax.ShapeDtypeStruct((8, CELLS, 256), BF16),
@@ -492,7 +536,7 @@
             pltpu.VMEM((columns + 2, members, latitudes), BF16),
             pltpu.VMEM((8, CELLS, 256), F32),
         ],
-        compiler_params=params(),
+        compiler_params=params(24),
         name="forecast",
     )(planes, left, right, layer_depth, turning)
     got = swap(sent)
@@ -505,31 +549,36 @@
         observe_kernel,
         out_shape=(
             jax.ShapeDtypeStruct((8, CELLS, 256), BF16),
-            jax.ShapeDtypeStruct((2, 272, 256), F32),
-            jax.ShapeDtypeStruct((2, 272, 256), BF16),
+            jax.ShapeDtypeStruct((2, PACKED, 256), F32),
+            jax.ShapeDtypeStruct((2, PACKED, 256), BF16),
         ),
         in_specs=[pl.BlockSpec(memory_space=pltpu.SMEM), vmem, vmem, vmem],
         scratch_shapes=[
             pltpu.VMEM((2, 8 * CELLS, LANES), F32),
             pltpu.VMEM((2, 2, slots, LANES), F32),
         ],
-        compiler_params=params(),
+        compiler_params=params(20),
         name="observe",
     )(rows, got, root, observed_value[0])
 
-    west = around(short[1], "band", 1)
-    east = around(short[0], "band", -1)
-    beside = jnp.stack([west.astype(F32) + gram[1], gram[0] + east.astype(F32)])
-    short = (gram + neighbour_weight * beside).astype(BF16)
     below = along(short, "mem", 1)
     above = along(short, "mem", -1)
+    one_tile = jax.ShapeDtypeStruct((PACKED, 256), BF16)
+    column, to_west, to_east = pl.pallas_call(
+        combine_kernel,
+        out_shape=(jax.ShapeDtypeStruct(gram.shape, F32), one_tile, one_tile),
+        compiler_params=params(8),
+        name="combine",
+    )(gram, below, above)
+    west = around(to_east, "band", 1)
+    east = around(to_west, "band", -1)
     back = pl.pallas_call(
         analyse_kernel,
         out_shape=jax.ShapeDtypeStruct((8, CELLS, 256), BF16),
-        scratch_shapes=[pltpu.VMEM((8, CELLS, 256), F32)],
-        compiler_params=params(),
+        scratch_shapes=[pltpu.VMEM((8, CELLS, 256), BF16)],
+        compiler_params=params(20),
         name="analyse",
-    )(held, gram, west, east, below, above)
+    )(held, column, west, east)
     returned = swap(back)
     planes = pl.pallas_call(
         return_kernel,
@@ -538,7 +587,7 @@
             pltpu.VMEM((8, CELLS, 256), F32),
             pltpu.VMEM((GROUPS, latitudes, 256), F32),
         ],
-        compiler_params=params(),
+        compiler_params=params(24),
         name="come_back",
     )(returned)
     return jnp.transpose(planes, (2, 0, 1, 3))

time: 128 us -> 103 us (0.80)
  Pallas kernels: 38.4 us -> 19.6 us
  blocking collectives: 32.1 us -> 29.6 us
  other arithmetic: 2.65 us -> 0.18 us
  waiting for transfers between devices: 34.2 us -> 32.2 us
    pallas_call x1, Pallas kernels: 15.8 us -> 7.55 us  [on_device_fast(): pl.pallas_call(analyse_kernel, out_shape=jax.ShapeDtypeStruct((8, CELLS,...]
    pallas_call x1, Pallas kernels: 10.4 us -> 5.97 us  [on_device_fast(): pl.pallas_call(observe_kernel, out_shape=(jax.ShapeDtypeStruct((8, CELLS,...]
    pallas_call x1, Pallas kernels: 6.42 us -> 3.29 us  [on_device_fast(): pl.pallas_call(forecast_kernel, out_shape=jax.ShapeDtypeStruct((8, CELLS,...]
    ppermute x4, waiting for transfers between devices: 9.95 us -> 6.88 us  [around(): lax.ppermute(value, axis, [(i, (i + step) % count) for i in range(count)])]
    all_to_all x1, blocking collectives: 32.1 us -> 29.6 us  [swap(): return lax.all_to_all(value, 'mem', split_axis=0, concat_axis=0, tiled=True)]
    unnamed x22 -> x20, local copies, waits for them, and re-layouts: 2 us -> 3.94 us
    pallas_call x1, Pallas kernels: 1.6 us -> 0.02 us  [on_device_fast(): pl.pallas_call(edge_kernel, grid=(1,), out_shape=(edge, edge), in_specs=[...]
    pallas_call x1, Pallas kernels: 4.19 us -> 2.67 us  [on_device_fast(): pl.pallas_call(return_kernel, out_shape=jax.ShapeDtypeStruct(planes.shape...]
  transfers between devices with their start and end apart: 7 -> 7, of which waited for: 6 -> 6; matrix products, arithmetic and copies ran while one was open for 1% -> 0% of each run, Pallas kernels for 0% -> 0%
where the time goes in v3:
time: 103 us
  waiting for transfers between devices  32.2 us (31%)
  blocking collectives  29.6 us (29%)
  Pallas kernels  19.6 us (19%)
  starting transfers between devices  17.2 us (17%)
  local copies, waits for them, and re-layouts  3.95 us (4%)
    all_to_all x1, blocking collectives, swap(): return lax.all_to_all(value, 'mem', split_axis=0, concat_axis=0, tiled=True)  29.6 us
    all_to_all x1, waiting for transfers between devices, swap(): return lax.all_to_all(value, 'mem', split_axis=0, concat_axis=0, tiled=True)  24.3 us
    ppermute x4, starting transfers between devices, around(): lax.ppermute(value, axis, [(i, (i + step) % count) for i in range(count)])  9.04 us
    pallas_call x1, Pallas kernels, on_device_fast(): pl.pallas_call(analyse_kernel, out_shape=jax.ShapeDtypeStruct((8, CELLS,...  7.55 us
    ppermute x4, waiting for transfers between devices, around(): lax.ppermute(value, axis, [(i, (i + step) % count) for i in range(count)])  6.88 us
    pallas_call x1, Pallas kernels, on_device_fast(): pl.pallas_call(observe_kernel, out_shape=(jax.ShapeDtypeStruct((8, CELLS,...  5.97 us
    ppermute x2, starting transfers between devices, along(): return lax.ppermute(value, axis, pairs)  4.33 us
    unnamed x20, local copies, waits for them, and re-layouts  3.94 us
  transfers between devices with their start and end apart: 7, of which 6 were waited for; matrix products, arithmetic and copies ran while one was open for 0% of the time, Pallas kernels for 0%

profile of v3, /device:TPU:0, one launch (start us, length us, event | category | flops | bytes accessed | tf_op | source)
XLA Modules:
  0.0 102.8 jit_solution(11615001886588097470)
XLA Ops:
  0.0 1.8 %copy-done = bf16[32,3,60,160]{3,0,2,1:T(8,128)(2,1)S(1)} copy-done((bf16[32,3,60,160]{3,0,2,1:T(8,128)(2,1)S(1)}, bf16[32,3,60,160]{3,0,2,1:T(8,128)(2,1)}, u32[]{:S(2)}) %copy-start) | copy-done | bytes 1843224
  1.8 0.8 copy-done.3
  2.7 3.1 %collective-permute-start = (bf16[4,32,160]{2,1,0:T(8,128)(2,1)S(1)}, bf16[4,32,160]{2,1,0:T(8,128)(2,1)S(1)}, u32[]{:S(2)}, u32[]{:S(2)}) collective-permute-start(bf16[4,32,160]{2,1,0:T(8,128)(2,1)S(1)} %get-tuple-element.13), channel_id=1, source_target_pairs={{0,1},{1,2},{2,3},{3,0},{4,5},{5,6},{6,7},{7,4},{8,9},{9,10},{10,1... | collective-permute-start | bytes 122888 | tf_op jit(solution)/shard_map/ppermute | solution.py:476
  5.8 2.1 %collective-permute-start.1 = (bf16[4,32,160]{2,1,0:T(8,128)(2,1)S(1)}, bf16[4,32,160]{2,1,0:T(8,128)(2,1)S(1)}, u32[]{:S(2)}, u32[]{:S(2)}) collective-permute-start(bf16[4,32,160]{2,1,0:T(8,128)(2,1)S(1)} %get-tuple-element.14), channel_id=1, source_target_pairs={{0,3},{1,0},{2,1},{3,2},{4,7},{5,4},{6,5},{7,6},{8,11},{9,8},{10,9... | collective-permute-start | bytes 122888 | tf_op jit(solution)/shard_map/ppermute | solution.py:476
  7.9 2.3 %collective-permute-done.left = bf16[4,32,160]{2,1,0:T(8,128)(2,1)S(1)} collective-permute-done((bf16[4,32,160]{2,1,0:T(8,128)(2,1)S(1)}, bf16[4,32,160]{2,1,0:T(8,128)(2,1)S(1)}, u32[]{:S(2)}, u32[]{:S(2)}) %collective-permute-start) | collective-permute-done | bytes 40992 | tf_op jit(solution)/shard_map/ppermute | solution.py:476
  10.2 0.5 collective-permute-done.1.right
  10.8 3.3 %forecast.1 = bf16[8,464,256]{2,1,0:T(8,128)(2,1)S(1)} custom-call(bf16[3,60,32,160]{3,2,1,0:T(8,128)(2,1)S(1)} %bitcast.44, bf16[4,32,160]{2,1,0:T(8,128)(2,1)S(1)} %collective-permute-done.left, bf16[4,32,160]{2,1,0:T(8,128)(2,1)S(1)} %collective-permute-done.1.right, f32[60,160]{1,0:T(8,128)S(1)} %copy-done.4, f32[8,160]{1,0:T(8,128)S(1)} %jit_solution_.3.turn), custom_call_target="tpu_custom_call" | custom-call | tf_op jit(solution)/shard_map/forecast/pallas_call | solution.py:530
  14.1 1.2 %copy-done.2 = bf16[8,464,256]{2,1,0:T(8,128)(2,1)} copy-done((bf16[8,464,256]{2,1,0:T(8,128)(2,1)}, bf16[8,464,256]{2,1,0:T(8,128)(2,1)S(1)}, u32[]{:S(2)}) %copy-start.2) | copy-done | bytes 1900568
  15.3 3.9 %all-to-all-start = ((bf16[8,464,256]{2,1,0:T(8,128)(2,1)}), bf16[8,464,256]{2,1,0:T(8,128)(2,1)S(1)}, u32[]{:S(2)}, u32[]{:S(2)}) async-start(bf16[8,464,256]{2,1,0:T(8,128)(2,1)} %copy-done.2), calls=%async_computation | async-start | bytes 3801088 | tf_op jit(solution)/shard_map/all_to_all | solution.py:486
  19.2 0.1 fusion.9.cells
  19.3 0.1 fusion.10.weight
  19.4 24.3 %all-to-all-done.got = bf16[8,464,256]{2,1,0:T(8,128)(2,1)S(1)} async-done(((bf16[8,464,256]{2,1,0:T(8,128)(2,1)}), bf16[8,464,256]{2,1,0:T(8,128)(2,1)S(1)}, u32[]{:S(2)}, u32[]{:S(2)}) %all-to-all-start) | async-done | bytes 1900576 | tf_op jit(solution)/shard_map/all_to_all | solution.py:486
  43.7 6.0 %observe.1 = (bf16[8,464,256]{2,1,0:T(8,128)(2,1)S(1)}, f32[2,144,256]{2,1,0:T(8,128)S(1)}, bf16[2,144,256]{2,1,0:T(8,128)(2,1)S(1)}) custom-call(s32[2,512]{1,0:T(2,128)S(1)} %fusion.9.cells, bf16[8,464,256]{2,1,0:T(8,128)(2,1)S(1)} %all-to-all-done.got, f32[2,512]{1,0:T(2,128)S(1)} %fusion.10.weight, f32[2,512]{1,0:T(2,128)S(1)} %bitcast.45), custom_call_target="tpu_custom_call" | custom-call | tf_op jit(solution)/shard_map/observe/pallas_call | solution.py:548
  49.7 1.3 %collective-permute-start.3 = (bf16[2,144,256]{2,1,0:T(8,128)(2,1)S(1)}, bf16[2,144,256]{2,1,0:T(8,128)(2,1)S(1)}, u32[]{:S(2)}, u32[]{:S(2)}) collective-permute-start(bf16[2,144,256]{2,1,0:T(8,128)(2,1)S(1)} %get-tuple-element.17), channel_id=1, source_target_pairs={{4,0},{8,4},{12,8},{16,12},{20,16},{24,20},{28,24},{5,1},{9,5},{13... | collective-permute-start | bytes 442376 | tf_op jit(solution)/shard_map/ppermute | solution.py:482
  51.0 3.0 %collective-permute-start.2 = (bf16[2,144,256]{2,1,0:T(8,128)(2,1)S(1)}, bf16[2,144,256]{2,1,0:T(8,128)(2,1)S(1)}, u32[]{:S(2)}, u32[]{:S(2)}) collective-permute-start(bf16[2,144,256]{2,1,0:T(8,128)(2,1)S(1)} %get-tuple-element.17), channel_id=1, source_target_pairs={{0,4},{4,8},{8,12},{12,16},{16,20},{20,24},{24,28},{1,5},{5,9},{9,... | collective-permute-start | bytes 442376 | tf_op jit(solution)/shard_map/ppermute | solution.py:482
  54.1 1.0 collective-permute-done.2.below
  55.0 0.1 combine.1
  55.1 1.2 %collective-permute-start.4 = (bf16[144,256]{1,0:T(8,128)(2,1)S(1)}, bf16[144,256]{1,0:T(8,128)(2,1)S(1)}, u32[]{:S(2)}, u32[]{:S(2)}) collective-permute-start(bf16[144,256]{1,0:T(8,128)(2,1)S(1)} %get-tuple-element.19), channel_id=1, source_target_pairs={{0,1},{1,2},{2,3},{3,0},{4,5},{5,6},{6,7},{7,4},{8,9},{9,10},{10,1... | collective-permute-start | bytes 221192 | tf_op jit(solution)/shard_map/ppermute | solution.py:476
  56.3 2.7 %collective-permute-start.5 = (bf16[144,256]{1,0:T(8,128)(2,1)S(1)}, bf16[144,256]{1,0:T(8,128)(2,1)S(1)}, u32[]{:S(2)}, u32[]{:S(2)}) collective-permute-start(bf16[144,256]{1,0:T(8,128)(2,1)S(1)} %get-tuple-element.20), channel_id=1, source_target_pairs={{0,3},{1,0},{2,1},{3,2},{4,7},{5,4},{6,5},{7,6},{8,11},{9,8},{10,9... | collective-permute-start | bytes 221192 | tf_op jit(solution)/shard_map/ppermute | solution.py:476
  59.0 3.0 %collective-permute-done.4.west = bf16[144,256]{1,0:T(8,128)(2,1)S(1)} collective-permute-done((bf16[144,256]{1,0:T(8,128)(2,1)S(1)}, bf16[144,256]{1,0:T(8,128)(2,1)S(1)}, u32[]{:S(2)}, u32[]{:S(2)}) %collective-permute-start.4) | collective-permute-done | bytes 73760 | tf_op jit(solution)/shard_map/ppermute | solution.py:476
  62.0 1.0 collective-permute-done.5.east
  63.0 7.6 %analyse.1 = bf16[8,464,256]{2,1,0:T(8,128)(2,1)S(1)} custom-call(bf16[8,464,256]{2,1,0:T(8,128)(2,1)S(1)} %get-tuple-element.15.held, f32[2,144,256]{2,1,0:T(8,128)S(1)} %get-tuple-element.18.column, bf16[144,256]{1,0:T(8,128)(2,1)S(1)} %collective-permute-done.4.west, bf16[144,256]{1,0:T(8,128)(2,1)S(1)} %collective-permute-done.5.east), custom_call_target="tpu_custom_call" | custom-call | tf_op jit(solution)/shard_map/analyse/pallas_call | solution.py:575
  70.5 29.6 %all_to_all.10.got = bf16[8,464,256]{2,1,0:T(8,128)(2,1)S(1)} all-to-all(bf16[8,464,256]{2,1,0:T(8,128)(2,1)S(1)} %analyse.1), channel_id=1, replica_groups=mesh['mem'=8,'band'=4] {'mem'}, dimensions={0} | all-to-all | bytes 3801088 | tf_op jit(solution)/shard_map/all_to_all | solution.py:486
  100.1 2.7 %come_back.1 = bf16[3,60,32,160]{3,2,1,0:T(8,128)(2,1)} custom-call(bf16[8,464,256]{2,1,0:T(8,128)(2,1)S(1)} %all_to_all.10.got), custom_call_target="tpu_custom_call" | custom-call | tf_op jit(solution)/shard_map/come_back/pallas_call | solution.py:583
  (21 shorter events, 0.1 us)
Async XLA Ops:
  0.0 1.8 %copy-start = (bf16[32,3,60,160]{3,0,2,1:T(8,128)(2,1)S(1)}, bf16[32,3,60,160]{3,0,2,1:T(8,128)(2,1)}, u32[]{:S(2)}) copy-start(bf16[32,3,60,160]{3,0,2,1:T(8,128)(2,1)} %param.7) | copy-start | bytes 5529604
  1.8 0.8 copy-start.3
  2.7 8.1 %copy-start.8 = (f32[160]{0:T(256)S(1)}, f32[160]{0:T(256)}, u32[]{:S(2)}) copy-start(f32[160]{0:T(256)} %constant.94.clone) | copy-start | bytes 1924
  2.7 8.1 %copy-start.1 = (bf16[32,3,60,160]{3,0,2,1:T(8,128)(2,1)S(1)}, bf16[32,3,60,160]{3,0,2,1:T(8,128)(2,1)}, u32[]{:S(2)}) copy-start(bf16[32,3,60,160]{3,0,2,1:T(8,128)(2,1)} %param.7) | copy-start | bytes 5529604
  2.7 8.1 %copy-start.4 = (f32[60,160]{1,0:T(8,128)S(1)}, f32[60,160]{1,0:T(8,128)}, u32[]{:S(2)}) copy-start(f32[60,160]{1,0:T(8,128)} %depth.3) | copy-start | bytes 115204
  2.7 7.5 %collective-permute-start = (bf16[4,32,160]{2,1,0:T(8,128)(2,1)S(1)}, bf16[4,32,160]{2,1,0:T(8,128)(2,1)S(1)}, u32[]{:S(2)}, u32[]{:S(2)}) collective-permute-start(bf16[4,32,160]{2,1,0:T(8,128)(2,1)S(1)} %get-tuple-element.13), channel_id=1, source_target_pairs={{0,1},{1,2},{2,3},{3,0},{4,5},{5,6},{6,7},{7,4},{8,9},{9,10},{10,1... | collective-permute-start | bytes 122888 | tf_op jit(solution)/shard_map/ppermute | solution.py:476
  5.8 5.0 %collective-permute-start.1 = (bf16[4,32,160]{2,1,0:T(8,128)(2,1)S(1)}, bf16[4,32,160]{2,1,0:T(8,128)(2,1)S(1)}, u32[]{:S(2)}, u32[]{:S(2)}) collective-permute-start(bf16[4,32,160]{2,1,0:T(8,128)(2,1)S(1)} %get-tuple-element.14), channel_id=1, source_target_pairs={{0,3},{1,0},{2,1},{3,2},{4,7},{5,4},{6,5},{7,6},{8,11},{9,8},{10,9... | collective-permute-start | bytes 122888 | tf_op jit(solution)/shard_map/ppermute | solution.py:476
  14.1 1.3 %copy-start.2 = (bf16[8,464,256]{2,1,0:T(8,128)(2,1)}, bf16[8,464,256]{2,1,0:T(8,128)(2,1)S(1)}, u32[]{:S(2)}) copy-start(bf16[8,464,256]{2,1,0:T(8,128)(2,1)S(1)} %forecast.1) | copy-start | bytes 5701636
  15.3 3.9 %copy-start.6 = (s32[1,2,512]{2,1,0:T(2,128)S(1)}, s32[1,2,512]{2,1,0:T(2,128)}, u32[]{:S(2)}) copy-start(s32[1,2,512]{2,1,0:T(2,128)} %param.9) | copy-start | bytes 12292
  15.3 4.0 %copy-start.7 = (f32[1,2,512]{2,1,0:T(2,128)S(1)}, f32[1,2,512]{2,1,0:T(2,128)}, u32[]{:S(2)}) copy-start(f32[1,2,512]{2,1,0:T(2,128)} %param.11) | copy-start | bytes 12292
  15.3 4.0 %copy-start.9 = (s32[1,2]{1,0:T(1,128)S(1)}, s32[1,2]{1,0:T(1,128)}, u32[]{:S(2)}) copy-start(s32[1,2]{1,0:T(1,128)} %param.12) | copy-start | bytes 28
  15.3 28.4 %copy-start.5 = (f32[1,2,512]{2,1,0:T(2,128)S(1)}, f32[1,2,512]{2,1,0:T(2,128)}, u32[]{:S(2)}) copy-start(f32[1,2,512]{2,1,0:T(2,128)} %param.10) | copy-start | bytes 12292
  15.3 28.4 %all-to-all-start = ((bf16[8,464,256]{2,1,0:T(8,128)(2,1)}), bf16[8,464,256]{2,1,0:T(8,128)(2,1)S(1)}, u32[]{:S(2)}, u32[]{:S(2)}) async-start(bf16[8,464,256]{2,1,0:T(8,128)(2,1)} %copy-done.2), calls=%async_computation | async-start | bytes 3801088 | tf_op jit(solution)/shard_map/all_to_all | solution.py:486
  49.7 4.3 %collective-permute-start.3 = (bf16[2,144,256]{2,1,0:T(8,128)(2,1)S(1)}, bf16[2,144,256]{2,1,0:T(8,128)(2,1)S(1)}, u32[]{:S(2)}, u32[]{:S(2)}) collective-permute-start(bf16[2,144,256]{2,1,0:T(8,128)(2,1)S(1)} %get-tuple-element.17), channel_id=1, source_target_pairs={{4,0},{8,4},{12,8},{16,12},{20,16},{24,20},{28,24},{5,1},{9,5},{13... | collective-permute-start | bytes 442376 | tf_op jit(solution)/shard_map/ppermute | solution.py:482
  51.0 4.0 %collective-permute-start.2 = (bf16[2,144,256]{2,1,0:T(8,128)(2,1)S(1)}, bf16[2,144,256]{2,1,0:T(8,128)(2,1)S(1)}, u32[]{:S(2)}, u32[]{:S(2)}) collective-permute-start(bf16[2,144,256]{2,1,0:T(8,128)(2,1)S(1)} %get-tuple-element.17), channel_id=1, source_target_pairs={{0,4},{4,8},{8,12},{12,16},{16,20},{20,24},{24,28},{1,5},{5,9},{9,... | collective-permute-start | bytes 442376 | tf_op jit(solution)/shard_map/ppermute | solution.py:482
  55.1 6.9 %collective-permute-start.4 = (bf16[144,256]{1,0:T(8,128)(2,1)S(1)}, bf16[144,256]{1,0:T(8,128)(2,1)S(1)}, u32[]{:S(2)}, u32[]{:S(2)}) collective-permute-start(bf16[144,256]{1,0:T(8,128)(2,1)S(1)} %get-tuple-element.19), channel_id=1, source_target_pairs={{0,1},{1,2},{2,3},{3,0},{4,5},{5,6},{6,7},{7,4},{8,9},{9,10},{10,1... | collective-permute-start | bytes 221192 | tf_op jit(solution)/shard_map/ppermute | solution.py:476
  56.3 6.7 %collective-permute-start.5 = (bf16[144,256]{1,0:T(8,128)(2,1)S(1)}, bf16[144,256]{1,0:T(8,128)(2,1)S(1)}, u32[]{:S(2)}, u32[]{:S(2)}) collective-permute-start(bf16[144,256]{1,0:T(8,128)(2,1)S(1)} %get-tuple-element.20), channel_id=1, source_target_pairs={{0,3},{1,0},{2,1},{3,2},{4,7},{5,4},{6,5},{7,6},{8,11},{9,8},{10,9... | collective-permute-start | bytes 221192 | tf_op jit(solution)/shard_map/ppermute | solution.py:476

commit v4 on v3

--- a/solution.py
+++ b/solution.py
@@ -165,6 +165,8 @@
 LANES = 128
 GROUPS = 23
 CELLS = 464
+INNER = 360
+OUTER = 104
 F32 = jnp.float32
 BF16 = jnp.bfloat16
 PACKED = 144
@@ -248,9 +250,11 @@
 
 
 def group_of(variable, index):
-    if index < 3:
-        return variable * 3 + index
-    return 9 + variable if index == 3 else 12 + variable * 3 + index - 4
+    if index == 0:
+        return 18 + variable
+    if index == 3:
+        return 9 + variable
+    return variable * 3 + index - 4 if index > 3 else 12 + variable * 2 + index - 1
 
 
 def edge_kernel(first, last, depth, to_west, to_east):
@@ -262,94 +266,163 @@
             out[plane] = (deep * block[v, k].astype(F32)).astype(BF16)
 
 
-def forecast_kernel(ens, left, right, depth, turn, out, deep, flux, height, staged):
-    columns, members, latitudes = ens.shape[1:]
-    rows = latitudes // 8
+def difference(latitudes):
     source = lax.broadcasted_iota(jnp.int32, (latitudes, latitudes), 0)
     target = lax.broadcasted_iota(jnp.int32, (latitudes, latitudes), 1)
     shift = (source == target + 1).astype(F32) - (source == target - 1).astype(F32)
-    shift = shift.astype(BF16)
+    return shift.astype(BF16)
+
+
+def rows_apart(value, shift):
+    flat = value.reshape(-1, value.shape[-1])
+    return dot_nn(flat, shift).reshape(value.shape)
+
+
+def fluxes(east, deep):
+    return (deep * east.astype(F32)).astype(BF16).astype(F32)
+
+
+def heights(field, north, deep, ahead, behind, shift):
+    flux_north = (deep * north.astype(F32)).astype(BF16)
+    raised = field.astype(F32) - half_step * ((ahead - behind) + rows_apart(flux_north, shift))
+    return raised.astype(BF16)
+
+
+def velocities(east, north, here, ahead, behind, turning, shift):
+    east, north = east.astype(F32), north.astype(F32)
+    apart = ahead.astype(F32) - behind.astype(F32)
+    new_east = east + turning * north - half_step * apart
+    new_north = north - turning * east - half_step * rows_apart(here, shift)
+    return new_east.astype(BF16), new_north.astype(BF16)
+
+
+def put_group(staged, block, eye, first):
+    latitudes = eye.shape[0]
+    rows = latitudes // 8
+    turned = dot_nt(eye, block.reshape(256, latitudes))
+    for s in range(8):
+        staged[s, first : first + rows, :] = turned[rows * s : rows * (s + 1)]
+
+
+def inner_kernel(ens, depth, turn, out, deep, flux, height, staged):
+    members, latitudes = ens.shape[2:]
+    shift = difference(latitudes)
     turning = turn[0:1, :][None]
-
-    def rows_apart(value):
-        flat = value.reshape(-1, latitudes)
-        return dot_nn(flat, shift).reshape(value.shape)
-
-    for c in range(columns):
-        deep[c] = jnp.broadcast_to(depth[c : c + 1, :], (members, latitudes))
-    flux[0] = left[3].astype(F32)
-    flux[1] = left[2].astype(F32)
-    flux[columns + 2] = right[2].astype(F32)
-    flux[columns + 3] = right[3].astype(F32)
-    batch = 12
-
-    def fluxes(index, carry):
-        first = index * batch
-        east = ens[1, pl.ds(first, batch)].astype(F32)
-        flux[pl.ds(first + 2, batch)] = (deep[pl.ds(first, batch)] * east).astype(BF16).astype(F32)
+    for c in range(6, 58):
+        deep[c - 6] = jnp.broadcast_to(depth[c : c + 1, :], (members, latitudes))
+
+    def flux_step(index, carry):
+        here = pl.ds(index * 13, 13)
+        flux[here] = fluxes(ens[1, pl.ds(index * 13 + 6, 13)], deep[here])
         return carry
 
-    lax.fori_loop(0, columns // batch, fluxes, 0)
-
-    def heights(index, carry):
-        first = index * batch
-        here = pl.ds(first, batch)
-        flux_north = (deep[here] * ens[2, here].astype(F32)).astype(BF16)
-        east_west = flux[pl.ds(first + 3, batch)] - flux[pl.ds(first + 1, batch)]
-        raised = ens[0, here].astype(F32) - half_step * (east_west + rows_apart(flux_north))
-        height[pl.ds(first + 1, batch)] = raised.astype(BF16)
+    lax.fori_loop(0, 4, flux_step, 0)
+
+    def height_step(index, carry):
+        first = index * 10
+        at = pl.ds(first + 7, 10)
+        ahead, behind = flux[pl.ds(first + 2, 10)], flux[pl.ds(first, 10)]
+        here = pl.ds(first + 1, 10)
+        height[here] = heights(ens[0, at], ens[2, at], deep[here], ahead, behind, shift)
         return carry
 
-    lax.fori_loop(0, columns // batch, heights, 0)
-    for edge, at in ((left, 0), (right, columns + 1)):
-        east_west = flux[at + 2] - flux[at]
-        raised = edge[0].astype(F32) - half_step * (east_west + rows_apart(edge[1]))
-        height[at] = raised.astype(BF16)
-
+    lax.fori_loop(0, 5, height_step, 0)
     eye = identity(latitudes, BF16)
-    staged[:, 460:464, :] = jnp.zeros((8, 4, 256), F32)
-
-    def put(block, g):
-        turned = dot_nt(eye, block.reshape(256, latitudes))
-        for s in range(8):
-            staged[s, rows * g : rows * (g + 1), :] = turned[rows * s : rows * (s + 1)]
-
-    def new_fields(first, count):
-        here = slice(first, first + count)
-        new_height = height[first + 1 : first + 1 + count]
-        east = ens[1, here].astype(F32)
-        north = ens[2, here].astype(F32)
-        ahead = height[first + 2 : first + 2 + count].astype(F32)
-        behind = height[first : first + count].astype(F32)
-        new_east = east + turning * north - half_step * (ahead - behind)
-        new_north = north - turning * east - half_step * rows_apart(new_height)
-        return new_height, new_east.astype(BF16), new_north.astype(BF16)
-
-    for index in range(7):
-        for v, field in enumerate(new_fields(8 * index, 8)):
-            put(field, group_of(v, index))
-    ends = new_fields(56, 4)
-    put(jnp.concatenate([ends[0], ends[1]], axis=0), 21)
-    put(jnp.concatenate([ends[2], jnp.zeros_like(ends[2])], axis=0), 22)
+    for index in range(1, 7):
+        first = 8 * index
+        at = slice(first, first + 8)
+        here = height[first - 6 : first + 2]
+        ahead, behind = height[first - 5 : first + 3], height[first - 7 : first + 1]
+        new = velocities(ens[1, at], ens[2, at], here, ahead, behind, turning, shift)
+        for v, field in enumerate((here,) + new):
+            put_group(staged, field, eye, 20 * group_of(v, index))
     out[...] = staged[...].astype(BF16)
 
 
-def observe_kernel(cells, got, weight, target, held, gram, short, wide, seen):
+def outer_kernel(ens, left, right, depth, turn, *refs):
+    outs, (flux, height, staged) = refs[:8], refs[8:]
+    members, latitudes = ens.shape[2:]
+    shift = difference(latitudes)
+    turning = turn[0:1, :][None]
+    eye = identity(latitudes, BF16)
+
+    def depths(first, count):
+        return jnp.stack(
+            [
+                jnp.broadcast_to(depth[c : c + 1, :], (members, latitudes))
+                for c in range(first, first + count)
+            ]
+        )
+
+    def window(edge, first, count, low, high):
+        is_left = low == 0
+        base = 2 if is_left else 0
+        flux[base : base + count] = fluxes(ens[1, first : first + count], depths(first, count))
+        at = 0 if is_left else count
+        near, far = (1, 0) if is_left else (at, at + 1)
+        flux[near] = edge[2].astype(F32)
+        flux[far] = edge[3].astype(F32)
+        wide = high - low + 1
+        skip = 0 if is_left else 1
+        columns = slice(first + skip, first + skip + wide)
+        new = heights(
+            ens[0, columns],
+            ens[2, columns],
+            depths(first + skip, wide),
+            flux[base + skip + 1 : base + skip + 1 + wide],
+            flux[base + skip - 1 : base + skip - 1 + wide],
+            shift,
+        )
+        start = 1 if is_left else 0
+        height[start : start + wide] = new
+        place = 0 if is_left else wide
+        middle = near
+        east_west = flux[middle + 1] - flux[middle - 1]
+        raised = edge[0].astype(F32) - half_step * (east_west + rows_apart(edge[1], shift))
+        height[place] = raised.astype(BF16)
+        count = high - low
+        here = height[1 : 1 + count]
+        ahead, behind = height[2 : 2 + count], height[0:count]
+        at = slice(low, high)
+        return (here,) + velocities(ens[1, at], ens[2, at], here, ahead, behind, turning, shift)
+
+    staged[:, 100:104, :] = jnp.zeros((8, 4, 256), F32)
+    for v, field in enumerate(window(left, 0, 10, 0, 8)):
+        put_group(staged, field, eye, 20 * v)
+    ends = window(right, 54, 6, 56, 60)
+    put_group(staged, jnp.concatenate([ends[0], ends[1]], axis=0), eye, 60)
+    put_group(staged, jnp.concatenate([ends[2], jnp.zeros_like(ends[2])], axis=0), eye, 80)
+    me = lax.axis_index("mem")
+    for d in range(8):
+        outs[d][...] = staged[me ^ d].astype(BF16)
+
+
+def observe_kernel(cells, weight, target, got, *refs):
+    edges, (held, gram, short, joined, wide, seen) = refs[:8], refs[8:]
     lane = lax.broadcasted_iota(jnp.int32, (16, LANES), 1)
-
-    def spread_out(index, carry):
-        here = pl.ds(pl.multiple_of(index * 16, 16), 16)
-        spans = [slice(h * LANES, (h + 1) * LANES) for h in range(2)]
-        blocks = [[got[q, here, span] for span in spans] for q in range(8)]
-        blocks = exchange_lanes(blocks, lane)
-        for q in range(8):
-            to = pl.ds(pl.multiple_of(q * CELLS + index * 16, 16), 16)
-            for h in range(2):
-                wide[h, to, :] = blocks[q][h].astype(F32)
-                held[q, here, spans[h]] = blocks[q][h]
-        return carry
-
-    lax.fori_loop(0, CELLS // 16, spread_out, 0, unroll=4)
+    me = lax.axis_index("mem")
+    for d in range(8):
+        joined[me ^ d, 8:112, :] = edges[d][...]
+    joined[:, 0:8, :] = got[:, 352:360, :]
+    spans = [slice(h * LANES, (h + 1) * LANES) for h in range(2)]
+
+    def spread_out(source, offset):
+        def step(index, carry):
+            here = pl.ds(pl.multiple_of(index * 16, 16), 16)
+            blocks = [[source[q, here, span] for span in spans] for q in range(8)]
+            blocks = exchange_lanes(blocks, lane)
+            there = pl.ds(pl.multiple_of(index * 16 + offset, 16), 16)
+            for q in range(8):
+                to = pl.ds(pl.multiple_of(q * CELLS + index * 16 + offset, 16), 16)
+                for h in range(2):
+                    wide[h, to, :] = blocks[q][h].astype(F32)
+                    held[q, there, spans[h]] = blocks[q][h]
+            return carry
+
+        return step
+
+    lax.fori_loop(0, 22, spread_out(got, 0), 0, unroll=4)
+    lax.fori_loop(0, 7, spread_out(joined, 352), 0, unroll=4)
     slots = seen.shape[2]
     unroll = 16
 
@@ -424,17 +497,19 @@
         cells = held[q]
         mean = dot_nn(cells, average)
         anomaly = (cells.astype(F32) - mean).astype(BF16)
-        if q < 6:
-            first = mean[0:240] + dot_nt(anomaly[0:240], maps[0])
-            second = mean[240:464] + dot_nt(anomaly[240:464], maps[1])
-            results[q, 0:240] = first.astype(BF16)
-            results[q, 240:464] = second.astype(BF16)
-        else:
-            first = mean[0:192] + dot_nt(anomaly[0:192], maps[0])
-            second = mean[176:464] + dot_nt(anomaly[176:464], maps[1])
-            results[q, 0:176] = first[0:176].astype(BF16)
-            results[q, 176:192] = jnp.where(near, first[176:192], second[0:16]).astype(BF16)
-            results[q, 192:464] = second[16:288].astype(BF16)
+        edge = 180 if q < 6 else 240
+        low, high = edge // 16 * 16, (edge + 15) // 16 * 16
+        second = mean[0:high] + dot_nt(anomaly[0:high], maps[1])
+        first = mean[low:432] + dot_nt(anomaly[low:432], maps[0])
+        last = mean[416:464] + dot_nt(anomaly[416:464], maps[1])
+        results[q, 0:low] = second[0:low].astype(BF16)
+        if low < high:
+            both = jnp.where(near, second[low:high], first[0:16])
+            results[q, low:high] = both.astype(BF16)
+        results[q, high:416] = first[high - low : 416 - low].astype(BF16)
+        both = jnp.where(near, first[416 - low : 432 - low], last[0:16])
+        results[q, 416:432] = both.astype(BF16)
+        results[q, 432:464] = last[16:48].astype(BF16)
     lane = lax.broadcasted_iota(jnp.int32, (16, LANES), 1)
 
     def gather_in(index, carry):
@@ -492,8 +567,9 @@
     column = tile * 30 + cell // 20 % 30
     index = column // 8
     place = column % 8
-    group = jnp.where(index < 3, variable * 3 + index, 8 + variable * 3 + index)
+    group = jnp.where(index > 3, variable * 3 + index - 4, 11 + variable * 2 + index)
     group = jnp.where(index == 3, 9 + variable, group)
+    group = jnp.where(index == 0, 18 + variable, group)
     is_last = column >= 56
     group = jnp.where(is_last, 21 + variable // 2, group)
     place = jnp.where(is_last, column - 56 + 4 * (variable % 2), place)
@@ -519,7 +595,7 @@
             pl.BlockSpec((columns, latitudes), lambda i: (0, 0)),
         ],
         out_specs=(whole, whole),
-        compiler_params=params(8),
+        compiler_params=params(60),
         name="edges",
     )(planes, planes, layer_depth)
     left = around(to_east, "band", 1)
@@ -528,18 +604,32 @@
     turning = coriolis_scale * np.sin(math.pi * position)
     turning = jnp.asarray(np.broadcast_to(turning.astype(np.float32), (8, latitudes)))
     sent = pl.pallas_call(
-        forecast_kernel,
-        out_shape=jax.ShapeDtypeStruct((8, CELLS, 256), BF16),
+        inner_kernel,
+        out_shape=jax.ShapeDtypeStruct((8, INNER, 256), BF16),
         scratch_shapes=[
-            pltpu.VMEM((columns, members, latitudes), F32),
-            pltpu.VMEM((columns + 4, members, latitudes), F32),
-            pltpu.VMEM((columns + 2, members, latitudes), BF16),
-            pltpu.VMEM((8, CELLS, 256), F32),
+            pltpu.VMEM((52, members, latitudes), F32),
+            pltpu.VMEM((52, members, latitudes), F32),
+            pltpu.VMEM((52, members, latitudes), BF16),
+            pltpu.VMEM((8, INNER, 256), F32),
         ],
         compiler_params=params(24),
-        name="forecast",
+        name="inner",
+    )(planes, layer_depth, turning)
+    got = swap(sent)
+    sent = pl.pallas_call(
+        outer_kernel,
+        out_shape=(jax.ShapeDtypeStruct((OUTER, 256), BF16),) * 8,
+        scratch_shapes=[
+            pltpu.VMEM((12, members, latitudes), F32),
+            pltpu.VMEM((10, members, latitudes), BF16),
+            pltpu.VMEM((8, OUTER, 256), F32),
+        ],
+        compiler_params=params(16),
+        name="outer",
     )(planes, left, right, layer_depth, turning)
-    got = swap(sent)
+    got_edges = [sent[0]]
+    for d in range(1, 8):
+        got_edges.append(lax.ppermute(sent[d], "mem", [(i, i ^ d) for i in range(8)]))
 
     rows = cell_rows(observed_cell[0])
     live = jnp.arange(slots, dtype=jnp.int32)[None, :] < observed_count[0][:, None]
@@ -552,14 +642,15 @@
             jax.ShapeDtypeStruct((2, PACKED, 256), F32),
             jax.ShapeDtypeStruct((2, PACKED, 256), BF16),
         ),
-        in_specs=[pl.BlockSpec(memory_space=pltpu.SMEM), vmem, vmem, vmem],
+        in_specs=[pl.BlockSpec(memory_space=pltpu.SMEM)] + [vmem] * 11,
         scratch_shapes=[
+            pltpu.VMEM((8, 112, 256), BF16),
             pltpu.VMEM((2, 8 * CELLS, LANES), F32),
             pltpu.VMEM((2, 2, slots, LANES), F32),
         ],
         compiler_params=params(20),
         name="observe",
-    )(rows, got, root, observed_value[0])
+    )(rows, root, observed_value[0], got, *got_edges)
 
     below = along(short, "mem", 1)
     above = along(short, "mem", -1)

time: 103 us -> 99.6 us (0.967)
  waiting for transfers between devices: 32.2 us -> 16.9 us
  starting transfers between devices: 17.2 us -> 24.5 us
  Pallas kernels: 19.6 us -> 24.5 us
    all_to_all x1, waiting for transfers between devices: 24.3 us -> 0.01 us  [swap(): return lax.all_to_all(value, 'mem', split_axis=0, concat_axis=0, tiled=True)]
    ppermute x0 -> x7, waiting for transfers between devices: none -> 7.84 us  [on_device_fast(): lax.ppermute(sent[d], 'mem', [(i, i ^ d) for i in range(8)])]
    ppermute x0 -> x7, starting transfers between devices: none -> 6.52 us  [on_device_fast(): lax.ppermute(sent[d], 'mem', [(i, i ^ d) for i in range(8)])]
    pallas_call x1, Pallas kernels: 0.02 us -> 1.78 us  [on_device_fast(): pl.pallas_call(edge_kernel, grid=(1,), out_shape=(edge, edge), in_specs=[...]
    pallas_call x1 -> x2, Pallas kernels: 3.29 us -> 4.67 us  [the longest x1 3.76 us: on_device_fast(): pl.pallas_call(inner_kernel, out_shape=jax.ShapeDtypeStruct((8, INNER, 25...]
    all_to_all x1, starting transfers between devices: 3.86 us -> 5.17 us  [swap(): return lax.all_to_all(value, 'mem', split_axis=0, concat_axis=0, tiled=True)]
    unnamed x20 -> x16, local copies, waits for them, and re-layouts: 3.94 us -> 2.7 us
    ppermute x4, waiting for transfers between devices: 6.88 us -> 8.11 us  [around(): lax.ppermute(value, axis, [(i, (i + step) % count) for i in range(count)])]
  transfers between devices with their start and end apart: 7 -> 14, of which waited for: 6 -> 9; matrix products, arithmetic and copies ran while one was open for 0% -> 0% of each run, Pallas kernels for 0% -> 3%
where the time goes in v4:
time: 99.6 us; the launch traced here: 99.2 us
  blocking collectives  29.6 us (30%)
  Pallas kernels  24.5 us (25%)
  starting transfers between devices  24.5 us (25%)
  waiting for transfers between devices  16.9 us (17%)
  local copies, waits for them, and re-layouts  3.38 us (3%)
    all_to_all x1, blocking collectives, swap(): return lax.all_to_all(value, 'mem', split_axis=0, concat_axis=0, tiled=True)  29.6 us
    ppermute x4, starting transfers between devices, around(): lax.ppermute(value, axis, [(i, (i + step) % count) for i in range(count)])  8.46 us
    pallas_call x1, Pallas kernels, on_device_fast(): pl.pallas_call(analyse_kernel, out_shape=jax.ShapeDtypeStruct((8, CELLS,...  8.18 us
    ppermute x4, waiting for transfers between devices, around(): lax.ppermute(value, axis, [(i, (i + step) % count) for i in range(count)])  8.11 us
    ppermute x7, waiting for transfers between devices, on_device_fast(): lax.ppermute(sent[d], 'mem', [(i, i ^ d) for i in range(8)])  7.84 us
    pallas_call x1, Pallas kernels, on_device_fast(): pl.pallas_call(observe_kernel, out_shape=(jax.ShapeDtypeStruct((8, CELLS,...  7.17 us
    ppermute x7, starting transfers between devices, on_device_fast(): lax.ppermute(sent[d], 'mem', [(i, i ^ d) for i in range(8)])  6.52 us
    all_to_all x1, starting transfers between devices, swap(): return lax.all_to_all(value, 'mem', split_axis=0, concat_axis=0, tiled=True)  5.17 us
  transfers between devices with their start and end apart: 14, of which 9 were waited for; matrix products, arithmetic and copies ran while one was open for 0% of the time, Pallas kernels for 3%

profile of v4, /device:TPU:0, one launch (start us, length us, event | category | flops | bytes accessed | tf_op | source)
XLA Modules:
  0.0 99.2 jit_solution(6144707969673376083)
XLA Ops:
  0.7 1.8 %copy-done = bf16[32,3,60,160]{3,0,2,1:T(8,128)(2,1)S(1)} copy-done((bf16[32,3,60,160]{3,0,2,1:T(8,128)(2,1)S(1)}, bf16[32,3,60,160]{3,0,2,1:T(8,128)(2,1)}, u32[]{:S(2)}) %copy-start) | copy-done | bytes 1843224
  3.4 3.8 %inner.1 = bf16[8,360,256]{2,1,0:T(8,128)(2,1)} custom-call(bf16[3,60,32,160]{3,2,1,0:T(8,128)(2,1)S(1)} %bitcast.44, f32[60,160]{1,0:T(8,128)S(1)} %copy-done.2, f32[8,160]{1,0:T(8,128)S(1)} %jit_solution_.3.turn), custom_call_target="tpu_custom_call" | custom-call | tf_op jit(solution)/shard_map/inner/pallas_call | solution.py:606
  7.1 5.2 %all-to-all-start = ((bf16[8,360,256]{2,1,0:T(8,128)(2,1)}), bf16[8,360,256]{2,1,0:T(8,128)(2,1)}, u32[]{:S(2)}, u32[]{:S(2)}) async-start(bf16[8,360,256]{2,1,0:T(8,128)(2,1)} %inner.1), calls=%async_computation | async-start | bytes 2949120 | tf_op jit(solution)/shard_map/all_to_all | solution.py:561
  12.3 1.8 %edges.1 = (bf16[4,32,160]{2,1,0:T(8,128)(2,1)}, bf16[4,32,160]{2,1,0:T(8,128)(2,1)}) custom-call(bf16[3,60,32,160]{3,2,1,0:T(8,128)(2,1)} %bitcast.42, bf16[3,60,32,160]{3,2,1,0:T(8,128)(2,1)} %bitcast.43, f32[60,160]{1,0:T(8,128)} %depth.5), custom_call_target="tpu_custom_call" | custom-call | tf_op jit(solution)/shard_map/edges/pallas_call | solution.py:588
  14.1 2.2 %collective-permute-start = (bf16[4,32,160]{2,1,0:T(8,128)(2,1)}, bf16[4,32,160]{2,1,0:T(8,128)(2,1)S(1)}, u32[]{:S(2)}, u32[]{:S(2)}) collective-permute-start(bf16[4,32,160]{2,1,0:T(8,128)(2,1)} %get-tuple-element.21), channel_id=1, source_target_pairs={{0,1},{1,2},{2,3},{3,0},{4,5},{5,6},{6,7},{7,4},{8,9},{9,10},{10,1... | collective-permute-start | bytes 122888 | tf_op jit(solution)/shard_map/ppermute | solution.py:551
  16.3 2.1 %collective-permute-start.1 = (bf16[4,32,160]{2,1,0:T(8,128)(2,1)}, bf16[4,32,160]{2,1,0:T(8,128)(2,1)S(1)}, u32[]{:S(2)}, u32[]{:S(2)}) collective-permute-start(bf16[4,32,160]{2,1,0:T(8,128)(2,1)} %get-tuple-element.22), channel_id=1, source_target_pairs={{0,3},{1,0},{2,1},{3,2},{4,7},{5,4},{6,5},{7,6},{8,11},{9,8},{10,9... | collective-permute-start | bytes 122888 | tf_op jit(solution)/shard_map/ppermute | solution.py:551
  18.4 2.9 %collective-permute-done.left = bf16[4,32,160]{2,1,0:T(8,128)(2,1)S(1)} collective-permute-done((bf16[4,32,160]{2,1,0:T(8,128)(2,1)}, bf16[4,32,160]{2,1,0:T(8,128)(2,1)S(1)}, u32[]{:S(2)}, u32[]{:S(2)}) %collective-permute-start) | collective-permute-done | bytes 40992 | tf_op jit(solution)/shard_map/ppermute | solution.py:551
  23.0 1.7 %collective-permute-start.3 = (bf16[104,256]{1,0:T(8,128)(2,1)S(1)}, bf16[104,256]{1,0:T(8,128)(2,1)S(1)}, u32[]{:S(2)}, u32[]{:S(2)}) collective-permute-start(bf16[104,256]{1,0:T(8,128)(2,1)S(1)} %get-tuple-element.25), channel_id=1, source_target_pairs={{0,8},{4,12},{8,0},{12,4},{16,24},{20,28},{24,16},{28,20},{1,9},{5... | collective-permute-start | bytes 159752 | tf_op jit(solution)/shard_map/ppermute | solution.py:632
  25.0 1.7 %collective-permute-start.5 = (bf16[104,256]{1,0:T(8,128)(2,1)S(1)}, bf16[104,256]{1,0:T(8,128)(2,1)S(1)}, u32[]{:S(2)}, u32[]{:S(2)}) collective-permute-start(bf16[104,256]{1,0:T(8,128)(2,1)S(1)} %get-tuple-element.27), channel_id=1, source_target_pairs={{0,16},{4,20},{8,24},{12,28},{16,0},{20,4},{24,8},{28,12},{1,17},{... | collective-permute-start | bytes 159752 | tf_op jit(solution)/shard_map/ppermute | solution.py:632
  26.7 2.6 %collective-permute-start.7 = (bf16[104,256]{1,0:T(8,128)(2,1)S(1)}, bf16[104,256]{1,0:T(8,128)(2,1)S(1)}, u32[]{:S(2)}, u32[]{:S(2)}) collective-permute-start(bf16[104,256]{1,0:T(8,128)(2,1)S(1)} %get-tuple-element.29), channel_id=1, source_target_pairs={{0,24},{4,28},{8,16},{12,20},{16,8},{20,12},{24,0},{28,4},{1,25},{... | collective-permute-start | bytes 159752 | tf_op jit(solution)/shard_map/ppermute | solution.py:632
  29.3 3.7 %collective-permute-done.3.refs_2_ = bf16[104,256]{1,0:T(8,128)(2,1)S(1)} collective-permute-done((bf16[104,256]{1,0:T(8,128)(2,1)S(1)}, bf16[104,256]{1,0:T(8,128)(2,1)S(1)}, u32[]{:S(2)}, u32[]{:S(2)}) %collective-permute-start.3) | collective-permute-done | bytes 53280 | tf_op jit(solution)/shard_map/ppermute | solution.py:632
  33.8 1.9 %collective-permute-done.7.refs_6_ = bf16[104,256]{1,0:T(8,128)(2,1)S(1)} collective-permute-done((bf16[104,256]{1,0:T(8,128)(2,1)S(1)}, bf16[104,256]{1,0:T(8,128)(2,1)S(1)}, u32[]{:S(2)}, u32[]{:S(2)}) %collective-permute-start.7) | collective-permute-done | bytes 53280 | tf_op jit(solution)/shard_map/ppermute | solution.py:632
  35.7 1.8 %collective-permute-done.8.refs_7_ = bf16[104,256]{1,0:T(8,128)(2,1)S(1)} collective-permute-done((bf16[104,256]{1,0:T(8,128)(2,1)S(1)}, bf16[104,256]{1,0:T(8,128)(2,1)S(1)}, u32[]{:S(2)}, u32[]{:S(2)}) %collective-permute-start.8) | collective-permute-done | bytes 53280 | tf_op jit(solution)/shard_map/ppermute | solution.py:632
  37.5 7.2 %observe.1 = (bf16[8,464,256]{2,1,0:T(8,128)(2,1)S(1)}, f32[2,144,256]{2,1,0:T(8,128)S(1)}, bf16[2,144,256]{2,1,0:T(8,128)(2,1)S(1)}) custom-call(s32[2,512]{1,0:T(2,128)S(1)} %fusion.9.cells, f32[2,512]{1,0:T(2,128)S(1)} %fusion.10.weight, f32[2,512]{1,0:T(2,128)S(1)} %bitcast.46, bf16[8,360,256]{2,1,0:T(8,128)(2,1)} %all-to-all-done.got, ...), custom_call_target="tpu_custom_call" | custom-call | tf_op jit(solution)/shard_map/observe/pallas_call | solution.py:638
  44.7 1.3 %collective-permute-start.10 = (bf16[2,144,256]{2,1,0:T(8,128)(2,1)S(1)}, bf16[2,144,256]{2,1,0:T(8,128)(2,1)S(1)}, u32[]{:S(2)}, u32[]{:S(2)}) collective-permute-start(bf16[2,144,256]{2,1,0:T(8,128)(2,1)S(1)} %get-tuple-element.33), channel_id=1, source_target_pairs={{4,0},{8,4},{12,8},{16,12},{20,16},{24,20},{28,24},{5,1},{9,5},{13... | collective-permute-start | bytes 442376 | tf_op jit(solution)/shard_map/ppermute | solution.py:557
  46.0 3.0 %collective-permute-start.9 = (bf16[2,144,256]{2,1,0:T(8,128)(2,1)S(1)}, bf16[2,144,256]{2,1,0:T(8,128)(2,1)S(1)}, u32[]{:S(2)}, u32[]{:S(2)}) collective-permute-start(bf16[2,144,256]{2,1,0:T(8,128)(2,1)S(1)} %get-tuple-element.33), channel_id=1, source_target_pairs={{0,4},{4,8},{8,12},{12,16},{16,20},{20,24},{24,28},{1,5},{5,9},{9,... | collective-permute-start | bytes 442376 | tf_op jit(solution)/shard_map/ppermute | solution.py:557
  49.0 1.0 collective-permute-done.9.below
  50.1 2.1 %collective-permute-start.11 = (bf16[144,256]{1,0:T(8,128)(2,1)S(1)}, bf16[144,256]{1,0:T(8,128)(2,1)S(1)}, u32[]{:S(2)}, u32[]{:S(2)}) collective-permute-start(bf16[144,256]{1,0:T(8,128)(2,1)S(1)} %get-tuple-element.35), channel_id=1, source_target_pairs={{0,1},{1,2},{2,3},{3,0},{4,5},{5,6},{6,7},{7,4},{8,9},{9,10},{10,1... | collective-permute-start | bytes 221192 | tf_op jit(solution)/shard_map/ppermute | solution.py:551
  52.1 2.1 %collective-permute-start.12 = (bf16[144,256]{1,0:T(8,128)(2,1)S(1)}, bf16[144,256]{1,0:T(8,128)(2,1)S(1)}, u32[]{:S(2)}, u32[]{:S(2)}) collective-permute-start(bf16[144,256]{1,0:T(8,128)(2,1)S(1)} %get-tuple-element.36), channel_id=1, source_target_pairs={{0,3},{1,0},{2,1},{3,2},{4,7},{5,4},{6,5},{7,6},{8,11},{9,8},{10,9... | collective-permute-start | bytes 221192 | tf_op jit(solution)/shard_map/ppermute | solution.py:551
  54.2 2.4 %collective-permute-done.11.west = bf16[144,256]{1,0:T(8,128)(2,1)S(1)} collective-permute-done((bf16[144,256]{1,0:T(8,128)(2,1)S(1)}, bf16[144,256]{1,0:T(8,128)(2,1)S(1)}, u32[]{:S(2)}, u32[]{:S(2)}) %collective-permute-start.11) | collective-permute-done | bytes 73760 | tf_op jit(solution)/shard_map/ppermute | solution.py:551
  56.6 2.1 %collective-permute-done.12.east = bf16[144,256]{1,0:T(8,128)(2,1)S(1)} collective-permute-done((bf16[144,256]{1,0:T(8,128)(2,1)S(1)}, bf16[144,256]{1,0:T(8,128)(2,1)S(1)}, u32[]{:S(2)}, u32[]{:S(2)}) %collective-permute-start.12) | collective-permute-done | bytes 73760 | tf_op jit(solution)/shard_map/ppermute | solution.py:551
  58.8 8.2 %analyse.1 = bf16[8,464,256]{2,1,0:T(8,128)(2,1)S(1)} custom-call(bf16[8,464,256]{2,1,0:T(8,128)(2,1)S(1)} %get-tuple-element.31.held, f32[2,144,256]{2,1,0:T(8,128)S(1)} %get-tuple-element.34.column, bf16[144,256]{1,0:T(8,128)(2,1)S(1)} %collective-permute-done.11.west, bf16[144,256]{1,0:T(8,128)(2,1)S(1)} %collective-permute-done.12.east), custom_call_target="tpu_custom_call" | custom-call | tf_op jit(solution)/shard_map/analyse/pallas_call | solution.py:666
  67.0 29.6 %all_to_all.10.got = bf16[8,464,256]{2,1,0:T(8,128)(2,1)S(1)} all-to-all(bf16[8,464,256]{2,1,0:T(8,128)(2,1)S(1)} %analyse.1), channel_id=1, replica_groups=mesh['mem'=8,'band'=4] {'mem'}, dimensions={0} | all-to-all | bytes 3801088 | tf_op jit(solution)/shard_map/all_to_all | solution.py:561
  96.6 2.7 %come_back.1 = bf16[3,60,32,160]{3,2,1,0:T(8,128)(2,1)} custom-call(bf16[8,464,256]{2,1,0:T(8,128)(2,1)S(1)} %all_to_all.10.got), custom_call_target="tpu_custom_call" | custom-call | tf_op jit(solution)/shard_map/come_back/pallas_call | solution.py:674
  (32 shorter events, 4.4 us)
Async XLA Ops:
  0.7 1.8 %copy-start = (bf16[32,3,60,160]{3,0,2,1:T(8,128)(2,1)S(1)}, bf16[32,3,60,160]{3,0,2,1:T(8,128)(2,1)}, u32[]{:S(2)}) copy-start(bf16[32,3,60,160]{3,0,2,1:T(8,128)(2,1)} %param.7) | copy-start | bytes 5529604
  2.5 0.8 copy-start.2
  7.1 30.4 %all-to-all-start = ((bf16[8,360,256]{2,1,0:T(8,128)(2,1)}), bf16[8,360,256]{2,1,0:T(8,128)(2,1)}, u32[]{:S(2)}, u32[]{:S(2)}) async-start(bf16[8,360,256]{2,1,0:T(8,128)(2,1)} %inner.1), calls=%async_computation | async-start | bytes 2949120 | tf_op jit(solution)/shard_map/all_to_all | solution.py:561
  12.3 9.7 %copy-start.1 = (bf16[32,3,60,160]{3,0,2,1:T(8,128)(2,1)S(1)}, bf16[32,3,60,160]{3,0,2,1:T(8,128)(2,1)}, u32[]{:S(2)}) copy-start(bf16[32,3,60,160]{3,0,2,1:T(8,128)(2,1)} %param.7) | copy-start | bytes 5529604
  12.3 9.7 %copy-start.3 = (f32[60,160]{1,0:T(8,128)S(1)}, f32[60,160]{1,0:T(8,128)}, u32[]{:S(2)}) copy-start(f32[60,160]{1,0:T(8,128)} %depth.5) | copy-start | bytes 115204
  14.1 10.7 %copy-start.5 = (s32[1,2,512]{2,1,0:T(2,128)S(1)}, s32[1,2,512]{2,1,0:T(2,128)}, u32[]{:S(2)}) copy-start(s32[1,2,512]{2,1,0:T(2,128)} %param.9) | copy-start | bytes 12292
  14.1 19.2 %copy-start.6 = (f32[1,2,512]{2,1,0:T(2,128)S(1)}, f32[1,2,512]{2,1,0:T(2,128)}, u32[]{:S(2)}) copy-start(f32[1,2,512]{2,1,0:T(2,128)} %param.11) | copy-start | bytes 12292
  14.1 19.2 %copy-start.7 = (s32[1,2]{1,0:T(1,128)S(1)}, s32[1,2]{1,0:T(1,128)}, u32[]{:S(2)}) copy-start(s32[1,2]{1,0:T(1,128)} %param.12) | copy-start | bytes 28
  14.1 23.4 %copy-start.4 = (f32[1,2,512]{2,1,0:T(2,128)S(1)}, f32[1,2,512]{2,1,0:T(2,128)}, u32[]{:S(2)}) copy-start(f32[1,2,512]{2,1,0:T(2,128)} %param.10) | copy-start | bytes 12292
  14.1 7.2 %collective-permute-start = (bf16[4,32,160]{2,1,0:T(8,128)(2,1)}, bf16[4,32,160]{2,1,0:T(8,128)(2,1)S(1)}, u32[]{:S(2)}, u32[]{:S(2)}) collective-permute-start(bf16[4,32,160]{2,1,0:T(8,128)(2,1)} %get-tuple-element.21), channel_id=1, source_target_pairs={{0,1},{1,2},{2,3},{3,0},{4,5},{5,6},{6,7},{7,4},{8,9},{9,10},{10,1... | collective-permute-start | bytes 122888 | tf_op jit(solution)/shard_map/ppermute | solution.py:551
  16.3 5.7 %collective-permute-start.1 = (bf16[4,32,160]{2,1,0:T(8,128)(2,1)}, bf16[4,32,160]{2,1,0:T(8,128)(2,1)S(1)}, u32[]{:S(2)}, u32[]{:S(2)}) collective-permute-start(bf16[4,32,160]{2,1,0:T(8,128)(2,1)} %get-tuple-element.22), channel_id=1, source_target_pairs={{0,3},{1,0},{2,1},{3,2},{4,7},{5,4},{6,5},{7,6},{8,11},{9,8},{10,9... | collective-permute-start | bytes 122888 | tf_op jit(solution)/shard_map/ppermute | solution.py:551
  22.9 3.8 %collective-permute-start.2 = (bf16[104,256]{1,0:T(8,128)(2,1)S(1)}, bf16[104,256]{1,0:T(8,128)(2,1)S(1)}, u32[]{:S(2)}, u32[]{:S(2)}) collective-permute-start(bf16[104,256]{1,0:T(8,128)(2,1)S(1)} %get-tuple-element.24), channel_id=1, source_target_pairs={{0,4},{4,0},{8,12},{12,8},{16,20},{20,16},{24,28},{28,24},{1,5},{5... | collective-permute-start | bytes 159752 | tf_op jit(solution)/shard_map/ppermute | solution.py:632
  23.0 10.0 %collective-permute-start.3 = (bf16[104,256]{1,0:T(8,128)(2,1)S(1)}, bf16[104,256]{1,0:T(8,128)(2,1)S(1)}, u32[]{:S(2)}, u32[]{:S(2)}) collective-permute-start(bf16[104,256]{1,0:T(8,128)(2,1)S(1)} %get-tuple-element.25), channel_id=1, source_target_pairs={{0,8},{4,12},{8,0},{12,4},{16,24},{20,28},{24,16},{28,20},{1,9},{5... | collective-permute-start | bytes 159752 | tf_op jit(solution)/shard_map/ppermute | solution.py:632
  24.8 8.5 %collective-permute-start.4 = (bf16[104,256]{1,0:T(8,128)(2,1)S(1)}, bf16[104,256]{1,0:T(8,128)(2,1)S(1)}, u32[]{:S(2)}, u32[]{:S(2)}) collective-permute-start(bf16[104,256]{1,0:T(8,128)(2,1)S(1)} %get-tuple-element.26), channel_id=1, source_target_pairs={{0,12},{4,8},{8,4},{12,0},{16,28},{20,24},{24,20},{28,16},{1,13},{... | collective-permute-start | bytes 159752 | tf_op jit(solution)/shard_map/ppermute | solution.py:632
  25.0 8.3 %collective-permute-start.5 = (bf16[104,256]{1,0:T(8,128)(2,1)S(1)}, bf16[104,256]{1,0:T(8,128)(2,1)S(1)}, u32[]{:S(2)}, u32[]{:S(2)}) collective-permute-start(bf16[104,256]{1,0:T(8,128)(2,1)S(1)} %get-tuple-element.27), channel_id=1, source_target_pairs={{0,16},{4,20},{8,24},{12,28},{16,0},{20,4},{24,8},{28,12},{1,17},{... | collective-permute-start | bytes 159752 | tf_op jit(solution)/shard_map/ppermute | solution.py:632
  26.7 7.1 %collective-permute-start.6 = (bf16[104,256]{1,0:T(8,128)(2,1)S(1)}, bf16[104,256]{1,0:T(8,128)(2,1)S(1)}, u32[]{:S(2)}, u32[]{:S(2)}) collective-permute-start(bf16[104,256]{1,0:T(8,128)(2,1)S(1)} %get-tuple-element.28), channel_id=1, source_target_pairs={{0,20},{4,16},{8,28},{12,24},{16,4},{20,0},{24,12},{28,8},{1,21},{... | collective-permute-start | bytes 159752 | tf_op jit(solution)/shard_map/ppermute | solution.py:632
  26.7 9.0 %collective-permute-start.7 = (bf16[104,256]{1,0:T(8,128)(2,1)S(1)}, bf16[104,256]{1,0:T(8,128)(2,1)S(1)}, u32[]{:S(2)}, u32[]{:S(2)}) collective-permute-start(bf16[104,256]{1,0:T(8,128)(2,1)S(1)} %get-tuple-element.29), channel_id=1, source_target_pairs={{0,24},{4,28},{8,16},{12,20},{16,8},{20,12},{24,0},{28,4},{1,25},{... | collective-permute-start | bytes 159752 | tf_op jit(solution)/shard_map/ppermute | solution.py:632
  33.0 4.5 %collective-permute-start.8 = (bf16[104,256]{1,0:T(8,128)(2,1)S(1)}, bf16[104,256]{1,0:T(8,128)(2,1)S(1)}, u32[]{:S(2)}, u32[]{:S(2)}) collective-permute-start(bf16[104,256]{1,0:T(8,128)(2,1)S(1)} %get-tuple-element.30), channel_id=1, source_target_pairs={{0,28},{4,24},{8,20},{12,16},{16,12},{20,8},{24,4},{28,0},{1,29},{... | collective-permute-start | bytes 159752 | tf_op jit(solution)/shard_map/ppermute | solution.py:632
  44.7 4.3 %collective-permute-start.10 = (bf16[2,144,256]{2,1,0:T(8,128)(2,1)S(1)}, bf16[2,144,256]{2,1,0:T(8,128)(2,1)S(1)}, u32[]{:S(2)}, u32[]{:S(2)}) collective-permute-start(bf16[2,144,256]{2,1,0:T(8,128)(2,1)S(1)} %get-tuple-element.33), channel_id=1, source_target_pairs={{4,0},{8,4},{12,8},{16,12},{20,16},{24,20},{28,24},{5,1},{9,5},{13... | collective-permute-start | bytes 442376 | tf_op jit(solution)/shard_map/ppermute | solution.py:557
  46.0 4.0 %collective-permute-start.9 = (bf16[2,144,256]{2,1,0:T(8,128)(2,1)S(1)}, bf16[2,144,256]{2,1,0:T(8,128)(2,1)S(1)}, u32[]{:S(2)}, u32[]{:S(2)}) collective-permute-start(bf16[2,144,256]{2,1,0:T(8,128)(2,1)S(1)} %get-tuple-element.33), channel_id=1, source_target_pairs={{0,4},{4,8},{8,12},{12,16},{16,20},{20,24},{24,28},{1,5},{5,9},{9,... | collective-permute-start | bytes 442376 | tf_op jit(solution)/shard_map/ppermute | solution.py:557
  50.1 6.5 %collective-permute-start.11 = (bf16[144,256]{1,0:T(8,128)(2,1)S(1)}, bf16[144,256]{1,0:T(8,128)(2,1)S(1)}, u32[]{:S(2)}, u32[]{:S(2)}) collective-permute-start(bf16[144,256]{1,0:T(8,128)(2,1)S(1)} %get-tuple-element.35), channel_id=1, source_target_pairs={{0,1},{1,2},{2,3},{3,0},{4,5},{5,6},{6,7},{7,4},{8,9},{9,10},{10,1... | collective-permute-start | bytes 221192 | tf_op jit(solution)/shard_map/ppermute | solution.py:551
  52.1 6.6 %collective-permute-start.12 = (bf16[144,256]{1,0:T(8,128)(2,1)S(1)}, bf16[144,256]{1,0:T(8,128)(2,1)S(1)}, u32[]{:S(2)}, u32[]{:S(2)}) collective-permute-start(bf16[144,256]{1,0:T(8,128)(2,1)S(1)} %get-tuple-element.36), channel_id=1, source_target_pairs={{0,3},{1,0},{2,1},{3,2},{4,7},{5,4},{6,5},{7,6},{8,11},{9,8},{10,9... | collective-permute-start | bytes 221192 | tf_op jit(solution)/shard_map/ppermute | solution.py:551

commit v5 on v4

--- a/solution.py
+++ b/solution.py
@@ -257,15 +257,6 @@
     return variable * 3 + index - 4 if index > 3 else 12 + variable * 2 + index - 1
 
 
-def edge_kernel(first, last, depth, to_west, to_east):
-    for out, block, columns, near in ((to_west, first, (0, 1), 0), (to_east, last, (58, 59), 1)):
-        far = 1 - near
-        out[0] = block[0, near]
-        for plane, v, k in ((1, 2, near), (2, 1, near), (3, 1, far)):
-            deep = depth[columns[k] : columns[k] + 1, :]
-            out[plane] = (deep * block[v, k].astype(F32)).astype(BF16)
-
-
 def difference(latitudes):
     source = lax.broadcasted_iota(jnp.int32, (latitudes, latitudes), 0)
     target = lax.broadcasted_iota(jnp.int32, (latitudes, latitudes), 1)
@@ -304,46 +295,68 @@
         staged[s, first : first + rows, :] = turned[rows * s : rows * (s + 1)]
 
 
-def inner_kernel(ens, depth, turn, out, deep, flux, height, staged):
-    members, latitudes = ens.shape[2:]
+def turning_row(latitudes):
+    position = lax.broadcasted_iota(jnp.int32, (8, latitudes), 1).astype(F32)
+    turning = coriolis_scale * jnp.sin(math.pi * ((position + 0.5) / latitudes - 0.5))
+    return turning[0:1, :][None]
+
+
+def inner_kernel(ens, depth, out, to_west, to_east, here, deep, flux, height, staged, arrived):
+    columns, members, latitudes = here.shape[1:]
+    batch = columns // 5
+    pieces = [pltpu.make_async_copy(depth, deep, arrived.at[5])]
+    for k in range(5):
+        span = pl.ds(k * batch, batch)
+        piece = pltpu.make_async_copy(ens.at[:, span], here.at[:, span], arrived.at[k])
+        pieces.append(piece)
+    for piece in pieces:
+        piece.start()
     shift = difference(latitudes)
-    turning = turn[0:1, :][None]
-    for c in range(6, 58):
-        deep[c - 6] = jnp.broadcast_to(depth[c : c + 1, :], (members, latitudes))
-
-    def flux_step(index, carry):
-        here = pl.ds(index * 13, 13)
-        flux[here] = fluxes(ens[1, pl.ds(index * 13 + 6, 13)], deep[here])
-        return carry
-
-    lax.fori_loop(0, 4, flux_step, 0)
-
-    def height_step(index, carry):
-        first = index * 10
-        at = pl.ds(first + 7, 10)
-        ahead, behind = flux[pl.ds(first + 2, 10)], flux[pl.ds(first, 10)]
-        here = pl.ds(first + 1, 10)
-        height[here] = heights(ens[0, at], ens[2, at], deep[here], ahead, behind, shift)
-        return carry
-
-    lax.fori_loop(0, 5, height_step, 0)
+    turning = turning_row(latitudes)
     eye = identity(latitudes, BF16)
-    for index in range(1, 7):
-        first = 8 * index
-        at = slice(first, first + 8)
-        here = height[first - 6 : first + 2]
-        ahead, behind = height[first - 5 : first + 3], height[first - 7 : first + 1]
-        new = velocities(ens[1, at], ens[2, at], here, ahead, behind, turning, shift)
-        for v, field in enumerate((here,) + new):
-            put_group(staged, field, eye, 20 * group_of(v, index))
+    pieces[0].wait()
+
+    def depths(first, count):
+        rows = [deep[c : c + 1, :] for c in range(first, first + count)]
+        return jnp.stack([jnp.broadcast_to(row, (members, latitudes)) for row in rows])
+
+    def edge(to, near, far):
+        to[0] = here[0, near]
+        to[1] = (deep[near : near + 1, :] * here[2, near].astype(F32)).astype(BF16)
+        to[2] = flux[near].astype(BF16)
+        to[3] = flux[far].astype(BF16)
+
+    done = 1
+    for k in range(5):
+        pieces[k + 1].wait()
+        first = k * batch
+        flux[first : first + batch] = fluxes(here[1, first : first + batch], depths(first, batch))
+        if k == 0:
+            edge(to_west, 0, 1)
+        if k == 4:
+            edge(to_east, columns - 1, columns - 2)
+        low, high = max(first - 1, 1), first + batch - 1
+        at = slice(low, high)
+        ahead, behind = flux[low + 1 : high + 1], flux[low - 1 : high - 1]
+        height[at] = heights(
+            here[0, at], here[2, at], depths(low, high - low), ahead, behind, shift
+        )
+        while done < 7 and 8 * done + 9 <= high:
+            first = 8 * done
+            at = slice(first, first + 8)
+            ahead, behind = height[first + 1 : first + 9], height[first - 1 : first + 7]
+            new = velocities(here[1, at], here[2, at], height[at], ahead, behind, turning, shift)
+            for v, field in enumerate((height[at],) + new):
+                put_group(staged, field, eye, 20 * group_of(v, done))
+            done += 1
     out[...] = staged[...].astype(BF16)
 
 
-def outer_kernel(ens, left, right, depth, turn, *refs):
+def outer_kernel(west_block, east_block, left, right, depth, *refs):
     outs, (flux, height, staged) = refs[:8], refs[8:]
-    members, latitudes = ens.shape[2:]
+    members, latitudes = west_block.shape[2:]
     shift = difference(latitudes)
-    turning = turn[0:1, :][None]
+    turning = turning_row(latitudes)
     eye = identity(latitudes, BF16)
 
     def depths(first, count):
@@ -354,17 +367,17 @@
             ]
         )
 
-    def window(edge, first, count, low, high):
+    def window(ens, edge, first, count, low, high):
         is_left = low == 0
         base = 2 if is_left else 0
-        flux[base : base + count] = fluxes(ens[1, first : first + count], depths(first, count))
+        flux[base : base + count] = fluxes(ens[1, 0:count], depths(first, count))
         at = 0 if is_left else count
         near, far = (1, 0) if is_left else (at, at + 1)
         flux[near] = edge[2].astype(F32)
         flux[far] = edge[3].astype(F32)
         wide = high - low + 1
         skip = 0 if is_left else 1
-        columns = slice(first + skip, first + skip + wide)
+        columns = slice(skip, skip + wide)
         new = heights(
             ens[0, columns],
             ens[2, columns],
@@ -383,13 +396,13 @@
         count = high - low
         here = height[1 : 1 + count]
         ahead, behind = height[2 : 2 + count], height[0:count]
-        at = slice(low, high)
+        at = slice(low - first, high - first)
         return (here,) + velocities(ens[1, at], ens[2, at], here, ahead, behind, turning, shift)
 
     staged[:, 100:104, :] = jnp.zeros((8, 4, 256), F32)
-    for v, field in enumerate(window(left, 0, 10, 0, 8)):
+    for v, field in enumerate(window(west_block, left, 0, 10, 0, 8)):
         put_group(staged, field, eye, 20 * v)
-    ends = window(right, 54, 6, 56, 60)
+    ends = window(east_block, right, 54, 6, 56, 60)
     put_group(staged, jnp.concatenate([ends[0], ends[1]], axis=0), eye, 60)
     put_group(staged, jnp.concatenate([ends[2], jnp.zeros_like(ends[2])], axis=0), eye, 80)
     me = lax.axis_index("mem")
@@ -458,7 +471,8 @@
     to_east[...] = total[1].astype(BF16)
 
 
-def analyse_kernel(held, column, west, east, out, results):
+def analyse_kernel(held, column, west, east, *refs):
+    outs, (results, ordered) = refs[:8], refs[8:]
     size = 256
     eye = identity(size, F32)
     beside = (west[...].astype(F32) + column[1], column[0] + east[...].astype(F32))
@@ -489,7 +503,10 @@
         half_pull = dot_nn(left_3(split(pulls[t])), right)
         shift = dot_nn(left_3(split(half_pull)), right) / norms[t]
         scale = math.sqrt(size - 1) / jnp.sqrt(norms[t])
-        maps.append((inverses[t] * scale + shift[0:1]).astype(BF16))
+        ordered[t] = (inverses[t] * scale + shift[0:1]).astype(BF16).reshape(8, 32, size)
+    me = lax.axis_index("mem")
+    for t in range(2):
+        maps.append(jnp.concatenate([ordered[t, me ^ d] for d in range(8)], axis=0))
     average = jnp.full((size, size), 1.0 / size, BF16)
     near = lax.broadcasted_iota(jnp.int32, (16, size), 0) < 4
 
@@ -519,16 +536,19 @@
         blocks = exchange_lanes(blocks, lane)
         for q in range(8):
             for h in range(2):
-                out[q, here, spans[h]] = blocks[q][h]
+                outs[q][here, spans[h]] = blocks[q][h]
         return carry
 
     lax.fori_loop(0, CELLS // 16, gather_in, 0, unroll=4)
 
 
-def return_kernel(got, out, wide, turned):
-    members, latitudes = out.shape[2:]
+def return_kernel(*refs):
+    got, (out, wide, turned, planes, sent) = refs[:8], refs[8:]
+    members, latitudes = planes.shape[2:]
     rows = latitudes // 8
-    wide[...] = got[...].astype(F32)
+    me = lax.axis_index("mem")
+    for d in range(8):
+        wide[me ^ d] = got[d][...].astype(F32)
     eye = identity(256, BF16)
 
     def take(g):
@@ -537,13 +557,18 @@
         block = dot_nt(eye, turned[g].astype(BF16)).astype(BF16)
         return block.reshape(8, members, latitudes)
 
+    mixed = take(21)
+    planes[0, 56:60] = mixed[0:4]
+    planes[1, 56:60] = mixed[4:8]
+    planes[2, 56:60] = take(22)[0:4]
+    copies = []
     for v in range(3):
         for index in range(7):
-            out[v, 8 * index : 8 * index + 8] = take(group_of(v, index))
-    mixed = take(21)
-    out[0, 56:60] = mixed[0:4]
-    out[1, 56:60] = mixed[4:8]
-    out[2, 56:60] = take(22)[0:4]
+            planes[v, 8 * index : 8 * index + 8] = take(group_of(v, index))
+        copies.append(pltpu.make_async_copy(planes.at[v], out.at[v], sent.at[v]))
+        copies[v].start()
+    for copy in copies:
+        copy.wait()
 
 
 def around(value, axis, step):
@@ -555,6 +580,12 @@
     count = lax.axis_size(axis)
     pairs = [(i, i + step) for i in range(count) if 0 <= i + step < count]
     return lax.ppermute(value, axis, pairs)
+
+
+def partners(values):
+    count = len(values)
+    pairs = [[(i, i ^ d) for i in range(count)] for d in range(count)]
+    return [values[0]] + [lax.ppermute(values[d], "mem", pairs[d]) for d in range(1, count)]
 
 
 def swap(value):
@@ -583,53 +614,48 @@
     slots = observed_cell.shape[2]
     planes = jnp.transpose(ensemble, (1, 2, 0, 3))
     edge = jax.ShapeDtypeStruct((4, members, latitudes), BF16)
-    pair = (3, 2, members, latitudes)
-    whole = pl.BlockSpec((4, members, latitudes), lambda i: (0, 0, 0))
-    to_west, to_east = pl.pallas_call(
-        edge_kernel,
+    far = pl.BlockSpec(memory_space=pltpu.HBM)
+    sent, to_west, to_east = pl.pallas_call(
+        inner_kernel,
+        out_shape=(jax.ShapeDtypeStruct((8, INNER, 256), BF16), edge, edge),
+        in_specs=[far, far],
+        scratch_shapes=[
+            pltpu.VMEM(planes.shape, BF16),
+            pltpu.VMEM((columns, latitudes), F32),
+            pltpu.VMEM((columns, members, latitudes), F32),
+            pltpu.VMEM((columns, members, latitudes), BF16),
+            pltpu.VMEM((8, INNER, 256), F32),
+            pltpu.SemaphoreType.DMA((6,)),
+        ],
+        compiler_params=params(60),
+        name="inner",
+    )(planes, layer_depth)
+    got = swap(sent)
+    left = around(to_east, "band", 1)
+    right = around(to_west, "band", -1)
+    flat = pl.BlockSpec((4, members, latitudes), lambda i: (0, 0, 0))
+    out_edge = jax.ShapeDtypeStruct((OUTER, 256), BF16)
+    sent = pl.pallas_call(
+        outer_kernel,
         grid=(1,),
-        out_shape=(edge, edge),
+        out_shape=(out_edge,) * 8,
         in_specs=[
-            pl.BlockSpec(pair, lambda i: (0, 0, 0, 0)),
-            pl.BlockSpec(pair, lambda i: (0, columns // 2 - 1, 0, 0)),
+            pl.BlockSpec((3, 10, members, latitudes), lambda i: (0, 0, 0, 0)),
+            pl.BlockSpec((3, 6, members, latitudes), lambda i: (0, 9, 0, 0)),
+            flat,
+            flat,
             pl.BlockSpec((columns, latitudes), lambda i: (0, 0)),
         ],
-        out_specs=(whole, whole),
-        compiler_params=params(60),
-        name="edges",
-    )(planes, planes, layer_depth)
-    left = around(to_east, "band", 1)
-    right = around(to_west, "band", -1)
-    position = (np.arange(latitudes) + 0.5) / latitudes - 0.5
-    turning = coriolis_scale * np.sin(math.pi * position)
-    turning = jnp.asarray(np.broadcast_to(turning.astype(np.float32), (8, latitudes)))
-    sent = pl.pallas_call(
-        inner_kernel,
-        out_shape=jax.ShapeDtypeStruct((8, INNER, 256), BF16),
-        scratch_shapes=[
-            pltpu.VMEM((52, members, latitudes), F32),
-            pltpu.VMEM((52, members, latitudes), F32),
-            pltpu.VMEM((52, members, latitudes), BF16),
-            pltpu.VMEM((8, INNER, 256), F32),
-        ],
-        compiler_params=params(24),
-        name="inner",
-    )(planes, layer_depth, turning)
-    got = swap(sent)
-    sent = pl.pallas_call(
-        outer_kernel,
-        out_shape=(jax.ShapeDtypeStruct((OUTER, 256), BF16),) * 8,
+        out_specs=(pl.BlockSpec((OUTER, 256), lambda i: (0, 0)),) * 8,
         scratch_shapes=[
             pltpu.VMEM((12, members, latitudes), F32),
             pltpu.VMEM((10, members, latitudes), BF16),
             pltpu.VMEM((8, OUTER, 256), F32),
         ],
-        compiler_params=params(16),
+        compiler_params=params(24),
         name="outer",
-    )(planes, left, right, layer_depth, turning)
-    got_edges = [sent[0]]
-    for d in range(1, 8):
-        got_edges.append(lax.ppermute(sent[d], "mem", [(i, i ^ d) for i in range(8)]))
+    )(planes, planes, left, right, layer_depth)
+    got_edges = partners(sent)
 
     rows = cell_rows(observed_cell[0])
     live = jnp.arange(slots, dtype=jnp.int32)[None, :] < observed_count[0][:, None]
@@ -665,22 +691,25 @@
     east = around(to_west, "band", -1)
     back = pl.pallas_call(
         analyse_kernel,
-        out_shape=jax.ShapeDtypeStruct((8, CELLS, 256), BF16),
-        scratch_shapes=[pltpu.VMEM((8, CELLS, 256), BF16)],
+        out_shape=(jax.ShapeDtypeStruct((CELLS, 256), BF16),) * 8,
+        scratch_shapes=[pltpu.VMEM((8, CELLS, 256), BF16), pltpu.VMEM((2, 8, 32, 256), BF16)],
         compiler_params=params(20),
         name="analyse",
     )(held, column, west, east)
-    returned = swap(back)
+    returned = partners(back)
     planes = pl.pallas_call(
         return_kernel,
         out_shape=jax.ShapeDtypeStruct(planes.shape, BF16),
+        out_specs=far,
         scratch_shapes=[
             pltpu.VMEM((8, CELLS, 256), F32),
             pltpu.VMEM((GROUPS, latitudes, 256), F32),
+            pltpu.VMEM(planes.shape, BF16),
+            pltpu.SemaphoreType.DMA((3,)),
         ],
         compiler_params=params(24),
         name="come_back",
-    )(returned)
+    )(*returned)
     return jnp.transpose(planes, (2, 0, 1, 3))
 
 

time: 99.6 us -> 95.2 us (0.956)
  blocking collectives: 29.6 us -> 0 us
  waiting for transfers between devices: 16.9 us -> 36.7 us
  starting transfers between devices: 24.5 us -> 34 us
  local copies, waits for them, and re-layouts: 3.38 us -> 0.03 us
    all_to_all x1 -> x0, blocking collectives: 29.6 us -> none  [swap(): return lax.all_to_all(value, 'mem', split_axis=0, concat_axis=0, tiled=True)]
    ppermute x7 -> x14, waiting for transfers between devices: 7.84 us -> 27.8 us  [partners(): lax.ppermute(values[d], 'mem', pairs[d])]
    ppermute x7 -> x14, starting transfers between devices: 6.52 us -> 15.6 us  [partners(): lax.ppermute(values[d], 'mem', pairs[d])]
    unnamed x16 -> x12, local copies, waits for them, and re-layouts: 2.7 us -> 0.03 us
    pallas_call x4 -> x3, Pallas kernels: 14.6 us -> 14.1 us  [the longest x1 8.23 us: on_device_fast(): pl.pallas_call(analyse_kernel, out_shape=(jax.ShapeDtypeStruct((CELLS, 25...]
  transfers between devices with their start and end apart: 14 -> 21, of which waited for: 9 -> 11; matrix products, arithmetic and copies ran while one was open for 0% -> 0% of each run, Pallas kernels for 3% -> 1%
where the time goes in v5:
time: 95.2 us; the launch traced here: 94.9 us
  waiting for transfers between devices  36.7 us (39%)
  starting transfers between devices  34 us (36%)
  Pallas kernels  23.8 us (25%)
    ppermute x14, waiting for transfers between devices, partners(): lax.ppermute(values[d], 'mem', pairs[d])  27.8 us
    ppermute x14, starting transfers between devices, partners(): lax.ppermute(values[d], 'mem', pairs[d])  15.6 us
    ppermute x4, starting transfers between devices, around(): lax.ppermute(value, axis, [(i, (i + step) % count) for i in range(count)])  8.65 us
    pallas_call x1, Pallas kernels, on_device_fast(): pl.pallas_call(analyse_kernel, out_shape=(jax.ShapeDtypeStruct((CELLS, 25...  8.23 us
    ppermute x4, waiting for transfers between devices, around(): lax.ppermute(value, axis, [(i, (i + step) % count) for i in range(count)])  7.88 us
    pallas_call x1, Pallas kernels, on_device_fast(): pl.pallas_call(observe_kernel, out_shape=(jax.ShapeDtypeStruct((8, CELLS,...  7.17 us
    all_to_all x1, starting transfers between devices, swap(): return lax.all_to_all(value, 'mem', split_axis=0, concat_axis=0, tiled=True)  5.44 us
    pallas_call x1, Pallas kernels, on_device_fast(): pl.pallas_call(inner_kernel, out_shape=(jax.ShapeDtypeStruct((8, INNER, 2...  4.98 us
  transfers between devices with their start and end apart: 21, of which 11 were waited for; matrix products, arithmetic and copies ran while one was open for 0% of the time, Pallas kernels for 1%

profile of v5, /device:TPU:0, one launch (start us, length us, event | category | flops | bytes accessed | tf_op | source)
XLA Modules:
  0.0 94.9 jit_solution(4148060995692774254)
XLA Ops:
  0.0 5.0 %inner.1 = (bf16[8,360,256]{2,1,0:T(8,128)(2,1)}, bf16[4,32,160]{2,1,0:T(8,128)(2,1)}, bf16[4,32,160]{2,1,0:T(8,128)(2,1)}) custom-call(bf16[3,60,32,160]{3,2,1,0:T(8,128)(2,1)} %bitcast.42, f32[60,160]{1,0:T(8,128)} %depth.3), custom_call_target="tpu_custom_call" | custom-call | tf_op jit(solution)/shard_map/inner/pallas_call | solution.py:618
  5.0 5.4 %all-to-all-start = ((bf16[8,360,256]{2,1,0:T(8,128)(2,1)}), bf16[8,360,256]{2,1,0:T(8,128)(2,1)}, u32[]{:S(2)}, u32[]{:S(2)}) async-start(bf16[8,360,256]{2,1,0:T(8,128)(2,1)} %get-tuple-element.30), calls=%async_computation | async-start | bytes 2949120 | tf_op jit(solution)/shard_map/all_to_all | solution.py:592
  10.5 2.2 %collective-permute-start = (bf16[4,32,160]{2,1,0:T(8,128)(2,1)}, bf16[4,32,160]{2,1,0:T(8,128)(2,1)S(1)}, u32[]{:S(2)}, u32[]{:S(2)}) collective-permute-start(bf16[4,32,160]{2,1,0:T(8,128)(2,1)} %get-tuple-element.31), channel_id=1, source_target_pairs={{0,1},{1,2},{2,3},{3,0},{4,5},{5,6},{6,7},{7,4},{8,9},{9,10},{10,1... | collective-permute-start | bytes 122888 | tf_op jit(solution)/shard_map/ppermute | solution.py:576
  12.7 2.1 %collective-permute-start.1 = (bf16[4,32,160]{2,1,0:T(8,128)(2,1)}, bf16[4,32,160]{2,1,0:T(8,128)(2,1)S(1)}, u32[]{:S(2)}, u32[]{:S(2)}) collective-permute-start(bf16[4,32,160]{2,1,0:T(8,128)(2,1)} %get-tuple-element.32), channel_id=1, source_target_pairs={{0,3},{1,0},{2,1},{3,2},{4,7},{5,4},{6,5},{7,6},{8,11},{9,8},{10,9... | collective-permute-start | bytes 122888 | tf_op jit(solution)/shard_map/ppermute | solution.py:576
  14.8 2.9 %collective-permute-done.left = bf16[4,32,160]{2,1,0:T(8,128)(2,1)S(1)} collective-permute-done((bf16[4,32,160]{2,1,0:T(8,128)(2,1)}, bf16[4,32,160]{2,1,0:T(8,128)(2,1)S(1)}, u32[]{:S(2)}, u32[]{:S(2)}) %collective-permute-start) | collective-permute-done | bytes 40992 | tf_op jit(solution)/shard_map/ppermute | solution.py:576
  19.3 1.7 %collective-permute-start.3 = (bf16[104,256]{1,0:T(8,128)(2,1)S(1)}, bf16[104,256]{1,0:T(8,128)(2,1)S(1)}, u32[]{:S(2)}, u32[]{:S(2)}) collective-permute-start(bf16[104,256]{1,0:T(8,128)(2,1)S(1)} %get-tuple-element.35), channel_id=1, source_target_pairs={{0,8},{4,12},{8,0},{12,4},{16,24},{20,28},{24,16},{28,20},{1,9},{5... | collective-permute-start | bytes 159752 | tf_op jit(solution)/shard_map/ppermute | solution.py:588
  23.1 2.6 %collective-permute-start.7 = (bf16[104,256]{1,0:T(8,128)(2,1)S(1)}, bf16[104,256]{1,0:T(8,128)(2,1)S(1)}, u32[]{:S(2)}, u32[]{:S(2)}) collective-permute-start(bf16[104,256]{1,0:T(8,128)(2,1)S(1)} %get-tuple-element.39), channel_id=1, source_target_pairs={{0,24},{4,28},{8,16},{12,20},{16,8},{20,12},{24,0},{28,4},{1,25},{... | collective-permute-start | bytes 159752 | tf_op jit(solution)/shard_map/ppermute | solution.py:588
  25.7 5.5 %collective-permute-done.3.refs_2_ = bf16[104,256]{1,0:T(8,128)(2,1)S(1)} collective-permute-done((bf16[104,256]{1,0:T(8,128)(2,1)S(1)}, bf16[104,256]{1,0:T(8,128)(2,1)S(1)}, u32[]{:S(2)}, u32[]{:S(2)}) %collective-permute-start.3) | collective-permute-done | bytes 53280 | tf_op jit(solution)/shard_map/ppermute | solution.py:588
  31.5 2.4 %collective-permute-done.7.refs_6_ = bf16[104,256]{1,0:T(8,128)(2,1)S(1)} collective-permute-done((bf16[104,256]{1,0:T(8,128)(2,1)S(1)}, bf16[104,256]{1,0:T(8,128)(2,1)S(1)}, u32[]{:S(2)}, u32[]{:S(2)}) %collective-permute-start.7) | collective-permute-done | bytes 53280 | tf_op jit(solution)/shard_map/ppermute | solution.py:588
  33.9 1.8 %collective-permute-done.8.refs_7_ = bf16[104,256]{1,0:T(8,128)(2,1)S(1)} collective-permute-done((bf16[104,256]{1,0:T(8,128)(2,1)S(1)}, bf16[104,256]{1,0:T(8,128)(2,1)S(1)}, u32[]{:S(2)}, u32[]{:S(2)}) %collective-permute-start.8) | collective-permute-done | bytes 53280 | tf_op jit(solution)/shard_map/ppermute | solution.py:588
  35.7 7.2 %observe.1 = (bf16[8,464,256]{2,1,0:T(8,128)(2,1)S(1)}, f32[2,144,256]{2,1,0:T(8,128)S(1)}, bf16[2,144,256]{2,1,0:T(8,128)(2,1)S(1)}) custom-call(s32[2,512]{1,0:T(2,128)S(1)} %fusion.9.cells, f32[2,512]{1,0:T(2,128)S(1)} %fusion.10.weight, f32[2,512]{1,0:T(2,128)S(1)} %bitcast.45, bf16[8,360,256]{2,1,0:T(8,128)(2,1)} %all-to-all-done.got, ...), custom_call_target="tpu_custom_call" | custom-call | tf_op jit(solution)/shard_map/observe/pallas_call | solution.py:664
  44.1 3.0 %collective-permute-start.9 = (bf16[2,144,256]{2,1,0:T(8,128)(2,1)S(1)}, bf16[2,144,256]{2,1,0:T(8,128)(2,1)S(1)}, u32[]{:S(2)}, u32[]{:S(2)}) collective-permute-start(bf16[2,144,256]{2,1,0:T(8,128)(2,1)S(1)} %get-tuple-element.43), channel_id=1, source_target_pairs={{0,4},{4,8},{8,12},{12,16},{16,20},{20,24},{24,28},{1,5},{5,9},{9,... | collective-permute-start | bytes 442376 | tf_op jit(solution)/shard_map/ppermute | solution.py:582
  48.2 2.1 %collective-permute-start.11 = (bf16[144,256]{1,0:T(8,128)(2,1)S(1)}, bf16[144,256]{1,0:T(8,128)(2,1)S(1)}, u32[]{:S(2)}, u32[]{:S(2)}) collective-permute-start(bf16[144,256]{1,0:T(8,128)(2,1)S(1)} %get-tuple-element.45), channel_id=1, source_target_pairs={{0,1},{1,2},{2,3},{3,0},{4,5},{5,6},{6,7},{7,4},{8,9},{9,10},{10,1... | collective-permute-start | bytes 221192 | tf_op jit(solution)/shard_map/ppermute | solution.py:576
  50.3 2.3 %collective-permute-start.12 = (bf16[144,256]{1,0:T(8,128)(2,1)S(1)}, bf16[144,256]{1,0:T(8,128)(2,1)S(1)}, u32[]{:S(2)}, u32[]{:S(2)}) collective-permute-start(bf16[144,256]{1,0:T(8,128)(2,1)S(1)} %get-tuple-element.46), channel_id=1, source_target_pairs={{0,3},{1,0},{2,1},{3,2},{4,7},{5,4},{6,5},{7,6},{8,11},{9,8},{10,9... | collective-permute-start | bytes 221192 | tf_op jit(solution)/shard_map/ppermute | solution.py:576
  52.6 2.2 %collective-permute-done.11.west = bf16[144,256]{1,0:T(8,128)(2,1)S(1)} collective-permute-done((bf16[144,256]{1,0:T(8,128)(2,1)S(1)}, bf16[144,256]{1,0:T(8,128)(2,1)S(1)}, u32[]{:S(2)}, u32[]{:S(2)}) %collective-permute-start.11) | collective-permute-done | bytes 73760 | tf_op jit(solution)/shard_map/ppermute | solution.py:576
  54.8 2.1 %collective-permute-done.12.east = bf16[144,256]{1,0:T(8,128)(2,1)S(1)} collective-permute-done((bf16[144,256]{1,0:T(8,128)(2,1)S(1)}, bf16[144,256]{1,0:T(8,128)(2,1)S(1)}, u32[]{:S(2)}, u32[]{:S(2)}) %collective-permute-start.12) | collective-permute-done | bytes 73760 | tf_op jit(solution)/shard_map/ppermute | solution.py:576
  56.9 8.2 %analyse.1 = (bf16[464,256]{1,0:T(8,128)(2,1)S(1)}, bf16[464,256]{1,0:T(8,128)(2,1)S(1)}, bf16[464,256]{1,0:T(8,128)(2,1)S(1)}, bf16[464,256]{1,0:T(8,128)(2,1)S...) custom-call(bf16[8,464,256]{2,1,0:T(8,128)(2,1)S(1)} %get-tuple-elem, ...), custom_call_target="tpu_custom_call" | custom-call | tf_op jit(solution)/shard_map/analyse/pallas_call | solution.py:692
  65.4 2.8 %collective-permute-start.14 = (bf16[464,256]{1,0:T(8,128)(2,1)S(1)}, bf16[464,256]{1,0:T(8,128)(2,1)S(1)}, u32[]{:S(2)}, u32[]{:S(2)}) collective-permute-start(bf16[464,256]{1,0:T(8,128)(2,1)S(1)} %get-tuple-element.49), channel_id=1, source_target_pairs={{0,8},{4,12},{8,0},{12,4},{16,24},{20,28},{24,16},{28,20},{1,9},{5... | collective-permute-start | bytes 712712 | tf_op jit(solution)/shard_map/ppermute | solution.py:588
  68.2 2.9 %collective-permute-start.16 = (bf16[464,256]{1,0:T(8,128)(2,1)S(1)}, bf16[464,256]{1,0:T(8,128)(2,1)S(1)}, u32[]{:S(2)}, u32[]{:S(2)}) collective-permute-start(bf16[464,256]{1,0:T(8,128)(2,1)S(1)} %get-tuple-element.51), channel_id=1, source_target_pairs={{0,16},{4,20},{8,24},{12,28},{16,0},{20,4},{24,8},{28,12},{1,17},{... | collective-permute-start | bytes 712712 | tf_op jit(solution)/shard_map/ppermute | solution.py:588
  72.4 2.4 %collective-permute-done.14.refs_2_ = bf16[464,256]{1,0:T(8,128)(2,1)S(1)} collective-permute-done((bf16[464,256]{1,0:T(8,128)(2,1)S(1)}, bf16[464,256]{1,0:T(8,128)(2,1)S(1)}, u32[]{:S(2)}, u32[]{:S(2)}) %collective-permute-start.14) | collective-permute-done | bytes 237600 | tf_op jit(solution)/shard_map/ppermute | solution.py:588
  74.8 1.8 %collective-permute-start.19 = (bf16[464,256]{1,0:T(8,128)(2,1)S(1)}, bf16[464,256]{1,0:T(8,128)(2,1)S(1)}, u32[]{:S(2)}, u32[]{:S(2)}) collective-permute-start(bf16[464,256]{1,0:T(8,128)(2,1)S(1)} %get-tuple-element.54), channel_id=1, source_target_pairs={{0,28},{4,24},{8,20},{12,16},{16,12},{20,8},{24,4},{28,0},{1,29},{... | collective-permute-start | bytes 712712 | tf_op jit(solution)/shard_map/ppermute | solution.py:588
  76.6 2.7 %collective-permute-done.15.refs_3_ = bf16[464,256]{1,0:T(8,128)(2,1)S(1)} collective-permute-done((bf16[464,256]{1,0:T(8,128)(2,1)S(1)}, bf16[464,256]{1,0:T(8,128)(2,1)S(1)}, u32[]{:S(2)}, u32[]{:S(2)}) %collective-permute-start.15) | collective-permute-done | bytes 237600 | tf_op jit(solution)/shard_map/ppermute | solution.py:588
  79.4 13.0 %collective-permute-done.17.refs_5_ = bf16[464,256]{1,0:T(8,128)(2,1)S(1)} collective-permute-done((bf16[464,256]{1,0:T(8,128)(2,1)S(1)}, bf16[464,256]{1,0:T(8,128)(2,1)S(1)}, u32[]{:S(2)}, u32[]{:S(2)}) %collective-permute-start.17) | collective-permute-done | bytes 237600 | tf_op jit(solution)/shard_map/ppermute | solution.py:588
  92.4 2.4 %come_back.1 = bf16[3,60,32,160]{3,2,1,0:T(8,128)(2,1)} custom-call(bf16[464,256]{1,0:T(8,128)(2,1)S(1)} %get-tuple-element.47.refs_0_, bf16[464,256]{1,0:T(8,128)(2,1)S(1)} %collective-permute-done.13.refs_1_, bf16[464,256]{1,0:T(8,128)(2,1)S(1)} %collective-permute-done.14.refs_2_, bf16[464,256]{1,0:T(8,128)(2,1)S(1)} %collective-permute-done.15.refs_3_, ...), custom_call_target="tpu_custom_call" | custom-call | tf_op jit(solution)/shard_map/come_back/pallas_call | solution.py:700
  (39 shorter events, 7.8 us)
Async XLA Ops:
  0.0 18.3 %copy-start.1 = (f32[60,160]{1,0:T(8,128)S(1)}, f32[60,160]{1,0:T(8,128)}, u32[]{:S(2)}) copy-start(f32[60,160]{1,0:T(8,128)} %depth.3) | copy-start | bytes 115204
  5.0 30.7 %all-to-all-start = ((bf16[8,360,256]{2,1,0:T(8,128)(2,1)}), bf16[8,360,256]{2,1,0:T(8,128)(2,1)}, u32[]{:S(2)}, u32[]{:S(2)}) async-start(bf16[8,360,256]{2,1,0:T(8,128)(2,1)} %get-tuple-element.30), calls=%async_computation | async-start | bytes 2949120 | tf_op jit(solution)/shard_map/all_to_all | solution.py:592
  10.5 7.2 %collective-permute-start = (bf16[4,32,160]{2,1,0:T(8,128)(2,1)}, bf16[4,32,160]{2,1,0:T(8,128)(2,1)S(1)}, u32[]{:S(2)}, u32[]{:S(2)}) collective-permute-start(bf16[4,32,160]{2,1,0:T(8,128)(2,1)} %get-tuple-element.31), channel_id=1, source_target_pairs={{0,1},{1,2},{2,3},{3,0},{4,5},{5,6},{6,7},{7,4},{8,9},{9,10},{10,1... | collective-permute-start | bytes 122888 | tf_op jit(solution)/shard_map/ppermute | solution.py:576
  12.7 5.7 %collective-permute-start.1 = (bf16[4,32,160]{2,1,0:T(8,128)(2,1)}, bf16[4,32,160]{2,1,0:T(8,128)(2,1)S(1)}, u32[]{:S(2)}, u32[]{:S(2)}) collective-permute-start(bf16[4,32,160]{2,1,0:T(8,128)(2,1)} %get-tuple-element.32), channel_id=1, source_target_pairs={{0,3},{1,0},{2,1},{3,2},{4,7},{5,4},{6,5},{7,6},{8,11},{9,8},{10,9... | collective-permute-start | bytes 122888 | tf_op jit(solution)/shard_map/ppermute | solution.py:576
  14.8 16.7 %copy-start.5 = (s32[1,2]{1,0:T(1,128)S(1)}, s32[1,2]{1,0:T(1,128)}, u32[]{:S(2)}) copy-start(s32[1,2]{1,0:T(1,128)} %param.11) | copy-start | bytes 28
  14.8 20.9 %copy-start.2 = (f32[1,2,512]{2,1,0:T(2,128)S(1)}, f32[1,2,512]{2,1,0:T(2,128)}, u32[]{:S(2)}) copy-start(f32[1,2,512]{2,1,0:T(2,128)} %param.9) | copy-start | bytes 12292
  19.3 3.8 %collective-permute-start.2 = (bf16[104,256]{1,0:T(8,128)(2,1)S(1)}, bf16[104,256]{1,0:T(8,128)(2,1)S(1)}, u32[]{:S(2)}, u32[]{:S(2)}) collective-permute-start(bf16[104,256]{1,0:T(8,128)(2,1)S(1)} %get-tuple-element.34), channel_id=1, source_target_pairs={{0,4},{4,0},{8,12},{12,8},{16,20},{20,16},{24,28},{28,24},{1,5},{5... | collective-permute-start | bytes 159752 | tf_op jit(solution)/shard_map/ppermute | solution.py:588
  19.3 11.8 %collective-permute-start.3 = (bf16[104,256]{1,0:T(8,128)(2,1)S(1)}, bf16[104,256]{1,0:T(8,128)(2,1)S(1)}, u32[]{:S(2)}, u32[]{:S(2)}) collective-permute-start(bf16[104,256]{1,0:T(8,128)(2,1)S(1)} %get-tuple-element.35), channel_id=1, source_target_pairs={{0,8},{4,12},{8,0},{12,4},{16,24},{20,28},{24,16},{28,20},{1,9},{5... | collective-permute-start | bytes 159752 | tf_op jit(solution)/shard_map/ppermute | solution.py:588
  21.2 10.3 %collective-permute-start.4 = (bf16[104,256]{1,0:T(8,128)(2,1)S(1)}, bf16[104,256]{1,0:T(8,128)(2,1)S(1)}, u32[]{:S(2)}, u32[]{:S(2)}) collective-permute-start(bf16[104,256]{1,0:T(8,128)(2,1)S(1)} %get-tuple-element.36), channel_id=1, source_target_pairs={{0,12},{4,8},{8,4},{12,0},{16,28},{20,24},{24,20},{28,16},{1,13},{... | collective-permute-start | bytes 159752 | tf_op jit(solution)/shard_map/ppermute | solution.py:588
  21.4 10.1 %collective-permute-start.5 = (bf16[104,256]{1,0:T(8,128)(2,1)S(1)}, bf16[104,256]{1,0:T(8,128)(2,1)S(1)}, u32[]{:S(2)}, u32[]{:S(2)}) collective-permute-start(bf16[104,256]{1,0:T(8,128)(2,1)S(1)} %get-tuple-element.37), channel_id=1, source_target_pairs={{0,16},{4,20},{8,24},{12,28},{16,0},{20,4},{24,8},{28,12},{1,17},{... | collective-permute-start | bytes 159752 | tf_op jit(solution)/shard_map/ppermute | solution.py:588
  23.1 8.5 %collective-permute-start.6 = (bf16[104,256]{1,0:T(8,128)(2,1)S(1)}, bf16[104,256]{1,0:T(8,128)(2,1)S(1)}, u32[]{:S(2)}, u32[]{:S(2)}) collective-permute-start(bf16[104,256]{1,0:T(8,128)(2,1)S(1)} %get-tuple-element.38), channel_id=1, source_target_pairs={{0,20},{4,16},{8,28},{12,24},{16,4},{20,0},{24,12},{28,8},{1,21},{... | collective-permute-start | bytes 159752 | tf_op jit(solution)/shard_map/ppermute | solution.py:588
  23.1 10.8 %collective-permute-start.7 = (bf16[104,256]{1,0:T(8,128)(2,1)S(1)}, bf16[104,256]{1,0:T(8,128)(2,1)S(1)}, u32[]{:S(2)}, u32[]{:S(2)}) collective-permute-start(bf16[104,256]{1,0:T(8,128)(2,1)S(1)} %get-tuple-element.39), channel_id=1, source_target_pairs={{0,24},{4,28},{8,16},{12,20},{16,8},{20,12},{24,0},{28,4},{1,25},{... | collective-permute-start | bytes 159752 | tf_op jit(solution)/shard_map/ppermute | solution.py:588
  31.2 4.5 %collective-permute-start.8 = (bf16[104,256]{1,0:T(8,128)(2,1)S(1)}, bf16[104,256]{1,0:T(8,128)(2,1)S(1)}, u32[]{:S(2)}, u32[]{:S(2)}) collective-permute-start(bf16[104,256]{1,0:T(8,128)(2,1)S(1)} %get-tuple-element.40), channel_id=1, source_target_pairs={{0,28},{4,24},{8,20},{12,16},{16,12},{20,8},{24,4},{28,0},{1,29},{... | collective-permute-start | bytes 159752 | tf_op jit(solution)/shard_map/ppermute | solution.py:588
  42.8 4.3 %collective-permute-start.10 = (bf16[2,144,256]{2,1,0:T(8,128)(2,1)S(1)}, bf16[2,144,256]{2,1,0:T(8,128)(2,1)S(1)}, u32[]{:S(2)}, u32[]{:S(2)}) collective-permute-start(bf16[2,144,256]{2,1,0:T(8,128)(2,1)S(1)} %get-tuple-element.43), channel_id=1, source_target_pairs={{4,0},{8,4},{12,8},{16,12},{20,16},{24,20},{28,24},{5,1},{9,5},{13... | collective-permute-start | bytes 442376 | tf_op jit(solution)/shard_map/ppermute | solution.py:582
  44.1 4.0 %collective-permute-start.9 = (bf16[2,144,256]{2,1,0:T(8,128)(2,1)S(1)}, bf16[2,144,256]{2,1,0:T(8,128)(2,1)S(1)}, u32[]{:S(2)}, u32[]{:S(2)}) collective-permute-start(bf16[2,144,256]{2,1,0:T(8,128)(2,1)S(1)} %get-tuple-element.43), channel_id=1, source_target_pairs={{0,4},{4,8},{8,12},{12,16},{16,20},{20,24},{24,28},{1,5},{5,9},{9,... | collective-permute-start | bytes 442376 | tf_op jit(solution)/shard_map/ppermute | solution.py:582
  48.2 6.5 %collective-permute-start.11 = (bf16[144,256]{1,0:T(8,128)(2,1)S(1)}, bf16[144,256]{1,0:T(8,128)(2,1)S(1)}, u32[]{:S(2)}, u32[]{:S(2)}) collective-permute-start(bf16[144,256]{1,0:T(8,128)(2,1)S(1)} %get-tuple-element.45), channel_id=1, source_target_pairs={{0,1},{1,2},{2,3},{3,0},{4,5},{5,6},{6,7},{7,4},{8,9},{9,10},{10,1... | collective-permute-start | bytes 221192 | tf_op jit(solution)/shard_map/ppermute | solution.py:576
  50.3 6.6 %collective-permute-start.12 = (bf16[144,256]{1,0:T(8,128)(2,1)S(1)}, bf16[144,256]{1,0:T(8,128)(2,1)S(1)}, u32[]{:S(2)}, u32[]{:S(2)}) collective-permute-start(bf16[144,256]{1,0:T(8,128)(2,1)S(1)} %get-tuple-element.46), channel_id=1, source_target_pairs={{0,3},{1,0},{2,1},{3,2},{4,7},{5,4},{6,5},{7,6},{8,11},{9,8},{10,9... | collective-permute-start | bytes 221192 | tf_op jit(solution)/shard_map/ppermute | solution.py:576
  65.2 6.0 %collective-permute-start.13 = (bf16[464,256]{1,0:T(8,128)(2,1)S(1)}, bf16[464,256]{1,0:T(8,128)(2,1)S(1)}, u32[]{:S(2)}, u32[]{:S(2)}) collective-permute-start(bf16[464,256]{1,0:T(8,128)(2,1)S(1)} %get-tuple-element.48), channel_id=1, source_target_pairs={{0,4},{4,0},{8,12},{12,8},{16,20},{20,16},{24,28},{28,24},{1,5},{5... | collective-permute-start | bytes 712712 | tf_op jit(solution)/shard_map/ppermute | solution.py:588
  65.4 9.4 %collective-permute-start.14 = (bf16[464,256]{1,0:T(8,128)(2,1)S(1)}, bf16[464,256]{1,0:T(8,128)(2,1)S(1)}, u32[]{:S(2)}, u32[]{:S(2)}) collective-permute-start(bf16[464,256]{1,0:T(8,128)(2,1)S(1)} %get-tuple-element.49), channel_id=1, source_target_pairs={{0,8},{4,12},{8,0},{12,4},{16,24},{20,28},{24,16},{28,20},{1,9},{5... | collective-permute-start | bytes 712712 | tf_op jit(solution)/shard_map/ppermute | solution.py:588
  68.2 11.2 %collective-permute-start.15 = (bf16[464,256]{1,0:T(8,128)(2,1)S(1)}, bf16[464,256]{1,0:T(8,128)(2,1)S(1)}, u32[]{:S(2)}, u32[]{:S(2)}) collective-permute-start(bf16[464,256]{1,0:T(8,128)(2,1)S(1)} %get-tuple-element.50), channel_id=1, source_target_pairs={{0,12},{4,8},{8,4},{12,0},{16,28},{20,24},{24,20},{28,16},{1,13},{... | collective-permute-start | bytes 712712 | tf_op jit(solution)/shard_map/ppermute | solution.py:588
  68.2 11.1 %collective-permute-start.16 = (bf16[464,256]{1,0:T(8,128)(2,1)S(1)}, bf16[464,256]{1,0:T(8,128)(2,1)S(1)}, u32[]{:S(2)}, u32[]{:S(2)}) collective-permute-start(bf16[464,256]{1,0:T(8,128)(2,1)S(1)} %get-tuple-element.51), channel_id=1, source_target_pairs={{0,16},{4,20},{8,24},{12,28},{16,0},{20,4},{24,8},{28,12},{1,17},{... | collective-permute-start | bytes 712712 | tf_op jit(solution)/shard_map/ppermute | solution.py:588
  71.2 21.2 %collective-permute-start.17 = (bf16[464,256]{1,0:T(8,128)(2,1)S(1)}, bf16[464,256]{1,0:T(8,128)(2,1)S(1)}, u32[]{:S(2)}, u32[]{:S(2)}) collective-permute-start(bf16[464,256]{1,0:T(8,128)(2,1)S(1)} %get-tuple-element.52), channel_id=1, source_target_pairs={{0,20},{4,16},{8,28},{12,24},{16,4},{20,0},{24,12},{28,8},{1,21},{... | collective-permute-start | bytes 712712 | tf_op jit(solution)/shard_map/ppermute | solution.py:588
  71.2 21.2 %collective-permute-start.18 = (bf16[464,256]{1,0:T(8,128)(2,1)S(1)}, bf16[464,256]{1,0:T(8,128)(2,1)S(1)}, u32[]{:S(2)}, u32[]{:S(2)}) collective-permute-start(bf16[464,256]{1,0:T(8,128)(2,1)S(1)} %get-tuple-element.53), channel_id=1, source_target_pairs={{0,24},{4,28},{8,16},{12,20},{16,8},{20,12},{24,0},{28,4},{1,25},{... | collective-permute-start | bytes 712712 | tf_op jit(solution)/shard_map/ppermute | solution.py:588
  74.8 17.6 %collective-permute-start.19 = (bf16[464,256]{1,0:T(8,128)(2,1)S(1)}, bf16[464,256]{1,0:T(8,128)(2,1)S(1)}, u32[]{:S(2)}, u32[]{:S(2)}) collective-permute-start(bf16[464,256]{1,0:T(8,128)(2,1)S(1)} %get-tuple-element.54), channel_id=1, source_target_pairs={{0,28},{4,24},{8,20},{12,16},{16,12},{20,8},{24,4},{28,0},{1,29},{... | collective-permute-start | bytes 712712 | tf_op jit(solution)/shard_map/ppermute | solution.py:588
  (3 other events, 36.3 us)

commit v6 on v5

--- a/solution.py
+++ b/solution.py
@@ -164,17 +164,24 @@
 
 LANES = 128
 GROUPS = 23
-CELLS = 464
 INNER = 360
 OUTER = 104
+BLOCK = 112
+FIRST = 240
+SECOND = 224
 F32 = jnp.float32
 BF16 = jnp.bfloat16
 PACKED = 144
+ORDER = (6, 7, 2, 4, 3, 5, 1, 0)
 MIB = 1024 * 1024
 
 
 def params(size):
     return pltpu.CompilerParams(vmem_limit_bytes=size * MIB)
+
+
+def cost(flops, moved):
+    return pl.CostEstimate(flops=flops, bytes_accessed=moved, transcendentals=0)
 
 
 def identity(size, dtype):
@@ -406,36 +413,42 @@
     put_group(staged, jnp.concatenate([ends[0], ends[1]], axis=0), eye, 60)
     put_group(staged, jnp.concatenate([ends[2], jnp.zeros_like(ends[2])], axis=0), eye, 80)
     me = lax.axis_index("mem")
-    for d in range(8):
-        outs[d][...] = staged[me ^ d].astype(BF16)
-
-
-def observe_kernel(cells, weight, target, got, *refs):
+    for k, d in enumerate(ORDER):
+        outs[k][...] = staged[me ^ d].astype(BF16)
+
+
+def spread_block(source, held, wide, start, lane):
+    spans = [slice(h * LANES, (h + 1) * LANES) for h in range(2)]
+    count = source.shape[1]
+    here = pl.ds(start, 16)
+    blocks = exchange_lanes([[source[q, here, span] for span in spans] for q in range(8)], lane)
+    for q in range(8):
+        to = pl.ds(pl.multiple_of(q * count + start, 8), 16)
+        for h in range(2):
+            wide[h, to, :] = blocks[q][h].astype(F32)
+            held[q, here, spans[h]] = blocks[q][h]
+
+
+def spread_kernel(got, held, wide):
+    lane = lax.broadcasted_iota(jnp.int32, (16, LANES), 1)
+
+    def step(index, carry):
+        spread_block(got, held, wide, pl.multiple_of(index * 16, 16), lane)
+        return carry
+
+    lax.fori_loop(0, 22, step, 0, unroll=4)
+    spread_block(got, held, wide, INNER - 16, lane)
+
+
+def observe_kernel(cells, weight, target, wide_inner, *refs):
     edges, (held, gram, short, joined, wide, seen) = refs[:8], refs[8:]
     lane = lax.broadcasted_iota(jnp.int32, (16, LANES), 1)
     me = lax.axis_index("mem")
-    for d in range(8):
-        joined[me ^ d, 8:112, :] = edges[d][...]
-    joined[:, 0:8, :] = got[:, 352:360, :]
-    spans = [slice(h * LANES, (h + 1) * LANES) for h in range(2)]
-
-    def spread_out(source, offset):
-        def step(index, carry):
-            here = pl.ds(pl.multiple_of(index * 16, 16), 16)
-            blocks = [[source[q, here, span] for span in spans] for q in range(8)]
-            blocks = exchange_lanes(blocks, lane)
-            there = pl.ds(pl.multiple_of(index * 16 + offset, 16), 16)
-            for q in range(8):
-                to = pl.ds(pl.multiple_of(q * CELLS + index * 16 + offset, 16), 16)
-                for h in range(2):
-                    wide[h, to, :] = blocks[q][h].astype(F32)
-                    held[q, there, spans[h]] = blocks[q][h]
-            return carry
-
-        return step
-
-    lax.fori_loop(0, 22, spread_out(got, 0), 0, unroll=4)
-    lax.fori_loop(0, 7, spread_out(joined, 352), 0, unroll=4)
+    for k, d in enumerate(ORDER):
+        joined[me ^ d, 0:OUTER, :] = edges[k][...]
+    joined[:, OUTER:BLOCK, :] = jnp.zeros((8, BLOCK - OUTER, 256), BF16)
+    for index in range(BLOCK // 16):
+        spread_block(joined, held, wide, index * 16, lane)
     slots = seen.shape[2]
     unroll = 16
 
@@ -444,8 +457,13 @@
             for k in range(unroll):
                 slot = index * unroll + k
                 row = cells[t, slot]
+                is_inner = row < 8 * INNER
+                near = jnp.where(is_inner, row, 0)
+                far = jnp.where(is_inner, 0, row - 8 * INNER)
                 for h in range(2):
-                    seen[t, h, pl.ds(slot, 1), :] = wide[h, pl.ds(row, 1), :]
+                    first = wide_inner[h, pl.ds(near, 1), :]
+                    second = wide[h, pl.ds(far, 1), :]
+                    seen[t, h, pl.ds(slot, 1), :] = jnp.where(is_inner, first, second)
         return carry
 
     lax.fori_loop(0, slots // unroll, pick, 0)
@@ -471,8 +489,59 @@
     to_east[...] = total[1].astype(BF16)
 
 
-def analyse_kernel(held, column, west, east, *refs):
-    outs, (results, ordered) = refs[:8], refs[8:]
+def prepare_kernel(inner, outer, *refs):
+    average = jnp.full((256, LANES), 1.0 / 256, BF16)
+    for q in range(8):
+        pieces = (inner[q, 0:FIRST], jnp.concatenate([inner[q, FIRST:INNER], outer[q, 0:OUTER]], axis=0))
+        for k, piece in enumerate(pieces):
+            mean = dot_nn(piece, average)
+            refs[2 * k + 1][q] = mean
+            mean = jnp.concatenate([mean, mean], axis=1)
+            refs[2 * k][q] = (piece.astype(F32) - mean).astype(BF16)
+
+
+def send_back(results, outs):
+    lane = lax.broadcasted_iota(jnp.int32, (16, LANES), 1)
+    spans = [slice(h * LANES, (h + 1) * LANES) for h in range(2)]
+
+    def step(index, carry):
+        here = pl.ds(pl.multiple_of(index * 16, 16), 16)
+        blocks = [[results[q, here, span] for span in spans] for q in range(8)]
+        blocks = exchange_lanes(blocks, lane)
+        for q in range(8):
+            for h in range(2):
+                outs[ORDER.index(q)][here, spans[h]] = blocks[q][h]
+        return carry
+
+    lax.fori_loop(0, results.shape[1] // 16, step, 0, unroll=4)
+
+
+def apply_maps(anomaly, mean, maps, results, q, edge, order):
+    count = results.shape[1]
+    low, high = edge // 16 * 16, (edge + 15) // 16 * 16
+    first = dot_nt(anomaly[q, 0:high], maps[order[0]])
+    centre = jnp.concatenate([mean[q], mean[q]], axis=1)
+    results[q, 0:low] = (centre[0:low] + first[0:low]).astype(BF16)
+    if low == count:
+        return
+    second = dot_nt(anomaly[q, low:count], maps[order[1]])
+    if low < high:
+        near = lax.broadcasted_iota(jnp.int32, (16, 256), 0) < edge - low
+        both = jnp.where(near, first[low:high], second[0:16])
+        results[q, low:high] = (centre[low:high] + both).astype(BF16)
+    results[q, high:count] = (centre[high:count] + second[high - low : count - low]).astype(BF16)
+
+
+def second_kernel(maps, anomaly, mean, *refs):
+    outs, results = refs[:8], refs[8]
+    both = [maps[0], maps[1]]
+    for q in range(8):
+        apply_maps(anomaly, mean, both, results, q, 180, (0, 1))
+    send_back(results, outs)
+
+
+def analyse_kernel(column, west, east, anomaly, mean, *refs):
+    outs, (kept, results, ordered) = refs[:8], refs[8:]
     size = 256
     eye = identity(size, F32)
     beside = (west[...].astype(F32) + column[1], column[0] + east[...].astype(F32))
@@ -507,66 +576,60 @@
     me = lax.axis_index("mem")
     for t in range(2):
         maps.append(jnp.concatenate([ordered[t, me ^ d] for d in range(8)], axis=0))
-    average = jnp.full((size, size), 1.0 / size, BF16)
-    near = lax.broadcasted_iota(jnp.int32, (16, size), 0) < 4
-
+        kept[t] = maps[t]
     for q in range(8):
-        cells = held[q]
-        mean = dot_nn(cells, average)
-        anomaly = (cells.astype(F32) - mean).astype(BF16)
-        edge = 180 if q < 6 else 240
-        low, high = edge // 16 * 16, (edge + 15) // 16 * 16
-        second = mean[0:high] + dot_nt(anomaly[0:high], maps[1])
-        first = mean[low:432] + dot_nt(anomaly[low:432], maps[0])
-        last = mean[416:464] + dot_nt(anomaly[416:464], maps[1])
-        results[q, 0:low] = second[0:low].astype(BF16)
-        if low < high:
-            both = jnp.where(near, second[low:high], first[0:16])
-            results[q, low:high] = both.astype(BF16)
-        results[q, high:416] = first[high - low : 416 - low].astype(BF16)
-        both = jnp.where(near, first[416 - low : 432 - low], last[0:16])
-        results[q, 416:432] = both.astype(BF16)
-        results[q, 432:464] = last[16:48].astype(BF16)
-    lane = lax.broadcasted_iota(jnp.int32, (16, LANES), 1)
-
-    def gather_in(index, carry):
-        here = pl.ds(pl.multiple_of(index * 16, 16), 16)
-        spans = [slice(h * LANES, (h + 1) * LANES) for h in range(2)]
-        blocks = [[results[q, here, span] for span in spans] for q in range(8)]
-        blocks = exchange_lanes(blocks, lane)
-        for q in range(8):
-            for h in range(2):
-                outs[q][here, spans[h]] = blocks[q][h]
-        return carry
-
-    lax.fori_loop(0, CELLS // 16, gather_in, 0, unroll=4)
-
-
-def return_kernel(*refs):
+        apply_maps(anomaly, mean, maps, results, q, 180 if q < 6 else FIRST, (1, 0))
+    send_back(results, outs)
+
+
+def spread_strips(got, wide):
+    me = lax.axis_index("mem")
+    for k, d in enumerate(ORDER):
+        wide[me ^ d] = got[k][...].astype(F32)
+
+
+def take_group(wide, turned, eye, g, shape):
+    rows = shape[2] // 8
+    for s in range(8):
+        turned[g, rows * s : rows * (s + 1), :] = wide[s, rows * g : rows * (g + 1), :]
+    return dot_nt(eye, turned[g].astype(BF16)).astype(BF16).reshape(shape)
+
+
+def first_return_kernel(*refs):
     got, (out, wide, turned, planes, sent) = refs[:8], refs[8:]
-    members, latitudes = planes.shape[2:]
-    rows = latitudes // 8
-    me = lax.axis_index("mem")
-    for d in range(8):
-        wide[me ^ d] = got[d][...].astype(F32)
+    shape = (8,) + planes.shape[2:]
+    spread_strips(got, wide)
     eye = identity(256, BF16)
-
-    def take(g):
-        for s in range(8):
-            turned[g, rows * s : rows * (s + 1), :] = wide[s, rows * g : rows * (g + 1), :]
-        block = dot_nt(eye, turned[g].astype(BF16)).astype(BF16)
-        return block.reshape(8, members, latitudes)
-
-    mixed = take(21)
-    planes[0, 56:60] = mixed[0:4]
-    planes[1, 56:60] = mixed[4:8]
-    planes[2, 56:60] = take(22)[0:4]
     copies = []
     for v in range(3):
-        for index in range(7):
-            planes[v, 8 * index : 8 * index + 8] = take(group_of(v, index))
-        copies.append(pltpu.make_async_copy(planes.at[v], out.at[v], sent.at[v]))
+        for index in range(3, 7):
+            at = 8 * (index - 3)
+            planes[v, at : at + 8] = take_group(wide, turned, eye, group_of(v, index), shape)
+        copies.append(pltpu.make_async_copy(planes.at[v], out.at[v, pl.ds(24, 32)], sent.at[v]))
         copies[v].start()
+    for copy in copies:
+        copy.wait()
+
+
+def second_return_kernel(*refs):
+    got, (_, out, wide, turned, planes, sent) = refs[:8], refs[8:]
+    shape = (8,) + planes.shape[2:]
+    spread_strips(got, wide)
+    eye = identity(256, BF16)
+    mixed = take_group(wide, turned, eye, 9, shape)
+    planes[0, 24:28] = mixed[0:4]
+    planes[1, 24:28] = mixed[4:8]
+    planes[2, 24:28] = take_group(wide, turned, eye, 10, shape)[0:4]
+    copies = []
+    for v in range(3):
+        for index in range(3):
+            at = 8 * index
+            block = take_group(wide, turned, eye, group_of(v, index) - 12, shape)
+            planes[v, at : at + 8] = block
+        for k, (at, to, count) in enumerate(((0, 0, 24), (24, 56, 4))):
+            source, target = planes.at[v, pl.ds(at, count)], out.at[v, pl.ds(to, count)]
+            copies.append(pltpu.make_async_copy(source, target, sent.at[2 * v + k]))
+            copies[-1].start()
     for copy in copies:
         copy.wait()
 
@@ -584,8 +647,11 @@
 
 def partners(values):
     count = len(values)
-    pairs = [[(i, i ^ d) for i in range(count)] for d in range(count)]
-    return [values[0]] + [lax.ppermute(values[d], "mem", pairs[d]) for d in range(1, count)]
+    moved = []
+    for d, value in zip(ORDER, values):
+        pairs = [(i, i ^ d) for i in range(count)]
+        moved.append(value if d == 0 else lax.ppermute(value, "mem", pairs))
+    return moved
 
 
 def swap(value):
@@ -604,7 +670,9 @@
     is_last = column >= 56
     group = jnp.where(is_last, 21 + variable // 2, group)
     place = jnp.where(is_last, column - 56 + 4 * (variable % 2), place)
-    return place * CELLS + group * 20 + cell % 20
+    first = place * INNER + group * 20
+    last = 8 * INNER + place * BLOCK + (group - 18) * 20
+    return jnp.where(group < 18, first, last) + cell % 20
 
 
 def on_device_fast(
@@ -661,22 +729,44 @@
     live = jnp.arange(slots, dtype=jnp.int32)[None, :] < observed_count[0][:, None]
     root = jnp.sqrt(jnp.where(live, 1.0 / error_variance[0], 0.0))
     vmem = pl.BlockSpec(memory_space=pltpu.VMEM)
-    held, gram, short = pl.pallas_call(
+    held_inner, wide = pl.pallas_call(
+        spread_kernel,
+        out_shape=(
+            jax.ShapeDtypeStruct((8, INNER, 256), BF16),
+            jax.ShapeDtypeStruct((2, 8 * INNER, LANES), F32),
+        ),
+        compiler_params=params(8),
+        cost_estimate=cost(1, 4 * MIB),
+        name="spread",
+    )(got)
+    held_outer, gram, short = pl.pallas_call(
         observe_kernel,
         out_shape=(
-            jax.ShapeDtypeStruct((8, CELLS, 256), BF16),
+            jax.ShapeDtypeStruct((8, BLOCK, 256), BF16),
             jax.ShapeDtypeStruct((2, PACKED, 256), F32),
             jax.ShapeDtypeStruct((2, PACKED, 256), BF16),
         ),
         in_specs=[pl.BlockSpec(memory_space=pltpu.SMEM)] + [vmem] * 11,
         scratch_shapes=[
-            pltpu.VMEM((8, 112, 256), BF16),
-            pltpu.VMEM((2, 8 * CELLS, LANES), F32),
+            pltpu.VMEM((8, BLOCK, 256), BF16),
+            pltpu.VMEM((2, 8 * BLOCK, LANES), F32),
             pltpu.VMEM((2, 2, slots, LANES), F32),
         ],
-        compiler_params=params(20),
+        compiler_params=params(16),
         name="observe",
-    )(rows, root, observed_value[0], got, *got_edges)
+    )(rows, root, observed_value[0], wide, *got_edges)
+    anomaly_1, mean_1, anomaly_2, mean_2 = pl.pallas_call(
+        prepare_kernel,
+        out_shape=(
+            jax.ShapeDtypeStruct((8, FIRST, 256), BF16),
+            jax.ShapeDtypeStruct((8, FIRST, LANES), F32),
+            jax.ShapeDtypeStruct((8, SECOND, 256), BF16),
+            jax.ShapeDtypeStruct((8, SECOND, LANES), F32),
+        ),
+        compiler_params=params(12),
+        cost_estimate=cost(1, 6 * MIB),
+        name="prepare",
+    )(held_inner, held_outer)
 
     below = along(short, "mem", 1)
     above = along(short, "mem", -1)
@@ -689,27 +779,54 @@
     )(gram, below, above)
     west = around(to_east, "band", 1)
     east = around(to_west, "band", -1)
-    back = pl.pallas_call(
+    *back, maps = pl.pallas_call(
         analyse_kernel,
-        out_shape=(jax.ShapeDtypeStruct((CELLS, 256), BF16),) * 8,
-        scratch_shapes=[pltpu.VMEM((8, CELLS, 256), BF16), pltpu.VMEM((2, 8, 32, 256), BF16)],
+        out_shape=(jax.ShapeDtypeStruct((FIRST, 256), BF16),) * 8
+        + (jax.ShapeDtypeStruct((2, 256, 256), BF16),),
+        scratch_shapes=[pltpu.VMEM((8, FIRST, 256), BF16), pltpu.VMEM((2, 8, 32, 256), BF16)],
         compiler_params=params(20),
         name="analyse",
-    )(held, column, west, east)
-    returned = partners(back)
-    planes = pl.pallas_call(
-        return_kernel,
-        out_shape=jax.ShapeDtypeStruct(planes.shape, BF16),
+    )(column, west, east, anomaly_1, mean_1)
+    first = partners(back)
+    back = pl.pallas_call(
+        second_kernel,
+        out_shape=(jax.ShapeDtypeStruct((SECOND, 256), BF16),) * 8,
+        scratch_shapes=[pltpu.VMEM((8, SECOND, 256), BF16)],
+        compiler_params=params(16),
+        cost_estimate=cost(1, 6 * MIB),
+        name="second",
+    )(maps, anomaly_2, mean_2)
+    second = partners(back)
+    result = jax.ShapeDtypeStruct(planes.shape, BF16)
+    half = pl.pallas_call(
+        first_return_kernel,
+        out_shape=result,
         out_specs=far,
         scratch_shapes=[
-            pltpu.VMEM((8, CELLS, 256), F32),
-            pltpu.VMEM((GROUPS, latitudes, 256), F32),
-            pltpu.VMEM(planes.shape, BF16),
+            pltpu.VMEM((8, FIRST, 256), F32),
+            pltpu.VMEM((12, latitudes, 256), F32),
+            pltpu.VMEM((3, 32, members, latitudes), BF16),
             pltpu.SemaphoreType.DMA((3,)),
         ],
-        compiler_params=params(24),
-        name="come_back",
-    )(*returned)
+        compiler_params=params(20),
+        cost_estimate=cost(1, 4 * MIB),
+        name="first_return",
+    )(*first)
+    planes = pl.pallas_call(
+        second_return_kernel,
+        out_shape=result,
+        in_specs=[vmem] * 8 + [far],
+        out_specs=far,
+        scratch_shapes=[
+            pltpu.VMEM((8, SECOND, 256), F32),
+            pltpu.VMEM((11, latitudes, 256), F32),
+            pltpu.VMEM((3, 28, members, latitudes), BF16),
+            pltpu.SemaphoreType.DMA((6,)),
+        ],
+        input_output_aliases={8: 0},
+        compiler_params=params(20),
+        name="second_return",
+    )(*second, half)
     return jnp.transpose(planes, (2, 0, 1, 3))
 
 

time: 95.2 us -> 92.2 us (0.968)
  waiting for transfers between devices: 36.7 us -> 20.3 us
  starting transfers between devices: 34 us -> 43.2 us
  Pallas kernels: 23.8 us -> 27.9 us
    ppermute x14 -> x21, waiting for transfers between devices: 27.8 us -> 12.6 us  [partners(): moved.append(value if d == 0 else lax.ppermute(value, 'mem', pairs))]
    ppermute x14 -> x21, starting transfers between devices: 15.6 us -> 24.8 us  [partners(): moved.append(value if d == 0 else lax.ppermute(value, 'mem', pairs))]
    pallas_call x3 -> x7, Pallas kernels: 17.8 us -> 21.8 us  [the longest x1 6.59 us: on_device_fast(): pl.pallas_call(observe_kernel, out_shape=(jax.ShapeDtypeStruct((8, BLOCK,...]
    ppermute x4, waiting for transfers between devices: 7.88 us -> 6.73 us  [around(): lax.ppermute(value, axis, [(i, (i + step) % count) for i in range(count)])]
  transfers between devices with their start and end apart: 21 -> 28, of which waited for: 11 -> 13; matrix products, arithmetic and copies ran while one was open for 0% -> 0% of each run, Pallas kernels for 1% -> 9%
where the time goes in v6:
time: 92.2 us; the launch traced here: 92 us
  starting transfers between devices  43.2 us (47%)
  Pallas kernels  27.9 us (30%)
  waiting for transfers between devices  20.3 us (22%)
    ppermute x21, starting transfers between devices, partners(): moved.append(value if d == 0 else lax.ppermute(value, 'mem', pairs))  24.8 us
    ppermute x21, waiting for transfers between devices, partners(): moved.append(value if d == 0 else lax.ppermute(value, 'mem', pairs))  12.6 us
    ppermute x4, starting transfers between devices, around(): lax.ppermute(value, axis, [(i, (i + step) % count) for i in range(count)])  8.68 us
    ppermute x4, waiting for transfers between devices, around(): lax.ppermute(value, axis, [(i, (i + step) % count) for i in range(count)])  6.73 us
    pallas_call x1, Pallas kernels, on_device_fast(): pl.pallas_call(observe_kernel, out_shape=(jax.ShapeDtypeStruct((8, BLOCK,...  6.59 us
    pallas_call x1, Pallas kernels, on_device_fast(): pl.pallas_call(analyse_kernel, out_shape=(jax.ShapeDtypeStruct((FIRST, 25...  6.06 us
    all_to_all x1, starting transfers between devices, swap(): return lax.all_to_all(value, 'mem', split_axis=0, concat_axis=0, tiled=True)  5.31 us
    pallas_call x1, Pallas kernels, on_device_fast(): pl.pallas_call(inner_kernel, out_shape=(jax.ShapeDtypeStruct((8, INNER, 2...  5.11 us
  transfers between devices with their start and end apart: 28, of which 13 were waited for; matrix products, arithmetic and copies ran while one was open for 0% of the time, Pallas kernels for 9%

profile of v6, /device:TPU:0, one launch (start us, length us, event | category | flops | bytes accessed | tf_op | source)
XLA Modules:
  0.0 92.0 jit_solution(5032269904931018039)
XLA Ops:
  0.0 5.1 %inner.1 = (bf16[8,360,256]{2,1,0:T(8,128)(2,1)}, bf16[4,32,160]{2,1,0:T(8,128)(2,1)}, bf16[4,32,160]{2,1,0:T(8,128)(2,1)}) custom-call(bf16[3,60,32,160]{3,2,1,0:T(8,128)(2,1)} %bitcast.42, f32[60,160]{1,0:T(8,128)} %depth.3), custom_call_target="tpu_custom_call" | custom-call | tf_op jit(solution)/shard_map/inner/pallas_call | solution.py:686
  5.1 5.3 %all-to-all-start = ((bf16[8,360,256]{2,1,0:T(8,128)(2,1)}), bf16[8,360,256]{2,1,0:T(8,128)(2,1)}, u32[]{:S(2)}, u32[]{:S(2)}) async-start(bf16[8,360,256]{2,1,0:T(8,128)(2,1)} %get-tuple-element.45), calls=%async_computation | async-start | bytes 2949120 | tf_op jit(solution)/shard_map/all_to_all | solution.py:658
  10.5 2.2 %collective-permute-start = (bf16[4,32,160]{2,1,0:T(8,128)(2,1)S(1)}, bf16[4,32,160]{2,1,0:T(8,128)(2,1)S(1)}, u32[]{:S(2)}, u32[]{:S(2)}) collective-permute-start(bf16[4,32,160]{2,1,0:T(8,128)(2,1)S(1)} %copy-done.7), channel_id=1, source_target_pairs={{0,1},{1,2},{2,3},{3,0},{4,5},{5,6},{6,7},{7,4},{8,9},{9,10},{10,1... | collective-permute-start | bytes 122888 | tf_op jit(solution)/shard_map/ppermute | solution.py:639
  12.7 2.1 %collective-permute-start.1 = (bf16[4,32,160]{2,1,0:T(8,128)(2,1)S(1)}, bf16[4,32,160]{2,1,0:T(8,128)(2,1)S(1)}, u32[]{:S(2)}, u32[]{:S(2)}) collective-permute-start(bf16[4,32,160]{2,1,0:T(8,128)(2,1)S(1)} %copy-done.6), channel_id=1, source_target_pairs={{0,3},{1,0},{2,1},{3,2},{4,7},{5,4},{6,5},{7,6},{8,11},{9,8},{10,9... | collective-permute-start | bytes 122888 | tf_op jit(solution)/shard_map/ppermute | solution.py:639
  14.8 2.6 %collective-permute-done.left = bf16[4,32,160]{2,1,0:T(8,128)(2,1)S(1)} collective-permute-done((bf16[4,32,160]{2,1,0:T(8,128)(2,1)S(1)}, bf16[4,32,160]{2,1,0:T(8,128)(2,1)S(1)}, u32[]{:S(2)}, u32[]{:S(2)}) %collective-permute-start) | collective-permute-done | bytes 40992 | tf_op jit(solution)/shard_map/ppermute | solution.py:639
  19.0 2.7 %collective-permute-start.2 = (bf16[104,256]{1,0:T(8,128)(2,1)S(1)}, bf16[104,256]{1,0:T(8,128)(2,1)S(1)}, u32[]{:S(2)}, u32[]{:S(2)}) collective-permute-start(bf16[104,256]{1,0:T(8,128)(2,1)S(1)} %get-tuple-element.49), channel_id=1, source_target_pairs={{0,24},{4,28},{8,16},{12,20},{16,8},{20,12},{24,0},{28,4},{1,25},{... | collective-permute-start | bytes 159752 | tf_op jit(solution)/shard_map/ppermute | solution.py:653
  25.1 7.1 %collective-permute-done.2.refs_0_ = bf16[104,256]{1,0:T(8,128)(2,1)S(1)} collective-permute-done((bf16[104,256]{1,0:T(8,128)(2,1)S(1)}, bf16[104,256]{1,0:T(8,128)(2,1)S(1)}, u32[]{:S(2)}, u32[]{:S(2)}) %collective-permute-start.2) | collective-permute-done | bytes 53280 | tf_op jit(solution)/shard_map/ppermute | solution.py:653
  33.1 3.3 %spread.1 = (bf16[8,360,256]{2,1,0:T(8,128)(2,1)S(1)}, f32[2,2880,128]{2,1,0:T(8,128)S(1)}) custom-call(bf16[8,360,256]{2,1,0:T(8,128)(2,1)} %all-to-all-done.got), custom_call_target="tpu_custom_call" | custom-call | flops 1 | bytes 4194304 | tf_op jit(solution)/shard_map/spread/pallas_call | solution.py:732
  36.5 6.6 %observe.1 = (bf16[8,112,256]{2,1,0:T(8,128)(2,1)S(1)}, f32[2,144,256]{2,1,0:T(8,128)S(1)}, bf16[2,144,256]{2,1,0:T(8,128)(2,1)S(1)}) custom-call(s32[2,512]{1,0:T(2,128)S(1)} %fusion.4.cells, f32[2,512]{1,0:T(2,128)S(1)} %fusion.8.weight, f32[2,512]{1,0:T(2,128)S(1)} %bitcast.45, f32[2,2880,128]{2,1,0:T(8,128)S(1)} %get-tuple-element.46.wide_inner, ...), custom_call_target="tpu_custom_call" | custom-call | tf_op jit(solution)/shard_map/observe/pallas_call | solution.py:742
  44.4 3.0 %collective-permute-start.9 = (bf16[2,144,256]{2,1,0:T(8,128)(2,1)S(1)}, bf16[2,144,256]{2,1,0:T(8,128)(2,1)S(1)}, u32[]{:S(2)}, u32[]{:S(2)}) collective-permute-start(bf16[2,144,256]{2,1,0:T(8,128)(2,1)S(1)} %get-tuple-element.58), channel_id=1, source_target_pairs={{0,4},{4,8},{8,12},{12,16},{16,20},{20,24},{24,28},{1,5},{5,9},{9,... | collective-permute-start | bytes 442376 | tf_op jit(solution)/shard_map/ppermute | solution.py:645
  48.5 2.1 %collective-permute-start.11 = (bf16[144,256]{1,0:T(8,128)(2,1)S(1)}, bf16[144,256]{1,0:T(8,128)(2,1)S(1)}, u32[]{:S(2)}, u32[]{:S(2)}) collective-permute-start(bf16[144,256]{1,0:T(8,128)(2,1)S(1)} %get-tuple-element.60), channel_id=1, source_target_pairs={{0,1},{1,2},{2,3},{3,0},{4,5},{5,6},{6,7},{7,4},{8,9},{9,10},{10,1... | collective-permute-start | bytes 221192 | tf_op jit(solution)/shard_map/ppermute | solution.py:639
  50.6 2.3 %collective-permute-start.12 = (bf16[144,256]{1,0:T(8,128)(2,1)S(1)}, bf16[144,256]{1,0:T(8,128)(2,1)S(1)}, u32[]{:S(2)}, u32[]{:S(2)}) collective-permute-start(bf16[144,256]{1,0:T(8,128)(2,1)S(1)} %get-tuple-element.61), channel_id=1, source_target_pairs={{0,3},{1,0},{2,1},{3,2},{4,7},{5,4},{6,5},{7,6},{8,11},{9,8},{10,9... | collective-permute-start | bytes 221192 | tf_op jit(solution)/shard_map/ppermute | solution.py:639
  55.0 1.9 %collective-permute-done.12.east = bf16[144,256]{1,0:T(8,128)(2,1)S(1)} collective-permute-done((bf16[144,256]{1,0:T(8,128)(2,1)S(1)}, bf16[144,256]{1,0:T(8,128)(2,1)S(1)}, u32[]{:S(2)}, u32[]{:S(2)}) %collective-permute-start.12) | collective-permute-done | bytes 73760 | tf_op jit(solution)/shard_map/ppermute | solution.py:639
  56.9 6.1 %analyse.1 = (bf16[240,256]{1,0:T(8,128)(2,1)S(1)}, bf16[240,256]{1,0:T(8,128)(2,1)S(1)}, bf16[240,256]{1,0:T(8,128)(2,1)S(1)}, bf16[240,256]{1,0:T(8,128)(2,1)S...) custom-call(f32[2,144,256]{2,1,0:T(8,128)S(1)} %get-tuple-element.59, ...), custom_call_target="tpu_custom_call" | custom-call | tf_op jit(solution)/shard_map/analyse/pallas_call | solution.py:782
  63.0 4.2 %collective-permute-start.20 = (bf16[240,256]{1,0:T(8,128)(2,1)S(1)}, bf16[240,256]{1,0:T(8,128)(2,1)S(1)}, u32[]{:S(2)}, u32[]{:S(2)}) collective-permute-start(bf16[240,256]{1,0:T(8,128)(2,1)S(1)} %get-tuple-element.77), channel_id=1, source_target_pairs={{0,24},{4,28},{8,16},{12,20},{16,8},{20,12},{24,0},{28,4},{1,25},{... | collective-permute-start | bytes 368648 | tf_op jit(solution)/shard_map/ppermute | solution.py:653
  67.2 2.0 %second.1 = (bf16[224,256]{1,0:T(8,128)(2,1)S(1)}, bf16[224,256]{1,0:T(8,128)(2,1)S(1)}, bf16[224,256]{1,0:T(8,128)(2,1)S(1)}, bf16[224,256]{1,0:T(8,128)(2,1)S(...) custom-call(bf16[2,256,256]{2,1,0:T(8,128)(2,1)S(1)} %get-tuple-elem, ...), custom_call_target="tpu_custom_call" | custom-call | flops 1 | bytes 6291456 | tf_op jit(solution)/shard_map/second/pallas_call | solution.py:791
  69.4 2.6 %collective-permute-start.14 = (bf16[224,256]{1,0:T(8,128)(2,1)S(1)}, bf16[224,256]{1,0:T(8,128)(2,1)S(1)}, u32[]{:S(2)}, u32[]{:S(2)}) collective-permute-start(bf16[224,256]{1,0:T(8,128)(2,1)S(1)} %get-tuple-element.70), channel_id=1, source_target_pairs={{0,28},{4,24},{8,20},{12,16},{16,12},{20,8},{24,4},{28,0},{1,29},{... | collective-permute-start | bytes 344072 | tf_op jit(solution)/shard_map/ppermute | solution.py:653
  72.0 1.9 %collective-permute-start.22 = (bf16[240,256]{1,0:T(8,128)(2,1)S(1)}, bf16[240,256]{1,0:T(8,128)(2,1)S(1)}, u32[]{:S(2)}, u32[]{:S(2)}) collective-permute-start(bf16[240,256]{1,0:T(8,128)(2,1)S(1)} %get-tuple-element.79), channel_id=1, source_target_pairs={{0,8},{4,12},{8,0},{12,4},{16,24},{20,28},{24,16},{28,20},{1,9},{5... | collective-permute-start | bytes 368648 | tf_op jit(solution)/shard_map/ppermute | solution.py:653
  73.9 2.2 %collective-permute-done.13.refs_0_ = bf16[224,256]{1,0:T(8,128)(2,1)S(1)} collective-permute-done((bf16[224,256]{1,0:T(8,128)(2,1)S(1)}, bf16[224,256]{1,0:T(8,128)(2,1)S(1)}, u32[]{:S(2)}, u32[]{:S(2)}) %collective-permute-start.13) | collective-permute-done | bytes 114720 | tf_op jit(solution)/shard_map/ppermute | solution.py:653
  76.1 1.9 %collective-permute-start.23 = (bf16[240,256]{1,0:T(8,128)(2,1)S(1)}, bf16[240,256]{1,0:T(8,128)(2,1)S(1)}, u32[]{:S(2)}, u32[]{:S(2)}) collective-permute-start(bf16[240,256]{1,0:T(8,128)(2,1)S(1)} %get-tuple-element.80), channel_id=1, source_target_pairs={{0,16},{4,20},{8,24},{12,28},{16,0},{20,4},{24,8},{28,12},{1,17},{... | collective-permute-start | bytes 368648 | tf_op jit(solution)/shard_map/ppermute | solution.py:653
  78.1 1.7 %collective-permute-start.24 = (bf16[240,256]{1,0:T(8,128)(2,1)S(1)}, bf16[240,256]{1,0:T(8,128)(2,1)S(1)}, u32[]{:S(2)}, u32[]{:S(2)}) collective-permute-start(bf16[240,256]{1,0:T(8,128)(2,1)S(1)} %get-tuple-element.81), channel_id=1, source_target_pairs={{0,12},{4,8},{8,4},{12,0},{16,28},{20,24},{24,20},{28,16},{1,13},{... | collective-permute-start | bytes 368648 | tf_op jit(solution)/shard_map/ppermute | solution.py:653
  85.2 1.8 %collective-permute-start.18 = (bf16[224,256]{1,0:T(8,128)(2,1)S(1)}, bf16[224,256]{1,0:T(8,128)(2,1)S(1)}, u32[]{:S(2)}, u32[]{:S(2)}) collective-permute-start(bf16[224,256]{1,0:T(8,128)(2,1)S(1)} %get-tuple-element.74), channel_id=1, source_target_pairs={{0,20},{4,16},{8,28},{12,24},{16,4},{20,0},{24,12},{28,8},{1,21},{... | collective-permute-start | bytes 344072 | tf_op jit(solution)/shard_map/ppermute | solution.py:653
  86.9 1.6 %first_return.1.refs_8_ = bf16[3,60,32,160]{3,2,1,0:T(8,128)(2,1)} custom-call(bf16[240,256]{1,0:T(8,128)(2,1)S(1)} %collective-permute-done.20.refs_0_, bf16[240,256]{1,0:T(8,128)(2,1)S(1)} %collective-permute-done.21.refs_1_, bf16[240,256]{1,0:T(8,128)(2,1)S(1)} %collective-permute-done.22.refs_2_, bf16[240,256]{1,0:T(8,128)(2,1)S(1)} %collective-permute-done.23.refs_3_, ...), custom_call_target="tpu_custom_call" | custom-call | flops 1 | bytes 4194304 | tf_op jit(solution)/shard_map/first_return/pallas_call | solution.py:801
  90.2 1.6 %second_return.1 = bf16[3,60,32,160]{3,2,1,0:T(8,128)(2,1)} custom-call(bf16[224,256]{1,0:T(8,128)(2,1)S(1)} %collective-permute-done.13.refs_0_, bf16[224,256]{1,0:T(8,128)(2,1)S(1)} %collective-permute-done.14.refs_1_, bf16[224,256]{1,0:T(8,128)(2,1)S(1)} %collective-permute-done.15.refs_2_, ...), custom_call_target="tpu_custom_call", output_to_operand_aliasing={{}: (8, {})} | custom-call | tf_op jit(solution)/shard_map/second_return/pallas_call | solution.py:815
  (61 shorter events, 17.6 us)
Async XLA Ops:
  5.1 28.0 %all-to-all-start = ((bf16[8,360,256]{2,1,0:T(8,128)(2,1)}), bf16[8,360,256]{2,1,0:T(8,128)(2,1)}, u32[]{:S(2)}, u32[]{:S(2)}) async-start(bf16[8,360,256]{2,1,0:T(8,128)(2,1)} %get-tuple-element.45), calls=%async_computation | async-start | bytes 2949120 | tf_op jit(solution)/shard_map/all_to_all | solution.py:658
  10.5 7.0 %collective-permute-start = (bf16[4,32,160]{2,1,0:T(8,128)(2,1)S(1)}, bf16[4,32,160]{2,1,0:T(8,128)(2,1)S(1)}, u32[]{:S(2)}, u32[]{:S(2)}) collective-permute-start(bf16[4,32,160]{2,1,0:T(8,128)(2,1)S(1)} %copy-done.7), channel_id=1, source_target_pairs={{0,1},{1,2},{2,3},{3,0},{4,5},{5,6},{6,7},{7,4},{8,9},{9,10},{10,1... | collective-permute-start | bytes 122888 | tf_op jit(solution)/shard_map/ppermute | solution.py:639
  12.7 5.4 %collective-permute-start.1 = (bf16[4,32,160]{2,1,0:T(8,128)(2,1)S(1)}, bf16[4,32,160]{2,1,0:T(8,128)(2,1)S(1)}, u32[]{:S(2)}, u32[]{:S(2)}) collective-permute-start(bf16[4,32,160]{2,1,0:T(8,128)(2,1)S(1)} %copy-done.6), channel_id=1, source_target_pairs={{0,3},{1,0},{2,1},{3,2},{4,7},{5,4},{6,5},{7,6},{8,11},{9,8},{10,9... | collective-permute-start | bytes 122888 | tf_op jit(solution)/shard_map/ppermute | solution.py:639
  19.0 13.1 %collective-permute-start.2 = (bf16[104,256]{1,0:T(8,128)(2,1)S(1)}, bf16[104,256]{1,0:T(8,128)(2,1)S(1)}, u32[]{:S(2)}, u32[]{:S(2)}) collective-permute-start(bf16[104,256]{1,0:T(8,128)(2,1)S(1)} %get-tuple-element.49), channel_id=1, source_target_pairs={{0,24},{4,28},{8,16},{12,20},{16,8},{20,12},{24,0},{28,4},{1,25},{... | collective-permute-start | bytes 159752 | tf_op jit(solution)/shard_map/ppermute | solution.py:653
  21.7 10.6 %collective-permute-start.3 = (bf16[104,256]{1,0:T(8,128)(2,1)S(1)}, bf16[104,256]{1,0:T(8,128)(2,1)S(1)}, u32[]{:S(2)}, u32[]{:S(2)}) collective-permute-start(bf16[104,256]{1,0:T(8,128)(2,1)S(1)} %get-tuple-element.50), channel_id=1, source_target_pairs={{0,28},{4,24},{8,20},{12,16},{16,12},{20,8},{24,4},{28,0},{1,29},{... | collective-permute-start | bytes 159752 | tf_op jit(solution)/shard_map/ppermute | solution.py:653
  21.8 14.6 %collective-permute-start.4 = (bf16[104,256]{1,0:T(8,128)(2,1)S(1)}, bf16[104,256]{1,0:T(8,128)(2,1)S(1)}, u32[]{:S(2)}, u32[]{:S(2)}) collective-permute-start(bf16[104,256]{1,0:T(8,128)(2,1)S(1)} %get-tuple-element.51), channel_id=1, source_target_pairs={{0,8},{4,12},{8,0},{12,4},{16,24},{20,28},{24,16},{28,20},{1,9},{5... | collective-permute-start | bytes 159752 | tf_op jit(solution)/shard_map/ppermute | solution.py:653
  22.8 13.7 %collective-permute-start.5 = (bf16[104,256]{1,0:T(8,128)(2,1)S(1)}, bf16[104,256]{1,0:T(8,128)(2,1)S(1)}, u32[]{:S(2)}, u32[]{:S(2)}) collective-permute-start(bf16[104,256]{1,0:T(8,128)(2,1)S(1)} %get-tuple-element.52), channel_id=1, source_target_pairs={{0,16},{4,20},{8,24},{12,28},{16,0},{20,4},{24,8},{28,12},{1,17},{... | collective-permute-start | bytes 159752 | tf_op jit(solution)/shard_map/ppermute | solution.py:653
  24.2 12.2 %collective-permute-start.6 = (bf16[104,256]{1,0:T(8,128)(2,1)S(1)}, bf16[104,256]{1,0:T(8,128)(2,1)S(1)}, u32[]{:S(2)}, u32[]{:S(2)}) collective-permute-start(bf16[104,256]{1,0:T(8,128)(2,1)S(1)} %get-tuple-element.53), channel_id=1, source_target_pairs={{0,12},{4,8},{8,4},{12,0},{16,28},{20,24},{24,20},{28,16},{1,13},{... | collective-permute-start | bytes 159752 | tf_op jit(solution)/shard_map/ppermute | solution.py:653
  43.1 4.3 %collective-permute-start.10 = (bf16[2,144,256]{2,1,0:T(8,128)(2,1)S(1)}, bf16[2,144,256]{2,1,0:T(8,128)(2,1)S(1)}, u32[]{:S(2)}, u32[]{:S(2)}) collective-permute-start(bf16[2,144,256]{2,1,0:T(8,128)(2,1)S(1)} %get-tuple-element.58), channel_id=1, source_target_pairs={{4,0},{8,4},{12,8},{16,12},{20,16},{24,20},{28,24},{5,1},{9,5},{13... | collective-permute-start | bytes 442376 | tf_op jit(solution)/shard_map/ppermute | solution.py:645
  48.5 6.6 %collective-permute-start.11 = (bf16[144,256]{1,0:T(8,128)(2,1)S(1)}, bf16[144,256]{1,0:T(8,128)(2,1)S(1)}, u32[]{:S(2)}, u32[]{:S(2)}) collective-permute-start(bf16[144,256]{1,0:T(8,128)(2,1)S(1)} %get-tuple-element.60), channel_id=1, source_target_pairs={{0,1},{1,2},{2,3},{3,0},{4,5},{5,6},{6,7},{7,4},{8,9},{9,10},{10,1... | collective-permute-start | bytes 221192 | tf_op jit(solution)/shard_map/ppermute | solution.py:639
  50.6 6.3 %collective-permute-start.12 = (bf16[144,256]{1,0:T(8,128)(2,1)S(1)}, bf16[144,256]{1,0:T(8,128)(2,1)S(1)}, u32[]{:S(2)}, u32[]{:S(2)}) collective-permute-start(bf16[144,256]{1,0:T(8,128)(2,1)S(1)} %get-tuple-element.61), channel_id=1, source_target_pairs={{0,3},{1,0},{2,1},{3,2},{4,7},{5,4},{6,5},{7,6},{8,11},{9,8},{10,9... | collective-permute-start | bytes 221192 | tf_op jit(solution)/shard_map/ppermute | solution.py:639
  63.0 16.8 %collective-permute-start.20 = (bf16[240,256]{1,0:T(8,128)(2,1)S(1)}, bf16[240,256]{1,0:T(8,128)(2,1)S(1)}, u32[]{:S(2)}, u32[]{:S(2)}) collective-permute-start(bf16[240,256]{1,0:T(8,128)(2,1)S(1)} %get-tuple-element.77), channel_id=1, source_target_pairs={{0,24},{4,28},{8,16},{12,20},{16,8},{20,12},{24,0},{28,4},{1,25},{... | collective-permute-start | bytes 368648 | tf_op jit(solution)/shard_map/ppermute | solution.py:653
  67.2 13.9 %collective-permute-start.21 = (bf16[240,256]{1,0:T(8,128)(2,1)S(1)}, bf16[240,256]{1,0:T(8,128)(2,1)S(1)}, u32[]{:S(2)}, u32[]{:S(2)}) collective-permute-start(bf16[240,256]{1,0:T(8,128)(2,1)S(1)} %get-tuple-element.78), channel_id=1, source_target_pairs={{0,28},{4,24},{8,20},{12,16},{16,12},{20,8},{24,4},{28,0},{1,29},{... | collective-permute-start | bytes 368648 | tf_op jit(solution)/shard_map/ppermute | solution.py:653
  69.2 6.9 %collective-permute-start.13 = (bf16[224,256]{1,0:T(8,128)(2,1)S(1)}, bf16[224,256]{1,0:T(8,128)(2,1)S(1)}, u32[]{:S(2)}, u32[]{:S(2)}) collective-permute-start(bf16[224,256]{1,0:T(8,128)(2,1)S(1)} %get-tuple-element.69), channel_id=1, source_target_pairs={{0,24},{4,28},{8,16},{12,20},{16,8},{20,12},{24,0},{28,4},{1,25},{... | collective-permute-start | bytes 344072 | tf_op jit(solution)/shard_map/ppermute | solution.py:653
  69.4 8.7 %collective-permute-start.14 = (bf16[224,256]{1,0:T(8,128)(2,1)S(1)}, bf16[224,256]{1,0:T(8,128)(2,1)S(1)}, u32[]{:S(2)}, u32[]{:S(2)}) collective-permute-start(bf16[224,256]{1,0:T(8,128)(2,1)S(1)} %get-tuple-element.70), channel_id=1, source_target_pairs={{0,28},{4,24},{8,20},{12,16},{16,12},{20,8},{24,4},{28,0},{1,29},{... | collective-permute-start | bytes 344072 | tf_op jit(solution)/shard_map/ppermute | solution.py:653
  72.0 9.7 %collective-permute-start.22 = (bf16[240,256]{1,0:T(8,128)(2,1)S(1)}, bf16[240,256]{1,0:T(8,128)(2,1)S(1)}, u32[]{:S(2)}, u32[]{:S(2)}) collective-permute-start(bf16[240,256]{1,0:T(8,128)(2,1)S(1)} %get-tuple-element.79), channel_id=1, source_target_pairs={{0,8},{4,12},{8,0},{12,4},{16,24},{20,28},{24,16},{28,20},{1,9},{5... | collective-permute-start | bytes 368648 | tf_op jit(solution)/shard_map/ppermute | solution.py:653
  76.1 6.7 %collective-permute-start.23 = (bf16[240,256]{1,0:T(8,128)(2,1)S(1)}, bf16[240,256]{1,0:T(8,128)(2,1)S(1)}, u32[]{:S(2)}, u32[]{:S(2)}) collective-permute-start(bf16[240,256]{1,0:T(8,128)(2,1)S(1)} %get-tuple-element.80), channel_id=1, source_target_pairs={{0,16},{4,20},{8,24},{12,28},{16,0},{20,4},{24,8},{28,12},{1,17},{... | collective-permute-start | bytes 368648 | tf_op jit(solution)/shard_map/ppermute | solution.py:653
  78.1 6.5 %collective-permute-start.24 = (bf16[240,256]{1,0:T(8,128)(2,1)S(1)}, bf16[240,256]{1,0:T(8,128)(2,1)S(1)}, u32[]{:S(2)}, u32[]{:S(2)}) collective-permute-start(bf16[240,256]{1,0:T(8,128)(2,1)S(1)} %get-tuple-element.81), channel_id=1, source_target_pairs={{0,12},{4,8},{8,4},{12,0},{16,28},{20,24},{24,20},{28,16},{1,13},{... | collective-permute-start | bytes 368648 | tf_op jit(solution)/shard_map/ppermute | solution.py:653
  79.8 5.4 %collective-permute-start.25 = (bf16[240,256]{1,0:T(8,128)(2,1)S(1)}, bf16[240,256]{1,0:T(8,128)(2,1)S(1)}, u32[]{:S(2)}, u32[]{:S(2)}) collective-permute-start(bf16[240,256]{1,0:T(8,128)(2,1)S(1)} %get-tuple-element.82), channel_id=1, source_target_pairs={{0,20},{4,16},{8,28},{12,24},{16,4},{20,0},{24,12},{28,8},{1,21},{... | collective-permute-start | bytes 368648 | tf_op jit(solution)/shard_map/ppermute | solution.py:653
  81.1 5.9 %collective-permute-start.26 = (bf16[240,256]{1,0:T(8,128)(2,1)S(1)}, bf16[240,256]{1,0:T(8,128)(2,1)S(1)}, u32[]{:S(2)}, u32[]{:S(2)}) collective-permute-start(bf16[240,256]{1,0:T(8,128)(2,1)S(1)} %get-tuple-element.83), channel_id=1, source_target_pairs={{0,4},{4,0},{8,12},{12,8},{16,20},{20,16},{24,28},{28,24},{1,5},{5... | collective-permute-start | bytes 368648 | tf_op jit(solution)/shard_map/ppermute | solution.py:653
  81.7 6.9 %collective-permute-start.15 = (bf16[224,256]{1,0:T(8,128)(2,1)S(1)}, bf16[224,256]{1,0:T(8,128)(2,1)S(1)}, u32[]{:S(2)}, u32[]{:S(2)}) collective-permute-start(bf16[224,256]{1,0:T(8,128)(2,1)S(1)} %get-tuple-element.71), channel_id=1, source_target_pairs={{0,8},{4,12},{8,0},{12,4},{16,24},{20,28},{24,16},{28,20},{1,9},{5... | collective-permute-start | bytes 344072 | tf_op jit(solution)/shard_map/ppermute | solution.py:653
  82.8 5.7 %collective-permute-start.16 = (bf16[224,256]{1,0:T(8,128)(2,1)S(1)}, bf16[224,256]{1,0:T(8,128)(2,1)S(1)}, u32[]{:S(2)}, u32[]{:S(2)}) collective-permute-start(bf16[224,256]{1,0:T(8,128)(2,1)S(1)} %get-tuple-element.72), channel_id=1, source_target_pairs={{0,16},{4,20},{8,24},{12,28},{16,0},{20,4},{24,8},{28,12},{1,17},{... | collective-permute-start | bytes 344072 | tf_op jit(solution)/shard_map/ppermute | solution.py:653
  84.6 5.4 %collective-permute-start.17 = (bf16[224,256]{1,0:T(8,128)(2,1)S(1)}, bf16[224,256]{1,0:T(8,128)(2,1)S(1)}, u32[]{:S(2)}, u32[]{:S(2)}) collective-permute-start(bf16[224,256]{1,0:T(8,128)(2,1)S(1)} %get-tuple-element.73), channel_id=1, source_target_pairs={{0,12},{4,8},{8,4},{12,0},{16,28},{20,24},{24,20},{28,16},{1,13},{... | collective-permute-start | bytes 344072 | tf_op jit(solution)/shard_map/ppermute | solution.py:653
  85.2 5.0 %collective-permute-start.18 = (bf16[224,256]{1,0:T(8,128)(2,1)S(1)}, bf16[224,256]{1,0:T(8,128)(2,1)S(1)}, u32[]{:S(2)}, u32[]{:S(2)}) collective-permute-start(bf16[224,256]{1,0:T(8,128)(2,1)S(1)} %get-tuple-element.74), channel_id=1, source_target_pairs={{0,20},{4,16},{8,28},{12,24},{16,4},{20,0},{24,12},{28,8},{1,21},{... | collective-permute-start | bytes 344072 | tf_op jit(solution)/shard_map/ppermute | solution.py:653
  (12 other events, 130.0 us)

commit v7 on v6

--- a/solution.py
+++ b/solution.py
@@ -172,7 +172,8 @@
 F32 = jnp.float32
 BF16 = jnp.bfloat16
 PACKED = 144
-ORDER = (6, 7, 2, 4, 3, 5, 1, 0)
+CHIPS = (0, 2, 4, 6)
+ORDER = (6, 2, 4, 7, 1, 3, 5, 0)
 MIB = 1024 * 1024
 
 
@@ -359,8 +360,9 @@
     out[...] = staged[...].astype(BF16)
 
 
-def outer_kernel(west_block, east_block, left, right, depth, *refs):
-    outs, (flux, height, staged) = refs[:8], refs[8:]
+def outer_kernel(
+    west_block, east_block, left, right, depth, straight, cross, flux, height, staged
+):
     members, latitudes = west_block.shape[2:]
     shift = difference(latitudes)
     turning = turning_row(latitudes)
@@ -413,8 +415,9 @@
     put_group(staged, jnp.concatenate([ends[0], ends[1]], axis=0), eye, 60)
     put_group(staged, jnp.concatenate([ends[2], jnp.zeros_like(ends[2])], axis=0), eye, 80)
     me = lax.axis_index("mem")
-    for k, d in enumerate(ORDER):
-        outs[k][...] = staged[me ^ d].astype(BF16)
+    for k, d in enumerate(CHIPS):
+        straight[k] = staged[me ^ d].astype(BF16)
+        cross[k] = staged[me ^ d ^ 1].astype(BF16)
 
 
 def spread_block(source, held, wide, start, lane):
@@ -429,7 +432,7 @@
             held[q, here, spans[h]] = blocks[q][h]
 
 
-def spread_kernel(got, held, wide):
+def spread_kernel(cells, got, held, seen, outer, wide):
     lane = lax.broadcasted_iota(jnp.int32, (16, LANES), 1)
 
     def step(index, carry):
@@ -438,38 +441,56 @@
 
     lax.fori_loop(0, 22, step, 0, unroll=4)
     spread_block(got, held, wide, INNER - 16, lane)
-
-
-def observe_kernel(cells, weight, target, wide_inner, *refs):
-    edges, (held, gram, short, joined, wide, seen) = refs[:8], refs[8:]
-    lane = lax.broadcasted_iota(jnp.int32, (16, LANES), 1)
-    me = lax.axis_index("mem")
-    for k, d in enumerate(ORDER):
-        joined[me ^ d, 0:OUTER, :] = edges[k][...]
-    joined[:, OUTER:BLOCK, :] = jnp.zeros((8, BLOCK - OUTER, 256), BF16)
-    for index in range(BLOCK // 16):
-        spread_block(joined, held, wide, index * 16, lane)
     slots = seen.shape[2]
     unroll = 16
 
-    def pick(index, carry):
+    def pick(index, counts):
+        counts = list(counts)
         for t in range(2):
             for k in range(unroll):
                 slot = index * unroll + k
                 row = cells[t, slot]
                 is_inner = row < 8 * INNER
                 near = jnp.where(is_inner, row, 0)
-                far = jnp.where(is_inner, 0, row - 8 * INNER)
                 for h in range(2):
-                    first = wide_inner[h, pl.ds(near, 1), :]
-                    second = wide[h, pl.ds(far, 1), :]
-                    seen[t, h, pl.ds(slot, 1), :] = jnp.where(is_inner, first, second)
-        return carry
-
-    lax.fori_loop(0, slots // unroll, pick, 0)
+                    seen[t, h, pl.ds(slot, 1), :] = wide[h, pl.ds(near, 1), :]
+                outer[t, counts[t]] = slot
+                counts[t] = counts[t] + jnp.where(is_inner, 0, 1)
+        return tuple(counts)
+
+    counts = lax.fori_loop(0, slots // unroll, pick, (jnp.int32(0), jnp.int32(0)))
+    for t in range(2):
+        for k in range(8):
+            outer[t, counts[t] + k] = slots
+        outer[t, slots + LANES - 1] = counts[t]
+
+
+def observe_kernel(cells, outer, weight, target, first, straight, cross, *refs):
+    edges, (held, gram, short, joined, wide, seen) = refs[:3], refs[3:]
+    lane = lax.broadcasted_iota(jnp.int32, (16, LANES), 1)
+    me = lax.axis_index("mem")
+    for k, d in enumerate(CHIPS):
+        joined[me ^ d, 0:OUTER, :] = straight[0] if k == 0 else edges[k - 1][0]
+        joined[me ^ d ^ 1, 0:OUTER, :] = cross[0] if k == 0 else edges[k - 1][1]
+    joined[:, OUTER:BLOCK, :] = jnp.zeros((8, BLOCK - OUTER, 256), BF16)
+    for index in range(BLOCK // 16):
+        spread_block(joined, held, wide, index * 16, lane)
+    slots = first.shape[2]
+    seen[:, :, 0:slots, :] = first[...]
+    for t in range(2):
+
+        def pick(index, carry):
+            for k in range(8):
+                slot = outer[t, index * 8 + k]
+                row = cells[t, slot] - 8 * INNER
+                for h in range(2):
+                    seen[t, h, pl.ds(slot, 1), :] = wide[h, pl.ds(row, 1), :]
+            return carry
+
+        lax.fori_loop(0, (outer[t, slots + LANES - 1] + 7) // 8, pick, 0)
     eye = identity(256, BF16)
     for t in range(2):
-        values = jnp.concatenate([seen[t, 0], seen[t, 1]], axis=1).astype(BF16)
+        values = jnp.concatenate([seen[t, h, 0:slots] for h in range(2)], axis=1).astype(BF16)
         turned = dot_nt(eye, values)
         mean = jnp.sum(turned, axis=0, keepdims=True) * (1.0 / 256)
         root = weight[t : t + 1, :]
@@ -645,13 +666,12 @@
     return lax.ppermute(value, axis, pairs)
 
 
+def across(value, difference):
+    return lax.ppermute(value, "mem", [(i, i ^ difference) for i in range(8)])
+
+
 def partners(values):
-    count = len(values)
-    moved = []
-    for d, value in zip(ORDER, values):
-        pairs = [(i, i ^ d) for i in range(count)]
-        moved.append(value if d == 0 else lax.ppermute(value, "mem", pairs))
-    return moved
+    return [across(value, d) if d else value for d, value in zip(ORDER, values)]
 
 
 def swap(value):
@@ -702,11 +722,10 @@
     left = around(to_east, "band", 1)
     right = around(to_west, "band", -1)
     flat = pl.BlockSpec((4, members, latitudes), lambda i: (0, 0, 0))
-    out_edge = jax.ShapeDtypeStruct((OUTER, 256), BF16)
-    sent = pl.pallas_call(
+    straight, cross = pl.pallas_call(
         outer_kernel,
         grid=(1,),
-        out_shape=(out_edge,) * 8,
+        out_shape=(jax.ShapeDtypeStruct((4, OUTER, 256), BF16),) * 2,
         in_specs=[
             pl.BlockSpec((3, 10, members, latitudes), lambda i: (0, 0, 0, 0)),
             pl.BlockSpec((3, 6, members, latitudes), lambda i: (0, 9, 0, 0)),
@@ -714,7 +733,7 @@
             flat,
             pl.BlockSpec((columns, latitudes), lambda i: (0, 0)),
         ],
-        out_specs=(pl.BlockSpec((OUTER, 256), lambda i: (0, 0)),) * 8,
+        out_specs=(pl.BlockSpec((4, OUTER, 256), lambda i: (0, 0, 0)),) * 2,
         scratch_shapes=[
             pltpu.VMEM((12, members, latitudes), F32),
             pltpu.VMEM((10, members, latitudes), BF16),
@@ -723,22 +742,30 @@
         compiler_params=params(24),
         name="outer",
     )(planes, planes, left, right, layer_depth)
-    got_edges = partners(sent)
+    cross = across(cross, 1)
+    got_edges = [across(jnp.stack([straight[k], cross[k]]), CHIPS[k]) for k in (3, 1, 2)]
+    got_edges = got_edges[1:] + got_edges[:1]
 
     rows = cell_rows(observed_cell[0])
     live = jnp.arange(slots, dtype=jnp.int32)[None, :] < observed_count[0][:, None]
     root = jnp.sqrt(jnp.where(live, 1.0 / error_variance[0], 0.0))
     vmem = pl.BlockSpec(memory_space=pltpu.VMEM)
-    held_inner, wide = pl.pallas_call(
+    rows = jnp.pad(rows, ((0, 0), (0, LANES)), constant_values=8 * INNER)
+    smem = pl.BlockSpec(memory_space=pltpu.SMEM)
+    held_inner, seen, outer = pl.pallas_call(
         spread_kernel,
         out_shape=(
             jax.ShapeDtypeStruct((8, INNER, 256), BF16),
-            jax.ShapeDtypeStruct((2, 8 * INNER, LANES), F32),
+            jax.ShapeDtypeStruct((2, 2, slots, LANES), F32),
+            jax.ShapeDtypeStruct((2, slots + LANES), jnp.int32),
         ),
-        compiler_params=params(8),
-        cost_estimate=cost(1, 4 * MIB),
+        in_specs=[smem, vmem],
+        out_specs=(vmem, vmem, smem),
+        scratch_shapes=[pltpu.VMEM((2, 8 * INNER, LANES), F32)],
+        compiler_params=params(12),
+        cost_estimate=cost(1, 8 * MIB),
         name="spread",
-    )(got)
+    )(rows, got)
     held_outer, gram, short = pl.pallas_call(
         observe_kernel,
         out_shape=(
@@ -746,15 +773,15 @@
             jax.ShapeDtypeStruct((2, PACKED, 256), F32),
             jax.ShapeDtypeStruct((2, PACKED, 256), BF16),
         ),
-        in_specs=[pl.BlockSpec(memory_space=pltpu.SMEM)] + [vmem] * 11,
+        in_specs=[smem, smem] + [vmem] * 8,
         scratch_shapes=[
             pltpu.VMEM((8, BLOCK, 256), BF16),
             pltpu.VMEM((2, 8 * BLOCK, LANES), F32),
-            pltpu.VMEM((2, 2, slots, LANES), F32),
+            pltpu.VMEM((2, 2, slots + 8, LANES), F32),
         ],
         compiler_params=params(16),
         name="observe",
-    )(rows, root, observed_value[0], wide, *got_edges)
+    )(rows, outer, root, observed_value[0], seen, straight, cross, *got_edges)
     anomaly_1, mean_1, anomaly_2, mean_2 = pl.pallas_call(
         prepare_kernel,
         out_shape=(
@@ -788,6 +815,7 @@
         name="analyse",
     )(column, west, east, anomaly_1, mean_1)
     first = partners(back)
+    maps, first[4] = lax.optimization_barrier((maps, first[4]))
     back = pl.pallas_call(
         second_kernel,
         out_shape=(jax.ShapeDtypeStruct((SECOND, 256), BF16),) * 8,

time: 92.2 us -> 93.3 us (1.012)
  starting transfers between devices: 43.2 us -> 34.4 us
  waiting for transfers between devices: 20.3 us -> 27 us
  Pallas kernels: 27.9 us -> 30.9 us
    ppermute x21 -> x18, starting transfers between devices: 24.8 us -> 16.2 us  [across(): return lax.ppermute(value, 'mem', [(i, i ^ difference) for i in range(8)])]
    all_to_all x1, waiting for transfers between devices: 0.01 us -> 6.63 us  [swap(): return lax.all_to_all(value, 'mem', split_axis=0, concat_axis=0, tiled=True)]
    pallas_call x1, Pallas kernels: 3.27 us -> 9.6 us  [on_device_fast(): pl.pallas_call(spread_kernel, out_shape=(jax.ShapeDtypeStruct((8, INNER,...]
    pallas_call x1, Pallas kernels: 6.59 us -> 3.31 us  [on_device_fast(): pl.pallas_call(observe_kernel, out_shape=(jax.ShapeDtypeStruct((8, BLOCK,...]
    ppermute x21 -> x18, waiting for transfers between devices: 12.6 us -> 12.5 us  [across(): return lax.ppermute(value, 'mem', [(i, i ^ difference) for i in range(8)])]
  transfers between devices with their start and end apart: 28 -> 25, of which waited for: 13 -> 14; matrix products, arithmetic and copies ran while one was open for 0% -> 0% of each run, Pallas kernels for 9% -> 16%
where the time goes in v7:
time: 93.3 us; the launch traced here: 93 us
  starting transfers between devices  34.4 us (37%)
  Pallas kernels  30.9 us (33%)
  waiting for transfers between devices  27 us (29%)
    ppermute x18, starting transfers between devices, across(): return lax.ppermute(value, 'mem', [(i, i ^ difference) for i in range(8)])  16.2 us
    ppermute x18, waiting for transfers between devices, across(): return lax.ppermute(value, 'mem', [(i, i ^ difference) for i in range(8)])  12.5 us
    pallas_call x1, Pallas kernels, on_device_fast(): pl.pallas_call(spread_kernel, out_shape=(jax.ShapeDtypeStruct((8, INNER,...  9.6 us
    ppermute x4, starting transfers between devices, around(): lax.ppermute(value, axis, [(i, (i + step) % count) for i in range(count)])  8.47 us
    ppermute x4, waiting for transfers between devices, around(): lax.ppermute(value, axis, [(i, (i + step) % count) for i in range(count)])  6.92 us
    all_to_all x1, waiting for transfers between devices, swap(): return lax.all_to_all(value, 'mem', split_axis=0, concat_axis=0, tiled=True)  6.63 us
    pallas_call x1, Pallas kernels, on_device_fast(): pl.pallas_call(analyse_kernel, out_shape=(jax.ShapeDtypeStruct((FIRST, 25...  6.06 us
    all_to_all x1, starting transfers between devices, swap(): return lax.all_to_all(value, 'mem', split_axis=0, concat_axis=0, tiled=True)  5.32 us
  transfers between devices with their start and end apart: 25, of which 14 were waited for; matrix products, arithmetic and copies ran while one was open for 0% of the time, Pallas kernels for 16%

profile of v7, /device:TPU:0, one launch (start us, length us, event | category | flops | bytes accessed | tf_op | source)
XLA Modules:
  0.0 93.0 jit_solution(15848311613614917837)
XLA Ops:
  0.0 5.1 %inner.1 = (bf16[8,360,256]{2,1,0:T(8,128)(2,1)}, bf16[4,32,160]{2,1,0:T(8,128)(2,1)}, bf16[4,32,160]{2,1,0:T(8,128)(2,1)}) custom-call(bf16[3,60,32,160]{3,2,1,0:T(8,128)(2,1)} %bitcast.42, f32[60,160]{1,0:T(8,128)} %depth.3), custom_call_target="tpu_custom_call" | custom-call | tf_op jit(solution)/shard_map/inner/pallas_call | solution.py:706
  5.1 5.3 %all-to-all-start = ((bf16[8,360,256]{2,1,0:T(8,128)(2,1)}), bf16[8,360,256]{2,1,0:T(8,128)(2,1)}, u32[]{:S(2)}, u32[]{:S(2)}) async-start(bf16[8,360,256]{2,1,0:T(8,128)(2,1)} %get-tuple-element.42), calls=%async_computation | async-start | bytes 2949120 | tf_op jit(solution)/shard_map/all_to_all | solution.py:678
  10.5 2.2 %collective-permute-start = (bf16[4,32,160]{2,1,0:T(8,128)(2,1)S(1)}, bf16[4,32,160]{2,1,0:T(8,128)(2,1)S(1)}, u32[]{:S(2)}, u32[]{:S(2)}) collective-permute-start(bf16[4,32,160]{2,1,0:T(8,128)(2,1)S(1)} %copy-done.7), channel_id=1, source_target_pairs={{0,1},{1,2},{2,3},{3,0},{4,5},{5,6},{6,7},{7,4},{8,9},{9,10},{10,1... | collective-permute-start | bytes 122888 | tf_op jit(solution)/shard_map/ppermute | solution.py:660
  12.7 2.1 %collective-permute-start.1 = (bf16[4,32,160]{2,1,0:T(8,128)(2,1)S(1)}, bf16[4,32,160]{2,1,0:T(8,128)(2,1)S(1)}, u32[]{:S(2)}, u32[]{:S(2)}) collective-permute-start(bf16[4,32,160]{2,1,0:T(8,128)(2,1)S(1)} %copy-done.6), channel_id=1, source_target_pairs={{0,3},{1,0},{2,1},{3,2},{4,7},{5,4},{6,5},{7,6},{8,11},{9,8},{10,9... | collective-permute-start | bytes 122888 | tf_op jit(solution)/shard_map/ppermute | solution.py:660
  14.9 2.5 %collective-permute-done.left = bf16[4,32,160]{2,1,0:T(8,128)(2,1)S(1)} collective-permute-done((bf16[4,32,160]{2,1,0:T(8,128)(2,1)S(1)}, bf16[4,32,160]{2,1,0:T(8,128)(2,1)S(1)}, u32[]{:S(2)}, u32[]{:S(2)}) %collective-permute-start) | collective-permute-done | bytes 40992 | tf_op jit(solution)/shard_map/ppermute | solution.py:660
  20.6 1.7 %collective-permute-start.3 = (bf16[2,104,256]{2,1,0:T(8,128)(2,1)S(1)}, bf16[2,104,256]{2,1,0:T(8,128)(2,1)S(1)}, u32[]{:S(2)}, u32[]{:S(2)}) collective-permute-start(bf16[2,104,256]{2,1,0:T(8,128)(2,1)S(1)} %pad_maximum_fusion), channel_id=1, source_target_pairs={{0,8},{4,12},{8,0},{12,4},{16,24},{20,28},{24,16},{28,20},{1,9},{5... | collective-permute-start | bytes 319496 | tf_op jit(solution)/shard_map/ppermute | solution.py:670
  24.4 6.6 %all-to-all-done.got = bf16[8,360,256]{2,1,0:T(8,128)(2,1)} async-done(((bf16[8,360,256]{2,1,0:T(8,128)(2,1)}), bf16[8,360,256]{2,1,0:T(8,128)(2,1)}, u32[]{:S(2)}, u32[]{:S(2)}) %all-to-all-start) | async-done | bytes 1474592 | tf_op jit(solution)/shard_map/all_to_all | solution.py:678
  31.1 9.6 %spread.1 = (bf16[8,360,256]{2,1,0:T(8,128)(2,1)S(1)}, f32[2,2,512,128]{3,2,1,0:T(8,128)S(1)}, s32[2,640]{1,0:T(2,128)S(1)}) custom-call(s32[2,640]{1,0:T(2,128)S(1)} %pad.4.cells, bf16[8,360,256]{2,1,0:T(8,128)(2,1)} %all-to-all-done.got), custom_call_target="tpu_custom_call" | custom-call | flops 1 | bytes 8388608 | tf_op jit(solution)/shard_map/spread/pallas_call | solution.py:755
  40.7 3.3 %observe.1 = (bf16[8,112,256]{2,1,0:T(8,128)(2,1)S(1)}, f32[2,144,256]{2,1,0:T(8,128)S(1)}, bf16[2,144,256]{2,1,0:T(8,128)(2,1)S(1)}) custom-call(s32[2,640]{1,0:T(2,128)S(1)} %pad.4.cells, s32[2,640]{1,0:T(2,128)S(1)} %get-tuple-element.43.outer, f32[2,512]{1,0:T(2,128)S(1)} %fusion.8.weight, f32[2,512]{1,0:T(2,128)S(1)} %bitcast.45, ...), custom_call_target="tpu_custom_call" | custom-call | tf_op jit(solution)/shard_map/observe/pallas_call | solution.py:769
  45.3 3.0 %collective-permute-start.6 = (bf16[2,144,256]{2,1,0:T(8,128)(2,1)S(1)}, bf16[2,144,256]{2,1,0:T(8,128)(2,1)S(1)}, u32[]{:S(2)}, u32[]{:S(2)}) collective-permute-start(bf16[2,144,256]{2,1,0:T(8,128)(2,1)S(1)} %get-tuple-element.50), channel_id=1, source_target_pairs={{0,4},{4,8},{8,12},{12,16},{16,20},{20,24},{24,28},{1,5},{5,9},{9,... | collective-permute-start | bytes 442376 | tf_op jit(solution)/shard_map/ppermute | solution.py:666
  49.4 2.0 %collective-permute-start.8 = (bf16[144,256]{1,0:T(8,128)(2,1)S(1)}, bf16[144,256]{1,0:T(8,128)(2,1)S(1)}, u32[]{:S(2)}, u32[]{:S(2)}) collective-permute-start(bf16[144,256]{1,0:T(8,128)(2,1)S(1)} %get-tuple-element.52), channel_id=1, source_target_pairs={{0,1},{1,2},{2,3},{3,0},{4,5},{5,6},{6,7},{7,4},{8,9},{9,10},{10,1... | collective-permute-start | bytes 221192 | tf_op jit(solution)/shard_map/ppermute | solution.py:660
  51.4 2.2 %collective-permute-start.9 = (bf16[144,256]{1,0:T(8,128)(2,1)S(1)}, bf16[144,256]{1,0:T(8,128)(2,1)S(1)}, u32[]{:S(2)}, u32[]{:S(2)}) collective-permute-start(bf16[144,256]{1,0:T(8,128)(2,1)S(1)} %get-tuple-element.53), channel_id=1, source_target_pairs={{0,3},{1,0},{2,1},{3,2},{4,7},{5,4},{6,5},{7,6},{8,11},{9,8},{10,9... | collective-permute-start | bytes 221192 | tf_op jit(solution)/shard_map/ppermute | solution.py:660
  54.2 2.0 %collective-permute-done.8.west = bf16[144,256]{1,0:T(8,128)(2,1)S(1)} collective-permute-done((bf16[144,256]{1,0:T(8,128)(2,1)S(1)}, bf16[144,256]{1,0:T(8,128)(2,1)S(1)}, u32[]{:S(2)}, u32[]{:S(2)}) %collective-permute-start.8) | collective-permute-done | bytes 73760 | tf_op jit(solution)/shard_map/ppermute | solution.py:660
  56.2 1.7 %collective-permute-done.9.east = bf16[144,256]{1,0:T(8,128)(2,1)S(1)} collective-permute-done((bf16[144,256]{1,0:T(8,128)(2,1)S(1)}, bf16[144,256]{1,0:T(8,128)(2,1)S(1)}, u32[]{:S(2)}, u32[]{:S(2)}) %collective-permute-start.9) | collective-permute-done | bytes 73760 | tf_op jit(solution)/shard_map/ppermute | solution.py:660
  57.9 6.1 %analyse.1 = (bf16[240,256]{1,0:T(8,128)(2,1)S(1)}, bf16[240,256]{1,0:T(8,128)(2,1)S(1)}, bf16[240,256]{1,0:T(8,128)(2,1)S(1)}, bf16[240,256]{1,0:T(8,128)(2,1)S...) custom-call(f32[2,144,256]{2,1,0:T(8,128)S(1)} %get-tuple-element.51, ...), custom_call_target="tpu_custom_call" | custom-call | tf_op jit(solution)/shard_map/analyse/pallas_call | solution.py:809
  64.1 2.5 %collective-permute-start.18 = (bf16[240,256]{1,0:T(8,128)(2,1)S(1)}, bf16[240,256]{1,0:T(8,128)(2,1)S(1)}, u32[]{:S(2)}, u32[]{:S(2)}) collective-permute-start(bf16[240,256]{1,0:T(8,128)(2,1)S(1)} %get-tuple-element.71), channel_id=1, source_target_pairs={{0,24},{4,28},{8,16},{12,20},{16,8},{20,12},{24,0},{28,4},{1,25},{... | collective-permute-start | bytes 368648 | tf_op jit(solution)/shard_map/ppermute | solution.py:670
  66.6 2.7 %collective-permute-start.19 = (bf16[240,256]{1,0:T(8,128)(2,1)S(1)}, bf16[240,256]{1,0:T(8,128)(2,1)S(1)}, u32[]{:S(2)}, u32[]{:S(2)}) collective-permute-start(bf16[240,256]{1,0:T(8,128)(2,1)S(1)} %get-tuple-element.72), channel_id=1, source_target_pairs={{0,8},{4,12},{8,0},{12,4},{16,24},{20,28},{24,16},{28,20},{1,9},{5... | collective-permute-start | bytes 368648 | tf_op jit(solution)/shard_map/ppermute | solution.py:670
  70.3 2.3 %collective-permute-start.22 = (bf16[240,256]{1,0:T(8,128)(2,1)S(1)}, bf16[240,256]{1,0:T(8,128)(2,1)S(1)}, u32[]{:S(2)}, u32[]{:S(2)}) collective-permute-start(bf16[240,256]{1,0:T(8,128)(2,1)S(1)} %get-tuple-element.76), channel_id=1, source_target_pairs={{0,12},{4,8},{8,4},{12,0},{16,28},{20,24},{24,20},{28,16},{1,13},{... | collective-permute-start | bytes 368648 | tf_op jit(solution)/shard_map/ppermute | solution.py:670
  73.7 2.0 %second.1 = (bf16[224,256]{1,0:T(8,128)(2,1)S(1)}, bf16[224,256]{1,0:T(8,128)(2,1)S(1)}, bf16[224,256]{1,0:T(8,128)(2,1)S(1)}, bf16[224,256]{1,0:T(8,128)(2,1)S(...) custom-call(bf16[2,256,256]{2,1,0:T(8,128)(2,1)S(1)} %get-tuple-elem, ...), custom_call_target="tpu_custom_call" | custom-call | flops 1 | bytes 6291456 | tf_op jit(solution)/shard_map/second/pallas_call | solution.py:819
  76.2 1.8 %collective-permute-done.20.refs_2_ = bf16[240,256]{1,0:T(8,128)(2,1)S(1)} collective-permute-done((bf16[240,256]{1,0:T(8,128)(2,1)S(1)}, bf16[240,256]{1,0:T(8,128)(2,1)S(1)}, u32[]{:S(2)}, u32[]{:S(2)}) %collective-permute-start.20) | collective-permute-done | bytes 122912 | tf_op jit(solution)/shard_map/ppermute | solution.py:670
  83.1 3.3 %collective-permute-done.12.refs_1_ = bf16[224,256]{1,0:T(8,128)(2,1)S(1)} collective-permute-done((bf16[224,256]{1,0:T(8,128)(2,1)S(1)}, bf16[224,256]{1,0:T(8,128)(2,1)S(1)}, u32[]{:S(2)}, u32[]{:S(2)}) %collective-permute-start.12) | collective-permute-done | bytes 114720 | tf_op jit(solution)/shard_map/ppermute | solution.py:670
  86.3 1.6 %first_return.1.refs_8_ = bf16[3,60,32,160]{3,2,1,0:T(8,128)(2,1)} custom-call(bf16[240,256]{1,0:T(8,128)(2,1)S(1)} %collective-permute-done.18.refs_0_, bf16[240,256]{1,0:T(8,128)(2,1)S(1)} %collective-permute-done.19.refs_1_, bf16[240,256]{1,0:T(8,128)(2,1)S(1)} %collective-permute-done.20.refs_2_, bf16[240,256]{1,0:T(8,128)(2,1)S(1)} %collective-permute-done.21.refs_3_, ...), custom_call_target="tpu_custom_call" | custom-call | flops 1 | bytes 4194304 | tf_op jit(solution)/shard_map/first_return/pallas_call | solution.py:829
  88.0 2.3 %collective-permute-done.16.refs_5_ = bf16[224,256]{1,0:T(8,128)(2,1)S(1)} collective-permute-done((bf16[224,256]{1,0:T(8,128)(2,1)S(1)}, bf16[224,256]{1,0:T(8,128)(2,1)S(1)}, u32[]{:S(2)}, u32[]{:S(2)}) %collective-permute-start.16) | collective-permute-done | bytes 114720 | tf_op jit(solution)/shard_map/ppermute | solution.py:670
  91.2 1.6 %second_return.1 = bf16[3,60,32,160]{3,2,1,0:T(8,128)(2,1)} custom-call(bf16[224,256]{1,0:T(8,128)(2,1)S(1)} %collective-permute-done.11.refs_0_, bf16[224,256]{1,0:T(8,128)(2,1)S(1)} %collective-permute-done.12.refs_1_, bf16[224,256]{1,0:T(8,128)(2,1)S(1)} %collective-permute-done.13.refs_2_, ...), custom_call_target="tpu_custom_call", output_to_operand_aliasing={{}: (8, {})} | custom-call | tf_op jit(solution)/shard_map/second_return/pallas_call | solution.py:843
  (61 shorter events, 17.0 us)
Async XLA Ops:
  5.1 25.9 %all-to-all-start = ((bf16[8,360,256]{2,1,0:T(8,128)(2,1)}), bf16[8,360,256]{2,1,0:T(8,128)(2,1)}, u32[]{:S(2)}, u32[]{:S(2)}) async-start(bf16[8,360,256]{2,1,0:T(8,128)(2,1)} %get-tuple-element.42), calls=%async_computation | async-start | bytes 2949120 | tf_op jit(solution)/shard_map/all_to_all | solution.py:678
  10.5 7.0 %collective-permute-start = (bf16[4,32,160]{2,1,0:T(8,128)(2,1)S(1)}, bf16[4,32,160]{2,1,0:T(8,128)(2,1)S(1)}, u32[]{:S(2)}, u32[]{:S(2)}) collective-permute-start(bf16[4,32,160]{2,1,0:T(8,128)(2,1)S(1)} %copy-done.7), channel_id=1, source_target_pairs={{0,1},{1,2},{2,3},{3,0},{4,5},{5,6},{6,7},{7,4},{8,9},{9,10},{10,1... | collective-permute-start | bytes 122888 | tf_op jit(solution)/shard_map/ppermute | solution.py:660
  12.7 5.4 %collective-permute-start.1 = (bf16[4,32,160]{2,1,0:T(8,128)(2,1)S(1)}, bf16[4,32,160]{2,1,0:T(8,128)(2,1)S(1)}, u32[]{:S(2)}, u32[]{:S(2)}) collective-permute-start(bf16[4,32,160]{2,1,0:T(8,128)(2,1)S(1)} %copy-done.6), channel_id=1, source_target_pairs={{0,3},{1,0},{2,1},{3,2},{4,7},{5,4},{6,5},{7,6},{8,11},{9,8},{10,9... | collective-permute-start | bytes 122888 | tf_op jit(solution)/shard_map/ppermute | solution.py:660
  20.6 20.0 %collective-permute-start.3 = (bf16[2,104,256]{2,1,0:T(8,128)(2,1)S(1)}, bf16[2,104,256]{2,1,0:T(8,128)(2,1)S(1)}, u32[]{:S(2)}, u32[]{:S(2)}) collective-permute-start(bf16[2,104,256]{2,1,0:T(8,128)(2,1)S(1)} %pad_maximum_fusion), channel_id=1, source_target_pairs={{0,8},{4,12},{8,0},{12,4},{16,24},{20,28},{24,16},{28,20},{1,9},{5... | collective-permute-start | bytes 319496 | tf_op jit(solution)/shard_map/ppermute | solution.py:670
  22.4 18.3 %collective-permute-start.4 = (bf16[2,104,256]{2,1,0:T(8,128)(2,1)S(1)}, bf16[2,104,256]{2,1,0:T(8,128)(2,1)S(1)}, u32[]{:S(2)}, u32[]{:S(2)}) collective-permute-start(bf16[2,104,256]{2,1,0:T(8,128)(2,1)S(1)} %pad_maximum_fusion.1), channel_id=1, source_target_pairs={{0,16},{4,20},{8,24},{12,28},{16,0},{20,4},{24,8},{28,12},{1,17},{... | collective-permute-start | bytes 319496 | tf_op jit(solution)/shard_map/ppermute | solution.py:670
  23.9 16.7 %collective-permute-start.5 = (bf16[2,104,256]{2,1,0:T(8,128)(2,1)S(1)}, bf16[2,104,256]{2,1,0:T(8,128)(2,1)S(1)}, u32[]{:S(2)}, u32[]{:S(2)}) collective-permute-start(bf16[2,104,256]{2,1,0:T(8,128)(2,1)S(1)} %pad_maximum_fusion.2), channel_id=1, source_target_pairs={{0,24},{4,28},{8,16},{12,20},{16,8},{20,12},{24,0},{28,4},{1,25},{... | collective-permute-start | bytes 319496 | tf_op jit(solution)/shard_map/ppermute | solution.py:670
  44.0 4.3 %collective-permute-start.7 = (bf16[2,144,256]{2,1,0:T(8,128)(2,1)S(1)}, bf16[2,144,256]{2,1,0:T(8,128)(2,1)S(1)}, u32[]{:S(2)}, u32[]{:S(2)}) collective-permute-start(bf16[2,144,256]{2,1,0:T(8,128)(2,1)S(1)} %get-tuple-element.50), channel_id=1, source_target_pairs={{4,0},{8,4},{12,8},{16,12},{20,16},{24,20},{28,24},{5,1},{9,5},{13... | collective-permute-start | bytes 442376 | tf_op jit(solution)/shard_map/ppermute | solution.py:666
  45.3 4.0 %collective-permute-start.6 = (bf16[2,144,256]{2,1,0:T(8,128)(2,1)S(1)}, bf16[2,144,256]{2,1,0:T(8,128)(2,1)S(1)}, u32[]{:S(2)}, u32[]{:S(2)}) collective-permute-start(bf16[2,144,256]{2,1,0:T(8,128)(2,1)S(1)} %get-tuple-element.50), channel_id=1, source_target_pairs={{0,4},{4,8},{8,12},{12,16},{16,20},{20,24},{24,28},{1,5},{5,9},{9,... | collective-permute-start | bytes 442376 | tf_op jit(solution)/shard_map/ppermute | solution.py:666
  49.4 6.8 %collective-permute-start.8 = (bf16[144,256]{1,0:T(8,128)(2,1)S(1)}, bf16[144,256]{1,0:T(8,128)(2,1)S(1)}, u32[]{:S(2)}, u32[]{:S(2)}) collective-permute-start(bf16[144,256]{1,0:T(8,128)(2,1)S(1)} %get-tuple-element.52), channel_id=1, source_target_pairs={{0,1},{1,2},{2,3},{3,0},{4,5},{5,6},{6,7},{7,4},{8,9},{9,10},{10,1... | collective-permute-start | bytes 221192 | tf_op jit(solution)/shard_map/ppermute | solution.py:660
  51.4 6.6 %collective-permute-start.9 = (bf16[144,256]{1,0:T(8,128)(2,1)S(1)}, bf16[144,256]{1,0:T(8,128)(2,1)S(1)}, u32[]{:S(2)}, u32[]{:S(2)}) collective-permute-start(bf16[144,256]{1,0:T(8,128)(2,1)S(1)} %get-tuple-element.53), channel_id=1, source_target_pairs={{0,3},{1,0},{2,1},{3,2},{4,7},{5,4},{6,5},{7,6},{8,11},{9,8},{10,9... | collective-permute-start | bytes 221192 | tf_op jit(solution)/shard_map/ppermute | solution.py:660
  64.0 6.2 %collective-permute-start.10 = (bf16[240,256]{1,0:T(8,128)(2,1)S(1)}, bf16[240,256]{1,0:T(8,128)(2,1)S(1)}, u32[]{:S(2)}, u32[]{:S(2)}) collective-permute-start(bf16[240,256]{1,0:T(8,128)(2,1)S(1)} %get-tuple-element.59), channel_id=1, source_target_pairs={{0,4},{4,0},{8,12},{12,8},{16,20},{20,16},{24,28},{28,24},{1,5},{5... | collective-permute-start | bytes 368648 | tf_op jit(solution)/shard_map/ppermute | solution.py:670
  64.1 8.4 %collective-permute-start.18 = (bf16[240,256]{1,0:T(8,128)(2,1)S(1)}, bf16[240,256]{1,0:T(8,128)(2,1)S(1)}, u32[]{:S(2)}, u32[]{:S(2)}) collective-permute-start(bf16[240,256]{1,0:T(8,128)(2,1)S(1)} %get-tuple-element.71), channel_id=1, source_target_pairs={{0,24},{4,28},{8,16},{12,20},{16,8},{20,12},{24,0},{28,4},{1,25},{... | collective-permute-start | bytes 368648 | tf_op jit(solution)/shard_map/ppermute | solution.py:670
  66.6 9.5 %collective-permute-start.19 = (bf16[240,256]{1,0:T(8,128)(2,1)S(1)}, bf16[240,256]{1,0:T(8,128)(2,1)S(1)}, u32[]{:S(2)}, u32[]{:S(2)}) collective-permute-start(bf16[240,256]{1,0:T(8,128)(2,1)S(1)} %get-tuple-element.72), channel_id=1, source_target_pairs={{0,8},{4,12},{8,0},{12,4},{16,24},{20,28},{24,16},{28,20},{1,9},{5... | collective-permute-start | bytes 368648 | tf_op jit(solution)/shard_map/ppermute | solution.py:670
  69.3 8.6 %collective-permute-start.20 = (bf16[240,256]{1,0:T(8,128)(2,1)S(1)}, bf16[240,256]{1,0:T(8,128)(2,1)S(1)}, u32[]{:S(2)}, u32[]{:S(2)}) collective-permute-start(bf16[240,256]{1,0:T(8,128)(2,1)S(1)} %get-tuple-element.73), channel_id=1, source_target_pairs={{0,16},{4,20},{8,24},{12,28},{16,0},{20,4},{24,8},{28,12},{1,17},{... | collective-permute-start | bytes 368648 | tf_op jit(solution)/shard_map/ppermute | solution.py:670
  69.3 9.1 %collective-permute-start.21 = (bf16[240,256]{1,0:T(8,128)(2,1)S(1)}, bf16[240,256]{1,0:T(8,128)(2,1)S(1)}, u32[]{:S(2)}, u32[]{:S(2)}) collective-permute-start(bf16[240,256]{1,0:T(8,128)(2,1)S(1)} %get-tuple-element.74), channel_id=1, source_target_pairs={{0,28},{4,24},{8,20},{12,16},{16,12},{20,8},{24,4},{28,0},{1,29},{... | collective-permute-start | bytes 368648 | tf_op jit(solution)/shard_map/ppermute | solution.py:670
  70.3 10.2 %collective-permute-start.22 = (bf16[240,256]{1,0:T(8,128)(2,1)S(1)}, bf16[240,256]{1,0:T(8,128)(2,1)S(1)}, u32[]{:S(2)}, u32[]{:S(2)}) collective-permute-start(bf16[240,256]{1,0:T(8,128)(2,1)S(1)} %get-tuple-element.76), channel_id=1, source_target_pairs={{0,12},{4,8},{8,4},{12,0},{16,28},{20,24},{24,20},{28,16},{1,13},{... | collective-permute-start | bytes 368648 | tf_op jit(solution)/shard_map/ppermute | solution.py:670
  72.5 8.7 %collective-permute-start.23 = (bf16[240,256]{1,0:T(8,128)(2,1)S(1)}, bf16[240,256]{1,0:T(8,128)(2,1)S(1)}, u32[]{:S(2)}, u32[]{:S(2)}) collective-permute-start(bf16[240,256]{1,0:T(8,128)(2,1)S(1)} %get-tuple-element.77), channel_id=1, source_target_pairs={{0,20},{4,16},{8,28},{12,24},{16,4},{20,0},{24,12},{28,8},{1,21},{... | collective-permute-start | bytes 368648 | tf_op jit(solution)/shard_map/ppermute | solution.py:670
  76.1 7.0 %collective-permute-start.11 = (bf16[224,256]{1,0:T(8,128)(2,1)S(1)}, bf16[224,256]{1,0:T(8,128)(2,1)S(1)}, u32[]{:S(2)}, u32[]{:S(2)}) collective-permute-start(bf16[224,256]{1,0:T(8,128)(2,1)S(1)} %get-tuple-element.63), channel_id=1, source_target_pairs={{0,24},{4,28},{8,16},{12,20},{16,8},{20,12},{24,0},{28,4},{1,25},{... | collective-permute-start | bytes 344072 | tf_op jit(solution)/shard_map/ppermute | solution.py:670
  77.9 8.4 %collective-permute-start.12 = (bf16[224,256]{1,0:T(8,128)(2,1)S(1)}, bf16[224,256]{1,0:T(8,128)(2,1)S(1)}, u32[]{:S(2)}, u32[]{:S(2)}) collective-permute-start(bf16[224,256]{1,0:T(8,128)(2,1)S(1)} %get-tuple-element.64), channel_id=1, source_target_pairs={{0,8},{4,12},{8,0},{12,4},{16,24},{20,28},{24,16},{28,20},{1,9},{5... | collective-permute-start | bytes 344072 | tf_op jit(solution)/shard_map/ppermute | solution.py:670
  78.4 9.6 %collective-permute-start.13 = (bf16[224,256]{1,0:T(8,128)(2,1)S(1)}, bf16[224,256]{1,0:T(8,128)(2,1)S(1)}, u32[]{:S(2)}, u32[]{:S(2)}) collective-permute-start(bf16[224,256]{1,0:T(8,128)(2,1)S(1)} %get-tuple-element.65), channel_id=1, source_target_pairs={{0,16},{4,20},{8,24},{12,28},{16,0},{20,4},{24,8},{28,12},{1,17},{... | collective-permute-start | bytes 344072 | tf_op jit(solution)/shard_map/ppermute | solution.py:670
  80.5 7.5 %collective-permute-start.14 = (bf16[224,256]{1,0:T(8,128)(2,1)S(1)}, bf16[224,256]{1,0:T(8,128)(2,1)S(1)}, u32[]{:S(2)}, u32[]{:S(2)}) collective-permute-start(bf16[224,256]{1,0:T(8,128)(2,1)S(1)} %get-tuple-element.66), channel_id=1, source_target_pairs={{0,28},{4,24},{8,20},{12,16},{16,12},{20,8},{24,4},{28,0},{1,29},{... | collective-permute-start | bytes 344072 | tf_op jit(solution)/shard_map/ppermute | solution.py:670
  81.2 6.8 %collective-permute-start.15 = (bf16[224,256]{1,0:T(8,128)(2,1)S(1)}, bf16[224,256]{1,0:T(8,128)(2,1)S(1)}, u32[]{:S(2)}, u32[]{:S(2)}) collective-permute-start(bf16[224,256]{1,0:T(8,128)(2,1)S(1)} %get-tuple-element.67), channel_id=1, source_target_pairs={{0,4},{4,0},{8,12},{12,8},{16,20},{20,16},{24,28},{28,24},{1,5},{5... | collective-permute-start | bytes 344072 | tf_op jit(solution)/shard_map/ppermute | solution.py:670
  83.1 7.3 %collective-permute-start.16 = (bf16[224,256]{1,0:T(8,128)(2,1)S(1)}, bf16[224,256]{1,0:T(8,128)(2,1)S(1)}, u32[]{:S(2)}, u32[]{:S(2)}) collective-permute-start(bf16[224,256]{1,0:T(8,128)(2,1)S(1)} %get-tuple-element.68), channel_id=1, source_target_pairs={{0,12},{4,8},{8,4},{12,0},{16,28},{20,24},{24,20},{28,16},{1,13},{... | collective-permute-start | bytes 344072 | tf_op jit(solution)/shard_map/ppermute | solution.py:670
  86.3 4.8 %collective-permute-start.17 = (bf16[224,256]{1,0:T(8,128)(2,1)S(1)}, bf16[224,256]{1,0:T(8,128)(2,1)S(1)}, u32[]{:S(2)}, u32[]{:S(2)}) collective-permute-start(bf16[224,256]{1,0:T(8,128)(2,1)S(1)} %get-tuple-element.69), channel_id=1, source_target_pairs={{0,20},{4,16},{8,28},{12,24},{16,4},{20,0},{24,12},{28,8},{1,21},{... | collective-permute-start | bytes 344072 | tf_op jit(solution)/shard_map/ppermute | solution.py:670
  (9 other events, 110.1 us)

commit v8 on v7

--- a/solution.py
+++ b/solution.py
@@ -309,7 +309,9 @@
     return turning[0:1, :][None]
 
 
-def inner_kernel(ens, depth, out, to_west, to_east, here, deep, flux, height, staged, arrived):
+def inner_kernel(
+    ens, depth, out, to_first, to_second, here, deep, flux, height, staged, edges, arrived
+):
     columns, members, latitudes = here.shape[1:]
     batch = columns // 5
     pieces = [pltpu.make_async_copy(depth, deep, arrived.at[5])]
@@ -328,11 +330,11 @@
         rows = [deep[c : c + 1, :] for c in range(first, first + count)]
         return jnp.stack([jnp.broadcast_to(row, (members, latitudes)) for row in rows])
 
-    def edge(to, near, far):
-        to[0] = here[0, near]
-        to[1] = (deep[near : near + 1, :] * here[2, near].astype(F32)).astype(BF16)
-        to[2] = flux[near].astype(BF16)
-        to[3] = flux[far].astype(BF16)
+    def edge(side, near, far):
+        edges[side, 0] = here[0, near]
+        edges[side, 1] = (deep[near : near + 1, :] * here[2, near].astype(F32)).astype(BF16)
+        edges[side, 2] = flux[near].astype(BF16)
+        edges[side, 3] = flux[far].astype(BF16)
 
     done = 1
     for k in range(5):
@@ -340,9 +342,9 @@
         first = k * batch
         flux[first : first + batch] = fluxes(here[1, first : first + batch], depths(first, batch))
         if k == 0:
-            edge(to_west, 0, 1)
+            edge(0, 0, 1)
         if k == 4:
-            edge(to_east, columns - 1, columns - 2)
+            edge(1, columns - 1, columns - 2)
         low, high = max(first - 1, 1), first + batch - 1
         at = slice(low, high)
         ahead, behind = flux[low + 1 : high + 1], flux[low - 1 : high - 1]
@@ -357,12 +359,20 @@
             for v, field in enumerate((height[at],) + new):
                 put_group(staged, field, eye, 20 * group_of(v, done))
             done += 1
+    odd = lax.axis_index("band") & 1
+    to_first[...] = edges[1 - odd]
+    to_second[...] = edges[odd]
     out[...] = staged[...].astype(BF16)
 
 
 def outer_kernel(
-    west_block, east_block, left, right, depth, straight, cross, flux, height, staged
+    west_block, east_block, first_swap, second_swap, depth, *refs
 ):
+    straight, cross, flux, height, staged, swapped = refs
+    odd = lax.axis_index("band") & 1
+    for side, block in enumerate((first_swap, second_swap)):
+        swapped[side] = block[...]
+    left, right = swapped.at[1 - odd], swapped.at[odd]
     members, latitudes = west_block.shape[2:]
     shift = difference(latitudes)
     turning = turning_row(latitudes)
@@ -432,7 +442,7 @@
             held[q, here, spans[h]] = blocks[q][h]
 
 
-def spread_kernel(cells, got, held, seen, outer, wide):
+def spread_kernel(cells, got, held, seen, wide):
     lane = lax.broadcasted_iota(jnp.int32, (16, LANES), 1)
 
     def step(index, carry):
@@ -444,29 +454,21 @@
     slots = seen.shape[2]
     unroll = 16
 
-    def pick(index, counts):
-        counts = list(counts)
+    def pick(index, carry):
         for t in range(2):
             for k in range(unroll):
                 slot = index * unroll + k
                 row = cells[t, slot]
-                is_inner = row < 8 * INNER
-                near = jnp.where(is_inner, row, 0)
                 for h in range(2):
-                    seen[t, h, pl.ds(slot, 1), :] = wide[h, pl.ds(near, 1), :]
-                outer[t, counts[t]] = slot
-                counts[t] = counts[t] + jnp.where(is_inner, 0, 1)
-        return tuple(counts)
-
-    counts = lax.fori_loop(0, slots // unroll, pick, (jnp.int32(0), jnp.int32(0)))
-    for t in range(2):
-        for k in range(8):
-            outer[t, counts[t] + k] = slots
-        outer[t, slots + LANES - 1] = counts[t]
+                    seen[t, h, pl.ds(slot, 1), :] = wide[h, pl.ds(row, 1), :]
+        return carry
+
+    lax.fori_loop(0, slots // unroll, pick, 0)
 
 
 def observe_kernel(cells, outer, weight, target, first, straight, cross, *refs):
-    edges, (held, gram, short, joined, wide, seen) = refs[:3], refs[3:]
+    edges, (held, gram, to_first, to_second, joined, wide, seen) = refs[:3], refs[3:]
+    wholes = []
     lane = lax.broadcasted_iota(jnp.int32, (16, LANES), 1)
     me = lax.axis_index("mem")
     for k, d in enumerate(CHIPS):
@@ -500,14 +502,20 @@
         pull = dot_nt(jnp.broadcast_to(misfit, (16, slots)), spread)
         whole = packed(block, pull[0:8])
         gram[t] = whole
-        short[t] = whole.astype(BF16)
-
-
-def combine_kernel(gram, below, above, column, to_west, to_east):
-    total = gram[...] + neighbour_weight * (below[...].astype(F32) + above[...].astype(F32))
-    column[...] = total
-    to_west[...] = total[0].astype(BF16)
-    to_east[...] = total[1].astype(BF16)
+        wholes.append(whole.astype(BF16))
+    odd = (lax.axis_index("band") & 1) == 1
+    to_first[...] = jnp.where(odd, wholes[0], wholes[1])
+    to_second[...] = jnp.where(odd, wholes[1], wholes[0])
+
+
+def combine_kernel(gram, first_swap, second_swap, line, short):
+    odd = (lax.axis_index("band") & 1) == 1
+    first, second = first_swap[...].astype(F32), second_swap[...].astype(F32)
+    west, east = jnp.where(odd, first, second), jnp.where(odd, second, first)
+    for t, beside in enumerate((west + gram[1], gram[0] + east)):
+        total = gram[t] + neighbour_weight * beside
+        line[t] = total
+        short[t] = total.astype(BF16)
 
 
 def prepare_kernel(inner, outer, *refs):
@@ -561,14 +569,14 @@
     send_back(results, outs)
 
 
-def analyse_kernel(column, west, east, anomaly, mean, *refs):
+def analyse_kernel(line, below, above, anomaly, mean, *refs):
     outs, (kept, results, ordered) = refs[:8], refs[8:]
     size = 256
     eye = identity(size, F32)
-    beside = (west[...].astype(F32) + column[1], column[0] + east[...].astype(F32))
     norms, pulls, roots, inverses = [], [], [], []
     for t in range(2):
-        block, pull = unpacked(column[t] + neighbour_weight * beside[t])
+        beside = below[t].astype(F32) + above[t].astype(F32)
+        block, pull = unpacked(line[t] + neighbour_weight * beside)
         system = (size - 1) * eye + block
         square = jnp.sum(jnp.sum(system * system, axis=0, keepdims=True), axis=1, keepdims=True)
         norms.append(jnp.sqrt(square))
@@ -655,15 +663,25 @@
         copy.wait()
 
 
-def around(value, axis, step):
-    count = lax.axis_size(axis)
-    return lax.ppermute(value, axis, [(i, (i + step) % count) for i in range(count)])
-
-
-def along(value, axis, step):
-    count = lax.axis_size(axis)
-    pairs = [(i, i + step) for i in range(count) if 0 <= i + step < count]
-    return lax.ppermute(value, axis, pairs)
+def swapped_pairs(values, axis, pairs):
+    moved = []
+    for value, some in zip(values, pairs):
+        both = some + [(j, i) for i, j in some]
+        moved.append(lax.ppermute(value, axis, both))
+    return moved
+
+
+def band_swaps(first, second):
+    count = lax.axis_size("band")
+    starts = range(0, count, 2)
+    pairs = [[(i, i + 1) for i in starts], [(i + 1, (i + 2) % count) for i in starts]]
+    return swapped_pairs((first, second), "band", pairs)
+
+
+def mem_swaps(value):
+    count = lax.axis_size("mem")
+    pairs = [[(i, i + 1) for i in range(k, count - 1, 2)] for k in range(2)]
+    return swapped_pairs((value, value), "mem", pairs)
 
 
 def across(value, difference):
@@ -703,7 +721,7 @@
     planes = jnp.transpose(ensemble, (1, 2, 0, 3))
     edge = jax.ShapeDtypeStruct((4, members, latitudes), BF16)
     far = pl.BlockSpec(memory_space=pltpu.HBM)
-    sent, to_west, to_east = pl.pallas_call(
+    sent, to_first, to_second = pl.pallas_call(
         inner_kernel,
         out_shape=(jax.ShapeDtypeStruct((8, INNER, 256), BF16), edge, edge),
         in_specs=[far, far],
@@ -713,14 +731,14 @@
             pltpu.VMEM((columns, members, latitudes), F32),
             pltpu.VMEM((columns, members, latitudes), BF16),
             pltpu.VMEM((8, INNER, 256), F32),
+            pltpu.VMEM((2, 4, members, latitudes), BF16),
             pltpu.SemaphoreType.DMA((6,)),
         ],
         compiler_params=params(60),
         name="inner",
     )(planes, layer_depth)
     got = swap(sent)
-    left = around(to_east, "band", 1)
-    right = around(to_west, "band", -1)
+    swaps = band_swaps(to_first, to_second)
     flat = pl.BlockSpec((4, members, latitudes), lambda i: (0, 0, 0))
     straight, cross = pl.pallas_call(
         outer_kernel,
@@ -738,10 +756,11 @@
             pltpu.VMEM((12, members, latitudes), F32),
             pltpu.VMEM((10, members, latitudes), BF16),
             pltpu.VMEM((8, OUTER, 256), F32),
+            pltpu.VMEM((2, 4, members, latitudes), BF16),
         ],
         compiler_params=params(24),
         name="outer",
-    )(planes, planes, left, right, layer_depth)
+    )(planes, planes, *swaps, layer_depth)
     cross = across(cross, 1)
     got_edges = [across(jnp.stack([straight[k], cross[k]]), CHIPS[k]) for k in (3, 1, 2)]
     got_edges = got_edges[1:] + got_edges[:1]
@@ -750,28 +769,38 @@
     live = jnp.arange(slots, dtype=jnp.int32)[None, :] < observed_count[0][:, None]
     root = jnp.sqrt(jnp.where(live, 1.0 / error_variance[0], 0.0))
     vmem = pl.BlockSpec(memory_space=pltpu.VMEM)
+    slot = jnp.arange(slots, dtype=jnp.int32)
+    place = jnp.arange(slots + LANES, dtype=jnp.int32)
+    is_outer = rows >= 8 * INNER
+    near = jnp.where(is_outer, 0, rows)
+    rank = jnp.sum(is_outer[:, None, :] & (slot[None, :] < slot[:, None])[None], axis=2)
+    count = jnp.sum(is_outer, axis=1, keepdims=True)
+    found = is_outer[:, None, :] & (rank[:, None, :] == place[None, :, None])
+    outer = jnp.sum(jnp.where(found, slot, 0), axis=2)
+    outer = jnp.where(place[None] < count, outer, slots)
+    outer = jnp.where(place[None] == slots + LANES - 1, count, outer).astype(jnp.int32)
     rows = jnp.pad(rows, ((0, 0), (0, LANES)), constant_values=8 * INNER)
     smem = pl.BlockSpec(memory_space=pltpu.SMEM)
-    held_inner, seen, outer = pl.pallas_call(
+    held_inner, seen = pl.pallas_call(
         spread_kernel,
         out_shape=(
             jax.ShapeDtypeStruct((8, INNER, 256), BF16),
             jax.ShapeDtypeStruct((2, 2, slots, LANES), F32),
-            jax.ShapeDtypeStruct((2, slots + LANES), jnp.int32),
         ),
         in_specs=[smem, vmem],
-        out_specs=(vmem, vmem, smem),
         scratch_shapes=[pltpu.VMEM((2, 8 * INNER, LANES), F32)],
         compiler_params=params(12),
         cost_estimate=cost(1, 8 * MIB),
         name="spread",
-    )(rows, got)
-    held_outer, gram, short = pl.pallas_call(
+    )(near, got)
+    one_tile = jax.ShapeDtypeStruct((PACKED, 256), BF16)
+    held_outer, gram, to_first, to_second = pl.pallas_call(
         observe_kernel,
         out_shape=(
             jax.ShapeDtypeStruct((8, BLOCK, 256), BF16),
             jax.ShapeDtypeStruct((2, PACKED, 256), F32),
-            jax.ShapeDtypeStruct((2, PACKED, 256), BF16),
+            one_tile,
+            one_tile,
         ),
         in_specs=[smem, smem] + [vmem] * 8,
         scratch_shapes=[
@@ -795,17 +824,16 @@
         name="prepare",
     )(held_inner, held_outer)
 
-    below = along(short, "mem", 1)
-    above = along(short, "mem", -1)
-    one_tile = jax.ShapeDtypeStruct((PACKED, 256), BF16)
-    column, to_west, to_east = pl.pallas_call(
+    line, short = pl.pallas_call(
         combine_kernel,
-        out_shape=(jax.ShapeDtypeStruct(gram.shape, F32), one_tile, one_tile),
+        out_shape=(
+            jax.ShapeDtypeStruct(gram.shape, F32),
+            jax.ShapeDtypeStruct(gram.shape, BF16),
+        ),
         compiler_params=params(8),
         name="combine",
-    )(gram, below, above)
-    west = around(to_east, "band", 1)
-    east = around(to_west, "band", -1)
+    )(gram, *band_swaps(to_first, to_second))
+    below, above = mem_swaps(short)
     *back, maps = pl.pallas_call(
         analyse_kernel,
         out_shape=(jax.ShapeDtypeStruct((FIRST, 256), BF16),) * 8
@@ -813,7 +841,7 @@
         scratch_shapes=[pltpu.VMEM((8, FIRST, 256), BF16), pltpu.VMEM((2, 8, 32, 256), BF16)],
         compiler_params=params(20),
         name="analyse",
-    )(column, west, east, anomaly_1, mean_1)
+    )(line, below, above, anomaly_1, mean_1)
     first = partners(back)
     maps, first[4] = lax.optimization_barrier((maps, first[4]))
     back = pl.pallas_call(
@@ -859,8 +887,9 @@
 
 
 def choose(ensemble, layer_depth, observed_cell, *rest):
-    shape = (lax.axis_size("mem"), ensemble.shape, observed_cell.shape[1])
-    fits = shape == (8, (32, 3, 60, 160), 2) and observed_cell.shape[2] % 16 == 0
+    mesh_shape = (lax.axis_size("mem"), lax.axis_size("band"))
+    shape = (mesh_shape, ensemble.shape, observed_cell.shape[1])
+    fits = shape == ((8, 4), (32, 3, 60, 160), 2) and observed_cell.shape[2] % 16 == 0
     chosen = on_device_fast if fits else on_device
     return chosen(ensemble, layer_depth, observed_cell, *rest)
 

time: 93.3 us -> 88.1 us (0.944)
  waiting for transfers between devices: 27 us -> 22 us
  Pallas kernels: 30.9 us -> 26.7 us
  starting transfers between devices: 34.4 us -> 37.1 us
  other arithmetic: 0.22 us -> 1.43 us
    pallas_call x1, Pallas kernels: 9.6 us -> 5.4 us  [on_device_fast(): pl.pallas_call(spread_kernel, out_shape=(jax.ShapeDtypeStruct((8, INNER,...]
    ppermute x18, starting transfers between devices: 16.2 us -> 20 us  [across(): return lax.ppermute(value, 'mem', [(i, i ^ difference) for i in range(8)])]
    ppermute x18, waiting for transfers between devices: 12.5 us -> 9.8 us  [across(): return lax.ppermute(value, 'mem', [(i, i ^ difference) for i in range(8)])]
    ppermute x6, waiting for transfers between devices: 7.89 us -> 6.42 us  [swapped_pairs(): moved.append(lax.ppermute(value, axis, both))]
    reduce_sum x0 -> x3, other arithmetic: none -> 1.04 us  [the longest x1 0.63 us: on_device_fast(): outer = jnp.sum(jnp.where(found, slot, 0), axis=2)]
    ppermute x6, starting transfers between devices: 12.8 us -> 11.8 us  [swapped_pairs(): moved.append(lax.ppermute(value, axis, both))]
  transfers between devices with their start and end apart: 25 -> 25, of which waited for: 14 -> 11; matrix products, arithmetic and copies ran while one was open for 0% -> 2% of each run, Pallas kernels for 16% -> 12%
where the time goes in v8:
time: 88.1 us; the launch traced here: 87.8 us
  starting transfers between devices  37.1 us (42%)
  Pallas kernels  26.7 us (30%)
  waiting for transfers between devices  22 us (25%)
  other arithmetic  1.43 us (2%)
    ppermute x18, starting transfers between devices, across(): return lax.ppermute(value, 'mem', [(i, i ^ difference) for i in range(8)])  20 us
    ppermute x6, starting transfers between devices, swapped_pairs(): moved.append(lax.ppermute(value, axis, both))  11.8 us
    ppermute x18, waiting for transfers between devices, across(): return lax.ppermute(value, 'mem', [(i, i ^ difference) for i in range(8)])  9.8 us
    ppermute x6, waiting for transfers between devices, swapped_pairs(): moved.append(lax.ppermute(value, axis, both))  6.42 us
    pallas_call x1, Pallas kernels, on_device_fast(): pl.pallas_call(analyse_kernel, out_shape=(jax.ShapeDtypeStruct((FIRST, 25...  6.06 us
    all_to_all x1, waiting for transfers between devices, swap(): return lax.all_to_all(value, 'mem', split_axis=0, concat_axis=0, tiled=True)  5.82 us
    pallas_call x1, Pallas kernels, on_device_fast(): pl.pallas_call(spread_kernel, out_shape=(jax.ShapeDtypeStruct((8, INNER,...  5.4 us
    all_to_all x1, starting transfers between devices, swap(): return lax.all_to_all(value, 'mem', split_axis=0, concat_axis=0, tiled=True)  5.32 us
  transfers between devices with their start and end apart: 25, of which 11 were waited for; matrix products, arithmetic and copies ran while one was open for 2% of the time, Pallas kernels for 12%

profile of v8, /device:TPU:0, one launch (start us, length us, event | category | flops | bytes accessed | tf_op | source)
XLA Modules:
  0.0 87.8 jit_solution(10110127477822478010)
XLA Ops:
  0.0 5.1 %inner.1 = (bf16[8,360,256]{2,1,0:T(8,128)(2,1)}, bf16[4,32,160]{2,1,0:T(8,128)(2,1)}, bf16[4,32,160]{2,1,0:T(8,128)(2,1)}) custom-call(bf16[3,60,32,160]{3,2,1,0:T(8,128)(2,1)} %bitcast.47, f32[60,160]{1,0:T(8,128)} %depth.3), custom_call_target="tpu_custom_call" | custom-call | tf_op jit(solution)/shard_map/inner/pallas_call | solution.py:724
  5.1 5.3 %all-to-all-start = ((bf16[8,360,256]{2,1,0:T(8,128)(2,1)}), bf16[8,360,256]{2,1,0:T(8,128)(2,1)}, u32[]{:S(2)}, u32[]{:S(2)}) async-start(bf16[8,360,256]{2,1,0:T(8,128)(2,1)} %get-tuple-element.41), calls=%async_computation | async-start | bytes 2949120 | tf_op jit(solution)/shard_map/all_to_all | solution.py:696
  10.5 2.2 %collective-permute-start = (bf16[4,32,160]{2,1,0:T(8,128)(2,1)S(1)}, bf16[4,32,160]{2,1,0:T(8,128)(2,1)S(1)}, u32[]{:S(2)}, u32[]{:S(2)}) collective-permute-start(bf16[4,32,160]{2,1,0:T(8,128)(2,1)S(1)} %copy-done.7), channel_id=1, source_target_pairs={{0,1},{2,3},{1,0},{3,2},{4,5},{6,7},{5,4},{7,6},{8,9},{10,11},{9,8... | collective-permute-start | bytes 122888 | tf_op jit(solution)/shard_map/ppermute | solution.py:670
  12.7 2.5 %collective-permute-start.1 = (bf16[4,32,160]{2,1,0:T(8,128)(2,1)S(1)}, bf16[4,32,160]{2,1,0:T(8,128)(2,1)S(1)}, u32[]{:S(2)}, u32[]{:S(2)}) collective-permute-start(bf16[4,32,160]{2,1,0:T(8,128)(2,1)S(1)} %copy-done.6), channel_id=1, source_target_pairs={{1,2},{3,0},{2,1},{0,3},{5,6},{7,4},{6,5},{4,7},{9,10},{11,8},{10,... | collective-permute-start | bytes 122888 | tf_op jit(solution)/shard_map/ppermute | solution.py:670
  16.5 2.4 %collective-permute-done.1.second_swap = bf16[4,32,160]{2,1,0:T(8,128)(2,1)S(1)} collective-permute-done((bf16[4,32,160]{2,1,0:T(8,128)(2,1)S(1)}, bf16[4,32,160]{2,1,0:T(8,128)(2,1)S(1)}, u32[]{:S(2)}, u32[]{:S(2)}) %collective-permute-start.1) | collective-permute-done | bytes 40992 | tf_op jit(solution)/shard_map/ppermute | solution.py:670
  21.4 1.9 %collective-permute-start.3 = (bf16[2,104,256]{2,1,0:T(8,128)(2,1)S(1)}, bf16[2,104,256]{2,1,0:T(8,128)(2,1)S(1)}, u32[]{:S(2)}, u32[]{:S(2)}) collective-permute-start(bf16[2,104,256]{2,1,0:T(8,128)(2,1)S(1)} %pad_maximum_fusion), channel_id=1, source_target_pairs={{0,8},{4,12},{8,0},{12,4},{16,24},{20,28},{24,16},{28,20},{1,9},{5... | collective-permute-start | bytes 319496 | tf_op jit(solution)/shard_map/ppermute | solution.py:688
  25.2 5.8 %all-to-all-done.got = bf16[8,360,256]{2,1,0:T(8,128)(2,1)} async-done(((bf16[8,360,256]{2,1,0:T(8,128)(2,1)}), bf16[8,360,256]{2,1,0:T(8,128)(2,1)}, u32[]{:S(2)}, u32[]{:S(2)}) %all-to-all-start) | async-done | bytes 1474592 | tf_op jit(solution)/shard_map/all_to_all | solution.py:696
  31.1 5.4 %spread.1 = (bf16[8,360,256]{2,1,0:T(8,128)(2,1)S(1)}, f32[2,2,512,128]{3,2,1,0:T(8,128)S(1)}) custom-call(s32[2,512]{1,0:T(2,128)S(1)} %get-tuple-element.77.cells, bf16[8,360,256]{2,1,0:T(8,128)(2,1)} %all-to-all-done.got), custom_call_target="tpu_custom_call" | custom-call | flops 1 | bytes 8388608 | tf_op jit(solution)/shard_map/spread/pallas_call | solution.py:784
  36.5 3.3 %observe.1 = (bf16[8,112,256]{2,1,0:T(8,128)(2,1)S(1)}, f32[2,144,256]{2,1,0:T(8,128)S(1)}, bf16[144,256]{1,0:T(8,128)(2,1)S(1)}, bf16[144,256]{1,0:T(8,128)(2,1)S(1)}) custom-call(s32[2,640]{1,0:T(2,128)S(1)} %pad.4.cells, s32[2,640]{1,0:T(2,128)S(1)} %fusion.3.outer, f32[2,512]{1,0:T(2,128)S(1)} %fusion.10.weight, f32[2,512]{1,0:T(2,128)S(1)} %bitcast.50, ...), custom_call_target="tpu_custom_call" | custom-call | tf_op jit(solution)/shard_map/observe/pallas_call | solution.py:797
  39.8 2.0 %collective-permute-start.6 = (bf16[144,256]{1,0:T(8,128)(2,1)S(1)}, bf16[144,256]{1,0:T(8,128)(2,1)S(1)}, u32[]{:S(2)}, u32[]{:S(2)}) collective-permute-start(bf16[144,256]{1,0:T(8,128)(2,1)S(1)} %get-tuple-element.48), channel_id=1, source_target_pairs={{0,1},{2,3},{1,0},{3,2},{4,5},{6,7},{5,4},{7,6},{8,9},{10,11},{9,8... | collective-permute-start | bytes 221192 | tf_op jit(solution)/shard_map/ppermute | solution.py:670
  41.8 2.5 %collective-permute-start.7 = (bf16[144,256]{1,0:T(8,128)(2,1)S(1)}, bf16[144,256]{1,0:T(8,128)(2,1)S(1)}, u32[]{:S(2)}, u32[]{:S(2)}) collective-permute-start(bf16[144,256]{1,0:T(8,128)(2,1)S(1)} %get-tuple-element.49), channel_id=1, source_target_pairs={{1,2},{3,0},{2,1},{0,3},{5,6},{7,4},{6,5},{4,7},{9,10},{11,8},{10,... | collective-permute-start | bytes 221192 | tf_op jit(solution)/shard_map/ppermute | solution.py:670
  44.3 3.7 %collective-permute-done.7.second_swap = bf16[144,256]{1,0:T(8,128)(2,1)S(1)} collective-permute-done((bf16[144,256]{1,0:T(8,128)(2,1)S(1)}, bf16[144,256]{1,0:T(8,128)(2,1)S(1)}, u32[]{:S(2)}, u32[]{:S(2)}) %collective-permute-start.7) | collective-permute-done | bytes 73760 | tf_op jit(solution)/shard_map/ppermute | solution.py:670
  48.9 1.8 %collective-permute-start.8 = (bf16[2,144,256]{2,1,0:T(8,128)(2,1)S(1)}, bf16[2,144,256]{2,1,0:T(8,128)(2,1)S(1)}, u32[]{:S(2)}, u32[]{:S(2)}) collective-permute-start(bf16[2,144,256]{2,1,0:T(8,128)(2,1)S(1)} %get-tuple-element.51), channel_id=1, source_target_pairs={{0,4},{8,12},{16,20},{24,28},{4,0},{12,8},{20,16},{28,24},{1,5},{9... | collective-permute-start | bytes 442376 | tf_op jit(solution)/shard_map/ppermute | solution.py:670
  51.7 6.1 %analyse.1 = (bf16[240,256]{1,0:T(8,128)(2,1)S(1)}, bf16[240,256]{1,0:T(8,128)(2,1)S(1)}, bf16[240,256]{1,0:T(8,128)(2,1)S(1)}, bf16[240,256]{1,0:T(8,128)(2,1)S...) custom-call(f32[2,144,256]{2,1,0:T(8,128)S(1)} %get-tuple-element.50, ...), custom_call_target="tpu_custom_call" | custom-call | tf_op jit(solution)/shard_map/analyse/pallas_call | solution.py:837
  57.7 2.0 %collective-permute-start.10 = (bf16[240,256]{1,0:T(8,128)(2,1)S(1)}, bf16[240,256]{1,0:T(8,128)(2,1)S(1)}, u32[]{:S(2)}, u32[]{:S(2)}) collective-permute-start(bf16[240,256]{1,0:T(8,128)(2,1)S(1)} %get-tuple-element.57), channel_id=1, source_target_pairs={{0,4},{4,0},{8,12},{12,8},{16,20},{20,16},{24,28},{28,24},{1,5},{5... | collective-permute-start | bytes 368648 | tf_op jit(solution)/shard_map/ppermute | solution.py:688
  59.8 2.7 %collective-permute-start.18 = (bf16[240,256]{1,0:T(8,128)(2,1)S(1)}, bf16[240,256]{1,0:T(8,128)(2,1)S(1)}, u32[]{:S(2)}, u32[]{:S(2)}) collective-permute-start(bf16[240,256]{1,0:T(8,128)(2,1)S(1)} %get-tuple-element.69), channel_id=1, source_target_pairs={{0,24},{4,28},{8,16},{12,20},{16,8},{20,12},{24,0},{28,4},{1,25},{... | collective-permute-start | bytes 368648 | tf_op jit(solution)/shard_map/ppermute | solution.py:688
  62.5 1.6 %collective-permute-start.19 = (bf16[240,256]{1,0:T(8,128)(2,1)S(1)}, bf16[240,256]{1,0:T(8,128)(2,1)S(1)}, u32[]{:S(2)}, u32[]{:S(2)}) collective-permute-start(bf16[240,256]{1,0:T(8,128)(2,1)S(1)} %get-tuple-element.70), channel_id=1, source_target_pairs={{0,8},{4,12},{8,0},{12,4},{16,24},{20,28},{24,16},{28,20},{1,9},{5... | collective-permute-start | bytes 368648 | tf_op jit(solution)/shard_map/ppermute | solution.py:688
  65.2 2.1 %collective-permute-start.22 = (bf16[240,256]{1,0:T(8,128)(2,1)S(1)}, bf16[240,256]{1,0:T(8,128)(2,1)S(1)}, u32[]{:S(2)}, u32[]{:S(2)}) collective-permute-start(bf16[240,256]{1,0:T(8,128)(2,1)S(1)} %get-tuple-element.74), channel_id=1, source_target_pairs={{0,12},{4,8},{8,4},{12,0},{16,28},{20,24},{24,20},{28,16},{1,13},{... | collective-permute-start | bytes 368648 | tf_op jit(solution)/shard_map/ppermute | solution.py:688
  68.6 2.0 %second.1 = (bf16[224,256]{1,0:T(8,128)(2,1)S(1)}, bf16[224,256]{1,0:T(8,128)(2,1)S(1)}, bf16[224,256]{1,0:T(8,128)(2,1)S(1)}, bf16[224,256]{1,0:T(8,128)(2,1)S(...) custom-call(bf16[2,256,256]{2,1,0:T(8,128)(2,1)S(1)} %get-tuple-elem, ...), custom_call_target="tpu_custom_call" | custom-call | flops 1 | bytes 6291456 | tf_op jit(solution)/shard_map/second/pallas_call | solution.py:847
  75.3 1.8 %collective-permute-start.14 = (bf16[224,256]{1,0:T(8,128)(2,1)S(1)}, bf16[224,256]{1,0:T(8,128)(2,1)S(1)}, u32[]{:S(2)}, u32[]{:S(2)}) collective-permute-start(bf16[224,256]{1,0:T(8,128)(2,1)S(1)} %get-tuple-element.64), channel_id=1, source_target_pairs={{0,28},{4,24},{8,20},{12,16},{16,12},{20,8},{24,4},{28,0},{1,29},{... | collective-permute-start | bytes 344072 | tf_op jit(solution)/shard_map/ppermute | solution.py:688
  78.0 3.2 %collective-permute-done.12.refs_1_ = bf16[224,256]{1,0:T(8,128)(2,1)S(1)} collective-permute-done((bf16[224,256]{1,0:T(8,128)(2,1)S(1)}, bf16[224,256]{1,0:T(8,128)(2,1)S(1)}, u32[]{:S(2)}, u32[]{:S(2)}) %collective-permute-start.12) | collective-permute-done | bytes 114720 | tf_op jit(solution)/shard_map/ppermute | solution.py:688
  81.2 1.6 %first_return.1.refs_8_ = bf16[3,60,32,160]{3,2,1,0:T(8,128)(2,1)} custom-call(bf16[240,256]{1,0:T(8,128)(2,1)S(1)} %collective-permute-done.18.refs_0_, bf16[240,256]{1,0:T(8,128)(2,1)S(1)} %collective-permute-done.19.refs_1_, bf16[240,256]{1,0:T(8,128)(2,1)S(1)} %collective-permute-done.20.refs_2_, bf16[240,256]{1,0:T(8,128)(2,1)S(1)} %collective-permute-done.21.refs_3_, ...), custom_call_target="tpu_custom_call" | custom-call | flops 1 | bytes 4194304 | tf_op jit(solution)/shard_map/first_return/pallas_call | solution.py:857
  82.9 2.3 %collective-permute-done.16.refs_5_ = bf16[224,256]{1,0:T(8,128)(2,1)S(1)} collective-permute-done((bf16[224,256]{1,0:T(8,128)(2,1)S(1)}, bf16[224,256]{1,0:T(8,128)(2,1)S(1)}, u32[]{:S(2)}, u32[]{:S(2)}) %collective-permute-start.16) | collective-permute-done | bytes 114720 | tf_op jit(solution)/shard_map/ppermute | solution.py:688
  86.0 1.6 %second_return.1 = bf16[3,60,32,160]{3,2,1,0:T(8,128)(2,1)} custom-call(bf16[224,256]{1,0:T(8,128)(2,1)S(1)} %collective-permute-done.11.refs_0_, bf16[224,256]{1,0:T(8,128)(2,1)S(1)} %collective-permute-done.12.refs_1_, bf16[224,256]{1,0:T(8,128)(2,1)S(1)} %collective-permute-done.13.refs_2_, ...), custom_call_target="tpu_custom_call", output_to_operand_aliasing={{}: (8, {})} | custom-call | tf_op jit(solution)/shard_map/second_return/pallas_call | solution.py:871
  (68 shorter events, 16.4 us)
Async XLA Ops:
  5.1 25.9 %all-to-all-start = ((bf16[8,360,256]{2,1,0:T(8,128)(2,1)}), bf16[8,360,256]{2,1,0:T(8,128)(2,1)}, u32[]{:S(2)}, u32[]{:S(2)}) async-start(bf16[8,360,256]{2,1,0:T(8,128)(2,1)} %get-tuple-element.41), calls=%async_computation | async-start | bytes 2949120 | tf_op jit(solution)/shard_map/all_to_all | solution.py:696
  10.5 6.0 %collective-permute-start = (bf16[4,32,160]{2,1,0:T(8,128)(2,1)S(1)}, bf16[4,32,160]{2,1,0:T(8,128)(2,1)S(1)}, u32[]{:S(2)}, u32[]{:S(2)}) collective-permute-start(bf16[4,32,160]{2,1,0:T(8,128)(2,1)S(1)} %copy-done.7), channel_id=1, source_target_pairs={{0,1},{2,3},{1,0},{3,2},{4,5},{6,7},{5,4},{7,6},{8,9},{10,11},{9,8... | collective-permute-start | bytes 122888 | tf_op jit(solution)/shard_map/ppermute | solution.py:670
  12.7 6.2 %collective-permute-start.1 = (bf16[4,32,160]{2,1,0:T(8,128)(2,1)S(1)}, bf16[4,32,160]{2,1,0:T(8,128)(2,1)S(1)}, u32[]{:S(2)}, u32[]{:S(2)}) collective-permute-start(bf16[4,32,160]{2,1,0:T(8,128)(2,1)S(1)} %copy-done.6), channel_id=1, source_target_pairs={{1,2},{3,0},{2,1},{0,3},{5,6},{7,4},{6,5},{4,7},{9,10},{11,8},{10,... | collective-permute-start | bytes 122888 | tf_op jit(solution)/shard_map/ppermute | solution.py:670
  21.4 15.0 %collective-permute-start.3 = (bf16[2,104,256]{2,1,0:T(8,128)(2,1)S(1)}, bf16[2,104,256]{2,1,0:T(8,128)(2,1)S(1)}, u32[]{:S(2)}, u32[]{:S(2)}) collective-permute-start(bf16[2,104,256]{2,1,0:T(8,128)(2,1)S(1)} %pad_maximum_fusion), channel_id=1, source_target_pairs={{0,8},{4,12},{8,0},{12,4},{16,24},{20,28},{24,16},{28,20},{1,9},{5... | collective-permute-start | bytes 319496 | tf_op jit(solution)/shard_map/ppermute | solution.py:688
  23.4 13.1 %collective-permute-start.4 = (bf16[2,104,256]{2,1,0:T(8,128)(2,1)S(1)}, bf16[2,104,256]{2,1,0:T(8,128)(2,1)S(1)}, u32[]{:S(2)}, u32[]{:S(2)}) collective-permute-start(bf16[2,104,256]{2,1,0:T(8,128)(2,1)S(1)} %pad_maximum_fusion.1), channel_id=1, source_target_pairs={{0,16},{4,20},{8,24},{12,28},{16,0},{20,4},{24,8},{28,12},{1,17},{... | collective-permute-start | bytes 319496 | tf_op jit(solution)/shard_map/ppermute | solution.py:688
  24.9 11.6 %collective-permute-start.5 = (bf16[2,104,256]{2,1,0:T(8,128)(2,1)S(1)}, bf16[2,104,256]{2,1,0:T(8,128)(2,1)S(1)}, u32[]{:S(2)}, u32[]{:S(2)}) collective-permute-start(bf16[2,104,256]{2,1,0:T(8,128)(2,1)S(1)} %pad_maximum_fusion.2), channel_id=1, source_target_pairs={{0,24},{4,28},{8,16},{12,20},{16,8},{20,12},{24,0},{28,4},{1,25},{... | collective-permute-start | bytes 319496 | tf_op jit(solution)/shard_map/ppermute | solution.py:688
  39.8 4.5 %collective-permute-start.6 = (bf16[144,256]{1,0:T(8,128)(2,1)S(1)}, bf16[144,256]{1,0:T(8,128)(2,1)S(1)}, u32[]{:S(2)}, u32[]{:S(2)}) collective-permute-start(bf16[144,256]{1,0:T(8,128)(2,1)S(1)} %get-tuple-element.48), channel_id=1, source_target_pairs={{0,1},{2,3},{1,0},{3,2},{4,5},{6,7},{5,4},{7,6},{8,9},{10,11},{9,8... | collective-permute-start | bytes 221192 | tf_op jit(solution)/shard_map/ppermute | solution.py:670
  41.8 6.2 %collective-permute-start.7 = (bf16[144,256]{1,0:T(8,128)(2,1)S(1)}, bf16[144,256]{1,0:T(8,128)(2,1)S(1)}, u32[]{:S(2)}, u32[]{:S(2)}) collective-permute-start(bf16[144,256]{1,0:T(8,128)(2,1)S(1)} %get-tuple-element.49), channel_id=1, source_target_pairs={{1,2},{3,0},{2,1},{0,3},{5,6},{7,4},{6,5},{4,7},{9,10},{11,8},{10,... | collective-permute-start | bytes 221192 | tf_op jit(solution)/shard_map/ppermute | solution.py:670
  48.1 3.3 %collective-permute-start.9 = (bf16[2,144,256]{2,1,0:T(8,128)(2,1)S(1)}, bf16[2,144,256]{2,1,0:T(8,128)(2,1)S(1)}, u32[]{:S(2)}, u32[]{:S(2)}) collective-permute-start(bf16[2,144,256]{2,1,0:T(8,128)(2,1)S(1)} %get-tuple-element.51), channel_id=1, source_target_pairs={{4,8},{12,16},{20,24},{8,4},{16,12},{24,20},{5,9},{13,17},{21,25},... | collective-permute-start | bytes 442376 | tf_op jit(solution)/shard_map/ppermute | solution.py:670
  48.9 2.8 %collective-permute-start.8 = (bf16[2,144,256]{2,1,0:T(8,128)(2,1)S(1)}, bf16[2,144,256]{2,1,0:T(8,128)(2,1)S(1)}, u32[]{:S(2)}, u32[]{:S(2)}) collective-permute-start(bf16[2,144,256]{2,1,0:T(8,128)(2,1)S(1)} %get-tuple-element.51), channel_id=1, source_target_pairs={{0,4},{8,12},{16,20},{24,28},{4,0},{12,8},{20,16},{28,24},{1,5},{9... | collective-permute-start | bytes 442376 | tf_op jit(solution)/shard_map/ppermute | solution.py:670
  57.7 7.5 %collective-permute-start.10 = (bf16[240,256]{1,0:T(8,128)(2,1)S(1)}, bf16[240,256]{1,0:T(8,128)(2,1)S(1)}, u32[]{:S(2)}, u32[]{:S(2)}) collective-permute-start(bf16[240,256]{1,0:T(8,128)(2,1)S(1)} %get-tuple-element.57), channel_id=1, source_target_pairs={{0,4},{4,0},{8,12},{12,8},{16,20},{20,16},{24,28},{28,24},{1,5},{5... | collective-permute-start | bytes 368648 | tf_op jit(solution)/shard_map/ppermute | solution.py:688
  59.8 7.6 %collective-permute-start.18 = (bf16[240,256]{1,0:T(8,128)(2,1)S(1)}, bf16[240,256]{1,0:T(8,128)(2,1)S(1)}, u32[]{:S(2)}, u32[]{:S(2)}) collective-permute-start(bf16[240,256]{1,0:T(8,128)(2,1)S(1)} %get-tuple-element.69), channel_id=1, source_target_pairs={{0,24},{4,28},{8,16},{12,20},{16,8},{20,12},{24,0},{28,4},{1,25},{... | collective-permute-start | bytes 368648 | tf_op jit(solution)/shard_map/ppermute | solution.py:688
  62.5 8.4 %collective-permute-start.19 = (bf16[240,256]{1,0:T(8,128)(2,1)S(1)}, bf16[240,256]{1,0:T(8,128)(2,1)S(1)}, u32[]{:S(2)}, u32[]{:S(2)}) collective-permute-start(bf16[240,256]{1,0:T(8,128)(2,1)S(1)} %get-tuple-element.70), channel_id=1, source_target_pairs={{0,8},{4,12},{8,0},{12,4},{16,24},{20,28},{24,16},{28,20},{1,9},{5... | collective-permute-start | bytes 368648 | tf_op jit(solution)/shard_map/ppermute | solution.py:688
  64.1 8.1 %collective-permute-start.20 = (bf16[240,256]{1,0:T(8,128)(2,1)S(1)}, bf16[240,256]{1,0:T(8,128)(2,1)S(1)}, u32[]{:S(2)}, u32[]{:S(2)}) collective-permute-start(bf16[240,256]{1,0:T(8,128)(2,1)S(1)} %get-tuple-element.71), channel_id=1, source_target_pairs={{0,16},{4,20},{8,24},{12,28},{16,0},{20,4},{24,8},{28,12},{1,17},{... | collective-permute-start | bytes 368648 | tf_op jit(solution)/shard_map/ppermute | solution.py:688
  64.1 9.1 %collective-permute-start.21 = (bf16[240,256]{1,0:T(8,128)(2,1)S(1)}, bf16[240,256]{1,0:T(8,128)(2,1)S(1)}, u32[]{:S(2)}, u32[]{:S(2)}) collective-permute-start(bf16[240,256]{1,0:T(8,128)(2,1)S(1)} %get-tuple-element.72), channel_id=1, source_target_pairs={{0,28},{4,24},{8,20},{12,16},{16,12},{20,8},{24,4},{28,0},{1,29},{... | collective-permute-start | bytes 368648 | tf_op jit(solution)/shard_map/ppermute | solution.py:688
  65.2 10.1 %collective-permute-start.22 = (bf16[240,256]{1,0:T(8,128)(2,1)S(1)}, bf16[240,256]{1,0:T(8,128)(2,1)S(1)}, u32[]{:S(2)}, u32[]{:S(2)}) collective-permute-start(bf16[240,256]{1,0:T(8,128)(2,1)S(1)} %get-tuple-element.74), channel_id=1, source_target_pairs={{0,12},{4,8},{8,4},{12,0},{16,28},{20,24},{24,20},{28,16},{1,13},{... | collective-permute-start | bytes 368648 | tf_op jit(solution)/shard_map/ppermute | solution.py:688
  67.4 9.8 %collective-permute-start.23 = (bf16[240,256]{1,0:T(8,128)(2,1)S(1)}, bf16[240,256]{1,0:T(8,128)(2,1)S(1)}, u32[]{:S(2)}, u32[]{:S(2)}) collective-permute-start(bf16[240,256]{1,0:T(8,128)(2,1)S(1)} %get-tuple-element.75), channel_id=1, source_target_pairs={{0,20},{4,16},{8,28},{12,24},{16,4},{20,0},{24,12},{28,8},{1,21},{... | collective-permute-start | bytes 368648 | tf_op jit(solution)/shard_map/ppermute | solution.py:688
  70.9 7.0 %collective-permute-start.11 = (bf16[224,256]{1,0:T(8,128)(2,1)S(1)}, bf16[224,256]{1,0:T(8,128)(2,1)S(1)}, u32[]{:S(2)}, u32[]{:S(2)}) collective-permute-start(bf16[224,256]{1,0:T(8,128)(2,1)S(1)} %get-tuple-element.61), channel_id=1, source_target_pairs={{0,24},{4,28},{8,16},{12,20},{16,8},{20,12},{24,0},{28,4},{1,25},{... | collective-permute-start | bytes 344072 | tf_op jit(solution)/shard_map/ppermute | solution.py:688
  72.3 8.9 %collective-permute-start.12 = (bf16[224,256]{1,0:T(8,128)(2,1)S(1)}, bf16[224,256]{1,0:T(8,128)(2,1)S(1)}, u32[]{:S(2)}, u32[]{:S(2)}) collective-permute-start(bf16[224,256]{1,0:T(8,128)(2,1)S(1)} %get-tuple-element.62), channel_id=1, source_target_pairs={{0,8},{4,12},{8,0},{12,4},{16,24},{20,28},{24,16},{28,20},{1,9},{5... | collective-permute-start | bytes 344072 | tf_op jit(solution)/shard_map/ppermute | solution.py:688
  73.3 9.5 %collective-permute-start.13 = (bf16[224,256]{1,0:T(8,128)(2,1)S(1)}, bf16[224,256]{1,0:T(8,128)(2,1)S(1)}, u32[]{:S(2)}, u32[]{:S(2)}) collective-permute-start(bf16[224,256]{1,0:T(8,128)(2,1)S(1)} %get-tuple-element.63), channel_id=1, source_target_pairs={{0,16},{4,20},{8,24},{12,28},{16,0},{20,4},{24,8},{28,12},{1,17},{... | collective-permute-start | bytes 344072 | tf_op jit(solution)/shard_map/ppermute | solution.py:688
  75.3 7.5 %collective-permute-start.14 = (bf16[224,256]{1,0:T(8,128)(2,1)S(1)}, bf16[224,256]{1,0:T(8,128)(2,1)S(1)}, u32[]{:S(2)}, u32[]{:S(2)}) collective-permute-start(bf16[224,256]{1,0:T(8,128)(2,1)S(1)} %get-tuple-element.64), channel_id=1, source_target_pairs={{0,28},{4,24},{8,20},{12,16},{16,12},{20,8},{24,4},{28,0},{1,29},{... | collective-permute-start | bytes 344072 | tf_op jit(solution)/shard_map/ppermute | solution.py:688
  77.2 5.7 %collective-permute-start.15 = (bf16[224,256]{1,0:T(8,128)(2,1)S(1)}, bf16[224,256]{1,0:T(8,128)(2,1)S(1)}, u32[]{:S(2)}, u32[]{:S(2)}) collective-permute-start(bf16[224,256]{1,0:T(8,128)(2,1)S(1)} %get-tuple-element.65), channel_id=1, source_target_pairs={{0,4},{4,0},{8,12},{12,8},{16,20},{20,16},{24,28},{28,24},{1,5},{5... | collective-permute-start | bytes 344072 | tf_op jit(solution)/shard_map/ppermute | solution.py:688
  77.9 7.3 %collective-permute-start.16 = (bf16[224,256]{1,0:T(8,128)(2,1)S(1)}, bf16[224,256]{1,0:T(8,128)(2,1)S(1)}, u32[]{:S(2)}, u32[]{:S(2)}) collective-permute-start(bf16[224,256]{1,0:T(8,128)(2,1)S(1)} %get-tuple-element.66), channel_id=1, source_target_pairs={{0,12},{4,8},{8,4},{12,0},{16,28},{20,24},{24,20},{28,16},{1,13},{... | collective-permute-start | bytes 344072 | tf_op jit(solution)/shard_map/ppermute | solution.py:688
  81.2 4.8 %collective-permute-start.17 = (bf16[224,256]{1,0:T(8,128)(2,1)S(1)}, bf16[224,256]{1,0:T(8,128)(2,1)S(1)}, u32[]{:S(2)}, u32[]{:S(2)}) collective-permute-start(bf16[224,256]{1,0:T(8,128)(2,1)S(1)} %get-tuple-element.67), channel_id=1, source_target_pairs={{0,20},{4,16},{8,28},{12,24},{16,4},{20,0},{24,12},{28,8},{1,21},{... | collective-permute-start | bytes 344072 | tf_op jit(solution)/shard_map/ppermute | solution.py:688
  (9 other events, 101.4 us)

commit v9 on v8

--- a/solution.py
+++ b/solution.py
@@ -173,7 +173,7 @@
 BF16 = jnp.bfloat16
 PACKED = 144
 CHIPS = (0, 2, 4, 6)
-ORDER = (6, 2, 4, 7, 1, 3, 5, 0)
+ORDER = (6, 7, 2, 4, 3, 5, 1, 0)
 MIB = 1024 * 1024
 
 
@@ -442,14 +442,22 @@
             held[q, here, spans[h]] = blocks[q][h]
 
 
-def spread_kernel(cells, got, held, seen, wide):
+def spread_kernel(cells, far, held, seen, wide, got, arrived):
+    copies = []
+    for k, (first, last) in enumerate(((0, 128), (128, 256), (256, INNER))):
+        span = pl.ds(first, last - first)
+        copies.append(pltpu.make_async_copy(far.at[:, span], got.at[:, span], arrived.at[k]))
+    for copy in copies:
+        copy.start()
     lane = lax.broadcasted_iota(jnp.int32, (16, LANES), 1)
 
     def step(index, carry):
         spread_block(got, held, wide, pl.multiple_of(index * 16, 16), lane)
         return carry
 
-    lax.fori_loop(0, 22, step, 0, unroll=4)
+    for copy, (first, last) in zip(copies, ((0, 8), (8, 16), (16, 22))):
+        copy.wait()
+        lax.fori_loop(first, last, step, 0, unroll=4)
     spread_block(got, held, wide, INNER - 16, lane)
     slots = seen.shape[2]
     unroll = 16
@@ -787,9 +795,13 @@
             jax.ShapeDtypeStruct((8, INNER, 256), BF16),
             jax.ShapeDtypeStruct((2, 2, slots, LANES), F32),
         ),
-        in_specs=[smem, vmem],
-        scratch_shapes=[pltpu.VMEM((2, 8 * INNER, LANES), F32)],
-        compiler_params=params(12),
+        in_specs=[smem, far],
+        scratch_shapes=[
+            pltpu.VMEM((2, 8 * INNER, LANES), F32),
+            pltpu.VMEM((8, INNER, 256), BF16),
+            pltpu.SemaphoreType.DMA((3,)),
+        ],
+        compiler_params=params(16),
         cost_estimate=cost(1, 8 * MIB),
         name="spread",
     )(near, got)
@@ -843,7 +855,7 @@
         name="analyse",
     )(line, below, above, anomaly_1, mean_1)
     first = partners(back)
-    maps, first[4] = lax.optimization_barrier((maps, first[4]))
+    maps, first[0] = lax.optimization_barrier((maps, first[0]))
     back = pl.pallas_call(
         second_kernel,
         out_shape=(jax.ShapeDtypeStruct((SECOND, 256), BF16),) * 8,

time: 88.1 us -> 88.4 us (level)
  transfers between devices with their start and end apart: 25 -> 25, of which waited for: 11 -> 13; matrix products, arithmetic and copies ran while one was open for 2% -> 2% of each run, Pallas kernels for 12% -> 12%
where the time goes in v9:
time: 88.4 us; the launch traced here: 88.1 us
  starting transfers between devices  36.8 us (42%)
  Pallas kernels  27 us (31%)
  waiting for transfers between devices  22.4 us (25%)
  other arithmetic  1.43 us (2%)
    ppermute x18, starting transfers between devices, across(): return lax.ppermute(value, 'mem', [(i, i ^ difference) for i in range(8)])  19.7 us
    ppermute x6, starting transfers between devices, swapped_pairs(): moved.append(lax.ppermute(value, axis, both))  11.8 us
    ppermute x18, waiting for transfers between devices, across(): return lax.ppermute(value, 'mem', [(i, i ^ difference) for i in range(8)])  10.1 us
    ppermute x6, waiting for transfers between devices, swapped_pairs(): moved.append(lax.ppermute(value, axis, both))  6.49 us
    pallas_call x1, Pallas kernels, on_device_fast(): pl.pallas_call(analyse_kernel, out_shape=(jax.ShapeDtypeStruct((FIRST, 25...  6.06 us
    all_to_all x1, waiting for transfers between devices, swap(): return lax.all_to_all(value, 'mem', split_axis=0, concat_axis=0, tiled=True)  5.82 us
    pallas_call x1, Pallas kernels, on_device_fast(): pl.pallas_call(spread_kernel, out_shape=(jax.ShapeDtypeStruct((8, INNER,...  5.68 us
    all_to_all x1, starting transfers between devices, swap(): return lax.all_to_all(value, 'mem', split_axis=0, concat_axis=0, tiled=True)  5.32 us
  transfers between devices with their start and end apart: 25, of which 13 were waited for; matrix products, arithmetic and copies ran while one was open for 2% of the time, Pallas kernels for 12%

profile of v9, /device:TPU:0, one launch (start us, length us, event | category | flops | bytes accessed | tf_op | source)
XLA Modules:
  0.0 88.1 jit_solution(1500608717045958661)
XLA Ops:
  0.0 5.1 %inner.1 = (bf16[8,360,256]{2,1,0:T(8,128)(2,1)}, bf16[4,32,160]{2,1,0:T(8,128)(2,1)}, bf16[4,32,160]{2,1,0:T(8,128)(2,1)}) custom-call(bf16[3,60,32,160]{3,2,1,0:T(8,128)(2,1)} %bitcast.47, f32[60,160]{1,0:T(8,128)} %depth.3), custom_call_target="tpu_custom_call" | custom-call | tf_op jit(solution)/shard_map/inner/pallas_call | solution.py:732
  5.1 5.3 %all-to-all-start = ((bf16[8,360,256]{2,1,0:T(8,128)(2,1)}), bf16[8,360,256]{2,1,0:T(8,128)(2,1)}, u32[]{:S(2)}, u32[]{:S(2)}) async-start(bf16[8,360,256]{2,1,0:T(8,128)(2,1)} %get-tuple-element.41), calls=%async_computation | async-start | bytes 2949120 | tf_op jit(solution)/shard_map/all_to_all | solution.py:704
  10.5 2.2 %collective-permute-start = (bf16[4,32,160]{2,1,0:T(8,128)(2,1)S(1)}, bf16[4,32,160]{2,1,0:T(8,128)(2,1)S(1)}, u32[]{:S(2)}, u32[]{:S(2)}) collective-permute-start(bf16[4,32,160]{2,1,0:T(8,128)(2,1)S(1)} %copy-done.7), channel_id=1, source_target_pairs={{0,1},{2,3},{1,0},{3,2},{4,5},{6,7},{5,4},{7,6},{8,9},{10,11},{9,8... | collective-permute-start | bytes 122888 | tf_op jit(solution)/shard_map/ppermute | solution.py:678
  12.7 2.5 %collective-permute-start.1 = (bf16[4,32,160]{2,1,0:T(8,128)(2,1)S(1)}, bf16[4,32,160]{2,1,0:T(8,128)(2,1)S(1)}, u32[]{:S(2)}, u32[]{:S(2)}) collective-permute-start(bf16[4,32,160]{2,1,0:T(8,128)(2,1)S(1)} %copy-done.6), channel_id=1, source_target_pairs={{1,2},{3,0},{2,1},{0,3},{5,6},{7,4},{6,5},{4,7},{9,10},{11,8},{10,... | collective-permute-start | bytes 122888 | tf_op jit(solution)/shard_map/ppermute | solution.py:678
  16.5 2.4 %collective-permute-done.1.second_swap = bf16[4,32,160]{2,1,0:T(8,128)(2,1)S(1)} collective-permute-done((bf16[4,32,160]{2,1,0:T(8,128)(2,1)S(1)}, bf16[4,32,160]{2,1,0:T(8,128)(2,1)S(1)}, u32[]{:S(2)}, u32[]{:S(2)}) %collective-permute-start.1) | collective-permute-done | bytes 40992 | tf_op jit(solution)/shard_map/ppermute | solution.py:678
  20.0 1.4 %collective-permute-done.2.cross = bf16[4,104,256]{2,1,0:T(8,128)(2,1)S(1)} collective-permute-done((bf16[4,104,256]{2,1,0:T(8,128)(2,1)S(1)}, bf16[4,104,256]{2,1,0:T(8,128)(2,1)S(1)}, u32[]{:S(2)}, u32[]{:S(2)}) %collective-permute-start.2) | collective-permute-done | bytes 213024 | tf_op jit(solution)/shard_map/ppermute | solution.py:696
  21.4 1.9 %collective-permute-start.3 = (bf16[2,104,256]{2,1,0:T(8,128)(2,1)S(1)}, bf16[2,104,256]{2,1,0:T(8,128)(2,1)S(1)}, u32[]{:S(2)}, u32[]{:S(2)}) collective-permute-start(bf16[2,104,256]{2,1,0:T(8,128)(2,1)S(1)} %pad_maximum_fusion), channel_id=1, source_target_pairs={{0,8},{4,12},{8,0},{12,4},{16,24},{20,28},{24,16},{28,20},{1,9},{5... | collective-permute-start | bytes 319496 | tf_op jit(solution)/shard_map/ppermute | solution.py:696
  23.4 1.6 %collective-permute-start.4 = (bf16[2,104,256]{2,1,0:T(8,128)(2,1)S(1)}, bf16[2,104,256]{2,1,0:T(8,128)(2,1)S(1)}, u32[]{:S(2)}, u32[]{:S(2)}) collective-permute-start(bf16[2,104,256]{2,1,0:T(8,128)(2,1)S(1)} %pad_maximum_fusion.1), channel_id=1, source_target_pairs={{0,16},{4,20},{8,24},{12,28},{16,0},{20,4},{24,8},{28,12},{1,17},{... | collective-permute-start | bytes 319496 | tf_op jit(solution)/shard_map/ppermute | solution.py:696
  25.2 5.8 %all-to-all-done.far = bf16[8,360,256]{2,1,0:T(8,128)(2,1)} async-done(((bf16[8,360,256]{2,1,0:T(8,128)(2,1)}), bf16[8,360,256]{2,1,0:T(8,128)(2,1)}, u32[]{:S(2)}, u32[]{:S(2)}) %all-to-all-start) | async-done | bytes 1474592 | tf_op jit(solution)/shard_map/all_to_all | solution.py:704
  31.1 5.7 %spread.1 = (bf16[8,360,256]{2,1,0:T(8,128)(2,1)S(1)}, f32[2,2,512,128]{3,2,1,0:T(8,128)S(1)}) custom-call(s32[2,512]{1,0:T(2,128)S(1)} %get-tuple-element.77.cells, bf16[8,360,256]{2,1,0:T(8,128)(2,1)} %all-to-all-done.far), custom_call_target="tpu_custom_call" | custom-call | flops 1 | bytes 8388608 | tf_op jit(solution)/shard_map/spread/pallas_call | solution.py:792
  36.8 3.3 %observe.1 = (bf16[8,112,256]{2,1,0:T(8,128)(2,1)S(1)}, f32[2,144,256]{2,1,0:T(8,128)S(1)}, bf16[144,256]{1,0:T(8,128)(2,1)S(1)}, bf16[144,256]{1,0:T(8,128)(2,1)S(1)}) custom-call(s32[2,640]{1,0:T(2,128)S(1)} %pad.4.cells, s32[2,640]{1,0:T(2,128)S(1)} %fusion.3.outer, f32[2,512]{1,0:T(2,128)S(1)} %fusion.10.weight, f32[2,512]{1,0:T(2,128)S(1)} %bitcast.50, ...), custom_call_target="tpu_custom_call" | custom-call | tf_op jit(solution)/shard_map/observe/pallas_call | solution.py:809
  40.1 2.2 %collective-permute-start.6 = (bf16[144,256]{1,0:T(8,128)(2,1)S(1)}, bf16[144,256]{1,0:T(8,128)(2,1)S(1)}, u32[]{:S(2)}, u32[]{:S(2)}) collective-permute-start(bf16[144,256]{1,0:T(8,128)(2,1)S(1)} %get-tuple-element.48), channel_id=1, source_target_pairs={{0,1},{2,3},{1,0},{3,2},{4,5},{6,7},{5,4},{7,6},{8,9},{10,11},{9,8... | collective-permute-start | bytes 221192 | tf_op jit(solution)/shard_map/ppermute | solution.py:678
  42.2 2.4 %collective-permute-start.7 = (bf16[144,256]{1,0:T(8,128)(2,1)S(1)}, bf16[144,256]{1,0:T(8,128)(2,1)S(1)}, u32[]{:S(2)}, u32[]{:S(2)}) collective-permute-start(bf16[144,256]{1,0:T(8,128)(2,1)S(1)} %get-tuple-element.49), channel_id=1, source_target_pairs={{1,2},{3,0},{2,1},{0,3},{5,6},{7,4},{6,5},{4,7},{9,10},{11,8},{10,... | collective-permute-start | bytes 221192 | tf_op jit(solution)/shard_map/ppermute | solution.py:678
  45.4 3.0 %collective-permute-done.7.second_swap = bf16[144,256]{1,0:T(8,128)(2,1)S(1)} collective-permute-done((bf16[144,256]{1,0:T(8,128)(2,1)S(1)}, bf16[144,256]{1,0:T(8,128)(2,1)S(1)}, u32[]{:S(2)}, u32[]{:S(2)}) %collective-permute-start.7) | collective-permute-done | bytes 73760 | tf_op jit(solution)/shard_map/ppermute | solution.py:678
  49.3 1.7 %collective-permute-start.8 = (bf16[2,144,256]{2,1,0:T(8,128)(2,1)S(1)}, bf16[2,144,256]{2,1,0:T(8,128)(2,1)S(1)}, u32[]{:S(2)}, u32[]{:S(2)}) collective-permute-start(bf16[2,144,256]{2,1,0:T(8,128)(2,1)S(1)} %get-tuple-element.51), channel_id=1, source_target_pairs={{0,4},{8,12},{16,20},{24,28},{4,0},{12,8},{20,16},{28,24},{1,5},{9... | collective-permute-start | bytes 442376 | tf_op jit(solution)/shard_map/ppermute | solution.py:678
  52.0 6.1 %analyse.1 = (bf16[240,256]{1,0:T(8,128)(2,1)S(1)}, bf16[240,256]{1,0:T(8,128)(2,1)S(1)}, bf16[240,256]{1,0:T(8,128)(2,1)S(1)}, bf16[240,256]{1,0:T(8,128)(2,1)S...) custom-call(f32[2,144,256]{2,1,0:T(8,128)S(1)} %get-tuple-element.50, ...), custom_call_target="tpu_custom_call" | custom-call | tf_op jit(solution)/shard_map/analyse/pallas_call | solution.py:849
  58.1 4.9 %collective-permute-start.10 = (bf16[240,256]{1,0:T(8,128)(2,1)S(1)}, bf16[240,256]{1,0:T(8,128)(2,1)S(1)}, u32[]{:S(2)}, u32[]{:S(2)}) collective-permute-start(bf16[240,256]{1,0:T(8,128)(2,1)S(1)} %get-tuple-element.57), channel_id=1, source_target_pairs={{0,24},{4,28},{8,16},{12,20},{16,8},{20,12},{24,0},{28,4},{1,25},{... | collective-permute-start | bytes 368648 | tf_op jit(solution)/shard_map/ppermute | solution.py:696
  62.9 2.2 %collective-permute-start.19 = (bf16[240,256]{1,0:T(8,128)(2,1)S(1)}, bf16[240,256]{1,0:T(8,128)(2,1)S(1)}, u32[]{:S(2)}, u32[]{:S(2)}) collective-permute-start(bf16[240,256]{1,0:T(8,128)(2,1)S(1)} %get-tuple-element.71), channel_id=1, source_target_pairs={{0,8},{4,12},{8,0},{12,4},{16,24},{20,28},{24,16},{28,20},{1,9},{5... | collective-permute-start | bytes 368648 | tf_op jit(solution)/shard_map/ppermute | solution.py:696
  65.1 1.9 %collective-permute-start.21 = (bf16[240,256]{1,0:T(8,128)(2,1)S(1)}, bf16[240,256]{1,0:T(8,128)(2,1)S(1)}, u32[]{:S(2)}, u32[]{:S(2)}) collective-permute-start(bf16[240,256]{1,0:T(8,128)(2,1)S(1)} %get-tuple-element.73), channel_id=1, source_target_pairs={{0,12},{4,8},{8,4},{12,0},{16,28},{20,24},{24,20},{28,16},{1,13},{... | collective-permute-start | bytes 368648 | tf_op jit(solution)/shard_map/ppermute | solution.py:696
  67.1 2.5 %collective-permute-done.18.refs_1_ = bf16[240,256]{1,0:T(8,128)(2,1)S(1)} collective-permute-done((bf16[240,256]{1,0:T(8,128)(2,1)S(1)}, bf16[240,256]{1,0:T(8,128)(2,1)S(1)}, u32[]{:S(2)}, u32[]{:S(2)}) %collective-permute-start.18) | collective-permute-done | bytes 122912 | tf_op jit(solution)/shard_map/ppermute | solution.py:696
  70.1 2.0 %second.1 = (bf16[224,256]{1,0:T(8,128)(2,1)S(1)}, bf16[224,256]{1,0:T(8,128)(2,1)S(1)}, bf16[224,256]{1,0:T(8,128)(2,1)S(1)}, bf16[224,256]{1,0:T(8,128)(2,1)S(...) custom-call(bf16[2,256,256]{2,1,0:T(8,128)(2,1)S(1)} %get-tuple-elem, ...), custom_call_target="tpu_custom_call" | custom-call | flops 1 | bytes 6291456 | tf_op jit(solution)/shard_map/second/pallas_call | solution.py:859
  74.5 1.9 %collective-permute-start.13 = (bf16[224,256]{1,0:T(8,128)(2,1)S(1)}, bf16[224,256]{1,0:T(8,128)(2,1)S(1)}, u32[]{:S(2)}, u32[]{:S(2)}) collective-permute-start(bf16[224,256]{1,0:T(8,128)(2,1)S(1)} %get-tuple-element.63), channel_id=1, source_target_pairs={{0,8},{4,12},{8,0},{12,4},{16,24},{20,28},{24,16},{28,20},{1,9},{5... | collective-permute-start | bytes 344072 | tf_op jit(solution)/shard_map/ppermute | solution.py:696
  82.0 1.6 %first_return.1.refs_8_ = bf16[3,60,32,160]{3,2,1,0:T(8,128)(2,1)} custom-call(bf16[240,256]{1,0:T(8,128)(2,1)S(1)} %collective-permute-done.10.refs_0_, bf16[240,256]{1,0:T(8,128)(2,1)S(1)} %collective-permute-done.18.refs_1_, bf16[240,256]{1,0:T(8,128)(2,1)S(1)} %collective-permute-done.19.refs_2_, bf16[240,256]{1,0:T(8,128)(2,1)S(1)} %collective-permute-done.20.refs_3_, ...), custom_call_target="tpu_custom_call" | custom-call | flops 1 | bytes 4194304 | tf_op jit(solution)/shard_map/first_return/pallas_call | solution.py:869
  86.3 1.6 %second_return.1 = bf16[3,60,32,160]{3,2,1,0:T(8,128)(2,1)} custom-call(bf16[224,256]{1,0:T(8,128)(2,1)S(1)} %collective-permute-done.11.refs_0_, bf16[224,256]{1,0:T(8,128)(2,1)S(1)} %collective-permute-done.12.refs_1_, bf16[224,256]{1,0:T(8,128)(2,1)S(1)} %collective-permute-done.13.refs_2_, ...), custom_call_target="tpu_custom_call", output_to_operand_aliasing={{}: (8, {})} | custom-call | tf_op jit(solution)/shard_map/second_return/pallas_call | solution.py:883
  (68 shorter events, 16.6 us)
Async XLA Ops:
  5.1 25.9 %all-to-all-start = ((bf16[8,360,256]{2,1,0:T(8,128)(2,1)}), bf16[8,360,256]{2,1,0:T(8,128)(2,1)}, u32[]{:S(2)}, u32[]{:S(2)}) async-start(bf16[8,360,256]{2,1,0:T(8,128)(2,1)} %get-tuple-element.41), calls=%async_computation | async-start | bytes 2949120 | tf_op jit(solution)/shard_map/all_to_all | solution.py:704
  10.5 6.0 %collective-permute-start = (bf16[4,32,160]{2,1,0:T(8,128)(2,1)S(1)}, bf16[4,32,160]{2,1,0:T(8,128)(2,1)S(1)}, u32[]{:S(2)}, u32[]{:S(2)}) collective-permute-start(bf16[4,32,160]{2,1,0:T(8,128)(2,1)S(1)} %copy-done.7), channel_id=1, source_target_pairs={{0,1},{2,3},{1,0},{3,2},{4,5},{6,7},{5,4},{7,6},{8,9},{10,11},{9,8... | collective-permute-start | bytes 122888 | tf_op jit(solution)/shard_map/ppermute | solution.py:678
  12.7 6.2 %collective-permute-start.1 = (bf16[4,32,160]{2,1,0:T(8,128)(2,1)S(1)}, bf16[4,32,160]{2,1,0:T(8,128)(2,1)S(1)}, u32[]{:S(2)}, u32[]{:S(2)}) collective-permute-start(bf16[4,32,160]{2,1,0:T(8,128)(2,1)S(1)} %copy-done.6), channel_id=1, source_target_pairs={{1,2},{3,0},{2,1},{0,3},{5,6},{7,4},{6,5},{4,7},{9,10},{11,8},{10,... | collective-permute-start | bytes 122888 | tf_op jit(solution)/shard_map/ppermute | solution.py:678
  21.4 15.3 %collective-permute-start.3 = (bf16[2,104,256]{2,1,0:T(8,128)(2,1)S(1)}, bf16[2,104,256]{2,1,0:T(8,128)(2,1)S(1)}, u32[]{:S(2)}, u32[]{:S(2)}) collective-permute-start(bf16[2,104,256]{2,1,0:T(8,128)(2,1)S(1)} %pad_maximum_fusion), channel_id=1, source_target_pairs={{0,8},{4,12},{8,0},{12,4},{16,24},{20,28},{24,16},{28,20},{1,9},{5... | collective-permute-start | bytes 319496 | tf_op jit(solution)/shard_map/ppermute | solution.py:696
  23.4 13.4 %collective-permute-start.4 = (bf16[2,104,256]{2,1,0:T(8,128)(2,1)S(1)}, bf16[2,104,256]{2,1,0:T(8,128)(2,1)S(1)}, u32[]{:S(2)}, u32[]{:S(2)}) collective-permute-start(bf16[2,104,256]{2,1,0:T(8,128)(2,1)S(1)} %pad_maximum_fusion.1), channel_id=1, source_target_pairs={{0,16},{4,20},{8,24},{12,28},{16,0},{20,4},{24,8},{28,12},{1,17},{... | collective-permute-start | bytes 319496 | tf_op jit(solution)/shard_map/ppermute | solution.py:696
  24.9 11.9 %collective-permute-start.5 = (bf16[2,104,256]{2,1,0:T(8,128)(2,1)S(1)}, bf16[2,104,256]{2,1,0:T(8,128)(2,1)S(1)}, u32[]{:S(2)}, u32[]{:S(2)}) collective-permute-start(bf16[2,104,256]{2,1,0:T(8,128)(2,1)S(1)} %pad_maximum_fusion.2), channel_id=1, source_target_pairs={{0,24},{4,28},{8,16},{12,20},{16,8},{20,12},{24,0},{28,4},{1,25},{... | collective-permute-start | bytes 319496 | tf_op jit(solution)/shard_map/ppermute | solution.py:696
  40.1 5.3 %collective-permute-start.6 = (bf16[144,256]{1,0:T(8,128)(2,1)S(1)}, bf16[144,256]{1,0:T(8,128)(2,1)S(1)}, u32[]{:S(2)}, u32[]{:S(2)}) collective-permute-start(bf16[144,256]{1,0:T(8,128)(2,1)S(1)} %get-tuple-element.48), channel_id=1, source_target_pairs={{0,1},{2,3},{1,0},{3,2},{4,5},{6,7},{5,4},{7,6},{8,9},{10,11},{9,8... | collective-permute-start | bytes 221192 | tf_op jit(solution)/shard_map/ppermute | solution.py:678
  42.2 6.2 %collective-permute-start.7 = (bf16[144,256]{1,0:T(8,128)(2,1)S(1)}, bf16[144,256]{1,0:T(8,128)(2,1)S(1)}, u32[]{:S(2)}, u32[]{:S(2)}) collective-permute-start(bf16[144,256]{1,0:T(8,128)(2,1)S(1)} %get-tuple-element.49), channel_id=1, source_target_pairs={{1,2},{3,0},{2,1},{0,3},{5,6},{7,4},{6,5},{4,7},{9,10},{11,8},{10,... | collective-permute-start | bytes 221192 | tf_op jit(solution)/shard_map/ppermute | solution.py:678
  48.4 3.2 %collective-permute-start.9 = (bf16[2,144,256]{2,1,0:T(8,128)(2,1)S(1)}, bf16[2,144,256]{2,1,0:T(8,128)(2,1)S(1)}, u32[]{:S(2)}, u32[]{:S(2)}) collective-permute-start(bf16[2,144,256]{2,1,0:T(8,128)(2,1)S(1)} %get-tuple-element.51), channel_id=1, source_target_pairs={{4,8},{12,16},{20,24},{8,4},{16,12},{24,20},{5,9},{13,17},{21,25},... | collective-permute-start | bytes 442376 | tf_op jit(solution)/shard_map/ppermute | solution.py:678
  49.3 2.7 %collective-permute-start.8 = (bf16[2,144,256]{2,1,0:T(8,128)(2,1)S(1)}, bf16[2,144,256]{2,1,0:T(8,128)(2,1)S(1)}, u32[]{:S(2)}, u32[]{:S(2)}) collective-permute-start(bf16[2,144,256]{2,1,0:T(8,128)(2,1)S(1)} %get-tuple-element.51), channel_id=1, source_target_pairs={{0,4},{8,12},{16,20},{24,28},{4,0},{12,8},{20,16},{28,24},{1,5},{9... | collective-permute-start | bytes 442376 | tf_op jit(solution)/shard_map/ppermute | solution.py:678
  58.1 9.0 %collective-permute-start.10 = (bf16[240,256]{1,0:T(8,128)(2,1)S(1)}, bf16[240,256]{1,0:T(8,128)(2,1)S(1)}, u32[]{:S(2)}, u32[]{:S(2)}) collective-permute-start(bf16[240,256]{1,0:T(8,128)(2,1)S(1)} %get-tuple-element.57), channel_id=1, source_target_pairs={{0,24},{4,28},{8,16},{12,20},{16,8},{20,12},{24,0},{28,4},{1,25},{... | collective-permute-start | bytes 368648 | tf_op jit(solution)/shard_map/ppermute | solution.py:696
  62.9 6.6 %collective-permute-start.18 = (bf16[240,256]{1,0:T(8,128)(2,1)S(1)}, bf16[240,256]{1,0:T(8,128)(2,1)S(1)}, u32[]{:S(2)}, u32[]{:S(2)}) collective-permute-start(bf16[240,256]{1,0:T(8,128)(2,1)S(1)} %get-tuple-element.70), channel_id=1, source_target_pairs={{0,28},{4,24},{8,20},{12,16},{16,12},{20,8},{24,4},{28,0},{1,29},{... | collective-permute-start | bytes 368648 | tf_op jit(solution)/shard_map/ppermute | solution.py:696
  62.9 10.4 %collective-permute-start.19 = (bf16[240,256]{1,0:T(8,128)(2,1)S(1)}, bf16[240,256]{1,0:T(8,128)(2,1)S(1)}, u32[]{:S(2)}, u32[]{:S(2)}) collective-permute-start(bf16[240,256]{1,0:T(8,128)(2,1)S(1)} %get-tuple-element.71), channel_id=1, source_target_pairs={{0,8},{4,12},{8,0},{12,4},{16,24},{20,28},{24,16},{28,20},{1,9},{5... | collective-permute-start | bytes 368648 | tf_op jit(solution)/shard_map/ppermute | solution.py:696
  65.1 9.3 %collective-permute-start.20 = (bf16[240,256]{1,0:T(8,128)(2,1)S(1)}, bf16[240,256]{1,0:T(8,128)(2,1)S(1)}, u32[]{:S(2)}, u32[]{:S(2)}) collective-permute-start(bf16[240,256]{1,0:T(8,128)(2,1)S(1)} %get-tuple-element.72), channel_id=1, source_target_pairs={{0,16},{4,20},{8,24},{12,28},{16,0},{20,4},{24,8},{28,12},{1,17},{... | collective-permute-start | bytes 368648 | tf_op jit(solution)/shard_map/ppermute | solution.py:696
  65.1 9.3 %collective-permute-start.21 = (bf16[240,256]{1,0:T(8,128)(2,1)S(1)}, bf16[240,256]{1,0:T(8,128)(2,1)S(1)}, u32[]{:S(2)}, u32[]{:S(2)}) collective-permute-start(bf16[240,256]{1,0:T(8,128)(2,1)S(1)} %get-tuple-element.73), channel_id=1, source_target_pairs={{0,12},{4,8},{8,4},{12,0},{16,28},{20,24},{24,20},{28,16},{1,13},{... | collective-permute-start | bytes 368648 | tf_op jit(solution)/shard_map/ppermute | solution.py:696
  67.0 9.4 %collective-permute-start.22 = (bf16[240,256]{1,0:T(8,128)(2,1)S(1)}, bf16[240,256]{1,0:T(8,128)(2,1)S(1)}, u32[]{:S(2)}, u32[]{:S(2)}) collective-permute-start(bf16[240,256]{1,0:T(8,128)(2,1)S(1)} %get-tuple-element.74), channel_id=1, source_target_pairs={{0,20},{4,16},{8,28},{12,24},{16,4},{20,0},{24,12},{28,8},{1,21},{... | collective-permute-start | bytes 368648 | tf_op jit(solution)/shard_map/ppermute | solution.py:696
  69.5 7.8 %collective-permute-start.23 = (bf16[240,256]{1,0:T(8,128)(2,1)S(1)}, bf16[240,256]{1,0:T(8,128)(2,1)S(1)}, u32[]{:S(2)}, u32[]{:S(2)}) collective-permute-start(bf16[240,256]{1,0:T(8,128)(2,1)S(1)} %get-tuple-element.75), channel_id=1, source_target_pairs={{0,4},{4,0},{8,12},{12,8},{16,20},{20,16},{24,28},{28,24},{1,5},{5... | collective-permute-start | bytes 368648 | tf_op jit(solution)/shard_map/ppermute | solution.py:696
  73.3 6.5 %collective-permute-start.11 = (bf16[224,256]{1,0:T(8,128)(2,1)S(1)}, bf16[224,256]{1,0:T(8,128)(2,1)S(1)}, u32[]{:S(2)}, u32[]{:S(2)}) collective-permute-start(bf16[224,256]{1,0:T(8,128)(2,1)S(1)} %get-tuple-element.61), channel_id=1, source_target_pairs={{0,24},{4,28},{8,16},{12,20},{16,8},{20,12},{24,0},{28,4},{1,25},{... | collective-permute-start | bytes 344072 | tf_op jit(solution)/shard_map/ppermute | solution.py:696
  74.5 6.4 %collective-permute-start.12 = (bf16[224,256]{1,0:T(8,128)(2,1)S(1)}, bf16[224,256]{1,0:T(8,128)(2,1)S(1)}, u32[]{:S(2)}, u32[]{:S(2)}) collective-permute-start(bf16[224,256]{1,0:T(8,128)(2,1)S(1)} %get-tuple-element.62), channel_id=1, source_target_pairs={{0,28},{4,24},{8,20},{12,16},{16,12},{20,8},{24,4},{28,0},{1,29},{... | collective-permute-start | bytes 344072 | tf_op jit(solution)/shard_map/ppermute | solution.py:696
  74.5 10.4 %collective-permute-start.13 = (bf16[224,256]{1,0:T(8,128)(2,1)S(1)}, bf16[224,256]{1,0:T(8,128)(2,1)S(1)}, u32[]{:S(2)}, u32[]{:S(2)}) collective-permute-start(bf16[224,256]{1,0:T(8,128)(2,1)S(1)} %get-tuple-element.63), channel_id=1, source_target_pairs={{0,8},{4,12},{8,0},{12,4},{16,24},{20,28},{24,16},{28,20},{1,9},{5... | collective-permute-start | bytes 344072 | tf_op jit(solution)/shard_map/ppermute | solution.py:696
  76.4 8.4 %collective-permute-start.14 = (bf16[224,256]{1,0:T(8,128)(2,1)S(1)}, bf16[224,256]{1,0:T(8,128)(2,1)S(1)}, u32[]{:S(2)}, u32[]{:S(2)}) collective-permute-start(bf16[224,256]{1,0:T(8,128)(2,1)S(1)} %get-tuple-element.64), channel_id=1, source_target_pairs={{0,16},{4,20},{8,24},{12,28},{16,0},{20,4},{24,8},{28,12},{1,17},{... | collective-permute-start | bytes 344072 | tf_op jit(solution)/shard_map/ppermute | solution.py:696
  77.3 8.1 %collective-permute-start.15 = (bf16[224,256]{1,0:T(8,128)(2,1)S(1)}, bf16[224,256]{1,0:T(8,128)(2,1)S(1)}, u32[]{:S(2)}, u32[]{:S(2)}) collective-permute-start(bf16[224,256]{1,0:T(8,128)(2,1)S(1)} %get-tuple-element.65), channel_id=1, source_target_pairs={{0,12},{4,8},{8,4},{12,0},{16,28},{20,24},{24,20},{28,16},{1,13},{... | collective-permute-start | bytes 344072 | tf_op jit(solution)/shard_map/ppermute | solution.py:696
  79.8 6.5 %collective-permute-start.16 = (bf16[224,256]{1,0:T(8,128)(2,1)S(1)}, bf16[224,256]{1,0:T(8,128)(2,1)S(1)}, u32[]{:S(2)}, u32[]{:S(2)}) collective-permute-start(bf16[224,256]{1,0:T(8,128)(2,1)S(1)} %get-tuple-element.66), channel_id=1, source_target_pairs={{0,20},{4,16},{8,28},{12,24},{16,4},{20,0},{24,12},{28,8},{1,21},{... | collective-permute-start | bytes 344072 | tf_op jit(solution)/shard_map/ppermute | solution.py:696
  80.9 5.5 %collective-permute-start.17 = (bf16[224,256]{1,0:T(8,128)(2,1)S(1)}, bf16[224,256]{1,0:T(8,128)(2,1)S(1)}, u32[]{:S(2)}, u32[]{:S(2)}) collective-permute-start(bf16[224,256]{1,0:T(8,128)(2,1)S(1)} %get-tuple-element.67), channel_id=1, source_target_pairs={{0,4},{4,0},{8,12},{12,8},{16,20},{20,16},{24,28},{28,24},{1,5},{5... | collective-permute-start | bytes 344072 | tf_op jit(solution)/shard_map/ppermute | solution.py:696
  (9 other events, 101.7 us)

commit v10 on v8

--- a/solution.py
+++ b/solution.py
@@ -310,7 +310,7 @@
 
 
 def inner_kernel(
-    ens, depth, out, to_first, to_second, here, deep, flux, height, staged, edges, arrived
+    ens, depth, out, to_second, to_first, here, deep, flux, height, staged, half, edges, arrived
 ):
     columns, members, latitudes = here.shape[1:]
     batch = columns // 5
@@ -359,14 +359,24 @@
             for v, field in enumerate((height[at],) + new):
                 put_group(staged, field, eye, 20 * group_of(v, done))
             done += 1
+        if k == 2:
+            half[:, FIRST:INNER] = staged[:, FIRST:INNER].astype(BF16)
+            span = pl.ds(FIRST, INNER - FIRST)
+            leaving = pltpu.make_async_copy(half.at[:, span], out.at[:, span], arrived.at[6])
+            leaving.start()
     odd = lax.axis_index("band") & 1
     to_first[...] = edges[1 - odd]
     to_second[...] = edges[odd]
-    out[...] = staged[...].astype(BF16)
+    half[:, 0:FIRST] = staged[:, 0:FIRST].astype(BF16)
+    span = pl.ds(0, FIRST)
+    last = pltpu.make_async_copy(half.at[:, span], out.at[:, span], arrived.at[7])
+    last.start()
+    leaving.wait()
+    last.wait()
 
 
 def outer_kernel(
-    west_block, east_block, first_swap, second_swap, depth, *refs
+    west_block, east_block, second_swap, first_swap, depth, *refs
 ):
     straight, cross, flux, height, staged, swapped = refs
     odd = lax.axis_index("band") & 1
@@ -430,7 +440,7 @@
         cross[k] = staged[me ^ d ^ 1].astype(BF16)
 
 
-def spread_block(source, held, wide, start, lane):
+def spread_block(source, wide, start, lane):
     spans = [slice(h * LANES, (h + 1) * LANES) for h in range(2)]
     count = source.shape[1]
     here = pl.ds(start, 16)
@@ -439,18 +449,17 @@
         to = pl.ds(pl.multiple_of(q * count + start, 8), 16)
         for h in range(2):
             wide[h, to, :] = blocks[q][h].astype(F32)
-            held[q, here, spans[h]] = blocks[q][h]
-
-
-def spread_kernel(cells, got, held, seen, wide):
+
+
+def spread_kernel(cells, got, wide, seen):
     lane = lax.broadcasted_iota(jnp.int32, (16, LANES), 1)
 
     def step(index, carry):
-        spread_block(got, held, wide, pl.multiple_of(index * 16, 16), lane)
+        spread_block(got, wide, pl.multiple_of(index * 16, 16), lane)
         return carry
 
     lax.fori_loop(0, 22, step, 0, unroll=4)
-    spread_block(got, held, wide, INNER - 16, lane)
+    spread_block(got, wide, INNER - 16, lane)
     slots = seen.shape[2]
     unroll = 16
 
@@ -467,7 +476,7 @@
 
 
 def observe_kernel(cells, outer, weight, target, first, straight, cross, *refs):
-    edges, (held, gram, to_first, to_second, joined, wide, seen) = refs[:3], refs[3:]
+    edges, (wide, gram, to_second, to_first, joined, seen) = refs[:3], refs[3:]
     wholes = []
     lane = lax.broadcasted_iota(jnp.int32, (16, LANES), 1)
     me = lax.axis_index("mem")
@@ -476,7 +485,7 @@
         joined[me ^ d ^ 1, 0:OUTER, :] = cross[0] if k == 0 else edges[k - 1][1]
     joined[:, OUTER:BLOCK, :] = jnp.zeros((8, BLOCK - OUTER, 256), BF16)
     for index in range(BLOCK // 16):
-        spread_block(joined, held, wide, index * 16, lane)
+        spread_block(joined, wide, index * 16, lane)
     slots = first.shape[2]
     seen[:, :, 0:slots, :] = first[...]
     for t in range(2):
@@ -508,7 +517,7 @@
     to_second[...] = jnp.where(odd, wholes[1], wholes[0])
 
 
-def combine_kernel(gram, first_swap, second_swap, line, short):
+def combine_kernel(gram, second_swap, first_swap, line, short):
     odd = (lax.axis_index("band") & 1) == 1
     first, second = first_swap[...].astype(F32), second_swap[...].astype(F32)
     west, east = jnp.where(odd, first, second), jnp.where(odd, second, first)
@@ -521,12 +530,15 @@
 def prepare_kernel(inner, outer, *refs):
     average = jnp.full((256, LANES), 1.0 / 256, BF16)
     for q in range(8):
-        pieces = (inner[q, 0:FIRST], jnp.concatenate([inner[q, FIRST:INNER], outer[q, 0:OUTER]], axis=0))
+        cells = [inner[h, q * INNER : (q + 1) * INNER, :] for h in range(2)]
+        rest = [outer[h, q * BLOCK : q * BLOCK + OUTER, :] for h in range(2)]
+        cells, rest = jnp.concatenate(cells, axis=1), jnp.concatenate(rest, axis=1)
+        pieces = (cells[0:FIRST], jnp.concatenate([cells[FIRST:INNER], rest], axis=0))
         for k, piece in enumerate(pieces):
-            mean = dot_nn(piece, average)
+            mean = dot_nn(piece.astype(BF16), average)
             refs[2 * k + 1][q] = mean
             mean = jnp.concatenate([mean, mean], axis=1)
-            refs[2 * k][q] = (piece.astype(F32) - mean).astype(BF16)
+            refs[2 * k][q] = (piece - mean).astype(BF16)
 
 
 def send_back(results, outs):
@@ -675,7 +687,7 @@
     count = lax.axis_size("band")
     starts = range(0, count, 2)
     pairs = [[(i, i + 1) for i in starts], [(i + 1, (i + 2) % count) for i in starts]]
-    return swapped_pairs((first, second), "band", pairs)
+    return swapped_pairs((second, first), "band", pairs[::-1])[::-1]
 
 
 def mem_swaps(value):
@@ -721,18 +733,21 @@
     planes = jnp.transpose(ensemble, (1, 2, 0, 3))
     edge = jax.ShapeDtypeStruct((4, members, latitudes), BF16)
     far = pl.BlockSpec(memory_space=pltpu.HBM)
-    sent, to_first, to_second = pl.pallas_call(
+    vmem = pl.BlockSpec(memory_space=pltpu.VMEM)
+    sent, to_second, to_first = pl.pallas_call(
         inner_kernel,
         out_shape=(jax.ShapeDtypeStruct((8, INNER, 256), BF16), edge, edge),
         in_specs=[far, far],
+        out_specs=(far, vmem, vmem),
         scratch_shapes=[
             pltpu.VMEM(planes.shape, BF16),
             pltpu.VMEM((columns, latitudes), F32),
             pltpu.VMEM((columns, members, latitudes), F32),
             pltpu.VMEM((columns, members, latitudes), BF16),
             pltpu.VMEM((8, INNER, 256), F32),
+            pltpu.VMEM((8, INNER, 256), BF16),
             pltpu.VMEM((2, 4, members, latitudes), BF16),
-            pltpu.SemaphoreType.DMA((6,)),
+            pltpu.SemaphoreType.DMA((8,)),
         ],
         compiler_params=params(60),
         name="inner",
@@ -760,7 +775,7 @@
         ],
         compiler_params=params(24),
         name="outer",
-    )(planes, planes, *swaps, layer_depth)
+    )(planes, planes, *swaps[::-1], layer_depth)
     cross = across(cross, 1)
     got_edges = [across(jnp.stack([straight[k], cross[k]]), CHIPS[k]) for k in (3, 1, 2)]
     got_edges = got_edges[1:] + got_edges[:1]
@@ -768,7 +783,6 @@
     rows = cell_rows(observed_cell[0])
     live = jnp.arange(slots, dtype=jnp.int32)[None, :] < observed_count[0][:, None]
     root = jnp.sqrt(jnp.where(live, 1.0 / error_variance[0], 0.0))
-    vmem = pl.BlockSpec(memory_space=pltpu.VMEM)
     slot = jnp.arange(slots, dtype=jnp.int32)
     place = jnp.arange(slots + LANES, dtype=jnp.int32)
     is_outer = rows >= 8 * INNER
@@ -784,20 +798,19 @@
     held_inner, seen = pl.pallas_call(
         spread_kernel,
         out_shape=(
-            jax.ShapeDtypeStruct((8, INNER, 256), BF16),
+            jax.ShapeDtypeStruct((2, 8 * INNER, LANES), F32),
             jax.ShapeDtypeStruct((2, 2, slots, LANES), F32),
         ),
         in_specs=[smem, vmem],
-        scratch_shapes=[pltpu.VMEM((2, 8 * INNER, LANES), F32)],
         compiler_params=params(12),
         cost_estimate=cost(1, 8 * MIB),
         name="spread",
     )(near, got)
     one_tile = jax.ShapeDtypeStruct((PACKED, 256), BF16)
-    held_outer, gram, to_first, to_second = pl.pallas_call(
+    held_outer, gram, to_second, to_first = pl.pallas_call(
         observe_kernel,
         out_shape=(
-            jax.ShapeDtypeStruct((8, BLOCK, 256), BF16),
+            jax.ShapeDtypeStruct((2, 8 * BLOCK, LANES), F32),
             jax.ShapeDtypeStruct((2, PACKED, 256), F32),
             one_tile,
             one_tile,
@@ -805,7 +818,6 @@
         in_specs=[smem, smem] + [vmem] * 8,
         scratch_shapes=[
             pltpu.VMEM((8, BLOCK, 256), BF16),
-            pltpu.VMEM((2, 8 * BLOCK, LANES), F32),
             pltpu.VMEM((2, 2, slots + 8, LANES), F32),
         ],
         compiler_params=params(16),
@@ -832,7 +844,7 @@
         ),
         compiler_params=params(8),
         name="combine",
-    )(gram, *band_swaps(to_first, to_second))
+    )(gram, *band_swaps(to_first, to_second)[::-1])
     below, above = mem_swaps(short)
     *back, maps = pl.pallas_call(
         analyse_kernel,

time: 88.1 us -> 88.6 us (level)
    ppermute x6, waiting for transfers between devices: 6.42 us -> 7.62 us  [swapped_pairs(): moved.append(lax.ppermute(value, axis, both))]
    ppermute x6, starting transfers between devices: 11.8 us -> 10.7 us  [swapped_pairs(): moved.append(lax.ppermute(value, axis, both))]
  transfers between devices with their start and end apart: 25 -> 25, of which waited for: 11 -> 13; matrix products, arithmetic and copies ran while one was open for 2% -> 2% of each run, Pallas kernels for 12% -> 12%
where the time goes in v10:
time: 88.6 us; the launch traced here: 88.4 us
  starting transfers between devices  36.7 us (41%)
  Pallas kernels  27.3 us (31%)
  waiting for transfers between devices  22.5 us (25%)
  other arithmetic  1.43 us (2%)
    ppermute x18, starting transfers between devices, across(): return lax.ppermute(value, 'mem', [(i, i ^ difference) for i in range(8)])  20.7 us
    ppermute x6, starting transfers between devices, swapped_pairs(): moved.append(lax.ppermute(value, axis, both))  10.7 us
    ppermute x18, waiting for transfers between devices, across(): return lax.ppermute(value, 'mem', [(i, i ^ difference) for i in range(8)])  9.14 us
    ppermute x6, waiting for transfers between devices, swapped_pairs(): moved.append(lax.ppermute(value, axis, both))  7.62 us
    pallas_call x1, Pallas kernels, on_device_fast(): pl.pallas_call(analyse_kernel, out_shape=(jax.ShapeDtypeStruct((FIRST, 25...  6.06 us
    all_to_all x1, waiting for transfers between devices, swap(): return lax.all_to_all(value, 'mem', split_axis=0, concat_axis=0, tiled=True)  5.74 us
    pallas_call x1, Pallas kernels, on_device_fast(): pl.pallas_call(inner_kernel, out_shape=(jax.ShapeDtypeStruct((8, INNER, 2...  5.63 us
    pallas_call x1, Pallas kernels, on_device_fast(): pl.pallas_call(spread_kernel, out_shape=(jax.ShapeDtypeStruct((2, 8 * INN...  5.42 us
  transfers between devices with their start and end apart: 25, of which 13 were waited for; matrix products, arithmetic and copies ran while one was open for 2% of the time, Pallas kernels for 12%

profile of v10, /device:TPU:0, one launch (start us, length us, event | category | flops | bytes accessed | tf_op | source)
XLA Modules:
  0.0 88.4 jit_solution(17587687247970197774)
XLA Ops:
  0.0 5.6 %inner.1 = (bf16[8,360,256]{2,1,0:T(8,128)(2,1)}, bf16[4,32,160]{2,1,0:T(8,128)(2,1)}, bf16[4,32,160]{2,1,0:T(8,128)(2,1)}) custom-call(bf16[3,60,32,160]{3,2,1,0:T(8,128)(2,1)} %bitcast.47, f32[60,160]{1,0:T(8,128)} %depth.3), custom_call_target="tpu_custom_call" | custom-call | tf_op jit(solution)/shard_map/inner/pallas_call | solution.py:737
  5.7 5.3 %all-to-all-start = ((bf16[8,360,256]{2,1,0:T(8,128)(2,1)}), bf16[8,360,256]{2,1,0:T(8,128)(2,1)}, u32[]{:S(2)}, u32[]{:S(2)}) async-start(bf16[8,360,256]{2,1,0:T(8,128)(2,1)} %get-tuple-element.41), calls=%async_computation | async-start | bytes 2949120 | tf_op jit(solution)/shard_map/all_to_all | solution.py:708
  11.0 4.2 %collective-permute-start = (bf16[4,32,160]{2,1,0:T(8,128)(2,1)S(1)}, bf16[4,32,160]{2,1,0:T(8,128)(2,1)S(1)}, u32[]{:S(2)}, u32[]{:S(2)}) collective-permute-start(bf16[4,32,160]{2,1,0:T(8,128)(2,1)S(1)} %copy-done.7), channel_id=1, source_target_pairs={{1,2},{3,0},{2,1},{0,3},{5,6},{7,4},{6,5},{4,7},{9,10},{11,8},{10,... | collective-permute-start | bytes 122888 | tf_op jit(solution)/shard_map/ppermute | solution.py:682
  16.6 1.6 %collective-permute-done.second_swap = bf16[4,32,160]{2,1,0:T(8,128)(2,1)S(1)} collective-permute-done((bf16[4,32,160]{2,1,0:T(8,128)(2,1)S(1)}, bf16[4,32,160]{2,1,0:T(8,128)(2,1)S(1)}, u32[]{:S(2)}, u32[]{:S(2)}) %collective-permute-start) | collective-permute-done | bytes 40992 | tf_op jit(solution)/shard_map/ppermute | solution.py:682
  22.0 1.9 %collective-permute-start.3 = (bf16[2,104,256]{2,1,0:T(8,128)(2,1)S(1)}, bf16[2,104,256]{2,1,0:T(8,128)(2,1)S(1)}, u32[]{:S(2)}, u32[]{:S(2)}) collective-permute-start(bf16[2,104,256]{2,1,0:T(8,128)(2,1)S(1)} %pad_maximum_fusion), channel_id=1, source_target_pairs={{0,8},{4,12},{8,0},{12,4},{16,24},{20,28},{24,16},{28,20},{1,9},{5... | collective-permute-start | bytes 319496 | tf_op jit(solution)/shard_map/ppermute | solution.py:700
  23.9 1.6 %collective-permute-start.4 = (bf16[2,104,256]{2,1,0:T(8,128)(2,1)S(1)}, bf16[2,104,256]{2,1,0:T(8,128)(2,1)S(1)}, u32[]{:S(2)}, u32[]{:S(2)}) collective-permute-start(bf16[2,104,256]{2,1,0:T(8,128)(2,1)S(1)} %pad_maximum_fusion.1), channel_id=1, source_target_pairs={{0,16},{4,20},{8,24},{12,28},{16,0},{20,4},{24,8},{28,12},{1,17},{... | collective-permute-start | bytes 319496 | tf_op jit(solution)/shard_map/ppermute | solution.py:700
  25.8 5.7 %all-to-all-done.got = bf16[8,360,256]{2,1,0:T(8,128)(2,1)} async-done(((bf16[8,360,256]{2,1,0:T(8,128)(2,1)}), bf16[8,360,256]{2,1,0:T(8,128)(2,1)}, u32[]{:S(2)}, u32[]{:S(2)}) %all-to-all-start) | async-done | bytes 1474592 | tf_op jit(solution)/shard_map/all_to_all | solution.py:708
  31.6 5.4 %spread.1 = (f32[2,2880,128]{2,1,0:T(8,128)S(1)}, f32[2,2,512,128]{3,2,1,0:T(8,128)S(1)}) custom-call(s32[2,512]{1,0:T(2,128)S(1)} %get-tuple-element.77.cells, bf16[8,360,256]{2,1,0:T(8,128)(2,1)} %all-to-all-done.got), custom_call_target="tpu_custom_call" | custom-call | flops 1 | bytes 8388608 | tf_op jit(solution)/shard_map/spread/pallas_call | solution.py:798
  37.0 3.3 %observe.1 = (f32[2,896,128]{2,1,0:T(8,128)S(1)}, f32[2,144,256]{2,1,0:T(8,128)S(1)}, bf16[144,256]{1,0:T(8,128)(2,1)S(1)}, bf16[144,256]{1,0:T(8,128)(2,1)S(1)}) custom-call(s32[2,640]{1,0:T(2,128)S(1)} %pad.4.cells, s32[2,640]{1,0:T(2,128)S(1)} %fusion.3.outer, f32[2,512]{1,0:T(2,128)S(1)} %fusion.10.weight, f32[2,512]{1,0:T(2,128)S(1)} %bitcast.50, ...), custom_call_target="tpu_custom_call" | custom-call | tf_op jit(solution)/shard_map/observe/pallas_call | solution.py:810
  40.3 4.1 %collective-permute-start.6 = (bf16[144,256]{1,0:T(8,128)(2,1)S(1)}, bf16[144,256]{1,0:T(8,128)(2,1)S(1)}, u32[]{:S(2)}, u32[]{:S(2)}) collective-permute-start(bf16[144,256]{1,0:T(8,128)(2,1)S(1)} %get-tuple-element.48), channel_id=1, source_target_pairs={{1,2},{3,0},{2,1},{0,3},{5,6},{7,4},{6,5},{4,7},{9,10},{11,8},{10,... | collective-permute-start | bytes 221192 | tf_op jit(solution)/shard_map/ppermute | solution.py:682
  44.5 2.4 %collective-permute-done.6.second_swap = bf16[144,256]{1,0:T(8,128)(2,1)S(1)} collective-permute-done((bf16[144,256]{1,0:T(8,128)(2,1)S(1)}, bf16[144,256]{1,0:T(8,128)(2,1)S(1)}, u32[]{:S(2)}, u32[]{:S(2)}) %collective-permute-start.6) | collective-permute-done | bytes 73760 | tf_op jit(solution)/shard_map/ppermute | solution.py:682
  46.9 1.9 %collective-permute-done.7.first_swap = bf16[144,256]{1,0:T(8,128)(2,1)S(1)} collective-permute-done((bf16[144,256]{1,0:T(8,128)(2,1)S(1)}, bf16[144,256]{1,0:T(8,128)(2,1)S(1)}, u32[]{:S(2)}, u32[]{:S(2)}) %collective-permute-start.7) | collective-permute-done | bytes 73760 | tf_op jit(solution)/shard_map/ppermute | solution.py:682
  52.2 6.1 %analyse.1 = (bf16[240,256]{1,0:T(8,128)(2,1)S(1)}, bf16[240,256]{1,0:T(8,128)(2,1)S(1)}, bf16[240,256]{1,0:T(8,128)(2,1)S(1)}, bf16[240,256]{1,0:T(8,128)(2,1)S...) custom-call(f32[2,144,256]{2,1,0:T(8,128)S(1)} %get-tuple-element.50, ...), custom_call_target="tpu_custom_call" | custom-call | tf_op jit(solution)/shard_map/analyse/pallas_call | solution.py:849
  58.3 1.8 %collective-permute-start.10 = (bf16[240,256]{1,0:T(8,128)(2,1)S(1)}, bf16[240,256]{1,0:T(8,128)(2,1)S(1)}, u32[]{:S(2)}, u32[]{:S(2)}) collective-permute-start(bf16[240,256]{1,0:T(8,128)(2,1)S(1)} %get-tuple-element.57), channel_id=1, source_target_pairs={{0,4},{4,0},{8,12},{12,8},{16,20},{20,16},{24,28},{28,24},{1,5},{5... | collective-permute-start | bytes 368648 | tf_op jit(solution)/shard_map/ppermute | solution.py:700
  60.1 3.6 %collective-permute-start.18 = (bf16[240,256]{1,0:T(8,128)(2,1)S(1)}, bf16[240,256]{1,0:T(8,128)(2,1)S(1)}, u32[]{:S(2)}, u32[]{:S(2)}) collective-permute-start(bf16[240,256]{1,0:T(8,128)(2,1)S(1)} %get-tuple-element.69), channel_id=1, source_target_pairs={{0,24},{4,28},{8,16},{12,20},{16,8},{20,12},{24,0},{28,4},{1,25},{... | collective-permute-start | bytes 368648 | tf_op jit(solution)/shard_map/ppermute | solution.py:700
  64.9 1.5 %collective-permute-start.21 = (bf16[240,256]{1,0:T(8,128)(2,1)S(1)}, bf16[240,256]{1,0:T(8,128)(2,1)S(1)}, u32[]{:S(2)}, u32[]{:S(2)}) collective-permute-start(bf16[240,256]{1,0:T(8,128)(2,1)S(1)} %get-tuple-element.72), channel_id=1, source_target_pairs={{0,28},{4,24},{8,20},{12,16},{16,12},{20,8},{24,4},{28,0},{1,29},{... | collective-permute-start | bytes 368648 | tf_op jit(solution)/shard_map/ppermute | solution.py:700
  66.4 1.5 %collective-permute-start.22 = (bf16[240,256]{1,0:T(8,128)(2,1)S(1)}, bf16[240,256]{1,0:T(8,128)(2,1)S(1)}, u32[]{:S(2)}, u32[]{:S(2)}) collective-permute-start(bf16[240,256]{1,0:T(8,128)(2,1)S(1)} %get-tuple-element.74), channel_id=1, source_target_pairs={{0,12},{4,8},{8,4},{12,0},{16,28},{20,24},{24,20},{28,16},{1,13},{... | collective-permute-start | bytes 368648 | tf_op jit(solution)/shard_map/ppermute | solution.py:700
  69.1 2.0 %second.1 = (bf16[224,256]{1,0:T(8,128)(2,1)S(1)}, bf16[224,256]{1,0:T(8,128)(2,1)S(1)}, bf16[224,256]{1,0:T(8,128)(2,1)S(1)}, bf16[224,256]{1,0:T(8,128)(2,1)S(...) custom-call(bf16[2,256,256]{2,1,0:T(8,128)(2,1)S(1)} %get-tuple-elem, ...), custom_call_target="tpu_custom_call" | custom-call | flops 1 | bytes 6291456 | tf_op jit(solution)/shard_map/second/pallas_call | solution.py:859
  71.5 1.7 %collective-permute-start.11 = (bf16[224,256]{1,0:T(8,128)(2,1)S(1)}, bf16[224,256]{1,0:T(8,128)(2,1)S(1)}, u32[]{:S(2)}, u32[]{:S(2)}) collective-permute-start(bf16[224,256]{1,0:T(8,128)(2,1)S(1)} %get-tuple-element.61), channel_id=1, source_target_pairs={{0,24},{4,28},{8,16},{12,20},{16,8},{20,12},{24,0},{28,4},{1,25},{... | collective-permute-start | bytes 344072 | tf_op jit(solution)/shard_map/ppermute | solution.py:700
  75.9 1.9 %collective-permute-start.14 = (bf16[224,256]{1,0:T(8,128)(2,1)S(1)}, bf16[224,256]{1,0:T(8,128)(2,1)S(1)}, u32[]{:S(2)}, u32[]{:S(2)}) collective-permute-start(bf16[224,256]{1,0:T(8,128)(2,1)S(1)} %get-tuple-element.64), channel_id=1, source_target_pairs={{0,28},{4,24},{8,20},{12,16},{16,12},{20,8},{24,4},{28,0},{1,29},{... | collective-permute-start | bytes 344072 | tf_op jit(solution)/shard_map/ppermute | solution.py:700
  79.2 2.5 %collective-permute-done.12.refs_1_ = bf16[224,256]{1,0:T(8,128)(2,1)S(1)} collective-permute-done((bf16[224,256]{1,0:T(8,128)(2,1)S(1)}, bf16[224,256]{1,0:T(8,128)(2,1)S(1)}, u32[]{:S(2)}, u32[]{:S(2)}) %collective-permute-start.12) | collective-permute-done | bytes 114720 | tf_op jit(solution)/shard_map/ppermute | solution.py:700
  81.7 1.6 %first_return.1.refs_8_ = bf16[3,60,32,160]{3,2,1,0:T(8,128)(2,1)} custom-call(bf16[240,256]{1,0:T(8,128)(2,1)S(1)} %collective-permute-done.18.refs_0_, bf16[240,256]{1,0:T(8,128)(2,1)S(1)} %collective-permute-done.19.refs_1_, bf16[240,256]{1,0:T(8,128)(2,1)S(1)} %collective-permute-done.20.refs_2_, bf16[240,256]{1,0:T(8,128)(2,1)S(1)} %collective-permute-done.21.refs_3_, ...), custom_call_target="tpu_custom_call" | custom-call | flops 1 | bytes 4194304 | tf_op jit(solution)/shard_map/first_return/pallas_call | solution.py:869
  83.4 2.3 %collective-permute-done.16.refs_5_ = bf16[224,256]{1,0:T(8,128)(2,1)S(1)} collective-permute-done((bf16[224,256]{1,0:T(8,128)(2,1)S(1)}, bf16[224,256]{1,0:T(8,128)(2,1)S(1)}, u32[]{:S(2)}, u32[]{:S(2)}) %collective-permute-start.16) | collective-permute-done | bytes 114720 | tf_op jit(solution)/shard_map/ppermute | solution.py:700
  86.6 1.6 %second_return.1 = bf16[3,60,32,160]{3,2,1,0:T(8,128)(2,1)} custom-call(bf16[224,256]{1,0:T(8,128)(2,1)S(1)} %collective-permute-done.11.refs_0_, bf16[224,256]{1,0:T(8,128)(2,1)S(1)} %collective-permute-done.12.refs_1_, bf16[224,256]{1,0:T(8,128)(2,1)S(1)} %collective-permute-done.13.refs_2_, ...), custom_call_target="tpu_custom_call", output_to_operand_aliasing={{}: (8, {})} | custom-call | tf_op jit(solution)/shard_map/second_return/pallas_call | solution.py:883
  (68 shorter events, 16.7 us)
Async XLA Ops:
  5.7 25.9 %all-to-all-start = ((bf16[8,360,256]{2,1,0:T(8,128)(2,1)}), bf16[8,360,256]{2,1,0:T(8,128)(2,1)}, u32[]{:S(2)}, u32[]{:S(2)}) async-start(bf16[8,360,256]{2,1,0:T(8,128)(2,1)} %get-tuple-element.41), calls=%async_computation | async-start | bytes 2949120 | tf_op jit(solution)/shard_map/all_to_all | solution.py:708
  11.0 7.1 %collective-permute-start = (bf16[4,32,160]{2,1,0:T(8,128)(2,1)S(1)}, bf16[4,32,160]{2,1,0:T(8,128)(2,1)S(1)}, u32[]{:S(2)}, u32[]{:S(2)}) collective-permute-start(bf16[4,32,160]{2,1,0:T(8,128)(2,1)S(1)} %copy-done.7), channel_id=1, source_target_pairs={{1,2},{3,0},{2,1},{0,3},{5,6},{7,4},{6,5},{4,7},{9,10},{11,8},{10,... | collective-permute-start | bytes 122888 | tf_op jit(solution)/shard_map/ppermute | solution.py:682
  15.2 4.3 %collective-permute-start.1 = (bf16[4,32,160]{2,1,0:T(8,128)(2,1)S(1)}, bf16[4,32,160]{2,1,0:T(8,128)(2,1)S(1)}, u32[]{:S(2)}, u32[]{:S(2)}) collective-permute-start(bf16[4,32,160]{2,1,0:T(8,128)(2,1)S(1)} %copy-done.6), channel_id=1, source_target_pairs={{0,1},{2,3},{1,0},{3,2},{4,5},{6,7},{5,4},{7,6},{8,9},{10,11},{9,8... | collective-permute-start | bytes 122888 | tf_op jit(solution)/shard_map/ppermute | solution.py:682
  22.0 15.0 %collective-permute-start.3 = (bf16[2,104,256]{2,1,0:T(8,128)(2,1)S(1)}, bf16[2,104,256]{2,1,0:T(8,128)(2,1)S(1)}, u32[]{:S(2)}, u32[]{:S(2)}) collective-permute-start(bf16[2,104,256]{2,1,0:T(8,128)(2,1)S(1)} %pad_maximum_fusion), channel_id=1, source_target_pairs={{0,8},{4,12},{8,0},{12,4},{16,24},{20,28},{24,16},{28,20},{1,9},{5... | collective-permute-start | bytes 319496 | tf_op jit(solution)/shard_map/ppermute | solution.py:700
  23.9 13.1 %collective-permute-start.4 = (bf16[2,104,256]{2,1,0:T(8,128)(2,1)S(1)}, bf16[2,104,256]{2,1,0:T(8,128)(2,1)S(1)}, u32[]{:S(2)}, u32[]{:S(2)}) collective-permute-start(bf16[2,104,256]{2,1,0:T(8,128)(2,1)S(1)} %pad_maximum_fusion.1), channel_id=1, source_target_pairs={{0,16},{4,20},{8,24},{12,28},{16,0},{20,4},{24,8},{28,12},{1,17},{... | collective-permute-start | bytes 319496 | tf_op jit(solution)/shard_map/ppermute | solution.py:700
  25.5 11.5 %collective-permute-start.5 = (bf16[2,104,256]{2,1,0:T(8,128)(2,1)S(1)}, bf16[2,104,256]{2,1,0:T(8,128)(2,1)S(1)}, u32[]{:S(2)}, u32[]{:S(2)}) collective-permute-start(bf16[2,104,256]{2,1,0:T(8,128)(2,1)S(1)} %pad_maximum_fusion.2), channel_id=1, source_target_pairs={{0,24},{4,28},{8,16},{12,20},{16,8},{20,12},{24,0},{28,4},{1,25},{... | collective-permute-start | bytes 319496 | tf_op jit(solution)/shard_map/ppermute | solution.py:700
  40.3 6.6 %collective-permute-start.6 = (bf16[144,256]{1,0:T(8,128)(2,1)S(1)}, bf16[144,256]{1,0:T(8,128)(2,1)S(1)}, u32[]{:S(2)}, u32[]{:S(2)}) collective-permute-start(bf16[144,256]{1,0:T(8,128)(2,1)S(1)} %get-tuple-element.48), channel_id=1, source_target_pairs={{1,2},{3,0},{2,1},{0,3},{5,6},{7,4},{6,5},{4,7},{9,10},{11,8},{10,... | collective-permute-start | bytes 221192 | tf_op jit(solution)/shard_map/ppermute | solution.py:682
  44.5 4.4 %collective-permute-start.7 = (bf16[144,256]{1,0:T(8,128)(2,1)S(1)}, bf16[144,256]{1,0:T(8,128)(2,1)S(1)}, u32[]{:S(2)}, u32[]{:S(2)}) collective-permute-start(bf16[144,256]{1,0:T(8,128)(2,1)S(1)} %get-tuple-element.49), channel_id=1, source_target_pairs={{0,1},{2,3},{1,0},{3,2},{4,5},{6,7},{5,4},{7,6},{8,9},{10,11},{9,8... | collective-permute-start | bytes 221192 | tf_op jit(solution)/shard_map/ppermute | solution.py:682
  48.9 3.0 %collective-permute-start.9 = (bf16[2,144,256]{2,1,0:T(8,128)(2,1)S(1)}, bf16[2,144,256]{2,1,0:T(8,128)(2,1)S(1)}, u32[]{:S(2)}, u32[]{:S(2)}) collective-permute-start(bf16[2,144,256]{2,1,0:T(8,128)(2,1)S(1)} %get-tuple-element.51), channel_id=1, source_target_pairs={{4,8},{12,16},{20,24},{8,4},{16,12},{24,20},{5,9},{13,17},{21,25},... | collective-permute-start | bytes 442376 | tf_op jit(solution)/shard_map/ppermute | solution.py:682
  49.7 2.5 %collective-permute-start.8 = (bf16[2,144,256]{2,1,0:T(8,128)(2,1)S(1)}, bf16[2,144,256]{2,1,0:T(8,128)(2,1)S(1)}, u32[]{:S(2)}, u32[]{:S(2)}) collective-permute-start(bf16[2,144,256]{2,1,0:T(8,128)(2,1)S(1)} %get-tuple-element.51), channel_id=1, source_target_pairs={{0,4},{8,12},{16,20},{24,28},{4,0},{12,8},{20,16},{28,24},{1,5},{9... | collective-permute-start | bytes 442376 | tf_op jit(solution)/shard_map/ppermute | solution.py:682
  58.3 8.1 %collective-permute-start.10 = (bf16[240,256]{1,0:T(8,128)(2,1)S(1)}, bf16[240,256]{1,0:T(8,128)(2,1)S(1)}, u32[]{:S(2)}, u32[]{:S(2)}) collective-permute-start(bf16[240,256]{1,0:T(8,128)(2,1)S(1)} %get-tuple-element.57), channel_id=1, source_target_pairs={{0,4},{4,0},{8,12},{12,8},{16,20},{20,16},{24,28},{28,24},{1,5},{5... | collective-permute-start | bytes 368648 | tf_op jit(solution)/shard_map/ppermute | solution.py:700
  60.1 7.8 %collective-permute-start.18 = (bf16[240,256]{1,0:T(8,128)(2,1)S(1)}, bf16[240,256]{1,0:T(8,128)(2,1)S(1)}, u32[]{:S(2)}, u32[]{:S(2)}) collective-permute-start(bf16[240,256]{1,0:T(8,128)(2,1)S(1)} %get-tuple-element.69), channel_id=1, source_target_pairs={{0,24},{4,28},{8,16},{12,20},{16,8},{20,12},{24,0},{28,4},{1,25},{... | collective-permute-start | bytes 368648 | tf_op jit(solution)/shard_map/ppermute | solution.py:700
  63.7 7.8 %collective-permute-start.19 = (bf16[240,256]{1,0:T(8,128)(2,1)S(1)}, bf16[240,256]{1,0:T(8,128)(2,1)S(1)}, u32[]{:S(2)}, u32[]{:S(2)}) collective-permute-start(bf16[240,256]{1,0:T(8,128)(2,1)S(1)} %get-tuple-element.70), channel_id=1, source_target_pairs={{0,8},{4,12},{8,0},{12,4},{16,24},{20,28},{24,16},{28,20},{1,9},{5... | collective-permute-start | bytes 368648 | tf_op jit(solution)/shard_map/ppermute | solution.py:700
  64.7 8.4 %collective-permute-start.20 = (bf16[240,256]{1,0:T(8,128)(2,1)S(1)}, bf16[240,256]{1,0:T(8,128)(2,1)S(1)}, u32[]{:S(2)}, u32[]{:S(2)}) collective-permute-start(bf16[240,256]{1,0:T(8,128)(2,1)S(1)} %get-tuple-element.71), channel_id=1, source_target_pairs={{0,16},{4,20},{8,24},{12,28},{16,0},{20,4},{24,8},{28,12},{1,17},{... | collective-permute-start | bytes 368648 | tf_op jit(solution)/shard_map/ppermute | solution.py:700
  64.9 8.9 %collective-permute-start.21 = (bf16[240,256]{1,0:T(8,128)(2,1)S(1)}, bf16[240,256]{1,0:T(8,128)(2,1)S(1)}, u32[]{:S(2)}, u32[]{:S(2)}) collective-permute-start(bf16[240,256]{1,0:T(8,128)(2,1)S(1)} %get-tuple-element.72), channel_id=1, source_target_pairs={{0,28},{4,24},{8,20},{12,16},{16,12},{20,8},{24,4},{28,0},{1,29},{... | collective-permute-start | bytes 368648 | tf_op jit(solution)/shard_map/ppermute | solution.py:700
  66.4 9.5 %collective-permute-start.22 = (bf16[240,256]{1,0:T(8,128)(2,1)S(1)}, bf16[240,256]{1,0:T(8,128)(2,1)S(1)}, u32[]{:S(2)}, u32[]{:S(2)}) collective-permute-start(bf16[240,256]{1,0:T(8,128)(2,1)S(1)} %get-tuple-element.74), channel_id=1, source_target_pairs={{0,12},{4,8},{8,4},{12,0},{16,28},{20,24},{24,20},{28,16},{1,13},{... | collective-permute-start | bytes 368648 | tf_op jit(solution)/shard_map/ppermute | solution.py:700
  67.9 9.8 %collective-permute-start.23 = (bf16[240,256]{1,0:T(8,128)(2,1)S(1)}, bf16[240,256]{1,0:T(8,128)(2,1)S(1)}, u32[]{:S(2)}, u32[]{:S(2)}) collective-permute-start(bf16[240,256]{1,0:T(8,128)(2,1)S(1)} %get-tuple-element.75), channel_id=1, source_target_pairs={{0,20},{4,16},{8,28},{12,24},{16,4},{20,0},{24,12},{28,8},{1,21},{... | collective-permute-start | bytes 368648 | tf_op jit(solution)/shard_map/ppermute | solution.py:700
  71.5 7.0 %collective-permute-start.11 = (bf16[224,256]{1,0:T(8,128)(2,1)S(1)}, bf16[224,256]{1,0:T(8,128)(2,1)S(1)}, u32[]{:S(2)}, u32[]{:S(2)}) collective-permute-start(bf16[224,256]{1,0:T(8,128)(2,1)S(1)} %get-tuple-element.61), channel_id=1, source_target_pairs={{0,24},{4,28},{8,16},{12,20},{16,8},{20,12},{24,0},{28,4},{1,25},{... | collective-permute-start | bytes 344072 | tf_op jit(solution)/shard_map/ppermute | solution.py:700
  73.1 8.6 %collective-permute-start.12 = (bf16[224,256]{1,0:T(8,128)(2,1)S(1)}, bf16[224,256]{1,0:T(8,128)(2,1)S(1)}, u32[]{:S(2)}, u32[]{:S(2)}) collective-permute-start(bf16[224,256]{1,0:T(8,128)(2,1)S(1)} %get-tuple-element.62), channel_id=1, source_target_pairs={{0,8},{4,12},{8,0},{12,4},{16,24},{20,28},{24,16},{28,20},{1,9},{5... | collective-permute-start | bytes 344072 | tf_op jit(solution)/shard_map/ppermute | solution.py:700
  73.8 9.6 %collective-permute-start.13 = (bf16[224,256]{1,0:T(8,128)(2,1)S(1)}, bf16[224,256]{1,0:T(8,128)(2,1)S(1)}, u32[]{:S(2)}, u32[]{:S(2)}) collective-permute-start(bf16[224,256]{1,0:T(8,128)(2,1)S(1)} %get-tuple-element.63), channel_id=1, source_target_pairs={{0,16},{4,20},{8,24},{12,28},{16,0},{20,4},{24,8},{28,12},{1,17},{... | collective-permute-start | bytes 344072 | tf_op jit(solution)/shard_map/ppermute | solution.py:700
  75.9 7.5 %collective-permute-start.14 = (bf16[224,256]{1,0:T(8,128)(2,1)S(1)}, bf16[224,256]{1,0:T(8,128)(2,1)S(1)}, u32[]{:S(2)}, u32[]{:S(2)}) collective-permute-start(bf16[224,256]{1,0:T(8,128)(2,1)S(1)} %get-tuple-element.64), channel_id=1, source_target_pairs={{0,28},{4,24},{8,20},{12,16},{16,12},{20,8},{24,4},{28,0},{1,29},{... | collective-permute-start | bytes 344072 | tf_op jit(solution)/shard_map/ppermute | solution.py:700
  77.8 5.6 %collective-permute-start.15 = (bf16[224,256]{1,0:T(8,128)(2,1)S(1)}, bf16[224,256]{1,0:T(8,128)(2,1)S(1)}, u32[]{:S(2)}, u32[]{:S(2)}) collective-permute-start(bf16[224,256]{1,0:T(8,128)(2,1)S(1)} %get-tuple-element.65), channel_id=1, source_target_pairs={{0,4},{4,0},{8,12},{12,8},{16,20},{20,16},{24,28},{28,24},{1,5},{5... | collective-permute-start | bytes 344072 | tf_op jit(solution)/shard_map/ppermute | solution.py:700
  78.5 7.3 %collective-permute-start.16 = (bf16[224,256]{1,0:T(8,128)(2,1)S(1)}, bf16[224,256]{1,0:T(8,128)(2,1)S(1)}, u32[]{:S(2)}, u32[]{:S(2)}) collective-permute-start(bf16[224,256]{1,0:T(8,128)(2,1)S(1)} %get-tuple-element.66), channel_id=1, source_target_pairs={{0,12},{4,8},{8,4},{12,0},{16,28},{20,24},{24,20},{28,16},{1,13},{... | collective-permute-start | bytes 344072 | tf_op jit(solution)/shard_map/ppermute | solution.py:700
  81.7 4.8 %collective-permute-start.17 = (bf16[224,256]{1,0:T(8,128)(2,1)S(1)}, bf16[224,256]{1,0:T(8,128)(2,1)S(1)}, u32[]{:S(2)}, u32[]{:S(2)}) collective-permute-start(bf16[224,256]{1,0:T(8,128)(2,1)S(1)} %get-tuple-element.67), channel_id=1, source_target_pairs={{0,20},{4,16},{8,28},{12,24},{16,4},{20,0},{24,12},{28,8},{1,21},{... | collective-permute-start | bytes 344072 | tf_op jit(solution)/shard_map/ppermute | solution.py:700
  (9 other events, 105.6 us)

commit v11 on v8

--- a/solution.py
+++ b/solution.py
@@ -164,9 +164,8 @@
 
 LANES = 128
 GROUPS = 23
-INNER = 360
-OUTER = 104
-BLOCK = 112
+INNER = 304
+OUTER = 160
 FIRST = 240
 SECOND = 224
 F32 = jnp.float32
@@ -258,11 +257,11 @@
 
 
 def group_of(variable, index):
-    if index == 0:
-        return 18 + variable
-    if index == 3:
-        return 9 + variable
-    return variable * 3 + index - 4 if index > 3 else 12 + variable * 2 + index - 1
+    return variable + (variable * 2 + index - 4 if index > 3 else 18 - 3 * index)
+
+
+def row_of(group):
+    return 20 * group + (4 if group >= 15 else 0)
 
 
 def difference(latitudes):
@@ -336,16 +335,18 @@
         edges[side, 2] = flux[near].astype(BF16)
         edges[side, 3] = flux[far].astype(BF16)
 
-    done = 1
+    staged[:, 300:INNER, :] = jnp.zeros((8, INNER - 300, 256), F32)
+    done = 2
     for k in range(5):
         pieces[k + 1].wait()
-        first = k * batch
-        flux[first : first + batch] = fluxes(here[1, first : first + batch], depths(first, batch))
+        first, count = k * batch, batch if k else 2
+        flux[first : first + count] = fluxes(here[1, first : first + count], depths(first, count))
         if k == 0:
             edge(0, 0, 1)
+            continue
         if k == 4:
             edge(1, columns - 1, columns - 2)
-        low, high = max(first - 1, 1), first + batch - 1
+        low, high = max(first - 1, batch + 1), first + batch - 1
         at = slice(low, high)
         ahead, behind = flux[low + 1 : high + 1], flux[low - 1 : high - 1]
         height[at] = heights(
@@ -357,7 +358,7 @@
             ahead, behind = height[first + 1 : first + 9], height[first - 1 : first + 7]
             new = velocities(here[1, at], here[2, at], height[at], ahead, behind, turning, shift)
             for v, field in enumerate((height[at],) + new):
-                put_group(staged, field, eye, 20 * group_of(v, done))
+                put_group(staged, field, eye, row_of(group_of(v, done)))
             done += 1
     odd = lax.axis_index("band") & 1
     to_first[...] = edges[1 - odd]
@@ -418,12 +419,13 @@
         at = slice(low - first, high - first)
         return (here,) + velocities(ens[1, at], ens[2, at], here, ahead, behind, turning, shift)
 
-    staged[:, 100:104, :] = jnp.zeros((8, 4, 256), F32)
-    for v, field in enumerate(window(west_block, left, 0, 10, 0, 8)):
-        put_group(staged, field, eye, 20 * v)
+    for v, field in enumerate(window(west_block, left, 0, 18, 0, 16)):
+        for index in range(2):
+            at = row_of(group_of(v, index)) - INNER
+            put_group(staged, field[8 * index : 8 * index + 8], eye, at)
     ends = window(east_block, right, 54, 6, 56, 60)
-    put_group(staged, jnp.concatenate([ends[0], ends[1]], axis=0), eye, 60)
-    put_group(staged, jnp.concatenate([ends[2], jnp.zeros_like(ends[2])], axis=0), eye, 80)
+    put_group(staged, jnp.concatenate([ends[0], ends[1]], axis=0), eye, 120)
+    put_group(staged, jnp.concatenate([ends[2], jnp.zeros_like(ends[2])], axis=0), eye, 140)
     me = lax.axis_index("mem")
     for k, d in enumerate(CHIPS):
         straight[k] = staged[me ^ d].astype(BF16)
@@ -449,8 +451,7 @@
         spread_block(got, held, wide, pl.multiple_of(index * 16, 16), lane)
         return carry
 
-    lax.fori_loop(0, 22, step, 0, unroll=4)
-    spread_block(got, held, wide, INNER - 16, lane)
+    lax.fori_loop(0, INNER // 16, step, 0, unroll=4)
     slots = seen.shape[2]
     unroll = 16
 
@@ -474,8 +475,7 @@
     for k, d in enumerate(CHIPS):
         joined[me ^ d, 0:OUTER, :] = straight[0] if k == 0 else edges[k - 1][0]
         joined[me ^ d ^ 1, 0:OUTER, :] = cross[0] if k == 0 else edges[k - 1][1]
-    joined[:, OUTER:BLOCK, :] = jnp.zeros((8, BLOCK - OUTER, 256), BF16)
-    for index in range(BLOCK // 16):
+    for index in range(OUTER // 16):
         spread_block(joined, held, wide, index * 16, lane)
     slots = first.shape[2]
     seen[:, :, 0:slots, :] = first[...]
@@ -565,7 +565,7 @@
     outs, results = refs[:8], refs[8]
     both = [maps[0], maps[1]]
     for q in range(8):
-        apply_maps(anomaly, mean, both, results, q, 180, (0, 1))
+        apply_maps(anomaly, mean, both, results, q, 184, (0, 1))
     send_back(results, outs)
 
 
@@ -617,10 +617,12 @@
         wide[me ^ d] = got[k][...].astype(F32)
 
 
-def take_group(wide, turned, eye, g, shape):
+def take_group(wide, turned, eye, g, shape, skipped=0):
     rows = shape[2] // 8
+    at = row_of(g) - row_of(skipped)
+    g = g - skipped
     for s in range(8):
-        turned[g, rows * s : rows * (s + 1), :] = wide[s, rows * g : rows * (g + 1), :]
+        turned[g, rows * s : rows * (s + 1), :] = wide[s, at : at + rows, :]
     return dot_nt(eye, turned[g].astype(BF16)).astype(BF16).reshape(shape)
 
 
@@ -645,15 +647,15 @@
     shape = (8,) + planes.shape[2:]
     spread_strips(got, wide)
     eye = identity(256, BF16)
-    mixed = take_group(wide, turned, eye, 9, shape)
+    mixed = take_group(wide, turned, eye, 21, shape, 12)
     planes[0, 24:28] = mixed[0:4]
     planes[1, 24:28] = mixed[4:8]
-    planes[2, 24:28] = take_group(wide, turned, eye, 10, shape)[0:4]
+    planes[2, 24:28] = take_group(wide, turned, eye, 22, shape, 12)[0:4]
     copies = []
     for v in range(3):
         for index in range(3):
             at = 8 * index
-            block = take_group(wide, turned, eye, group_of(v, index) - 12, shape)
+            block = take_group(wide, turned, eye, group_of(v, index), shape, 12)
             planes[v, at : at + 8] = block
         for k, (at, to, count) in enumerate(((0, 0, 24), (24, 56, 4))):
             source, target = planes.at[v, pl.ds(at, count)], out.at[v, pl.ds(to, count)]
@@ -702,15 +704,13 @@
     column = tile * 30 + cell // 20 % 30
     index = column // 8
     place = column % 8
-    group = jnp.where(index > 3, variable * 3 + index - 4, 11 + variable * 2 + index)
-    group = jnp.where(index == 3, 9 + variable, group)
-    group = jnp.where(index == 0, 18 + variable, group)
+    group = variable + jnp.where(index > 3, variable * 2 + index - 4, 18 - 3 * index)
     is_last = column >= 56
     group = jnp.where(is_last, 21 + variable // 2, group)
     place = jnp.where(is_last, column - 56 + 4 * (variable % 2), place)
     first = place * INNER + group * 20
-    last = 8 * INNER + place * BLOCK + (group - 18) * 20
-    return jnp.where(group < 18, first, last) + cell % 20
+    last = 8 * INNER + place * OUTER + (group - 15) * 20
+    return jnp.where(group < 15, first, last) + cell % 20
 
 
 def on_device_fast(
@@ -745,7 +745,7 @@
         grid=(1,),
         out_shape=(jax.ShapeDtypeStruct((4, OUTER, 256), BF16),) * 2,
         in_specs=[
-            pl.BlockSpec((3, 10, members, latitudes), lambda i: (0, 0, 0, 0)),
+            pl.BlockSpec((3, 20, members, latitudes), lambda i: (0, 0, 0, 0)),
             pl.BlockSpec((3, 6, members, latitudes), lambda i: (0, 9, 0, 0)),
             flat,
             flat,
@@ -753,8 +753,8 @@
         ],
         out_specs=(pl.BlockSpec((4, OUTER, 256), lambda i: (0, 0, 0)),) * 2,
         scratch_shapes=[
-            pltpu.VMEM((12, members, latitudes), F32),
-            pltpu.VMEM((10, members, latitudes), BF16),
+            pltpu.VMEM((20, members, latitudes), F32),
+            pltpu.VMEM((18, members, latitudes), BF16),
             pltpu.VMEM((8, OUTER, 256), F32),
             pltpu.VMEM((2, 4, members, latitudes), BF16),
         ],
@@ -797,15 +797,15 @@
     held_outer, gram, to_first, to_second = pl.pallas_call(
         observe_kernel,
         out_shape=(
-            jax.ShapeDtypeStruct((8, BLOCK, 256), BF16),
+            jax.ShapeDtypeStruct((8, OUTER, 256), BF16),
             jax.ShapeDtypeStruct((2, PACKED, 256), F32),
             one_tile,
             one_tile,
         ),
         in_specs=[smem, smem] + [vmem] * 8,
         scratch_shapes=[
-            pltpu.VMEM((8, BLOCK, 256), BF16),
-            pltpu.VMEM((2, 8 * BLOCK, LANES), F32),
+            pltpu.VMEM((8, OUTER, 256), BF16),
+            pltpu.VMEM((2, 8 * OUTER, LANES), F32),
             pltpu.VMEM((2, 2, slots + 8, LANES), F32),
         ],
         compiler_params=params(16),

time: 88.1 us -> 87 us (0.988)
    all_to_all x1, waiting for transfers between devices: 5.82 us -> 2.73 us  [swap(): return lax.all_to_all(value, 'mem', split_axis=0, concat_axis=0, tiled=True)]
    ppermute x18, waiting for transfers between devices: 9.8 us -> 11.9 us  [across(): return lax.ppermute(value, 'mem', [(i, i ^ difference) for i in range(8)])]
  transfers between devices with their start and end apart: 25 -> 25, of which waited for: 11 -> 13; matrix products, arithmetic and copies ran while one was open for 2% -> 2% of each run, Pallas kernels for 12% -> 12%
where the time goes in v11:
time: 87 us; the launch traced here: 86.8 us
  starting transfers between devices  36.5 us (42%)
  Pallas kernels  27.1 us (31%)
  waiting for transfers between devices  21.3 us (24%)
  other arithmetic  1.44 us (2%)
    ppermute x18, starting transfers between devices, across(): return lax.ppermute(value, 'mem', [(i, i ^ difference) for i in range(8)])  19.4 us
    ppermute x6, starting transfers between devices, swapped_pairs(): moved.append(lax.ppermute(value, axis, both))  11.9 us
    ppermute x18, waiting for transfers between devices, across(): return lax.ppermute(value, 'mem', [(i, i ^ difference) for i in range(8)])  11.9 us
    ppermute x6, waiting for transfers between devices, swapped_pairs(): moved.append(lax.ppermute(value, axis, both))  6.72 us
    pallas_call x1, Pallas kernels, on_device_fast(): pl.pallas_call(analyse_kernel, out_shape=(jax.ShapeDtypeStruct((FIRST, 25...  6.06 us
    all_to_all x1, starting transfers between devices, swap(): return lax.all_to_all(value, 'mem', split_axis=0, concat_axis=0, tiled=True)  5.19 us
    pallas_call x1, Pallas kernels, on_device_fast(): pl.pallas_call(spread_kernel, out_shape=(jax.ShapeDtypeStruct((8, INNER,...  5.04 us
    pallas_call x1, Pallas kernels, on_device_fast(): pl.pallas_call(inner_kernel, out_shape=(jax.ShapeDtypeStruct((8, INNER, 2...  4.7 us
  transfers between devices with their start and end apart: 25, of which 13 were waited for; matrix products, arithmetic and copies ran while one was open for 2% of the time, Pallas kernels for 12%

profile of v11, /device:TPU:0, one launch (start us, length us, event | category | flops | bytes accessed | tf_op | source)
XLA Modules:
  0.0 86.8 jit_solution(13231237044879416479)
XLA Ops:
  0.0 4.7 %inner.1 = (bf16[8,304,256]{2,1,0:T(8,128)(2,1)}, bf16[4,32,160]{2,1,0:T(8,128)(2,1)}, bf16[4,32,160]{2,1,0:T(8,128)(2,1)}) custom-call(bf16[3,60,32,160]{3,2,1,0:T(8,128)(2,1)} %bitcast.47, f32[60,160]{1,0:T(8,128)} %depth.3), custom_call_target="tpu_custom_call" | custom-call | tf_op jit(solution)/shard_map/inner/pallas_call | solution.py:724
  4.7 5.2 %all-to-all-start = ((bf16[8,304,256]{2,1,0:T(8,128)(2,1)}), bf16[8,304,256]{2,1,0:T(8,128)(2,1)}, u32[]{:S(2)}, u32[]{:S(2)}) async-start(bf16[8,304,256]{2,1,0:T(8,128)(2,1)} %get-tuple-element.41), calls=%async_computation | async-start | bytes 2490368 | tf_op jit(solution)/shard_map/all_to_all | solution.py:698
  9.9 2.2 %collective-permute-start = (bf16[4,32,160]{2,1,0:T(8,128)(2,1)}, bf16[4,32,160]{2,1,0:T(8,128)(2,1)S(1)}, u32[]{:S(2)}, u32[]{:S(2)}) collective-permute-start(bf16[4,32,160]{2,1,0:T(8,128)(2,1)} %get-tuple-element.43), channel_id=1, source_target_pairs={{0,1},{2,3},{1,0},{3,2},{4,5},{6,7},{5,4},{7,6},{8,9},{10,11},{9,8... | collective-permute-start | bytes 122888 | tf_op jit(solution)/shard_map/ppermute | solution.py:672
  12.1 2.5 %collective-permute-start.1 = (bf16[4,32,160]{2,1,0:T(8,128)(2,1)}, bf16[4,32,160]{2,1,0:T(8,128)(2,1)S(1)}, u32[]{:S(2)}, u32[]{:S(2)}) collective-permute-start(bf16[4,32,160]{2,1,0:T(8,128)(2,1)} %get-tuple-element.44), channel_id=1, source_target_pairs={{1,2},{3,0},{2,1},{0,3},{5,6},{7,4},{6,5},{4,7},{9,10},{11,8},{10,... | collective-permute-start | bytes 122888 | tf_op jit(solution)/shard_map/ppermute | solution.py:672
  15.9 2.7 %collective-permute-done.1.second_swap = bf16[4,32,160]{2,1,0:T(8,128)(2,1)S(1)} collective-permute-done((bf16[4,32,160]{2,1,0:T(8,128)(2,1)}, bf16[4,32,160]{2,1,0:T(8,128)(2,1)S(1)}, u32[]{:S(2)}, u32[]{:S(2)}) %collective-permute-start.1) | collective-permute-done | bytes 40992 | tf_op jit(solution)/shard_map/ppermute | solution.py:672
  19.9 1.5 %collective-permute-done.2.cross = bf16[4,160,256]{2,1,0:T(8,128)(2,1)S(1)} collective-permute-done((bf16[4,160,256]{2,1,0:T(8,128)(2,1)S(1)}, bf16[4,160,256]{2,1,0:T(8,128)(2,1)S(1)}, u32[]{:S(2)}, u32[]{:S(2)}) %collective-permute-start.2) | collective-permute-done | bytes 327712 | tf_op jit(solution)/shard_map/ppermute | solution.py:690
  21.5 1.9 %collective-permute-start.3 = (bf16[2,160,256]{2,1,0:T(8,128)(2,1)S(1)}, bf16[2,160,256]{2,1,0:T(8,128)(2,1)S(1)}, u32[]{:S(2)}, u32[]{:S(2)}) collective-permute-start(bf16[2,160,256]{2,1,0:T(8,128)(2,1)S(1)} %pad_maximum_fusion), channel_id=1, source_target_pairs={{0,8},{4,12},{8,0},{12,4},{16,24},{20,28},{24,16},{28,20},{1,9},{5... | collective-permute-start | bytes 491528 | tf_op jit(solution)/shard_map/ppermute | solution.py:690
  23.4 1.6 %collective-permute-start.4 = (bf16[2,160,256]{2,1,0:T(8,128)(2,1)S(1)}, bf16[2,160,256]{2,1,0:T(8,128)(2,1)S(1)}, u32[]{:S(2)}, u32[]{:S(2)}) collective-permute-start(bf16[2,160,256]{2,1,0:T(8,128)(2,1)S(1)} %pad_maximum_fusion.1), channel_id=1, source_target_pairs={{0,16},{4,20},{8,24},{12,28},{16,0},{20,4},{24,8},{28,12},{1,17},{... | collective-permute-start | bytes 491528 | tf_op jit(solution)/shard_map/ppermute | solution.py:690
  25.3 2.7 %all-to-all-done.got = bf16[8,304,256]{2,1,0:T(8,128)(2,1)} async-done(((bf16[8,304,256]{2,1,0:T(8,128)(2,1)}), bf16[8,304,256]{2,1,0:T(8,128)(2,1)}, u32[]{:S(2)}, u32[]{:S(2)}) %all-to-all-start) | async-done | bytes 1245216 | tf_op jit(solution)/shard_map/all_to_all | solution.py:698
  28.0 5.0 %spread.1 = (bf16[8,304,256]{2,1,0:T(8,128)(2,1)S(1)}, f32[2,2,512,128]{3,2,1,0:T(8,128)S(1)}) custom-call(s32[2,512]{1,0:T(2,128)S(1)} %get-tuple-element.77.cells, bf16[8,304,256]{2,1,0:T(8,128)(2,1)} %all-to-all-done.got), custom_call_target="tpu_custom_call" | custom-call | flops 1 | bytes 8388608 | tf_op jit(solution)/shard_map/spread/pallas_call | solution.py:784
  34.4 4.1 %observe.1 = (bf16[8,160,256]{2,1,0:T(8,128)(2,1)S(1)}, f32[2,144,256]{2,1,0:T(8,128)S(1)}, bf16[144,256]{1,0:T(8,128)(2,1)S(1)}, bf16[144,256]{1,0:T(8,128)(2,1)S(1)}) custom-call(s32[2,640]{1,0:T(2,128)S(1)} %pad.4.cells, s32[2,640]{1,0:T(2,128)S(1)} %fusion.3.outer, f32[2,512]{1,0:T(2,128)S(1)} %fusion.11.weight, f32[2,512]{1,0:T(2,128)S(1)} %bitcast.50, ...), custom_call_target="tpu_custom_call" | custom-call | tf_op jit(solution)/shard_map/observe/pallas_call | solution.py:797
  38.6 2.0 %collective-permute-start.6 = (bf16[144,256]{1,0:T(8,128)(2,1)S(1)}, bf16[144,256]{1,0:T(8,128)(2,1)S(1)}, u32[]{:S(2)}, u32[]{:S(2)}) collective-permute-start(bf16[144,256]{1,0:T(8,128)(2,1)S(1)} %get-tuple-element.48), channel_id=1, source_target_pairs={{0,1},{2,3},{1,0},{3,2},{4,5},{6,7},{5,4},{7,6},{8,9},{10,11},{9,8... | collective-permute-start | bytes 221192 | tf_op jit(solution)/shard_map/ppermute | solution.py:672
  40.6 2.6 %collective-permute-start.7 = (bf16[144,256]{1,0:T(8,128)(2,1)S(1)}, bf16[144,256]{1,0:T(8,128)(2,1)S(1)}, u32[]{:S(2)}, u32[]{:S(2)}) collective-permute-start(bf16[144,256]{1,0:T(8,128)(2,1)S(1)} %get-tuple-element.49), channel_id=1, source_target_pairs={{1,2},{3,0},{2,1},{0,3},{5,6},{7,4},{6,5},{4,7},{9,10},{11,8},{10,... | collective-permute-start | bytes 221192 | tf_op jit(solution)/shard_map/ppermute | solution.py:672
  43.2 3.7 %collective-permute-done.7.second_swap = bf16[144,256]{1,0:T(8,128)(2,1)S(1)} collective-permute-done((bf16[144,256]{1,0:T(8,128)(2,1)S(1)}, bf16[144,256]{1,0:T(8,128)(2,1)S(1)}, u32[]{:S(2)}, u32[]{:S(2)}) %collective-permute-start.7) | collective-permute-done | bytes 73760 | tf_op jit(solution)/shard_map/ppermute | solution.py:672
  47.8 1.9 %collective-permute-start.8 = (bf16[2,144,256]{2,1,0:T(8,128)(2,1)S(1)}, bf16[2,144,256]{2,1,0:T(8,128)(2,1)S(1)}, u32[]{:S(2)}, u32[]{:S(2)}) collective-permute-start(bf16[2,144,256]{2,1,0:T(8,128)(2,1)S(1)} %get-tuple-element.51), channel_id=1, source_target_pairs={{0,4},{8,12},{16,20},{24,28},{4,0},{12,8},{20,16},{28,24},{1,5},{9... | collective-permute-start | bytes 442376 | tf_op jit(solution)/shard_map/ppermute | solution.py:672
  50.7 6.1 %analyse.1 = (bf16[240,256]{1,0:T(8,128)(2,1)S(1)}, bf16[240,256]{1,0:T(8,128)(2,1)S(1)}, bf16[240,256]{1,0:T(8,128)(2,1)S(1)}, bf16[240,256]{1,0:T(8,128)(2,1)S...) custom-call(f32[2,144,256]{2,1,0:T(8,128)S(1)} %get-tuple-element.50, ...), custom_call_target="tpu_custom_call" | custom-call | tf_op jit(solution)/shard_map/analyse/pallas_call | solution.py:837
  56.7 2.4 %collective-permute-start.10 = (bf16[240,256]{1,0:T(8,128)(2,1)S(1)}, bf16[240,256]{1,0:T(8,128)(2,1)S(1)}, u32[]{:S(2)}, u32[]{:S(2)}) collective-permute-start(bf16[240,256]{1,0:T(8,128)(2,1)S(1)} %get-tuple-element.57), channel_id=1, source_target_pairs={{0,4},{4,0},{8,12},{12,8},{16,20},{20,16},{24,28},{28,24},{1,5},{5... | collective-permute-start | bytes 368648 | tf_op jit(solution)/shard_map/ppermute | solution.py:690
  59.1 2.6 %collective-permute-start.18 = (bf16[240,256]{1,0:T(8,128)(2,1)S(1)}, bf16[240,256]{1,0:T(8,128)(2,1)S(1)}, u32[]{:S(2)}, u32[]{:S(2)}) collective-permute-start(bf16[240,256]{1,0:T(8,128)(2,1)S(1)} %get-tuple-element.69), channel_id=1, source_target_pairs={{0,24},{4,28},{8,16},{12,20},{16,8},{20,12},{24,0},{28,4},{1,25},{... | collective-permute-start | bytes 368648 | tf_op jit(solution)/shard_map/ppermute | solution.py:690
  64.4 2.0 %collective-permute-start.22 = (bf16[240,256]{1,0:T(8,128)(2,1)S(1)}, bf16[240,256]{1,0:T(8,128)(2,1)S(1)}, u32[]{:S(2)}, u32[]{:S(2)}) collective-permute-start(bf16[240,256]{1,0:T(8,128)(2,1)S(1)} %get-tuple-element.74), channel_id=1, source_target_pairs={{0,12},{4,8},{8,4},{12,0},{16,28},{20,24},{24,20},{28,16},{1,13},{... | collective-permute-start | bytes 368648 | tf_op jit(solution)/shard_map/ppermute | solution.py:690
  67.6 2.0 %second.1 = (bf16[224,256]{1,0:T(8,128)(2,1)S(1)}, bf16[224,256]{1,0:T(8,128)(2,1)S(1)}, bf16[224,256]{1,0:T(8,128)(2,1)S(1)}, bf16[224,256]{1,0:T(8,128)(2,1)S(...) custom-call(bf16[2,256,256]{2,1,0:T(8,128)(2,1)S(1)} %get-tuple-elem, ...), custom_call_target="tpu_custom_call" | custom-call | flops 1 | bytes 6291456 | tf_op jit(solution)/shard_map/second/pallas_call | solution.py:847
  77.2 3.0 %collective-permute-done.12.refs_1_ = bf16[224,256]{1,0:T(8,128)(2,1)S(1)} collective-permute-done((bf16[224,256]{1,0:T(8,128)(2,1)S(1)}, bf16[224,256]{1,0:T(8,128)(2,1)S(1)}, u32[]{:S(2)}, u32[]{:S(2)}) %collective-permute-start.12) | collective-permute-done | bytes 114720 | tf_op jit(solution)/shard_map/ppermute | solution.py:690
  80.2 1.6 %first_return.1.refs_8_ = bf16[3,60,32,160]{3,2,1,0:T(8,128)(2,1)} custom-call(bf16[240,256]{1,0:T(8,128)(2,1)S(1)} %collective-permute-done.18.refs_0_, bf16[240,256]{1,0:T(8,128)(2,1)S(1)} %collective-permute-done.19.refs_1_, bf16[240,256]{1,0:T(8,128)(2,1)S(1)} %collective-permute-done.20.refs_2_, bf16[240,256]{1,0:T(8,128)(2,1)S(1)} %collective-permute-done.21.refs_3_, ...), custom_call_target="tpu_custom_call" | custom-call | flops 1 | bytes 4194304 | tf_op jit(solution)/shard_map/first_return/pallas_call | solution.py:857
  81.9 2.3 %collective-permute-done.16.refs_5_ = bf16[224,256]{1,0:T(8,128)(2,1)S(1)} collective-permute-done((bf16[224,256]{1,0:T(8,128)(2,1)S(1)}, bf16[224,256]{1,0:T(8,128)(2,1)S(1)}, u32[]{:S(2)}, u32[]{:S(2)}) %collective-permute-start.16) | collective-permute-done | bytes 114720 | tf_op jit(solution)/shard_map/ppermute | solution.py:690
  85.0 1.6 %second_return.1 = bf16[3,60,32,160]{3,2,1,0:T(8,128)(2,1)} custom-call(bf16[224,256]{1,0:T(8,128)(2,1)S(1)} %collective-permute-done.11.refs_0_, bf16[224,256]{1,0:T(8,128)(2,1)S(1)} %collective-permute-done.12.refs_1_, bf16[224,256]{1,0:T(8,128)(2,1)S(1)} %collective-permute-done.13.refs_2_, ...), custom_call_target="tpu_custom_call", output_to_operand_aliasing={{}: (8, {})} | custom-call | tf_op jit(solution)/shard_map/second_return/pallas_call | solution.py:871
  (64 shorter events, 18.6 us)
Async XLA Ops:
  4.7 23.3 %all-to-all-start = ((bf16[8,304,256]{2,1,0:T(8,128)(2,1)}), bf16[8,304,256]{2,1,0:T(8,128)(2,1)}, u32[]{:S(2)}, u32[]{:S(2)}) async-start(bf16[8,304,256]{2,1,0:T(8,128)(2,1)} %get-tuple-element.41), calls=%async_computation | async-start | bytes 2490368 | tf_op jit(solution)/shard_map/all_to_all | solution.py:698
  9.9 5.9 %collective-permute-start = (bf16[4,32,160]{2,1,0:T(8,128)(2,1)}, bf16[4,32,160]{2,1,0:T(8,128)(2,1)S(1)}, u32[]{:S(2)}, u32[]{:S(2)}) collective-permute-start(bf16[4,32,160]{2,1,0:T(8,128)(2,1)} %get-tuple-element.43), channel_id=1, source_target_pairs={{0,1},{2,3},{1,0},{3,2},{4,5},{6,7},{5,4},{7,6},{8,9},{10,11},{9,8... | collective-permute-start | bytes 122888 | tf_op jit(solution)/shard_map/ppermute | solution.py:672
  12.1 6.4 %collective-permute-start.1 = (bf16[4,32,160]{2,1,0:T(8,128)(2,1)}, bf16[4,32,160]{2,1,0:T(8,128)(2,1)S(1)}, u32[]{:S(2)}, u32[]{:S(2)}) collective-permute-start(bf16[4,32,160]{2,1,0:T(8,128)(2,1)} %get-tuple-element.44), channel_id=1, source_target_pairs={{1,2},{3,0},{2,1},{0,3},{5,6},{7,4},{6,5},{4,7},{9,10},{11,8},{10,... | collective-permute-start | bytes 122888 | tf_op jit(solution)/shard_map/ppermute | solution.py:672
  21.5 11.6 %collective-permute-start.3 = (bf16[2,160,256]{2,1,0:T(8,128)(2,1)S(1)}, bf16[2,160,256]{2,1,0:T(8,128)(2,1)S(1)}, u32[]{:S(2)}, u32[]{:S(2)}) collective-permute-start(bf16[2,160,256]{2,1,0:T(8,128)(2,1)S(1)} %pad_maximum_fusion), channel_id=1, source_target_pairs={{0,8},{4,12},{8,0},{12,4},{16,24},{20,28},{24,16},{28,20},{1,9},{5... | collective-permute-start | bytes 491528 | tf_op jit(solution)/shard_map/ppermute | solution.py:690
  23.4 9.7 %collective-permute-start.4 = (bf16[2,160,256]{2,1,0:T(8,128)(2,1)S(1)}, bf16[2,160,256]{2,1,0:T(8,128)(2,1)S(1)}, u32[]{:S(2)}, u32[]{:S(2)}) collective-permute-start(bf16[2,160,256]{2,1,0:T(8,128)(2,1)S(1)} %pad_maximum_fusion.1), channel_id=1, source_target_pairs={{0,16},{4,20},{8,24},{12,28},{16,0},{20,4},{24,8},{28,12},{1,17},{... | collective-permute-start | bytes 491528 | tf_op jit(solution)/shard_map/ppermute | solution.py:690
  25.0 9.5 %collective-permute-start.5 = (bf16[2,160,256]{2,1,0:T(8,128)(2,1)S(1)}, bf16[2,160,256]{2,1,0:T(8,128)(2,1)S(1)}, u32[]{:S(2)}, u32[]{:S(2)}) collective-permute-start(bf16[2,160,256]{2,1,0:T(8,128)(2,1)S(1)} %pad_maximum_fusion.2), channel_id=1, source_target_pairs={{0,24},{4,28},{8,16},{12,20},{16,8},{20,12},{24,0},{28,4},{1,25},{... | collective-permute-start | bytes 491528 | tf_op jit(solution)/shard_map/ppermute | solution.py:690
  38.6 4.6 %collective-permute-start.6 = (bf16[144,256]{1,0:T(8,128)(2,1)S(1)}, bf16[144,256]{1,0:T(8,128)(2,1)S(1)}, u32[]{:S(2)}, u32[]{:S(2)}) collective-permute-start(bf16[144,256]{1,0:T(8,128)(2,1)S(1)} %get-tuple-element.48), channel_id=1, source_target_pairs={{0,1},{2,3},{1,0},{3,2},{4,5},{6,7},{5,4},{7,6},{8,9},{10,11},{9,8... | collective-permute-start | bytes 221192 | tf_op jit(solution)/shard_map/ppermute | solution.py:672
  40.6 6.3 %collective-permute-start.7 = (bf16[144,256]{1,0:T(8,128)(2,1)S(1)}, bf16[144,256]{1,0:T(8,128)(2,1)S(1)}, u32[]{:S(2)}, u32[]{:S(2)}) collective-permute-start(bf16[144,256]{1,0:T(8,128)(2,1)S(1)} %get-tuple-element.49), channel_id=1, source_target_pairs={{1,2},{3,0},{2,1},{0,3},{5,6},{7,4},{6,5},{4,7},{9,10},{11,8},{10,... | collective-permute-start | bytes 221192 | tf_op jit(solution)/shard_map/ppermute | solution.py:672
  46.9 3.4 %collective-permute-start.9 = (bf16[2,144,256]{2,1,0:T(8,128)(2,1)S(1)}, bf16[2,144,256]{2,1,0:T(8,128)(2,1)S(1)}, u32[]{:S(2)}, u32[]{:S(2)}) collective-permute-start(bf16[2,144,256]{2,1,0:T(8,128)(2,1)S(1)} %get-tuple-element.51), channel_id=1, source_target_pairs={{4,8},{12,16},{20,24},{8,4},{16,12},{24,20},{5,9},{13,17},{21,25},... | collective-permute-start | bytes 442376 | tf_op jit(solution)/shard_map/ppermute | solution.py:672
  47.8 2.9 %collective-permute-start.8 = (bf16[2,144,256]{2,1,0:T(8,128)(2,1)S(1)}, bf16[2,144,256]{2,1,0:T(8,128)(2,1)S(1)}, u32[]{:S(2)}, u32[]{:S(2)}) collective-permute-start(bf16[2,144,256]{2,1,0:T(8,128)(2,1)S(1)} %get-tuple-element.51), channel_id=1, source_target_pairs={{0,4},{8,12},{16,20},{24,28},{4,0},{12,8},{20,16},{28,24},{1,5},{9... | collective-permute-start | bytes 442376 | tf_op jit(solution)/shard_map/ppermute | solution.py:672
  56.7 7.6 %collective-permute-start.10 = (bf16[240,256]{1,0:T(8,128)(2,1)S(1)}, bf16[240,256]{1,0:T(8,128)(2,1)S(1)}, u32[]{:S(2)}, u32[]{:S(2)}) collective-permute-start(bf16[240,256]{1,0:T(8,128)(2,1)S(1)} %get-tuple-element.57), channel_id=1, source_target_pairs={{0,4},{4,0},{8,12},{12,8},{16,20},{20,16},{24,28},{28,24},{1,5},{5... | collective-permute-start | bytes 368648 | tf_op jit(solution)/shard_map/ppermute | solution.py:690
  59.1 7.2 %collective-permute-start.18 = (bf16[240,256]{1,0:T(8,128)(2,1)S(1)}, bf16[240,256]{1,0:T(8,128)(2,1)S(1)}, u32[]{:S(2)}, u32[]{:S(2)}) collective-permute-start(bf16[240,256]{1,0:T(8,128)(2,1)S(1)} %get-tuple-element.69), channel_id=1, source_target_pairs={{0,24},{4,28},{8,16},{12,20},{16,8},{20,12},{24,0},{28,4},{1,25},{... | collective-permute-start | bytes 368648 | tf_op jit(solution)/shard_map/ppermute | solution.py:690
  61.7 8.2 %collective-permute-start.19 = (bf16[240,256]{1,0:T(8,128)(2,1)S(1)}, bf16[240,256]{1,0:T(8,128)(2,1)S(1)}, u32[]{:S(2)}, u32[]{:S(2)}) collective-permute-start(bf16[240,256]{1,0:T(8,128)(2,1)S(1)} %get-tuple-element.70), channel_id=1, source_target_pairs={{0,8},{4,12},{8,0},{12,4},{16,24},{20,28},{24,16},{28,20},{1,9},{5... | collective-permute-start | bytes 368648 | tf_op jit(solution)/shard_map/ppermute | solution.py:690
  63.1 8.0 %collective-permute-start.20 = (bf16[240,256]{1,0:T(8,128)(2,1)S(1)}, bf16[240,256]{1,0:T(8,128)(2,1)S(1)}, u32[]{:S(2)}, u32[]{:S(2)}) collective-permute-start(bf16[240,256]{1,0:T(8,128)(2,1)S(1)} %get-tuple-element.71), channel_id=1, source_target_pairs={{0,16},{4,20},{8,24},{12,28},{16,0},{20,4},{24,8},{28,12},{1,17},{... | collective-permute-start | bytes 368648 | tf_op jit(solution)/shard_map/ppermute | solution.py:690
  63.1 9.1 %collective-permute-start.21 = (bf16[240,256]{1,0:T(8,128)(2,1)S(1)}, bf16[240,256]{1,0:T(8,128)(2,1)S(1)}, u32[]{:S(2)}, u32[]{:S(2)}) collective-permute-start(bf16[240,256]{1,0:T(8,128)(2,1)S(1)} %get-tuple-element.72), channel_id=1, source_target_pairs={{0,28},{4,24},{8,20},{12,16},{16,12},{20,8},{24,4},{28,0},{1,29},{... | collective-permute-start | bytes 368648 | tf_op jit(solution)/shard_map/ppermute | solution.py:690
  64.4 9.9 %collective-permute-start.22 = (bf16[240,256]{1,0:T(8,128)(2,1)S(1)}, bf16[240,256]{1,0:T(8,128)(2,1)S(1)}, u32[]{:S(2)}, u32[]{:S(2)}) collective-permute-start(bf16[240,256]{1,0:T(8,128)(2,1)S(1)} %get-tuple-element.74), channel_id=1, source_target_pairs={{0,12},{4,8},{8,4},{12,0},{16,28},{20,24},{24,20},{28,16},{1,13},{... | collective-permute-start | bytes 368648 | tf_op jit(solution)/shard_map/ppermute | solution.py:690
  66.4 9.2 %collective-permute-start.23 = (bf16[240,256]{1,0:T(8,128)(2,1)S(1)}, bf16[240,256]{1,0:T(8,128)(2,1)S(1)}, u32[]{:S(2)}, u32[]{:S(2)}) collective-permute-start(bf16[240,256]{1,0:T(8,128)(2,1)S(1)} %get-tuple-element.75), channel_id=1, source_target_pairs={{0,20},{4,16},{8,28},{12,24},{16,4},{20,0},{24,12},{28,8},{1,21},{... | collective-permute-start | bytes 368648 | tf_op jit(solution)/shard_map/ppermute | solution.py:690
  69.9 7.0 %collective-permute-start.11 = (bf16[224,256]{1,0:T(8,128)(2,1)S(1)}, bf16[224,256]{1,0:T(8,128)(2,1)S(1)}, u32[]{:S(2)}, u32[]{:S(2)}) collective-permute-start(bf16[224,256]{1,0:T(8,128)(2,1)S(1)} %get-tuple-element.61), channel_id=1, source_target_pairs={{0,24},{4,28},{8,16},{12,20},{16,8},{20,12},{24,0},{28,4},{1,25},{... | collective-permute-start | bytes 344072 | tf_op jit(solution)/shard_map/ppermute | solution.py:690
  71.1 9.1 %collective-permute-start.12 = (bf16[224,256]{1,0:T(8,128)(2,1)S(1)}, bf16[224,256]{1,0:T(8,128)(2,1)S(1)}, u32[]{:S(2)}, u32[]{:S(2)}) collective-permute-start(bf16[224,256]{1,0:T(8,128)(2,1)S(1)} %get-tuple-element.62), channel_id=1, source_target_pairs={{0,8},{4,12},{8,0},{12,4},{16,24},{20,28},{24,16},{28,20},{1,9},{5... | collective-permute-start | bytes 344072 | tf_op jit(solution)/shard_map/ppermute | solution.py:690
  72.3 9.5 %collective-permute-start.13 = (bf16[224,256]{1,0:T(8,128)(2,1)S(1)}, bf16[224,256]{1,0:T(8,128)(2,1)S(1)}, u32[]{:S(2)}, u32[]{:S(2)}) collective-permute-start(bf16[224,256]{1,0:T(8,128)(2,1)S(1)} %get-tuple-element.63), channel_id=1, source_target_pairs={{0,16},{4,20},{8,24},{12,28},{16,0},{20,4},{24,8},{28,12},{1,17},{... | collective-permute-start | bytes 344072 | tf_op jit(solution)/shard_map/ppermute | solution.py:690
  74.3 7.5 %collective-permute-start.14 = (bf16[224,256]{1,0:T(8,128)(2,1)S(1)}, bf16[224,256]{1,0:T(8,128)(2,1)S(1)}, u32[]{:S(2)}, u32[]{:S(2)}) collective-permute-start(bf16[224,256]{1,0:T(8,128)(2,1)S(1)} %get-tuple-element.64), channel_id=1, source_target_pairs={{0,28},{4,24},{8,20},{12,16},{16,12},{20,8},{24,4},{28,0},{1,29},{... | collective-permute-start | bytes 344072 | tf_op jit(solution)/shard_map/ppermute | solution.py:690
  75.5 6.3 %collective-permute-start.15 = (bf16[224,256]{1,0:T(8,128)(2,1)S(1)}, bf16[224,256]{1,0:T(8,128)(2,1)S(1)}, u32[]{:S(2)}, u32[]{:S(2)}) collective-permute-start(bf16[224,256]{1,0:T(8,128)(2,1)S(1)} %get-tuple-element.65), channel_id=1, source_target_pairs={{0,4},{4,0},{8,12},{12,8},{16,20},{20,16},{24,28},{28,24},{1,5},{5... | collective-permute-start | bytes 344072 | tf_op jit(solution)/shard_map/ppermute | solution.py:690
  76.9 7.3 %collective-permute-start.16 = (bf16[224,256]{1,0:T(8,128)(2,1)S(1)}, bf16[224,256]{1,0:T(8,128)(2,1)S(1)}, u32[]{:S(2)}, u32[]{:S(2)}) collective-permute-start(bf16[224,256]{1,0:T(8,128)(2,1)S(1)} %get-tuple-element.66), channel_id=1, source_target_pairs={{0,12},{4,8},{8,4},{12,0},{16,28},{20,24},{24,20},{28,16},{1,13},{... | collective-permute-start | bytes 344072 | tf_op jit(solution)/shard_map/ppermute | solution.py:690
  80.2 4.8 %collective-permute-start.17 = (bf16[224,256]{1,0:T(8,128)(2,1)S(1)}, bf16[224,256]{1,0:T(8,128)(2,1)S(1)}, u32[]{:S(2)}, u32[]{:S(2)}) collective-permute-start(bf16[224,256]{1,0:T(8,128)(2,1)S(1)} %get-tuple-element.67), channel_id=1, source_target_pairs={{0,20},{4,16},{8,28},{12,24},{16,4},{20,0},{24,12},{28,8},{1,21},{... | collective-permute-start | bytes 344072 | tf_op jit(solution)/shard_map/ppermute | solution.py:690
  (7 other events, 86.8 us)

commit v12 on v11

--- a/solution.py
+++ b/solution.py
@@ -165,12 +165,12 @@
 LANES = 128
 GROUPS = 23
 INNER = 304
-OUTER = 160
+OUTER = 152
 FIRST = 240
-SECOND = 224
+SECOND = 216
 F32 = jnp.float32
 BF16 = jnp.bfloat16
-PACKED = 144
+PACKED = 136
 CHIPS = (0, 2, 4, 6)
 ORDER = (6, 2, 4, 7, 1, 3, 5, 0)
 MIB = 1024 * 1024
@@ -224,7 +224,8 @@
     middle = jnp.sum(jnp.where(row == column, last, 0.0), axis=0, keepdims=True)
     middle = jnp.concatenate([jnp.zeros_like(middle), middle], axis=1)
     top = jnp.concatenate([block[128:256, 0:128], corner], axis=1)
-    return jnp.concatenate([top, pull, jnp.broadcast_to(middle, (8, 256))], axis=0)
+    tail = jnp.where(lax.broadcasted_iota(jnp.int32, (8, 256), 0) == 0, pull, middle)
+    return jnp.concatenate([top, tail], axis=0)
 
 
 def unpacked(value):
@@ -233,7 +234,7 @@
     other = jnp.transpose(corner)
     first = jnp.where(row >= column, corner, other)
     last = jnp.where(row < column, corner, other)
-    last = jnp.where(row == column, value[136:137, 128:256], last)
+    last = jnp.where(row == column, value[129:130, 128:256], last)
     top = jnp.concatenate([first, jnp.transpose(low)], axis=1)
     return jnp.concatenate([top, jnp.concatenate([low, last], axis=1)], axis=0), value[128:136]
 
@@ -425,7 +426,13 @@
             put_group(staged, field[8 * index : 8 * index + 8], eye, at)
     ends = window(east_block, right, 54, 6, 56, 60)
     put_group(staged, jnp.concatenate([ends[0], ends[1]], axis=0), eye, 120)
-    put_group(staged, jnp.concatenate([ends[2], jnp.zeros_like(ends[2])], axis=0), eye, 140)
+    block = jnp.concatenate([ends[2], ends[2]], axis=0).reshape(256, latitudes)
+    turned = dot_nt(eye, block)
+    lower = lax.broadcasted_iota(jnp.int32, (10, 256), 1) < LANES
+    for s in range(8):
+        rows = [turned[20 * s + 10 * k : 20 * s + 10 * k + 10] for k in range(2)]
+        staged[s, 140:150, :] = jnp.where(lower, rows[0], rows[1])
+    staged[:, 150:OUTER, :] = jnp.zeros((8, OUTER - 150, 256), F32)
     me = lax.axis_index("mem")
     for k, d in enumerate(CHIPS):
         straight[k] = staged[me ^ d].astype(BF16)
@@ -475,8 +482,8 @@
     for k, d in enumerate(CHIPS):
         joined[me ^ d, 0:OUTER, :] = straight[0] if k == 0 else edges[k - 1][0]
         joined[me ^ d ^ 1, 0:OUTER, :] = cross[0] if k == 0 else edges[k - 1][1]
-    for index in range(OUTER // 16):
-        spread_block(joined, held, wide, index * 16, lane)
+    for start in (*range(0, OUTER - 16, 16), OUTER - 16):
+        spread_block(joined, held, wide, start, lane)
     slots = first.shape[2]
     seen[:, :, 0:slots, :] = first[...]
     for t in range(2):
@@ -533,16 +540,22 @@
     lane = lax.broadcasted_iota(jnp.int32, (16, LANES), 1)
     spans = [slice(h * LANES, (h + 1) * LANES) for h in range(2)]
 
-    def step(index, carry):
-        here = pl.ds(pl.multiple_of(index * 16, 16), 16)
+    def move(start):
+        here = pl.ds(start, 16)
         blocks = [[results[q, here, span] for span in spans] for q in range(8)]
         blocks = exchange_lanes(blocks, lane)
         for q in range(8):
             for h in range(2):
                 outs[ORDER.index(q)][here, spans[h]] = blocks[q][h]
+
+    def step(index, carry):
+        move(pl.multiple_of(index * 16, 16))
         return carry
 
-    lax.fori_loop(0, results.shape[1] // 16, step, 0, unroll=4)
+    count = results.shape[1]
+    lax.fori_loop(0, count // 16, step, 0, unroll=4)
+    if count % 16:
+        move(count - 16)
 
 
 def apply_maps(anomaly, mean, maps, results, q, edge, order):
@@ -650,7 +663,15 @@
     mixed = take_group(wide, turned, eye, 21, shape, 12)
     planes[0, 24:28] = mixed[0:4]
     planes[1, 24:28] = mixed[4:8]
-    planes[2, 24:28] = take_group(wide, turned, eye, 22, shape, 12)[0:4]
+    at = row_of(22) - row_of(12)
+    turned[10] = jnp.zeros(turned.shape[1:], F32)
+    for s in range(8):
+        for k in range(2):
+            to = 20 * s + 10 * k
+            half = wide[s, at : at + 10, k * LANES : (k + 1) * LANES]
+            turned[10, to : to + 10, 0:LANES] = half
+    block = dot_nt(eye, turned[10].astype(BF16)).astype(BF16).reshape(shape)
+    planes[2, 24:28] = block[0:4]
     copies = []
     for v in range(3):
         for index in range(3):
@@ -708,9 +729,12 @@
     is_last = column >= 56
     group = jnp.where(is_last, 21 + variable // 2, group)
     place = jnp.where(is_last, column - 56 + 4 * (variable % 2), place)
+    row = cell % 20
+    place = jnp.where(group == 22, place + 4 * (row // 10), place)
+    row = jnp.where(group == 22, row % 10, row)
     first = place * INNER + group * 20
     last = 8 * INNER + place * OUTER + (group - 15) * 20
-    return jnp.where(group < 15, first, last) + cell % 20
+    return jnp.where(group < 15, first, last) + row
 
 
 def on_device_fast(

time: 87 us -> 86.2 us (level)
  no operation moved by 1% of the time
where the time goes in v12:
time: 86.2 us; the launch traced here: 86 us
  starting transfers between devices  36.4 us (42%)
  Pallas kernels  26.8 us (31%)
  waiting for transfers between devices  20.9 us (24%)
  other arithmetic  1.44 us (2%)
    ppermute x18, starting transfers between devices, across(): return lax.ppermute(value, 'mem', [(i, i ^ difference) for i in range(8)])  19.1 us
    ppermute x6, starting transfers between devices, swapped_pairs(): moved.append(lax.ppermute(value, axis, both))  12.1 us
    ppermute x18, waiting for transfers between devices, across(): return lax.ppermute(value, 'mem', [(i, i ^ difference) for i in range(8)])  11.5 us
    ppermute x6, waiting for transfers between devices, swapped_pairs(): moved.append(lax.ppermute(value, axis, both))  6.67 us
    pallas_call x1, Pallas kernels, on_device_fast(): pl.pallas_call(analyse_kernel, out_shape=(jax.ShapeDtypeStruct((FIRST, 25...  6.06 us
    all_to_all x1, starting transfers between devices, swap(): return lax.all_to_all(value, 'mem', split_axis=0, concat_axis=0, tiled=True)  5.19 us
    pallas_call x1, Pallas kernels, on_device_fast(): pl.pallas_call(spread_kernel, out_shape=(jax.ShapeDtypeStruct((8, INNER,...  5.04 us
    pallas_call x1, Pallas kernels, on_device_fast(): pl.pallas_call(inner_kernel, out_shape=(jax.ShapeDtypeStruct((8, INNER, 2...  4.7 us
  transfers between devices with their start and end apart: 25, of which 13 were waited for; matrix products, arithmetic and copies ran while one was open for 2% of the time, Pallas kernels for 12%

profile of v12, /device:TPU:0, one launch (start us, length us, event | category | flops | bytes accessed | tf_op | source)
XLA Modules:
  0.0 86.0 jit_solution(6141910374815737969)
XLA Ops:
  0.0 4.7 %inner.1 = (bf16[8,304,256]{2,1,0:T(8,128)(2,1)}, bf16[4,32,160]{2,1,0:T(8,128)(2,1)}, bf16[4,32,160]{2,1,0:T(8,128)(2,1)}) custom-call(bf16[3,60,32,160]{3,2,1,0:T(8,128)(2,1)} %bitcast.49, f32[60,160]{1,0:T(8,128)} %depth.3), custom_call_target="tpu_custom_call" | custom-call | tf_op jit(solution)/shard_map/inner/pallas_call | solution.py:748
  4.7 5.2 %all-to-all-start = ((bf16[8,304,256]{2,1,0:T(8,128)(2,1)}), bf16[8,304,256]{2,1,0:T(8,128)(2,1)}, u32[]{:S(2)}, u32[]{:S(2)}) async-start(bf16[8,304,256]{2,1,0:T(8,128)(2,1)} %get-tuple-element.41), calls=%async_computation | async-start | bytes 2490368 | tf_op jit(solution)/shard_map/all_to_all | solution.py:719
  9.9 2.2 %collective-permute-start = (bf16[4,32,160]{2,1,0:T(8,128)(2,1)}, bf16[4,32,160]{2,1,0:T(8,128)(2,1)S(1)}, u32[]{:S(2)}, u32[]{:S(2)}) collective-permute-start(bf16[4,32,160]{2,1,0:T(8,128)(2,1)} %get-tuple-element.43), channel_id=1, source_target_pairs={{0,1},{2,3},{1,0},{3,2},{4,5},{6,7},{5,4},{7,6},{8,9},{10,11},{9,8... | collective-permute-start | bytes 122888 | tf_op jit(solution)/shard_map/ppermute | solution.py:693
  12.1 2.5 %collective-permute-start.1 = (bf16[4,32,160]{2,1,0:T(8,128)(2,1)}, bf16[4,32,160]{2,1,0:T(8,128)(2,1)S(1)}, u32[]{:S(2)}, u32[]{:S(2)}) collective-permute-start(bf16[4,32,160]{2,1,0:T(8,128)(2,1)} %get-tuple-element.44), channel_id=1, source_target_pairs={{1,2},{3,0},{2,1},{0,3},{5,6},{7,4},{6,5},{4,7},{9,10},{11,8},{10,... | collective-permute-start | bytes 122888 | tf_op jit(solution)/shard_map/ppermute | solution.py:693
  15.9 2.7 %collective-permute-done.1.second_swap = bf16[4,32,160]{2,1,0:T(8,128)(2,1)S(1)} collective-permute-done((bf16[4,32,160]{2,1,0:T(8,128)(2,1)}, bf16[4,32,160]{2,1,0:T(8,128)(2,1)S(1)}, u32[]{:S(2)}, u32[]{:S(2)}) %collective-permute-start.1) | collective-permute-done | bytes 40992 | tf_op jit(solution)/shard_map/ppermute | solution.py:693
  21.5 1.9 %collective-permute-start.3 = (bf16[2,152,256]{2,1,0:T(8,128)(2,1)S(1)}, bf16[2,152,256]{2,1,0:T(8,128)(2,1)S(1)}, u32[]{:S(2)}, u32[]{:S(2)}) collective-permute-start(bf16[2,152,256]{2,1,0:T(8,128)(2,1)S(1)} %pad_maximum_fusion), channel_id=1, source_target_pairs={{0,8},{4,12},{8,0},{12,4},{16,24},{20,28},{24,16},{28,20},{1,9},{5... | collective-permute-start | bytes 466952 | tf_op jit(solution)/shard_map/ppermute | solution.py:711
  25.3 2.7 %all-to-all-done.got = bf16[8,304,256]{2,1,0:T(8,128)(2,1)} async-done(((bf16[8,304,256]{2,1,0:T(8,128)(2,1)}), bf16[8,304,256]{2,1,0:T(8,128)(2,1)}, u32[]{:S(2)}, u32[]{:S(2)}) %all-to-all-start) | async-done | bytes 1245216 | tf_op jit(solution)/shard_map/all_to_all | solution.py:719
  28.0 5.0 %spread.1 = (bf16[8,304,256]{2,1,0:T(8,128)(2,1)S(1)}, f32[2,2,512,128]{3,2,1,0:T(8,128)S(1)}) custom-call(s32[2,512]{1,0:T(2,128)S(1)} %get-tuple-element.77.cells, bf16[8,304,256]{2,1,0:T(8,128)(2,1)} %all-to-all-done.got), custom_call_target="tpu_custom_call" | custom-call | flops 1 | bytes 8388608 | tf_op jit(solution)/shard_map/spread/pallas_call | solution.py:808
  34.1 4.0 %observe.1 = (bf16[8,152,256]{2,1,0:T(8,128)(2,1)S(1)}, f32[2,136,256]{2,1,0:T(8,128)S(1)}, bf16[136,256]{1,0:T(8,128)(2,1)S(1)}, bf16[136,256]{1,0:T(8,128)(2,1)S(1)}) custom-call(s32[2,640]{1,0:T(2,128)S(1)} %pad.4.cells, s32[2,640]{1,0:T(2,128)S(1)} %fusion.3.outer, f32[2,512]{1,0:T(2,128)S(1)} %fusion.12.weight, f32[2,512]{1,0:T(2,128)S(1)} %bitcast.52, ...), custom_call_target="tpu_custom_call" | custom-call | tf_op jit(solution)/shard_map/observe/pallas_call | solution.py:821
  38.1 2.1 %collective-permute-start.6 = (bf16[136,256]{1,0:T(8,128)(2,1)S(1)}, bf16[136,256]{1,0:T(8,128)(2,1)S(1)}, u32[]{:S(2)}, u32[]{:S(2)}) collective-permute-start(bf16[136,256]{1,0:T(8,128)(2,1)S(1)} %get-tuple-element.48), channel_id=1, source_target_pairs={{0,1},{2,3},{1,0},{3,2},{4,5},{6,7},{5,4},{7,6},{8,9},{10,11},{9,8... | collective-permute-start | bytes 208904 | tf_op jit(solution)/shard_map/ppermute | solution.py:693
  40.2 2.5 %collective-permute-start.7 = (bf16[136,256]{1,0:T(8,128)(2,1)S(1)}, bf16[136,256]{1,0:T(8,128)(2,1)S(1)}, u32[]{:S(2)}, u32[]{:S(2)}) collective-permute-start(bf16[136,256]{1,0:T(8,128)(2,1)S(1)} %get-tuple-element.49), channel_id=1, source_target_pairs={{1,2},{3,0},{2,1},{0,3},{5,6},{7,4},{6,5},{4,7},{9,10},{11,8},{10,... | collective-permute-start | bytes 208904 | tf_op jit(solution)/shard_map/ppermute | solution.py:693
  42.7 3.7 %collective-permute-done.7.second_swap = bf16[136,256]{1,0:T(8,128)(2,1)S(1)} collective-permute-done((bf16[136,256]{1,0:T(8,128)(2,1)S(1)}, bf16[136,256]{1,0:T(8,128)(2,1)S(1)}, u32[]{:S(2)}, u32[]{:S(2)}) %collective-permute-start.7) | collective-permute-done | bytes 69664 | tf_op jit(solution)/shard_map/ppermute | solution.py:693
  47.3 2.0 %collective-permute-start.8 = (bf16[2,136,256]{2,1,0:T(8,128)(2,1)S(1)}, bf16[2,136,256]{2,1,0:T(8,128)(2,1)S(1)}, u32[]{:S(2)}, u32[]{:S(2)}) collective-permute-start(bf16[2,136,256]{2,1,0:T(8,128)(2,1)S(1)} %get-tuple-element.51), channel_id=1, source_target_pairs={{0,4},{8,12},{16,20},{24,28},{4,0},{12,8},{20,16},{28,24},{1,5},{9... | collective-permute-start | bytes 417800 | tf_op jit(solution)/shard_map/ppermute | solution.py:693
  50.3 6.1 %analyse.1 = (bf16[240,256]{1,0:T(8,128)(2,1)S(1)}, bf16[240,256]{1,0:T(8,128)(2,1)S(1)}, bf16[240,256]{1,0:T(8,128)(2,1)S(1)}, bf16[240,256]{1,0:T(8,128)(2,1)S...) custom-call(f32[2,136,256]{2,1,0:T(8,128)S(1)} %get-tuple-element.50, ...), custom_call_target="tpu_custom_call" | custom-call | tf_op jit(solution)/shard_map/analyse/pallas_call | solution.py:861
  56.3 2.1 %collective-permute-start.10 = (bf16[240,256]{1,0:T(8,128)(2,1)S(1)}, bf16[240,256]{1,0:T(8,128)(2,1)S(1)}, u32[]{:S(2)}, u32[]{:S(2)}) collective-permute-start(bf16[240,256]{1,0:T(8,128)(2,1)S(1)} %get-tuple-element.57), channel_id=1, source_target_pairs={{0,4},{4,0},{8,12},{12,8},{16,20},{20,16},{24,28},{28,24},{1,5},{5... | collective-permute-start | bytes 368648 | tf_op jit(solution)/shard_map/ppermute | solution.py:711
  58.5 2.3 %collective-permute-start.18 = (bf16[240,256]{1,0:T(8,128)(2,1)S(1)}, bf16[240,256]{1,0:T(8,128)(2,1)S(1)}, u32[]{:S(2)}, u32[]{:S(2)}) collective-permute-start(bf16[240,256]{1,0:T(8,128)(2,1)S(1)} %get-tuple-element.69), channel_id=1, source_target_pairs={{0,24},{4,28},{8,16},{12,20},{16,8},{20,12},{24,0},{28,4},{1,25},{... | collective-permute-start | bytes 368648 | tf_op jit(solution)/shard_map/ppermute | solution.py:711
  60.8 1.8 %collective-permute-start.19 = (bf16[240,256]{1,0:T(8,128)(2,1)S(1)}, bf16[240,256]{1,0:T(8,128)(2,1)S(1)}, u32[]{:S(2)}, u32[]{:S(2)}) collective-permute-start(bf16[240,256]{1,0:T(8,128)(2,1)S(1)} %get-tuple-element.70), channel_id=1, source_target_pairs={{0,8},{4,12},{8,0},{12,4},{16,24},{20,28},{24,16},{28,20},{1,9},{5... | collective-permute-start | bytes 368648 | tf_op jit(solution)/shard_map/ppermute | solution.py:711
  63.5 2.3 %collective-permute-start.22 = (bf16[240,256]{1,0:T(8,128)(2,1)S(1)}, bf16[240,256]{1,0:T(8,128)(2,1)S(1)}, u32[]{:S(2)}, u32[]{:S(2)}) collective-permute-start(bf16[240,256]{1,0:T(8,128)(2,1)S(1)} %get-tuple-element.74), channel_id=1, source_target_pairs={{0,12},{4,8},{8,4},{12,0},{16,28},{20,24},{24,20},{28,16},{1,13},{... | collective-permute-start | bytes 368648 | tf_op jit(solution)/shard_map/ppermute | solution.py:711
  67.0 1.8 %second.1 = (bf16[216,256]{1,0:T(8,128)(2,1)S(1)}, bf16[216,256]{1,0:T(8,128)(2,1)S(1)}, bf16[216,256]{1,0:T(8,128)(2,1)S(1)}, bf16[216,256]{1,0:T(8,128)(2,1)S(...) custom-call(bf16[2,256,256]{2,1,0:T(8,128)(2,1)S(1)} %get-tuple-elem, ...), custom_call_target="tpu_custom_call" | custom-call | flops 1 | bytes 6291456 | tf_op jit(solution)/shard_map/second/pallas_call | solution.py:871
  73.8 1.7 %collective-permute-start.14 = (bf16[216,256]{1,0:T(8,128)(2,1)S(1)}, bf16[216,256]{1,0:T(8,128)(2,1)S(1)}, u32[]{:S(2)}, u32[]{:S(2)}) collective-permute-start(bf16[216,256]{1,0:T(8,128)(2,1)S(1)} %get-tuple-element.64), channel_id=1, source_target_pairs={{0,28},{4,24},{8,20},{12,16},{16,12},{20,8},{24,4},{28,0},{1,29},{... | collective-permute-start | bytes 331784 | tf_op jit(solution)/shard_map/ppermute | solution.py:711
  76.2 3.2 %collective-permute-done.12.refs_1_ = bf16[216,256]{1,0:T(8,128)(2,1)S(1)} collective-permute-done((bf16[216,256]{1,0:T(8,128)(2,1)S(1)}, bf16[216,256]{1,0:T(8,128)(2,1)S(1)}, u32[]{:S(2)}, u32[]{:S(2)}) %collective-permute-start.12) | collective-permute-done | bytes 110624 | tf_op jit(solution)/shard_map/ppermute | solution.py:711
  79.4 1.6 %first_return.1.refs_8_ = bf16[3,60,32,160]{3,2,1,0:T(8,128)(2,1)} custom-call(bf16[240,256]{1,0:T(8,128)(2,1)S(1)} %collective-permute-done.18.refs_0_, bf16[240,256]{1,0:T(8,128)(2,1)S(1)} %collective-permute-done.19.refs_1_, bf16[240,256]{1,0:T(8,128)(2,1)S(1)} %collective-permute-done.20.refs_2_, bf16[240,256]{1,0:T(8,128)(2,1)S(1)} %collective-permute-done.21.refs_3_, ...), custom_call_target="tpu_custom_call" | custom-call | flops 1 | bytes 4194304 | tf_op jit(solution)/shard_map/first_return/pallas_call | solution.py:881
  81.1 2.2 %collective-permute-done.16.refs_5_ = bf16[216,256]{1,0:T(8,128)(2,1)S(1)} collective-permute-done((bf16[216,256]{1,0:T(8,128)(2,1)S(1)}, bf16[216,256]{1,0:T(8,128)(2,1)S(1)}, u32[]{:S(2)}, u32[]{:S(2)}) %collective-permute-start.16) | collective-permute-done | bytes 110624 | tf_op jit(solution)/shard_map/ppermute | solution.py:711
  84.2 1.6 %second_return.1 = bf16[3,60,32,160]{3,2,1,0:T(8,128)(2,1)} custom-call(bf16[216,256]{1,0:T(8,128)(2,1)S(1)} %collective-permute-done.11.refs_0_, bf16[216,256]{1,0:T(8,128)(2,1)S(1)} %collective-permute-done.12.refs_1_, bf16[216,256]{1,0:T(8,128)(2,1)S(1)} %collective-permute-done.13.refs_2_, ...), custom_call_target="tpu_custom_call", output_to_operand_aliasing={{}: (8, {})} | custom-call | tf_op jit(solution)/shard_map/second_return/pallas_call | solution.py:895
  (64 shorter events, 17.8 us)
Async XLA Ops:
  4.7 23.3 %all-to-all-start = ((bf16[8,304,256]{2,1,0:T(8,128)(2,1)}), bf16[8,304,256]{2,1,0:T(8,128)(2,1)}, u32[]{:S(2)}, u32[]{:S(2)}) async-start(bf16[8,304,256]{2,1,0:T(8,128)(2,1)} %get-tuple-element.41), calls=%async_computation | async-start | bytes 2490368 | tf_op jit(solution)/shard_map/all_to_all | solution.py:719
  9.9 5.9 %collective-permute-start = (bf16[4,32,160]{2,1,0:T(8,128)(2,1)}, bf16[4,32,160]{2,1,0:T(8,128)(2,1)S(1)}, u32[]{:S(2)}, u32[]{:S(2)}) collective-permute-start(bf16[4,32,160]{2,1,0:T(8,128)(2,1)} %get-tuple-element.43), channel_id=1, source_target_pairs={{0,1},{2,3},{1,0},{3,2},{4,5},{6,7},{5,4},{7,6},{8,9},{10,11},{9,8... | collective-permute-start | bytes 122888 | tf_op jit(solution)/shard_map/ppermute | solution.py:693
  12.1 6.4 %collective-permute-start.1 = (bf16[4,32,160]{2,1,0:T(8,128)(2,1)}, bf16[4,32,160]{2,1,0:T(8,128)(2,1)S(1)}, u32[]{:S(2)}, u32[]{:S(2)}) collective-permute-start(bf16[4,32,160]{2,1,0:T(8,128)(2,1)} %get-tuple-element.44), channel_id=1, source_target_pairs={{1,2},{3,0},{2,1},{0,3},{5,6},{7,4},{6,5},{4,7},{9,10},{11,8},{10,... | collective-permute-start | bytes 122888 | tf_op jit(solution)/shard_map/ppermute | solution.py:693
  21.5 11.6 %collective-permute-start.3 = (bf16[2,152,256]{2,1,0:T(8,128)(2,1)S(1)}, bf16[2,152,256]{2,1,0:T(8,128)(2,1)S(1)}, u32[]{:S(2)}, u32[]{:S(2)}) collective-permute-start(bf16[2,152,256]{2,1,0:T(8,128)(2,1)S(1)} %pad_maximum_fusion), channel_id=1, source_target_pairs={{0,8},{4,12},{8,0},{12,4},{16,24},{20,28},{24,16},{28,20},{1,9},{5... | collective-permute-start | bytes 466952 | tf_op jit(solution)/shard_map/ppermute | solution.py:711
  23.4 9.7 %collective-permute-start.4 = (bf16[2,152,256]{2,1,0:T(8,128)(2,1)S(1)}, bf16[2,152,256]{2,1,0:T(8,128)(2,1)S(1)}, u32[]{:S(2)}, u32[]{:S(2)}) collective-permute-start(bf16[2,152,256]{2,1,0:T(8,128)(2,1)S(1)} %pad_maximum_fusion.1), channel_id=1, source_target_pairs={{0,16},{4,20},{8,24},{12,28},{16,0},{20,4},{24,8},{28,12},{1,17},{... | collective-permute-start | bytes 466952 | tf_op jit(solution)/shard_map/ppermute | solution.py:711
  25.0 9.1 %collective-permute-start.5 = (bf16[2,152,256]{2,1,0:T(8,128)(2,1)S(1)}, bf16[2,152,256]{2,1,0:T(8,128)(2,1)S(1)}, u32[]{:S(2)}, u32[]{:S(2)}) collective-permute-start(bf16[2,152,256]{2,1,0:T(8,128)(2,1)S(1)} %pad_maximum_fusion.2), channel_id=1, source_target_pairs={{0,24},{4,28},{8,16},{12,20},{16,8},{20,12},{24,0},{28,4},{1,25},{... | collective-permute-start | bytes 466952 | tf_op jit(solution)/shard_map/ppermute | solution.py:711
  38.1 4.6 %collective-permute-start.6 = (bf16[136,256]{1,0:T(8,128)(2,1)S(1)}, bf16[136,256]{1,0:T(8,128)(2,1)S(1)}, u32[]{:S(2)}, u32[]{:S(2)}) collective-permute-start(bf16[136,256]{1,0:T(8,128)(2,1)S(1)} %get-tuple-element.48), channel_id=1, source_target_pairs={{0,1},{2,3},{1,0},{3,2},{4,5},{6,7},{5,4},{7,6},{8,9},{10,11},{9,8... | collective-permute-start | bytes 208904 | tf_op jit(solution)/shard_map/ppermute | solution.py:693
  40.2 6.1 %collective-permute-start.7 = (bf16[136,256]{1,0:T(8,128)(2,1)S(1)}, bf16[136,256]{1,0:T(8,128)(2,1)S(1)}, u32[]{:S(2)}, u32[]{:S(2)}) collective-permute-start(bf16[136,256]{1,0:T(8,128)(2,1)S(1)} %get-tuple-element.49), channel_id=1, source_target_pairs={{1,2},{3,0},{2,1},{0,3},{5,6},{7,4},{6,5},{4,7},{9,10},{11,8},{10,... | collective-permute-start | bytes 208904 | tf_op jit(solution)/shard_map/ppermute | solution.py:693
  46.4 3.5 %collective-permute-start.9 = (bf16[2,136,256]{2,1,0:T(8,128)(2,1)S(1)}, bf16[2,136,256]{2,1,0:T(8,128)(2,1)S(1)}, u32[]{:S(2)}, u32[]{:S(2)}) collective-permute-start(bf16[2,136,256]{2,1,0:T(8,128)(2,1)S(1)} %get-tuple-element.51), channel_id=1, source_target_pairs={{4,8},{12,16},{20,24},{8,4},{16,12},{24,20},{5,9},{13,17},{21,25},... | collective-permute-start | bytes 417800 | tf_op jit(solution)/shard_map/ppermute | solution.py:693
  47.3 3.0 %collective-permute-start.8 = (bf16[2,136,256]{2,1,0:T(8,128)(2,1)S(1)}, bf16[2,136,256]{2,1,0:T(8,128)(2,1)S(1)}, u32[]{:S(2)}, u32[]{:S(2)}) collective-permute-start(bf16[2,136,256]{2,1,0:T(8,128)(2,1)S(1)} %get-tuple-element.51), channel_id=1, source_target_pairs={{0,4},{8,12},{16,20},{24,28},{4,0},{12,8},{20,16},{28,24},{1,5},{9... | collective-permute-start | bytes 417800 | tf_op jit(solution)/shard_map/ppermute | solution.py:693
  56.3 7.2 %collective-permute-start.10 = (bf16[240,256]{1,0:T(8,128)(2,1)S(1)}, bf16[240,256]{1,0:T(8,128)(2,1)S(1)}, u32[]{:S(2)}, u32[]{:S(2)}) collective-permute-start(bf16[240,256]{1,0:T(8,128)(2,1)S(1)} %get-tuple-element.57), channel_id=1, source_target_pairs={{0,4},{4,0},{8,12},{12,8},{16,20},{20,16},{24,28},{28,24},{1,5},{5... | collective-permute-start | bytes 368648 | tf_op jit(solution)/shard_map/ppermute | solution.py:711
  58.5 7.3 %collective-permute-start.18 = (bf16[240,256]{1,0:T(8,128)(2,1)S(1)}, bf16[240,256]{1,0:T(8,128)(2,1)S(1)}, u32[]{:S(2)}, u32[]{:S(2)}) collective-permute-start(bf16[240,256]{1,0:T(8,128)(2,1)S(1)} %get-tuple-element.69), channel_id=1, source_target_pairs={{0,24},{4,28},{8,16},{12,20},{16,8},{20,12},{24,0},{28,4},{1,25},{... | collective-permute-start | bytes 368648 | tf_op jit(solution)/shard_map/ppermute | solution.py:711
  60.8 8.5 %collective-permute-start.19 = (bf16[240,256]{1,0:T(8,128)(2,1)S(1)}, bf16[240,256]{1,0:T(8,128)(2,1)S(1)}, u32[]{:S(2)}, u32[]{:S(2)}) collective-permute-start(bf16[240,256]{1,0:T(8,128)(2,1)S(1)} %get-tuple-element.70), channel_id=1, source_target_pairs={{0,8},{4,12},{8,0},{12,4},{16,24},{20,28},{24,16},{28,20},{1,9},{5... | collective-permute-start | bytes 368648 | tf_op jit(solution)/shard_map/ppermute | solution.py:711
  62.6 8.3 %collective-permute-start.20 = (bf16[240,256]{1,0:T(8,128)(2,1)S(1)}, bf16[240,256]{1,0:T(8,128)(2,1)S(1)}, u32[]{:S(2)}, u32[]{:S(2)}) collective-permute-start(bf16[240,256]{1,0:T(8,128)(2,1)S(1)} %get-tuple-element.71), channel_id=1, source_target_pairs={{0,16},{4,20},{8,24},{12,28},{16,0},{20,4},{24,8},{28,12},{1,17},{... | collective-permute-start | bytes 368648 | tf_op jit(solution)/shard_map/ppermute | solution.py:711
  62.6 9.0 %collective-permute-start.21 = (bf16[240,256]{1,0:T(8,128)(2,1)S(1)}, bf16[240,256]{1,0:T(8,128)(2,1)S(1)}, u32[]{:S(2)}, u32[]{:S(2)}) collective-permute-start(bf16[240,256]{1,0:T(8,128)(2,1)S(1)} %get-tuple-element.72), channel_id=1, source_target_pairs={{0,28},{4,24},{8,20},{12,16},{16,12},{20,8},{24,4},{28,0},{1,29},{... | collective-permute-start | bytes 368648 | tf_op jit(solution)/shard_map/ppermute | solution.py:711
  63.5 10.2 %collective-permute-start.22 = (bf16[240,256]{1,0:T(8,128)(2,1)S(1)}, bf16[240,256]{1,0:T(8,128)(2,1)S(1)}, u32[]{:S(2)}, u32[]{:S(2)}) collective-permute-start(bf16[240,256]{1,0:T(8,128)(2,1)S(1)} %get-tuple-element.74), channel_id=1, source_target_pairs={{0,12},{4,8},{8,4},{12,0},{16,28},{20,24},{24,20},{28,16},{1,13},{... | collective-permute-start | bytes 368648 | tf_op jit(solution)/shard_map/ppermute | solution.py:711
  65.8 9.6 %collective-permute-start.23 = (bf16[240,256]{1,0:T(8,128)(2,1)S(1)}, bf16[240,256]{1,0:T(8,128)(2,1)S(1)}, u32[]{:S(2)}, u32[]{:S(2)}) collective-permute-start(bf16[240,256]{1,0:T(8,128)(2,1)S(1)} %get-tuple-element.75), channel_id=1, source_target_pairs={{0,20},{4,16},{8,28},{12,24},{16,4},{20,0},{24,12},{28,8},{1,21},{... | collective-permute-start | bytes 368648 | tf_op jit(solution)/shard_map/ppermute | solution.py:711
  69.3 6.9 %collective-permute-start.11 = (bf16[216,256]{1,0:T(8,128)(2,1)S(1)}, bf16[216,256]{1,0:T(8,128)(2,1)S(1)}, u32[]{:S(2)}, u32[]{:S(2)}) collective-permute-start(bf16[216,256]{1,0:T(8,128)(2,1)S(1)} %get-tuple-element.61), channel_id=1, source_target_pairs={{0,24},{4,28},{8,16},{12,20},{16,8},{20,12},{24,0},{28,4},{1,25},{... | collective-permute-start | bytes 331784 | tf_op jit(solution)/shard_map/ppermute | solution.py:711
  70.9 8.6 %collective-permute-start.12 = (bf16[216,256]{1,0:T(8,128)(2,1)S(1)}, bf16[216,256]{1,0:T(8,128)(2,1)S(1)}, u32[]{:S(2)}, u32[]{:S(2)}) collective-permute-start(bf16[216,256]{1,0:T(8,128)(2,1)S(1)} %get-tuple-element.62), channel_id=1, source_target_pairs={{0,8},{4,12},{8,0},{12,4},{16,24},{20,28},{24,16},{28,20},{1,9},{5... | collective-permute-start | bytes 331784 | tf_op jit(solution)/shard_map/ppermute | solution.py:711
  71.6 9.5 %collective-permute-start.13 = (bf16[216,256]{1,0:T(8,128)(2,1)S(1)}, bf16[216,256]{1,0:T(8,128)(2,1)S(1)}, u32[]{:S(2)}, u32[]{:S(2)}) collective-permute-start(bf16[216,256]{1,0:T(8,128)(2,1)S(1)} %get-tuple-element.63), channel_id=1, source_target_pairs={{0,16},{4,20},{8,24},{12,28},{16,0},{20,4},{24,8},{28,12},{1,17},{... | collective-permute-start | bytes 331784 | tf_op jit(solution)/shard_map/ppermute | solution.py:711
  73.8 7.3 %collective-permute-start.14 = (bf16[216,256]{1,0:T(8,128)(2,1)S(1)}, bf16[216,256]{1,0:T(8,128)(2,1)S(1)}, u32[]{:S(2)}, u32[]{:S(2)}) collective-permute-start(bf16[216,256]{1,0:T(8,128)(2,1)S(1)} %get-tuple-element.64), channel_id=1, source_target_pairs={{0,28},{4,24},{8,20},{12,16},{16,12},{20,8},{24,4},{28,0},{1,29},{... | collective-permute-start | bytes 331784 | tf_op jit(solution)/shard_map/ppermute | solution.py:711
  75.4 5.7 %collective-permute-start.15 = (bf16[216,256]{1,0:T(8,128)(2,1)S(1)}, bf16[216,256]{1,0:T(8,128)(2,1)S(1)}, u32[]{:S(2)}, u32[]{:S(2)}) collective-permute-start(bf16[216,256]{1,0:T(8,128)(2,1)S(1)} %get-tuple-element.65), channel_id=1, source_target_pairs={{0,4},{4,0},{8,12},{12,8},{16,20},{20,16},{24,28},{28,24},{1,5},{5... | collective-permute-start | bytes 331784 | tf_op jit(solution)/shard_map/ppermute | solution.py:711
  76.2 7.1 %collective-permute-start.16 = (bf16[216,256]{1,0:T(8,128)(2,1)S(1)}, bf16[216,256]{1,0:T(8,128)(2,1)S(1)}, u32[]{:S(2)}, u32[]{:S(2)}) collective-permute-start(bf16[216,256]{1,0:T(8,128)(2,1)S(1)} %get-tuple-element.66), channel_id=1, source_target_pairs={{0,12},{4,8},{8,4},{12,0},{16,28},{20,24},{24,20},{28,16},{1,13},{... | collective-permute-start | bytes 331784 | tf_op jit(solution)/shard_map/ppermute | solution.py:711
  79.4 4.7 %collective-permute-start.17 = (bf16[216,256]{1,0:T(8,128)(2,1)S(1)}, bf16[216,256]{1,0:T(8,128)(2,1)S(1)}, u32[]{:S(2)}, u32[]{:S(2)}) collective-permute-start(bf16[216,256]{1,0:T(8,128)(2,1)S(1)} %get-tuple-element.67), channel_id=1, source_target_pairs={{0,20},{4,16},{8,28},{12,24},{16,4},{20,0},{24,12},{28,8},{1,21},{... | collective-permute-start | bytes 331784 | tf_op jit(solution)/shard_map/ppermute | solution.py:711
  (7 other events, 86.4 us)

commit v13 on v12

--- a/solution.py
+++ b/solution.py
@@ -486,17 +486,19 @@
         spread_block(joined, held, wide, start, lane)
     slots = first.shape[2]
     seen[:, :, 0:slots, :] = first[...]
-    for t in range(2):
-
-        def pick(index, carry):
-            for k in range(8):
+
+    def pick(index, carry):
+        for k in range(8):
+            for t in range(2):
                 slot = outer[t, index * 8 + k]
-                row = cells[t, slot] - 8 * INNER
+                row = cells[t, index * 8 + k]
                 for h in range(2):
                     seen[t, h, pl.ds(slot, 1), :] = wide[h, pl.ds(row, 1), :]
-            return carry
-
-        lax.fori_loop(0, (outer[t, slots + LANES - 1] + 7) // 8, pick, 0)
+        return carry
+
+    last = slots + LANES - 1
+    most = jnp.maximum(outer[0, last], outer[1, last])
+    lax.fori_loop(0, (most + 7) // 8, pick, 0)
     eye = identity(256, BF16)
     for t in range(2):
         values = jnp.concatenate([seen[t, h, 0:slots] for h in range(2)], axis=1).astype(BF16)
@@ -803,7 +805,8 @@
     outer = jnp.sum(jnp.where(found, slot, 0), axis=2)
     outer = jnp.where(place[None] < count, outer, slots)
     outer = jnp.where(place[None] == slots + LANES - 1, count, outer).astype(jnp.int32)
-    rows = jnp.pad(rows, ((0, 0), (0, LANES)), constant_values=8 * INNER)
+    beyond = (rows - 8 * INNER)[:, None, :]
+    rows = jnp.sum(jnp.where(found, beyond, 0), axis=2).astype(jnp.int32)
     smem = pl.BlockSpec(memory_space=pltpu.SMEM)
     held_inner, seen = pl.pallas_call(
         spread_kernel,

time: 86.2 us -> 86.4 us (level)
  waiting for transfers between devices: 20.9 us -> 20 us
where the time goes in v13:
time: 86.4 us; the launch traced here: 86.1 us
  starting transfers between devices  36.6 us (42%)
  Pallas kernels  27 us (31%)
  waiting for transfers between devices  20 us (23%)
  other arithmetic  2.12 us (2%)
    ppermute x18, starting transfers between devices, across(): return lax.ppermute(value, 'mem', [(i, i ^ difference) for i in range(8)])  19.4 us
    ppermute x6, starting transfers between devices, swapped_pairs(): moved.append(lax.ppermute(value, axis, both))  12 us
    ppermute x18, waiting for transfers between devices, across(): return lax.ppermute(value, 'mem', [(i, i ^ difference) for i in range(8)])  11.2 us
    pallas_call x1, Pallas kernels, on_device_fast(): pl.pallas_call(analyse_kernel, out_shape=(jax.ShapeDtypeStruct((FIRST, 25...  6.05 us
    ppermute x6, waiting for transfers between devices, swapped_pairs(): moved.append(lax.ppermute(value, axis, both))  6.05 us
    all_to_all x1, starting transfers between devices, swap(): return lax.all_to_all(value, 'mem', split_axis=0, concat_axis=0, tiled=True)  5.19 us
    pallas_call x1, Pallas kernels, on_device_fast(): pl.pallas_call(spread_kernel, out_shape=(jax.ShapeDtypeStruct((8, INNER,...  5.04 us
    pallas_call x1, Pallas kernels, on_device_fast(): pl.pallas_call(inner_kernel, out_shape=(jax.ShapeDtypeStruct((8, INNER, 2...  4.7 us
  transfers between devices with their start and end apart: 25, of which 13 were waited for; matrix products, arithmetic and copies ran while one was open for 2% of the time, Pallas kernels for 12%

profile of v13, /device:TPU:0, one launch (start us, length us, event | category | flops | bytes accessed | tf_op | source)
XLA Modules:
  0.0 86.1 jit_solution(18116641988968521677)
XLA Ops:
  0.0 4.7 %inner.1 = (bf16[8,304,256]{2,1,0:T(8,128)(2,1)}, bf16[4,32,160]{2,1,0:T(8,128)(2,1)}, bf16[4,32,160]{2,1,0:T(8,128)(2,1)}) custom-call(bf16[3,60,32,160]{3,2,1,0:T(8,128)(2,1)} %bitcast.49, f32[60,160]{1,0:T(8,128)} %depth.3), custom_call_target="tpu_custom_call" | custom-call | tf_op jit(solution)/shard_map/inner/pallas_call | solution.py:750
  4.7 5.2 %all-to-all-start = ((bf16[8,304,256]{2,1,0:T(8,128)(2,1)}), bf16[8,304,256]{2,1,0:T(8,128)(2,1)}, u32[]{:S(2)}, u32[]{:S(2)}) async-start(bf16[8,304,256]{2,1,0:T(8,128)(2,1)} %get-tuple-element.41), calls=%async_computation | async-start | bytes 2490368 | tf_op jit(solution)/shard_map/all_to_all | solution.py:721
  9.9 2.2 %collective-permute-start = (bf16[4,32,160]{2,1,0:T(8,128)(2,1)}, bf16[4,32,160]{2,1,0:T(8,128)(2,1)S(1)}, u32[]{:S(2)}, u32[]{:S(2)}) collective-permute-start(bf16[4,32,160]{2,1,0:T(8,128)(2,1)} %get-tuple-element.43), channel_id=1, source_target_pairs={{0,1},{2,3},{1,0},{3,2},{4,5},{6,7},{5,4},{7,6},{8,9},{10,11},{9,8... | collective-permute-start | bytes 122888 | tf_op jit(solution)/shard_map/ppermute | solution.py:695
  12.1 2.5 %collective-permute-start.1 = (bf16[4,32,160]{2,1,0:T(8,128)(2,1)}, bf16[4,32,160]{2,1,0:T(8,128)(2,1)S(1)}, u32[]{:S(2)}, u32[]{:S(2)}) collective-permute-start(bf16[4,32,160]{2,1,0:T(8,128)(2,1)} %get-tuple-element.44), channel_id=1, source_target_pairs={{1,2},{3,0},{2,1},{0,3},{5,6},{7,4},{6,5},{4,7},{9,10},{11,8},{10,... | collective-permute-start | bytes 122888 | tf_op jit(solution)/shard_map/ppermute | solution.py:695
  16.5 2.0 %collective-permute-done.1.second_swap = bf16[4,32,160]{2,1,0:T(8,128)(2,1)S(1)} collective-permute-done((bf16[4,32,160]{2,1,0:T(8,128)(2,1)}, bf16[4,32,160]{2,1,0:T(8,128)(2,1)S(1)}, u32[]{:S(2)}, u32[]{:S(2)}) %collective-permute-start.1) | collective-permute-done | bytes 40992 | tf_op jit(solution)/shard_map/ppermute | solution.py:695
  21.5 1.9 %collective-permute-start.3 = (bf16[2,152,256]{2,1,0:T(8,128)(2,1)S(1)}, bf16[2,152,256]{2,1,0:T(8,128)(2,1)S(1)}, u32[]{:S(2)}, u32[]{:S(2)}) collective-permute-start(bf16[2,152,256]{2,1,0:T(8,128)(2,1)S(1)} %pad_maximum_fusion), channel_id=1, source_target_pairs={{0,8},{4,12},{8,0},{12,4},{16,24},{20,28},{24,16},{28,20},{1,9},{5... | collective-permute-start | bytes 466952 | tf_op jit(solution)/shard_map/ppermute | solution.py:713
  25.3 2.7 %all-to-all-done.got = bf16[8,304,256]{2,1,0:T(8,128)(2,1)} async-done(((bf16[8,304,256]{2,1,0:T(8,128)(2,1)}), bf16[8,304,256]{2,1,0:T(8,128)(2,1)}, u32[]{:S(2)}, u32[]{:S(2)}) %all-to-all-start) | async-done | bytes 1245216 | tf_op jit(solution)/shard_map/all_to_all | solution.py:721
  28.0 5.0 %spread.1 = (bf16[8,304,256]{2,1,0:T(8,128)(2,1)S(1)}, f32[2,2,512,128]{3,2,1,0:T(8,128)S(1)}) custom-call(s32[2,512]{1,0:T(2,128)S(1)} %get-tuple-element.79.cells, bf16[8,304,256]{2,1,0:T(8,128)(2,1)} %all-to-all-done.got), custom_call_target="tpu_custom_call" | custom-call | flops 1 | bytes 8388608 | tf_op jit(solution)/shard_map/spread/pallas_call | solution.py:811
  34.1 4.2 %observe.1 = (bf16[8,152,256]{2,1,0:T(8,128)(2,1)S(1)}, f32[2,136,256]{2,1,0:T(8,128)S(1)}, bf16[136,256]{1,0:T(8,128)(2,1)S(1)}, bf16[136,256]{1,0:T(8,128)(2,1)S(1)}) custom-call(s32[2,640]{1,0:T(2,128)S(1)} %get-tuple-element.78.cells, s32[2,640]{1,0:T(2,128)S(1)} %fusion.3.outer, f32[2,512]{1,0:T(2,128)S(1)} %fusion.12.weight, f32[2,512]{1,0:T(2,128)S(1)} %bitcast.52, ...), custom_call_target="tpu_custom_call" | custom-call | tf_op jit(solution)/shard_map/observe/pallas_call | solution.py:824
  38.3 2.4 %collective-permute-start.6 = (bf16[136,256]{1,0:T(8,128)(2,1)S(1)}, bf16[136,256]{1,0:T(8,128)(2,1)S(1)}, u32[]{:S(2)}, u32[]{:S(2)}) collective-permute-start(bf16[136,256]{1,0:T(8,128)(2,1)S(1)} %get-tuple-element.48), channel_id=1, source_target_pairs={{0,1},{2,3},{1,0},{3,2},{4,5},{6,7},{5,4},{7,6},{8,9},{10,11},{9,8... | collective-permute-start | bytes 208904 | tf_op jit(solution)/shard_map/ppermute | solution.py:695
  40.6 2.4 %collective-permute-start.7 = (bf16[136,256]{1,0:T(8,128)(2,1)S(1)}, bf16[136,256]{1,0:T(8,128)(2,1)S(1)}, u32[]{:S(2)}, u32[]{:S(2)}) collective-permute-start(bf16[136,256]{1,0:T(8,128)(2,1)S(1)} %get-tuple-element.49), channel_id=1, source_target_pairs={{1,2},{3,0},{2,1},{0,3},{5,6},{7,4},{6,5},{4,7},{9,10},{11,8},{10,... | collective-permute-start | bytes 208904 | tf_op jit(solution)/shard_map/ppermute | solution.py:695
  43.0 3.7 %collective-permute-done.7.second_swap = bf16[136,256]{1,0:T(8,128)(2,1)S(1)} collective-permute-done((bf16[136,256]{1,0:T(8,128)(2,1)S(1)}, bf16[136,256]{1,0:T(8,128)(2,1)S(1)}, u32[]{:S(2)}, u32[]{:S(2)}) %collective-permute-start.7) | collective-permute-done | bytes 69664 | tf_op jit(solution)/shard_map/ppermute | solution.py:695
  47.7 1.8 %collective-permute-start.8 = (bf16[2,136,256]{2,1,0:T(8,128)(2,1)S(1)}, bf16[2,136,256]{2,1,0:T(8,128)(2,1)S(1)}, u32[]{:S(2)}, u32[]{:S(2)}) collective-permute-start(bf16[2,136,256]{2,1,0:T(8,128)(2,1)S(1)} %get-tuple-element.51), channel_id=1, source_target_pairs={{0,4},{8,12},{16,20},{24,28},{4,0},{12,8},{20,16},{28,24},{1,5},{9... | collective-permute-start | bytes 417800 | tf_op jit(solution)/shard_map/ppermute | solution.py:695
  50.4 6.1 %analyse.1 = (bf16[240,256]{1,0:T(8,128)(2,1)S(1)}, bf16[240,256]{1,0:T(8,128)(2,1)S(1)}, bf16[240,256]{1,0:T(8,128)(2,1)S(1)}, bf16[240,256]{1,0:T(8,128)(2,1)S...) custom-call(f32[2,136,256]{2,1,0:T(8,128)S(1)} %get-tuple-element.50, ...), custom_call_target="tpu_custom_call" | custom-call | tf_op jit(solution)/shard_map/analyse/pallas_call | solution.py:864
  56.5 2.1 %collective-permute-start.10 = (bf16[240,256]{1,0:T(8,128)(2,1)S(1)}, bf16[240,256]{1,0:T(8,128)(2,1)S(1)}, u32[]{:S(2)}, u32[]{:S(2)}) collective-permute-start(bf16[240,256]{1,0:T(8,128)(2,1)S(1)} %get-tuple-element.57), channel_id=1, source_target_pairs={{0,4},{4,0},{8,12},{12,8},{16,20},{20,16},{24,28},{28,24},{1,5},{5... | collective-permute-start | bytes 368648 | tf_op jit(solution)/shard_map/ppermute | solution.py:713
  58.6 2.5 %collective-permute-start.18 = (bf16[240,256]{1,0:T(8,128)(2,1)S(1)}, bf16[240,256]{1,0:T(8,128)(2,1)S(1)}, u32[]{:S(2)}, u32[]{:S(2)}) collective-permute-start(bf16[240,256]{1,0:T(8,128)(2,1)S(1)} %get-tuple-element.69), channel_id=1, source_target_pairs={{0,24},{4,28},{8,16},{12,20},{16,8},{20,12},{24,0},{28,4},{1,25},{... | collective-permute-start | bytes 368648 | tf_op jit(solution)/shard_map/ppermute | solution.py:713
  61.1 1.6 %collective-permute-start.19 = (bf16[240,256]{1,0:T(8,128)(2,1)S(1)}, bf16[240,256]{1,0:T(8,128)(2,1)S(1)}, u32[]{:S(2)}, u32[]{:S(2)}) collective-permute-start(bf16[240,256]{1,0:T(8,128)(2,1)S(1)} %get-tuple-element.70), channel_id=1, source_target_pairs={{0,8},{4,12},{8,0},{12,4},{16,24},{20,28},{24,16},{28,20},{1,9},{5... | collective-permute-start | bytes 368648 | tf_op jit(solution)/shard_map/ppermute | solution.py:713
  63.8 2.1 %collective-permute-start.22 = (bf16[240,256]{1,0:T(8,128)(2,1)S(1)}, bf16[240,256]{1,0:T(8,128)(2,1)S(1)}, u32[]{:S(2)}, u32[]{:S(2)}) collective-permute-start(bf16[240,256]{1,0:T(8,128)(2,1)S(1)} %get-tuple-element.74), channel_id=1, source_target_pairs={{0,12},{4,8},{8,4},{12,0},{16,28},{20,24},{24,20},{28,16},{1,13},{... | collective-permute-start | bytes 368648 | tf_op jit(solution)/shard_map/ppermute | solution.py:713
  67.1 1.8 %second.1 = (bf16[216,256]{1,0:T(8,128)(2,1)S(1)}, bf16[216,256]{1,0:T(8,128)(2,1)S(1)}, bf16[216,256]{1,0:T(8,128)(2,1)S(1)}, bf16[216,256]{1,0:T(8,128)(2,1)S(...) custom-call(bf16[2,256,256]{2,1,0:T(8,128)(2,1)S(1)} %get-tuple-elem, ...), custom_call_target="tpu_custom_call" | custom-call | flops 1 | bytes 6291456 | tf_op jit(solution)/shard_map/second/pallas_call | solution.py:874
  73.9 1.7 %collective-permute-start.14 = (bf16[216,256]{1,0:T(8,128)(2,1)S(1)}, bf16[216,256]{1,0:T(8,128)(2,1)S(1)}, u32[]{:S(2)}, u32[]{:S(2)}) collective-permute-start(bf16[216,256]{1,0:T(8,128)(2,1)S(1)} %get-tuple-element.64), channel_id=1, source_target_pairs={{0,28},{4,24},{8,20},{12,16},{16,12},{20,8},{24,4},{28,0},{1,29},{... | collective-permute-start | bytes 331784 | tf_op jit(solution)/shard_map/ppermute | solution.py:713
  76.4 3.2 %collective-permute-done.12.refs_1_ = bf16[216,256]{1,0:T(8,128)(2,1)S(1)} collective-permute-done((bf16[216,256]{1,0:T(8,128)(2,1)S(1)}, bf16[216,256]{1,0:T(8,128)(2,1)S(1)}, u32[]{:S(2)}, u32[]{:S(2)}) %collective-permute-start.12) | collective-permute-done | bytes 110624 | tf_op jit(solution)/shard_map/ppermute | solution.py:713
  79.6 1.6 %first_return.1.refs_8_ = bf16[3,60,32,160]{3,2,1,0:T(8,128)(2,1)} custom-call(bf16[240,256]{1,0:T(8,128)(2,1)S(1)} %collective-permute-done.18.refs_0_, bf16[240,256]{1,0:T(8,128)(2,1)S(1)} %collective-permute-done.19.refs_1_, bf16[240,256]{1,0:T(8,128)(2,1)S(1)} %collective-permute-done.20.refs_2_, bf16[240,256]{1,0:T(8,128)(2,1)S(1)} %collective-permute-done.21.refs_3_, ...), custom_call_target="tpu_custom_call" | custom-call | flops 1 | bytes 4194304 | tf_op jit(solution)/shard_map/first_return/pallas_call | solution.py:884
  81.3 2.2 %collective-permute-done.16.refs_5_ = bf16[216,256]{1,0:T(8,128)(2,1)S(1)} collective-permute-done((bf16[216,256]{1,0:T(8,128)(2,1)S(1)}, bf16[216,256]{1,0:T(8,128)(2,1)S(1)}, u32[]{:S(2)}, u32[]{:S(2)}) %collective-permute-start.16) | collective-permute-done | bytes 110624 | tf_op jit(solution)/shard_map/ppermute | solution.py:713
  84.3 1.6 %second_return.1 = bf16[3,60,32,160]{3,2,1,0:T(8,128)(2,1)} custom-call(bf16[216,256]{1,0:T(8,128)(2,1)S(1)} %collective-permute-done.11.refs_0_, bf16[216,256]{1,0:T(8,128)(2,1)S(1)} %collective-permute-done.12.refs_1_, bf16[216,256]{1,0:T(8,128)(2,1)S(1)} %collective-permute-done.13.refs_2_, ...), custom_call_target="tpu_custom_call", output_to_operand_aliasing={{}: (8, {})} | custom-call | tf_op jit(solution)/shard_map/second_return/pallas_call | solution.py:898
  (63 shorter events, 18.6 us)
Async XLA Ops:
  4.7 23.3 %all-to-all-start = ((bf16[8,304,256]{2,1,0:T(8,128)(2,1)}), bf16[8,304,256]{2,1,0:T(8,128)(2,1)}, u32[]{:S(2)}, u32[]{:S(2)}) async-start(bf16[8,304,256]{2,1,0:T(8,128)(2,1)} %get-tuple-element.41), calls=%async_computation | async-start | bytes 2490368 | tf_op jit(solution)/shard_map/all_to_all | solution.py:721
  9.9 6.6 %collective-permute-start = (bf16[4,32,160]{2,1,0:T(8,128)(2,1)}, bf16[4,32,160]{2,1,0:T(8,128)(2,1)S(1)}, u32[]{:S(2)}, u32[]{:S(2)}) collective-permute-start(bf16[4,32,160]{2,1,0:T(8,128)(2,1)} %get-tuple-element.43), channel_id=1, source_target_pairs={{0,1},{2,3},{1,0},{3,2},{4,5},{6,7},{5,4},{7,6},{8,9},{10,11},{9,8... | collective-permute-start | bytes 122888 | tf_op jit(solution)/shard_map/ppermute | solution.py:695
  12.1 6.4 %collective-permute-start.1 = (bf16[4,32,160]{2,1,0:T(8,128)(2,1)}, bf16[4,32,160]{2,1,0:T(8,128)(2,1)S(1)}, u32[]{:S(2)}, u32[]{:S(2)}) collective-permute-start(bf16[4,32,160]{2,1,0:T(8,128)(2,1)} %get-tuple-element.44), channel_id=1, source_target_pairs={{1,2},{3,0},{2,1},{0,3},{5,6},{7,4},{6,5},{4,7},{9,10},{11,8},{10,... | collective-permute-start | bytes 122888 | tf_op jit(solution)/shard_map/ppermute | solution.py:695
  21.5 11.6 %collective-permute-start.3 = (bf16[2,152,256]{2,1,0:T(8,128)(2,1)S(1)}, bf16[2,152,256]{2,1,0:T(8,128)(2,1)S(1)}, u32[]{:S(2)}, u32[]{:S(2)}) collective-permute-start(bf16[2,152,256]{2,1,0:T(8,128)(2,1)S(1)} %pad_maximum_fusion), channel_id=1, source_target_pairs={{0,8},{4,12},{8,0},{12,4},{16,24},{20,28},{24,16},{28,20},{1,9},{5... | collective-permute-start | bytes 466952 | tf_op jit(solution)/shard_map/ppermute | solution.py:713
  23.4 9.7 %collective-permute-start.4 = (bf16[2,152,256]{2,1,0:T(8,128)(2,1)S(1)}, bf16[2,152,256]{2,1,0:T(8,128)(2,1)S(1)}, u32[]{:S(2)}, u32[]{:S(2)}) collective-permute-start(bf16[2,152,256]{2,1,0:T(8,128)(2,1)S(1)} %pad_maximum_fusion.1), channel_id=1, source_target_pairs={{0,16},{4,20},{8,24},{12,28},{16,0},{20,4},{24,8},{28,12},{1,17},{... | collective-permute-start | bytes 466952 | tf_op jit(solution)/shard_map/ppermute | solution.py:713
  25.0 9.1 %collective-permute-start.5 = (bf16[2,152,256]{2,1,0:T(8,128)(2,1)S(1)}, bf16[2,152,256]{2,1,0:T(8,128)(2,1)S(1)}, u32[]{:S(2)}, u32[]{:S(2)}) collective-permute-start(bf16[2,152,256]{2,1,0:T(8,128)(2,1)S(1)} %pad_maximum_fusion.2), channel_id=1, source_target_pairs={{0,24},{4,28},{8,16},{12,20},{16,8},{20,12},{24,0},{28,4},{1,25},{... | collective-permute-start | bytes 466952 | tf_op jit(solution)/shard_map/ppermute | solution.py:713
  38.3 4.7 %collective-permute-start.6 = (bf16[136,256]{1,0:T(8,128)(2,1)S(1)}, bf16[136,256]{1,0:T(8,128)(2,1)S(1)}, u32[]{:S(2)}, u32[]{:S(2)}) collective-permute-start(bf16[136,256]{1,0:T(8,128)(2,1)S(1)} %get-tuple-element.48), channel_id=1, source_target_pairs={{0,1},{2,3},{1,0},{3,2},{4,5},{6,7},{5,4},{7,6},{8,9},{10,11},{9,8... | collective-permute-start | bytes 208904 | tf_op jit(solution)/shard_map/ppermute | solution.py:695
  40.6 6.1 %collective-permute-start.7 = (bf16[136,256]{1,0:T(8,128)(2,1)S(1)}, bf16[136,256]{1,0:T(8,128)(2,1)S(1)}, u32[]{:S(2)}, u32[]{:S(2)}) collective-permute-start(bf16[136,256]{1,0:T(8,128)(2,1)S(1)} %get-tuple-element.49), channel_id=1, source_target_pairs={{1,2},{3,0},{2,1},{0,3},{5,6},{7,4},{6,5},{4,7},{9,10},{11,8},{10,... | collective-permute-start | bytes 208904 | tf_op jit(solution)/shard_map/ppermute | solution.py:695
  46.8 3.3 %collective-permute-start.9 = (bf16[2,136,256]{2,1,0:T(8,128)(2,1)S(1)}, bf16[2,136,256]{2,1,0:T(8,128)(2,1)S(1)}, u32[]{:S(2)}, u32[]{:S(2)}) collective-permute-start(bf16[2,136,256]{2,1,0:T(8,128)(2,1)S(1)} %get-tuple-element.51), channel_id=1, source_target_pairs={{4,8},{12,16},{20,24},{8,4},{16,12},{24,20},{5,9},{13,17},{21,25},... | collective-permute-start | bytes 417800 | tf_op jit(solution)/shard_map/ppermute | solution.py:695
  47.7 2.8 %collective-permute-start.8 = (bf16[2,136,256]{2,1,0:T(8,128)(2,1)S(1)}, bf16[2,136,256]{2,1,0:T(8,128)(2,1)S(1)}, u32[]{:S(2)}, u32[]{:S(2)}) collective-permute-start(bf16[2,136,256]{2,1,0:T(8,128)(2,1)S(1)} %get-tuple-element.51), channel_id=1, source_target_pairs={{0,4},{8,12},{16,20},{24,28},{4,0},{12,8},{20,16},{28,24},{1,5},{9... | collective-permute-start | bytes 417800 | tf_op jit(solution)/shard_map/ppermute | solution.py:695
  56.5 7.3 %collective-permute-start.10 = (bf16[240,256]{1,0:T(8,128)(2,1)S(1)}, bf16[240,256]{1,0:T(8,128)(2,1)S(1)}, u32[]{:S(2)}, u32[]{:S(2)}) collective-permute-start(bf16[240,256]{1,0:T(8,128)(2,1)S(1)} %get-tuple-element.57), channel_id=1, source_target_pairs={{0,4},{4,0},{8,12},{12,8},{16,20},{20,16},{24,28},{28,24},{1,5},{5... | collective-permute-start | bytes 368648 | tf_op jit(solution)/shard_map/ppermute | solution.py:713
  58.6 7.4 %collective-permute-start.18 = (bf16[240,256]{1,0:T(8,128)(2,1)S(1)}, bf16[240,256]{1,0:T(8,128)(2,1)S(1)}, u32[]{:S(2)}, u32[]{:S(2)}) collective-permute-start(bf16[240,256]{1,0:T(8,128)(2,1)S(1)} %get-tuple-element.69), channel_id=1, source_target_pairs={{0,24},{4,28},{8,16},{12,20},{16,8},{20,12},{24,0},{28,4},{1,25},{... | collective-permute-start | bytes 368648 | tf_op jit(solution)/shard_map/ppermute | solution.py:713
  61.1 8.4 %collective-permute-start.19 = (bf16[240,256]{1,0:T(8,128)(2,1)S(1)}, bf16[240,256]{1,0:T(8,128)(2,1)S(1)}, u32[]{:S(2)}, u32[]{:S(2)}) collective-permute-start(bf16[240,256]{1,0:T(8,128)(2,1)S(1)} %get-tuple-element.70), channel_id=1, source_target_pairs={{0,8},{4,12},{8,0},{12,4},{16,24},{20,28},{24,16},{28,20},{1,9},{5... | collective-permute-start | bytes 368648 | tf_op jit(solution)/shard_map/ppermute | solution.py:713
  62.7 8.1 %collective-permute-start.20 = (bf16[240,256]{1,0:T(8,128)(2,1)S(1)}, bf16[240,256]{1,0:T(8,128)(2,1)S(1)}, u32[]{:S(2)}, u32[]{:S(2)}) collective-permute-start(bf16[240,256]{1,0:T(8,128)(2,1)S(1)} %get-tuple-element.71), channel_id=1, source_target_pairs={{0,16},{4,20},{8,24},{12,28},{16,0},{20,4},{24,8},{28,12},{1,17},{... | collective-permute-start | bytes 368648 | tf_op jit(solution)/shard_map/ppermute | solution.py:713
  62.7 9.0 %collective-permute-start.21 = (bf16[240,256]{1,0:T(8,128)(2,1)S(1)}, bf16[240,256]{1,0:T(8,128)(2,1)S(1)}, u32[]{:S(2)}, u32[]{:S(2)}) collective-permute-start(bf16[240,256]{1,0:T(8,128)(2,1)S(1)} %get-tuple-element.72), channel_id=1, source_target_pairs={{0,28},{4,24},{8,20},{12,16},{16,12},{20,8},{24,4},{28,0},{1,29},{... | collective-permute-start | bytes 368648 | tf_op jit(solution)/shard_map/ppermute | solution.py:713
  63.8 10.1 %collective-permute-start.22 = (bf16[240,256]{1,0:T(8,128)(2,1)S(1)}, bf16[240,256]{1,0:T(8,128)(2,1)S(1)}, u32[]{:S(2)}, u32[]{:S(2)}) collective-permute-start(bf16[240,256]{1,0:T(8,128)(2,1)S(1)} %get-tuple-element.74), channel_id=1, source_target_pairs={{0,12},{4,8},{8,4},{12,0},{16,28},{20,24},{24,20},{28,16},{1,13},{... | collective-permute-start | bytes 368648 | tf_op jit(solution)/shard_map/ppermute | solution.py:713
  65.9 9.6 %collective-permute-start.23 = (bf16[240,256]{1,0:T(8,128)(2,1)S(1)}, bf16[240,256]{1,0:T(8,128)(2,1)S(1)}, u32[]{:S(2)}, u32[]{:S(2)}) collective-permute-start(bf16[240,256]{1,0:T(8,128)(2,1)S(1)} %get-tuple-element.75), channel_id=1, source_target_pairs={{0,20},{4,16},{8,28},{12,24},{16,4},{20,0},{24,12},{28,8},{1,21},{... | collective-permute-start | bytes 368648 | tf_op jit(solution)/shard_map/ppermute | solution.py:713
  69.5 6.9 %collective-permute-start.11 = (bf16[216,256]{1,0:T(8,128)(2,1)S(1)}, bf16[216,256]{1,0:T(8,128)(2,1)S(1)}, u32[]{:S(2)}, u32[]{:S(2)}) collective-permute-start(bf16[216,256]{1,0:T(8,128)(2,1)S(1)} %get-tuple-element.61), channel_id=1, source_target_pairs={{0,24},{4,28},{8,16},{12,20},{16,8},{20,12},{24,0},{28,4},{1,25},{... | collective-permute-start | bytes 331784 | tf_op jit(solution)/shard_map/ppermute | solution.py:713
  70.9 8.7 %collective-permute-start.12 = (bf16[216,256]{1,0:T(8,128)(2,1)S(1)}, bf16[216,256]{1,0:T(8,128)(2,1)S(1)}, u32[]{:S(2)}, u32[]{:S(2)}) collective-permute-start(bf16[216,256]{1,0:T(8,128)(2,1)S(1)} %get-tuple-element.62), channel_id=1, source_target_pairs={{0,8},{4,12},{8,0},{12,4},{16,24},{20,28},{24,16},{28,20},{1,9},{5... | collective-permute-start | bytes 331784 | tf_op jit(solution)/shard_map/ppermute | solution.py:713
  71.7 9.5 %collective-permute-start.13 = (bf16[216,256]{1,0:T(8,128)(2,1)S(1)}, bf16[216,256]{1,0:T(8,128)(2,1)S(1)}, u32[]{:S(2)}, u32[]{:S(2)}) collective-permute-start(bf16[216,256]{1,0:T(8,128)(2,1)S(1)} %get-tuple-element.63), channel_id=1, source_target_pairs={{0,16},{4,20},{8,24},{12,28},{16,0},{20,4},{24,8},{28,12},{1,17},{... | collective-permute-start | bytes 331784 | tf_op jit(solution)/shard_map/ppermute | solution.py:713
  73.9 7.3 %collective-permute-start.14 = (bf16[216,256]{1,0:T(8,128)(2,1)S(1)}, bf16[216,256]{1,0:T(8,128)(2,1)S(1)}, u32[]{:S(2)}, u32[]{:S(2)}) collective-permute-start(bf16[216,256]{1,0:T(8,128)(2,1)S(1)} %get-tuple-element.64), channel_id=1, source_target_pairs={{0,28},{4,24},{8,20},{12,16},{16,12},{20,8},{24,4},{28,0},{1,29},{... | collective-permute-start | bytes 331784 | tf_op jit(solution)/shard_map/ppermute | solution.py:713
  75.6 5.7 %collective-permute-start.15 = (bf16[216,256]{1,0:T(8,128)(2,1)S(1)}, bf16[216,256]{1,0:T(8,128)(2,1)S(1)}, u32[]{:S(2)}, u32[]{:S(2)}) collective-permute-start(bf16[216,256]{1,0:T(8,128)(2,1)S(1)} %get-tuple-element.65), channel_id=1, source_target_pairs={{0,4},{4,0},{8,12},{12,8},{16,20},{20,16},{24,28},{28,24},{1,5},{5... | collective-permute-start | bytes 331784 | tf_op jit(solution)/shard_map/ppermute | solution.py:713
  76.4 7.1 %collective-permute-start.16 = (bf16[216,256]{1,0:T(8,128)(2,1)S(1)}, bf16[216,256]{1,0:T(8,128)(2,1)S(1)}, u32[]{:S(2)}, u32[]{:S(2)}) collective-permute-start(bf16[216,256]{1,0:T(8,128)(2,1)S(1)} %get-tuple-element.66), channel_id=1, source_target_pairs={{0,12},{4,8},{8,4},{12,0},{16,28},{20,24},{24,20},{28,16},{1,13},{... | collective-permute-start | bytes 331784 | tf_op jit(solution)/shard_map/ppermute | solution.py:713
  79.6 4.7 %collective-permute-start.17 = (bf16[216,256]{1,0:T(8,128)(2,1)S(1)}, bf16[216,256]{1,0:T(8,128)(2,1)S(1)}, u32[]{:S(2)}, u32[]{:S(2)}) collective-permute-start(bf16[216,256]{1,0:T(8,128)(2,1)S(1)} %get-tuple-element.67), channel_id=1, source_target_pairs={{0,20},{4,16},{8,28},{12,24},{16,4},{20,0},{24,12},{28,8},{1,21},{... | collective-permute-start | bytes 331784 | tf_op jit(solution)/shard_map/ppermute | solution.py:713
  (7 other events, 85.0 us)

commit v14 on v12

--- a/solution.py
+++ b/solution.py
@@ -172,7 +172,7 @@
 BF16 = jnp.bfloat16
 PACKED = 136
 CHIPS = (0, 2, 4, 6)
-ORDER = (6, 2, 4, 7, 1, 3, 5, 0)
+ORDER = (6, 7, 2, 4, 3, 5, 1, 0)
 MIB = 1024 * 1024
 
 
@@ -867,7 +867,6 @@
         name="analyse",
     )(line, below, above, anomaly_1, mean_1)
     first = partners(back)
-    maps, first[4] = lax.optimization_barrier((maps, first[4]))
     back = pl.pallas_call(
         second_kernel,
         out_shape=(jax.ShapeDtypeStruct((SECOND, 256), BF16),) * 8,

time: 86.2 us -> 86.6 us (level)
  starting transfers between devices: 36.4 us -> 38.3 us
  waiting for transfers between devices: 20.9 us -> 19.1 us
    ppermute x18, starting transfers between devices: 19.1 us -> 21.2 us  [across(): return lax.ppermute(value, 'mem', [(i, i ^ difference) for i in range(8)])]
    ppermute x18, waiting for transfers between devices: 11.5 us -> 9.68 us  [across(): return lax.ppermute(value, 'mem', [(i, i ^ difference) for i in range(8)])]
  transfers between devices with their start and end apart: 25 -> 25, of which waited for: 13 -> 12; matrix products, arithmetic and copies ran while one was open for 2% -> 2% of each run, Pallas kernels for 12% -> 12%
where the time goes in v14:
time: 86.6 us; the launch traced here: 86.4 us
  starting transfers between devices  38.3 us (44%)
  Pallas kernels  27.1 us (31%)
  waiting for transfers between devices  19.1 us (22%)
  other arithmetic  1.44 us (2%)
    ppermute x18, starting transfers between devices, across(): return lax.ppermute(value, 'mem', [(i, i ^ difference) for i in range(8)])  21.2 us
    ppermute x6, starting transfers between devices, swapped_pairs(): moved.append(lax.ppermute(value, axis, both))  11.9 us
    ppermute x18, waiting for transfers between devices, across(): return lax.ppermute(value, 'mem', [(i, i ^ difference) for i in range(8)])  9.68 us
    ppermute x6, waiting for transfers between devices, swapped_pairs(): moved.append(lax.ppermute(value, axis, both))  6.71 us
    pallas_call x1, Pallas kernels, on_device_fast(): pl.pallas_call(analyse_kernel, out_shape=(jax.ShapeDtypeStruct((FIRST, 25...  6.06 us
    all_to_all x1, starting transfers between devices, swap(): return lax.all_to_all(value, 'mem', split_axis=0, concat_axis=0, tiled=True)  5.19 us
    pallas_call x1, Pallas kernels, on_device_fast(): pl.pallas_call(spread_kernel, out_shape=(jax.ShapeDtypeStruct((8, INNER,...  5.04 us
    pallas_call x1, Pallas kernels, on_device_fast(): pl.pallas_call(inner_kernel, out_shape=(jax.ShapeDtypeStruct((8, INNER, 2...  4.7 us
  transfers between devices with their start and end apart: 25, of which 12 were waited for; matrix products, arithmetic and copies ran while one was open for 2% of the time, Pallas kernels for 12%

profile of v14, /device:TPU:0, one launch (start us, length us, event | category | flops | bytes accessed | tf_op | source)
XLA Modules:
  0.0 86.4 jit_solution(18007232538432935240)
XLA Ops:
  0.0 4.7 %inner.1 = (bf16[8,304,256]{2,1,0:T(8,128)(2,1)}, bf16[4,32,160]{2,1,0:T(8,128)(2,1)}, bf16[4,32,160]{2,1,0:T(8,128)(2,1)}) custom-call(bf16[3,60,32,160]{3,2,1,0:T(8,128)(2,1)} %bitcast.49, f32[60,160]{1,0:T(8,128)} %depth.3), custom_call_target="tpu_custom_call" | custom-call | tf_op jit(solution)/shard_map/inner/pallas_call | solution.py:748
  4.7 5.2 %all-to-all-start = ((bf16[8,304,256]{2,1,0:T(8,128)(2,1)}), bf16[8,304,256]{2,1,0:T(8,128)(2,1)}, u32[]{:S(2)}, u32[]{:S(2)}) async-start(bf16[8,304,256]{2,1,0:T(8,128)(2,1)} %get-tuple-element.39), calls=%async_computation | async-start | bytes 2490368 | tf_op jit(solution)/shard_map/all_to_all | solution.py:719
  9.9 2.2 %collective-permute-start = (bf16[4,32,160]{2,1,0:T(8,128)(2,1)}, bf16[4,32,160]{2,1,0:T(8,128)(2,1)S(1)}, u32[]{:S(2)}, u32[]{:S(2)}) collective-permute-start(bf16[4,32,160]{2,1,0:T(8,128)(2,1)} %get-tuple-element.41), channel_id=1, source_target_pairs={{0,1},{2,3},{1,0},{3,2},{4,5},{6,7},{5,4},{7,6},{8,9},{10,11},{9,8... | collective-permute-start | bytes 122888 | tf_op jit(solution)/shard_map/ppermute | solution.py:693
  12.1 2.5 %collective-permute-start.1 = (bf16[4,32,160]{2,1,0:T(8,128)(2,1)}, bf16[4,32,160]{2,1,0:T(8,128)(2,1)S(1)}, u32[]{:S(2)}, u32[]{:S(2)}) collective-permute-start(bf16[4,32,160]{2,1,0:T(8,128)(2,1)} %get-tuple-element.42), channel_id=1, source_target_pairs={{1,2},{3,0},{2,1},{0,3},{5,6},{7,4},{6,5},{4,7},{9,10},{11,8},{10,... | collective-permute-start | bytes 122888 | tf_op jit(solution)/shard_map/ppermute | solution.py:693
  15.9 2.7 %collective-permute-done.1.second_swap = bf16[4,32,160]{2,1,0:T(8,128)(2,1)S(1)} collective-permute-done((bf16[4,32,160]{2,1,0:T(8,128)(2,1)}, bf16[4,32,160]{2,1,0:T(8,128)(2,1)S(1)}, u32[]{:S(2)}, u32[]{:S(2)}) %collective-permute-start.1) | collective-permute-done | bytes 40992 | tf_op jit(solution)/shard_map/ppermute | solution.py:693
  21.5 1.9 %collective-permute-start.3 = (bf16[2,152,256]{2,1,0:T(8,128)(2,1)S(1)}, bf16[2,152,256]{2,1,0:T(8,128)(2,1)S(1)}, u32[]{:S(2)}, u32[]{:S(2)}) collective-permute-start(bf16[2,152,256]{2,1,0:T(8,128)(2,1)S(1)} %pad_maximum_fusion), channel_id=1, source_target_pairs={{0,8},{4,12},{8,0},{12,4},{16,24},{20,28},{24,16},{28,20},{1,9},{5... | collective-permute-start | bytes 466952 | tf_op jit(solution)/shard_map/ppermute | solution.py:711
  25.3 2.7 %all-to-all-done.got = bf16[8,304,256]{2,1,0:T(8,128)(2,1)} async-done(((bf16[8,304,256]{2,1,0:T(8,128)(2,1)}), bf16[8,304,256]{2,1,0:T(8,128)(2,1)}, u32[]{:S(2)}, u32[]{:S(2)}) %all-to-all-start) | async-done | bytes 1245216 | tf_op jit(solution)/shard_map/all_to_all | solution.py:719
  28.0 5.0 %spread.1 = (bf16[8,304,256]{2,1,0:T(8,128)(2,1)S(1)}, f32[2,2,512,128]{3,2,1,0:T(8,128)S(1)}) custom-call(s32[2,512]{1,0:T(2,128)S(1)} %get-tuple-element.73.cells, bf16[8,304,256]{2,1,0:T(8,128)(2,1)} %all-to-all-done.got), custom_call_target="tpu_custom_call" | custom-call | flops 1 | bytes 8388608 | tf_op jit(solution)/shard_map/spread/pallas_call | solution.py:808
  34.1 4.2 %observe.1 = (bf16[8,152,256]{2,1,0:T(8,128)(2,1)S(1)}, f32[2,136,256]{2,1,0:T(8,128)S(1)}, bf16[136,256]{1,0:T(8,128)(2,1)S(1)}, bf16[136,256]{1,0:T(8,128)(2,1)S(1)}) custom-call(s32[2,640]{1,0:T(2,128)S(1)} %pad.4.cells, s32[2,640]{1,0:T(2,128)S(1)} %fusion.3.outer, f32[2,512]{1,0:T(2,128)S(1)} %fusion.12.weight, f32[2,512]{1,0:T(2,128)S(1)} %bitcast.52, ...), custom_call_target="tpu_custom_call" | custom-call | tf_op jit(solution)/shard_map/observe/pallas_call | solution.py:821
  38.3 2.0 %collective-permute-start.6 = (bf16[136,256]{1,0:T(8,128)(2,1)S(1)}, bf16[136,256]{1,0:T(8,128)(2,1)S(1)}, u32[]{:S(2)}, u32[]{:S(2)}) collective-permute-start(bf16[136,256]{1,0:T(8,128)(2,1)S(1)} %get-tuple-element.46), channel_id=1, source_target_pairs={{0,1},{2,3},{1,0},{3,2},{4,5},{6,7},{5,4},{7,6},{8,9},{10,11},{9,8... | collective-permute-start | bytes 208904 | tf_op jit(solution)/shard_map/ppermute | solution.py:693
  40.3 2.4 %collective-permute-start.7 = (bf16[136,256]{1,0:T(8,128)(2,1)S(1)}, bf16[136,256]{1,0:T(8,128)(2,1)S(1)}, u32[]{:S(2)}, u32[]{:S(2)}) collective-permute-start(bf16[136,256]{1,0:T(8,128)(2,1)S(1)} %get-tuple-element.47), channel_id=1, source_target_pairs={{1,2},{3,0},{2,1},{0,3},{5,6},{7,4},{6,5},{4,7},{9,10},{11,8},{10,... | collective-permute-start | bytes 208904 | tf_op jit(solution)/shard_map/ppermute | solution.py:693
  42.8 3.7 %collective-permute-done.7.second_swap = bf16[136,256]{1,0:T(8,128)(2,1)S(1)} collective-permute-done((bf16[136,256]{1,0:T(8,128)(2,1)S(1)}, bf16[136,256]{1,0:T(8,128)(2,1)S(1)}, u32[]{:S(2)}, u32[]{:S(2)}) %collective-permute-start.7) | collective-permute-done | bytes 69664 | tf_op jit(solution)/shard_map/ppermute | solution.py:693
  47.4 2.0 %collective-permute-start.8 = (bf16[2,136,256]{2,1,0:T(8,128)(2,1)S(1)}, bf16[2,136,256]{2,1,0:T(8,128)(2,1)S(1)}, u32[]{:S(2)}, u32[]{:S(2)}) collective-permute-start(bf16[2,136,256]{2,1,0:T(8,128)(2,1)S(1)} %get-tuple-element.49), channel_id=1, source_target_pairs={{0,4},{8,12},{16,20},{24,28},{4,0},{12,8},{20,16},{28,24},{1,5},{9... | collective-permute-start | bytes 417800 | tf_op jit(solution)/shard_map/ppermute | solution.py:693
  50.4 6.1 %analyse.1 = (bf16[240,256]{1,0:T(8,128)(2,1)S(1)}, bf16[240,256]{1,0:T(8,128)(2,1)S(1)}, bf16[240,256]{1,0:T(8,128)(2,1)S(1)}, bf16[240,256]{1,0:T(8,128)(2,1)S...) custom-call(f32[2,136,256]{2,1,0:T(8,128)S(1)} %get-tuple-element.48, ...), custom_call_target="tpu_custom_call" | custom-call | tf_op jit(solution)/shard_map/analyse/pallas_call | solution.py:861
  56.5 4.3 %collective-permute-start.17 = (bf16[240,256]{1,0:T(8,128)(2,1)S(1)}, bf16[240,256]{1,0:T(8,128)(2,1)S(1)}, u32[]{:S(2)}, u32[]{:S(2)}) collective-permute-start(bf16[240,256]{1,0:T(8,128)(2,1)S(1)} %get-tuple-element.65), channel_id=1, source_target_pairs={{0,24},{4,28},{8,16},{12,20},{16,8},{20,12},{24,0},{28,4},{1,25},{... | collective-permute-start | bytes 368648 | tf_op jit(solution)/shard_map/ppermute | solution.py:711
  61.0 1.8 %second.1 = (bf16[216,256]{1,0:T(8,128)(2,1)S(1)}, bf16[216,256]{1,0:T(8,128)(2,1)S(1)}, bf16[216,256]{1,0:T(8,128)(2,1)S(1)}, bf16[216,256]{1,0:T(8,128)(2,1)S(...) custom-call(bf16[2,256,256]{2,1,0:T(8,128)(2,1)S(1)} %get-tuple-elem, ...), custom_call_target="tpu_custom_call" | custom-call | flops 1 | bytes 6291456 | tf_op jit(solution)/shard_map/second/pallas_call | solution.py:870
  63.3 2.2 %collective-permute-start.11 = (bf16[216,256]{1,0:T(8,128)(2,1)S(1)}, bf16[216,256]{1,0:T(8,128)(2,1)S(1)}, u32[]{:S(2)}, u32[]{:S(2)}) collective-permute-start(bf16[216,256]{1,0:T(8,128)(2,1)S(1)} %get-tuple-element.58), channel_id=1, source_target_pairs={{0,28},{4,24},{8,20},{12,16},{16,12},{20,8},{24,4},{28,0},{1,29},{... | collective-permute-start | bytes 331784 | tf_op jit(solution)/shard_map/ppermute | solution.py:711
  65.4 1.8 %collective-permute-start.19 = (bf16[240,256]{1,0:T(8,128)(2,1)S(1)}, bf16[240,256]{1,0:T(8,128)(2,1)S(1)}, u32[]{:S(2)}, u32[]{:S(2)}) collective-permute-start(bf16[240,256]{1,0:T(8,128)(2,1)S(1)} %get-tuple-element.67), channel_id=1, source_target_pairs={{0,8},{4,12},{8,0},{12,4},{16,24},{20,28},{24,16},{28,20},{1,9},{5... | collective-permute-start | bytes 368648 | tf_op jit(solution)/shard_map/ppermute | solution.py:711
  67.2 2.7 %collective-permute-done.10.refs_0_ = bf16[216,256]{1,0:T(8,128)(2,1)S(1)} collective-permute-done((bf16[216,256]{1,0:T(8,128)(2,1)S(1)}, bf16[216,256]{1,0:T(8,128)(2,1)S(1)}, u32[]{:S(2)}, u32[]{:S(2)}) %collective-permute-start.10) | collective-permute-done | bytes 110624 | tf_op jit(solution)/shard_map/ppermute | solution.py:711
  72.1 1.7 %collective-permute-start.21 = (bf16[240,256]{1,0:T(8,128)(2,1)S(1)}, bf16[240,256]{1,0:T(8,128)(2,1)S(1)}, u32[]{:S(2)}, u32[]{:S(2)}) collective-permute-start(bf16[240,256]{1,0:T(8,128)(2,1)S(1)} %get-tuple-element.69), channel_id=1, source_target_pairs={{0,12},{4,8},{8,4},{12,0},{16,28},{20,24},{24,20},{28,16},{1,13},{... | collective-permute-start | bytes 368648 | tf_op jit(solution)/shard_map/ppermute | solution.py:711
  74.5 1.7 %collective-permute-start.12 = (bf16[216,256]{1,0:T(8,128)(2,1)S(1)}, bf16[216,256]{1,0:T(8,128)(2,1)S(1)}, u32[]{:S(2)}, u32[]{:S(2)}) collective-permute-start(bf16[216,256]{1,0:T(8,128)(2,1)S(1)} %get-tuple-element.59), channel_id=1, source_target_pairs={{0,8},{4,12},{8,0},{12,4},{16,24},{20,28},{24,16},{28,20},{1,9},{5... | collective-permute-start | bytes 331784 | tf_op jit(solution)/shard_map/ppermute | solution.py:711
  77.6 2.1 %collective-permute-start.14 = (bf16[216,256]{1,0:T(8,128)(2,1)S(1)}, bf16[216,256]{1,0:T(8,128)(2,1)S(1)}, u32[]{:S(2)}, u32[]{:S(2)}) collective-permute-start(bf16[216,256]{1,0:T(8,128)(2,1)S(1)} %get-tuple-element.61), channel_id=1, source_target_pairs={{0,12},{4,8},{8,4},{12,0},{16,28},{20,24},{24,20},{28,16},{1,13},{... | collective-permute-start | bytes 331784 | tf_op jit(solution)/shard_map/ppermute | solution.py:711
  80.0 1.6 %first_return.1.refs_8_ = bf16[3,60,32,160]{3,2,1,0:T(8,128)(2,1)} custom-call(bf16[240,256]{1,0:T(8,128)(2,1)S(1)} %collective-permute-done.17.refs_0_, bf16[240,256]{1,0:T(8,128)(2,1)S(1)} %collective-permute-done.18.refs_1_, bf16[240,256]{1,0:T(8,128)(2,1)S(1)} %collective-permute-done.19.refs_2_, bf16[240,256]{1,0:T(8,128)(2,1)S(1)} %collective-permute-done.20.refs_3_, ...), custom_call_target="tpu_custom_call" | custom-call | flops 1 | bytes 4194304 | tf_op jit(solution)/shard_map/first_return/pallas_call | solution.py:880
  84.6 1.6 %second_return.1 = bf16[3,60,32,160]{3,2,1,0:T(8,128)(2,1)} custom-call(bf16[216,256]{1,0:T(8,128)(2,1)S(1)} %collective-permute-done.10.refs_0_, bf16[216,256]{1,0:T(8,128)(2,1)S(1)} %collective-permute-done.11.refs_1_, bf16[216,256]{1,0:T(8,128)(2,1)S(1)} %collective-permute-done.12.refs_2_, ...), custom_call_target="tpu_custom_call", output_to_operand_aliasing={{}: (8, {})} | custom-call | tf_op jit(solution)/shard_map/second_return/pallas_call | solution.py:894
  (64 shorter events, 17.0 us)
Async XLA Ops:
  4.7 23.3 %all-to-all-start = ((bf16[8,304,256]{2,1,0:T(8,128)(2,1)}), bf16[8,304,256]{2,1,0:T(8,128)(2,1)}, u32[]{:S(2)}, u32[]{:S(2)}) async-start(bf16[8,304,256]{2,1,0:T(8,128)(2,1)} %get-tuple-element.39), calls=%async_computation | async-start | bytes 2490368 | tf_op jit(solution)/shard_map/all_to_all | solution.py:719
  9.9 5.9 %collective-permute-start = (bf16[4,32,160]{2,1,0:T(8,128)(2,1)}, bf16[4,32,160]{2,1,0:T(8,128)(2,1)S(1)}, u32[]{:S(2)}, u32[]{:S(2)}) collective-permute-start(bf16[4,32,160]{2,1,0:T(8,128)(2,1)} %get-tuple-element.41), channel_id=1, source_target_pairs={{0,1},{2,3},{1,0},{3,2},{4,5},{6,7},{5,4},{7,6},{8,9},{10,11},{9,8... | collective-permute-start | bytes 122888 | tf_op jit(solution)/shard_map/ppermute | solution.py:693
  12.1 6.4 %collective-permute-start.1 = (bf16[4,32,160]{2,1,0:T(8,128)(2,1)}, bf16[4,32,160]{2,1,0:T(8,128)(2,1)S(1)}, u32[]{:S(2)}, u32[]{:S(2)}) collective-permute-start(bf16[4,32,160]{2,1,0:T(8,128)(2,1)} %get-tuple-element.42), channel_id=1, source_target_pairs={{1,2},{3,0},{2,1},{0,3},{5,6},{7,4},{6,5},{4,7},{9,10},{11,8},{10,... | collective-permute-start | bytes 122888 | tf_op jit(solution)/shard_map/ppermute | solution.py:693
  21.5 11.6 %collective-permute-start.3 = (bf16[2,152,256]{2,1,0:T(8,128)(2,1)S(1)}, bf16[2,152,256]{2,1,0:T(8,128)(2,1)S(1)}, u32[]{:S(2)}, u32[]{:S(2)}) collective-permute-start(bf16[2,152,256]{2,1,0:T(8,128)(2,1)S(1)} %pad_maximum_fusion), channel_id=1, source_target_pairs={{0,8},{4,12},{8,0},{12,4},{16,24},{20,28},{24,16},{28,20},{1,9},{5... | collective-permute-start | bytes 466952 | tf_op jit(solution)/shard_map/ppermute | solution.py:711
  23.4 9.7 %collective-permute-start.4 = (bf16[2,152,256]{2,1,0:T(8,128)(2,1)S(1)}, bf16[2,152,256]{2,1,0:T(8,128)(2,1)S(1)}, u32[]{:S(2)}, u32[]{:S(2)}) collective-permute-start(bf16[2,152,256]{2,1,0:T(8,128)(2,1)S(1)} %pad_maximum_fusion.1), channel_id=1, source_target_pairs={{0,16},{4,20},{8,24},{12,28},{16,0},{20,4},{24,8},{28,12},{1,17},{... | collective-permute-start | bytes 466952 | tf_op jit(solution)/shard_map/ppermute | solution.py:711
  25.0 9.1 %collective-permute-start.5 = (bf16[2,152,256]{2,1,0:T(8,128)(2,1)S(1)}, bf16[2,152,256]{2,1,0:T(8,128)(2,1)S(1)}, u32[]{:S(2)}, u32[]{:S(2)}) collective-permute-start(bf16[2,152,256]{2,1,0:T(8,128)(2,1)S(1)} %pad_maximum_fusion.2), channel_id=1, source_target_pairs={{0,24},{4,28},{8,16},{12,20},{16,8},{20,12},{24,0},{28,4},{1,25},{... | collective-permute-start | bytes 466952 | tf_op jit(solution)/shard_map/ppermute | solution.py:711
  38.3 4.4 %collective-permute-start.6 = (bf16[136,256]{1,0:T(8,128)(2,1)S(1)}, bf16[136,256]{1,0:T(8,128)(2,1)S(1)}, u32[]{:S(2)}, u32[]{:S(2)}) collective-permute-start(bf16[136,256]{1,0:T(8,128)(2,1)S(1)} %get-tuple-element.46), channel_id=1, source_target_pairs={{0,1},{2,3},{1,0},{3,2},{4,5},{6,7},{5,4},{7,6},{8,9},{10,11},{9,8... | collective-permute-start | bytes 208904 | tf_op jit(solution)/shard_map/ppermute | solution.py:693
  40.3 6.1 %collective-permute-start.7 = (bf16[136,256]{1,0:T(8,128)(2,1)S(1)}, bf16[136,256]{1,0:T(8,128)(2,1)S(1)}, u32[]{:S(2)}, u32[]{:S(2)}) collective-permute-start(bf16[136,256]{1,0:T(8,128)(2,1)S(1)} %get-tuple-element.47), channel_id=1, source_target_pairs={{1,2},{3,0},{2,1},{0,3},{5,6},{7,4},{6,5},{4,7},{9,10},{11,8},{10,... | collective-permute-start | bytes 208904 | tf_op jit(solution)/shard_map/ppermute | solution.py:693
  46.5 3.5 %collective-permute-start.9 = (bf16[2,136,256]{2,1,0:T(8,128)(2,1)S(1)}, bf16[2,136,256]{2,1,0:T(8,128)(2,1)S(1)}, u32[]{:S(2)}, u32[]{:S(2)}) collective-permute-start(bf16[2,136,256]{2,1,0:T(8,128)(2,1)S(1)} %get-tuple-element.49), channel_id=1, source_target_pairs={{4,8},{12,16},{20,24},{8,4},{16,12},{24,20},{5,9},{13,17},{21,25},... | collective-permute-start | bytes 417800 | tf_op jit(solution)/shard_map/ppermute | solution.py:693
  47.4 3.0 %collective-permute-start.8 = (bf16[2,136,256]{2,1,0:T(8,128)(2,1)S(1)}, bf16[2,136,256]{2,1,0:T(8,128)(2,1)S(1)}, u32[]{:S(2)}, u32[]{:S(2)}) collective-permute-start(bf16[2,136,256]{2,1,0:T(8,128)(2,1)S(1)} %get-tuple-element.49), channel_id=1, source_target_pairs={{0,4},{8,12},{16,20},{24,28},{4,0},{12,8},{20,16},{28,24},{1,5},{9... | collective-permute-start | bytes 417800 | tf_op jit(solution)/shard_map/ppermute | solution.py:693
  56.5 17.4 %collective-permute-start.17 = (bf16[240,256]{1,0:T(8,128)(2,1)S(1)}, bf16[240,256]{1,0:T(8,128)(2,1)S(1)}, u32[]{:S(2)}, u32[]{:S(2)}) collective-permute-start(bf16[240,256]{1,0:T(8,128)(2,1)S(1)} %get-tuple-element.65), channel_id=1, source_target_pairs={{0,24},{4,28},{8,16},{12,20},{16,8},{20,12},{24,0},{28,4},{1,25},{... | collective-permute-start | bytes 368648 | tf_op jit(solution)/shard_map/ppermute | solution.py:711
  60.8 13.5 %collective-permute-start.18 = (bf16[240,256]{1,0:T(8,128)(2,1)S(1)}, bf16[240,256]{1,0:T(8,128)(2,1)S(1)}, u32[]{:S(2)}, u32[]{:S(2)}) collective-permute-start(bf16[240,256]{1,0:T(8,128)(2,1)S(1)} %get-tuple-element.66), channel_id=1, source_target_pairs={{0,28},{4,24},{8,20},{12,16},{16,12},{20,8},{24,4},{28,0},{1,29},{... | collective-permute-start | bytes 368648 | tf_op jit(solution)/shard_map/ppermute | solution.py:711
  62.8 7.1 %collective-permute-start.10 = (bf16[216,256]{1,0:T(8,128)(2,1)S(1)}, bf16[216,256]{1,0:T(8,128)(2,1)S(1)}, u32[]{:S(2)}, u32[]{:S(2)}) collective-permute-start(bf16[216,256]{1,0:T(8,128)(2,1)S(1)} %get-tuple-element.57), channel_id=1, source_target_pairs={{0,24},{4,28},{8,16},{12,20},{16,8},{20,12},{24,0},{28,4},{1,25},{... | collective-permute-start | bytes 331784 | tf_op jit(solution)/shard_map/ppermute | solution.py:711
  63.3 8.9 %collective-permute-start.11 = (bf16[216,256]{1,0:T(8,128)(2,1)S(1)}, bf16[216,256]{1,0:T(8,128)(2,1)S(1)}, u32[]{:S(2)}, u32[]{:S(2)}) collective-permute-start(bf16[216,256]{1,0:T(8,128)(2,1)S(1)} %get-tuple-element.58), channel_id=1, source_target_pairs={{0,28},{4,24},{8,20},{12,16},{16,12},{20,8},{24,4},{28,0},{1,29},{... | collective-permute-start | bytes 331784 | tf_op jit(solution)/shard_map/ppermute | solution.py:711
  65.4 9.1 %collective-permute-start.19 = (bf16[240,256]{1,0:T(8,128)(2,1)S(1)}, bf16[240,256]{1,0:T(8,128)(2,1)S(1)}, u32[]{:S(2)}, u32[]{:S(2)}) collective-permute-start(bf16[240,256]{1,0:T(8,128)(2,1)S(1)} %get-tuple-element.67), channel_id=1, source_target_pairs={{0,8},{4,12},{8,0},{12,4},{16,24},{20,28},{24,16},{28,20},{1,9},{5... | collective-permute-start | bytes 368648 | tf_op jit(solution)/shard_map/ppermute | solution.py:711
  70.0 6.3 %collective-permute-start.20 = (bf16[240,256]{1,0:T(8,128)(2,1)S(1)}, bf16[240,256]{1,0:T(8,128)(2,1)S(1)}, u32[]{:S(2)}, u32[]{:S(2)}) collective-permute-start(bf16[240,256]{1,0:T(8,128)(2,1)S(1)} %get-tuple-element.68), channel_id=1, source_target_pairs={{0,16},{4,20},{8,24},{12,28},{16,0},{20,4},{24,8},{28,12},{1,17},{... | collective-permute-start | bytes 368648 | tf_op jit(solution)/shard_map/ppermute | solution.py:711
  72.1 5.4 %collective-permute-start.21 = (bf16[240,256]{1,0:T(8,128)(2,1)S(1)}, bf16[240,256]{1,0:T(8,128)(2,1)S(1)}, u32[]{:S(2)}, u32[]{:S(2)}) collective-permute-start(bf16[240,256]{1,0:T(8,128)(2,1)S(1)} %get-tuple-element.69), channel_id=1, source_target_pairs={{0,12},{4,8},{8,4},{12,0},{16,28},{20,24},{24,20},{28,16},{1,13},{... | collective-permute-start | bytes 368648 | tf_op jit(solution)/shard_map/ppermute | solution.py:711
  73.9 5.8 %collective-permute-start.22 = (bf16[240,256]{1,0:T(8,128)(2,1)S(1)}, bf16[240,256]{1,0:T(8,128)(2,1)S(1)}, u32[]{:S(2)}, u32[]{:S(2)}) collective-permute-start(bf16[240,256]{1,0:T(8,128)(2,1)S(1)} %get-tuple-element.70), channel_id=1, source_target_pairs={{0,20},{4,16},{8,28},{12,24},{16,4},{20,0},{24,12},{28,8},{1,21},{... | collective-permute-start | bytes 368648 | tf_op jit(solution)/shard_map/ppermute | solution.py:711
  74.3 5.6 %collective-permute-start.23 = (bf16[240,256]{1,0:T(8,128)(2,1)S(1)}, bf16[240,256]{1,0:T(8,128)(2,1)S(1)}, u32[]{:S(2)}, u32[]{:S(2)}) collective-permute-start(bf16[240,256]{1,0:T(8,128)(2,1)S(1)} %get-tuple-element.71), channel_id=1, source_target_pairs={{0,4},{4,0},{8,12},{12,8},{16,20},{20,16},{24,28},{28,24},{1,5},{5... | collective-permute-start | bytes 368648 | tf_op jit(solution)/shard_map/ppermute | solution.py:711
  74.5 7.2 %collective-permute-start.12 = (bf16[216,256]{1,0:T(8,128)(2,1)S(1)}, bf16[216,256]{1,0:T(8,128)(2,1)S(1)}, u32[]{:S(2)}, u32[]{:S(2)}) collective-permute-start(bf16[216,256]{1,0:T(8,128)(2,1)S(1)} %get-tuple-element.59), channel_id=1, source_target_pairs={{0,8},{4,12},{8,0},{12,4},{16,24},{20,28},{24,16},{28,20},{1,9},{5... | collective-permute-start | bytes 331784 | tf_op jit(solution)/shard_map/ppermute | solution.py:711
  76.2 5.6 %collective-permute-start.13 = (bf16[216,256]{1,0:T(8,128)(2,1)S(1)}, bf16[216,256]{1,0:T(8,128)(2,1)S(1)}, u32[]{:S(2)}, u32[]{:S(2)}) collective-permute-start(bf16[216,256]{1,0:T(8,128)(2,1)S(1)} %get-tuple-element.60), channel_id=1, source_target_pairs={{0,16},{4,20},{8,24},{12,28},{16,0},{20,4},{24,8},{28,12},{1,17},{... | collective-permute-start | bytes 331784 | tf_op jit(solution)/shard_map/ppermute | solution.py:711
  77.6 5.6 %collective-permute-start.14 = (bf16[216,256]{1,0:T(8,128)(2,1)S(1)}, bf16[216,256]{1,0:T(8,128)(2,1)S(1)}, u32[]{:S(2)}, u32[]{:S(2)}) collective-permute-start(bf16[216,256]{1,0:T(8,128)(2,1)S(1)} %get-tuple-element.61), channel_id=1, source_target_pairs={{0,12},{4,8},{8,4},{12,0},{16,28},{20,24},{24,20},{28,16},{1,13},{... | collective-permute-start | bytes 331784 | tf_op jit(solution)/shard_map/ppermute | solution.py:711
  79.7 4.9 %collective-permute-start.15 = (bf16[216,256]{1,0:T(8,128)(2,1)S(1)}, bf16[216,256]{1,0:T(8,128)(2,1)S(1)}, u32[]{:S(2)}, u32[]{:S(2)}) collective-permute-start(bf16[216,256]{1,0:T(8,128)(2,1)S(1)} %get-tuple-element.62), channel_id=1, source_target_pairs={{0,20},{4,16},{8,28},{12,24},{16,4},{20,0},{24,12},{28,8},{1,21},{... | collective-permute-start | bytes 331784 | tf_op jit(solution)/shard_map/ppermute | solution.py:711
  79.9 4.7 %collective-permute-start.16 = (bf16[216,256]{1,0:T(8,128)(2,1)S(1)}, bf16[216,256]{1,0:T(8,128)(2,1)S(1)}, u32[]{:S(2)}, u32[]{:S(2)}) collective-permute-start(bf16[216,256]{1,0:T(8,128)(2,1)S(1)} %get-tuple-element.63), channel_id=1, source_target_pairs={{0,4},{4,0},{8,12},{12,8},{16,20},{20,16},{24,28},{28,24},{1,5},{5... | collective-permute-start | bytes 331784 | tf_op jit(solution)/shard_map/ppermute | solution.py:711
  (7 other events, 86.4 us)

commit v15 on v12

--- a/solution.py
+++ b/solution.py
@@ -316,11 +316,11 @@
     batch = columns // 5
     pieces = [pltpu.make_async_copy(depth, deep, arrived.at[5])]
     for k in range(5):
-        span = pl.ds(k * batch, batch)
+        span = pl.ds(k * batch, batch if k else 2)
         piece = pltpu.make_async_copy(ens.at[:, span], here.at[:, span], arrived.at[k])
         pieces.append(piece)
-    for piece in pieces:
-        piece.start()
+    for k in (0, 2, 3, 4, 5, 1):
+        pieces[k].start()
     shift = difference(latitudes)
     turning = turning_row(latitudes)
     eye = identity(latitudes, BF16)
@@ -338,7 +338,7 @@
 
     staged[:, 300:INNER, :] = jnp.zeros((8, INNER - 300, 256), F32)
     done = 2
-    for k in range(5):
+    for k in (1, 2, 3, 4, 0):
         pieces[k + 1].wait()
         first, count = k * batch, batch if k else 2
         flux[first : first + count] = fluxes(here[1, first : first + count], depths(first, count))
@@ -594,7 +594,7 @@
         square = jnp.sum(jnp.sum(system * system, axis=0, keepdims=True), axis=1, keepdims=True)
         norms.append(jnp.sqrt(square))
         pulls.append(pull)
-        roots.append(system / norms[t])
+        roots.append(system * (1.0 / norms[t]))
     for sweep in range(SWEEPS):
         rights = [right_3(split(root)) for root in roots]
         if sweep == 0:

time: 86.2 us -> 86.1 us (level)
  no operation moved by 1% of the time
where the time goes in v15:
time: 86.1 us; the launch traced here: 85.8 us
  starting transfers between devices  36.5 us (42%)
  Pallas kernels  26.8 us (31%)
  waiting for transfers between devices  20.7 us (24%)
  other arithmetic  1.44 us (2%)
    ppermute x18, starting transfers between devices, across(): return lax.ppermute(value, 'mem', [(i, i ^ difference) for i in range(8)])  19.3 us
    ppermute x6, starting transfers between devices, swapped_pairs(): moved.append(lax.ppermute(value, axis, both))  12 us
    ppermute x18, waiting for transfers between devices, across(): return lax.ppermute(value, 'mem', [(i, i ^ difference) for i in range(8)])  11.3 us
    ppermute x6, waiting for transfers between devices, swapped_pairs(): moved.append(lax.ppermute(value, axis, both))  6.64 us
    pallas_call x1, Pallas kernels, on_device_fast(): pl.pallas_call(analyse_kernel, out_shape=(jax.ShapeDtypeStruct((FIRST, 25...  6.05 us
    all_to_all x1, starting transfers between devices, swap(): return lax.all_to_all(value, 'mem', split_axis=0, concat_axis=0, tiled=True)  5.19 us
    pallas_call x1, Pallas kernels, on_device_fast(): pl.pallas_call(spread_kernel, out_shape=(jax.ShapeDtypeStruct((8, INNER,...  5.04 us
    pallas_call x1, Pallas kernels, on_device_fast(): pl.pallas_call(inner_kernel, out_shape=(jax.ShapeDtypeStruct((8, INNER, 2...  4.63 us
  transfers between devices with their start and end apart: 25, of which 13 were waited for; matrix products, arithmetic and copies ran while one was open for 2% of the time, Pallas kernels for 12%

profile of v15, /device:TPU:0, one launch (start us, length us, event | category | flops | bytes accessed | tf_op | source)
XLA Modules:
  0.0 85.8 jit_solution(4340979818963637824)
XLA Ops:
  0.0 4.6 %inner.1 = (bf16[8,304,256]{2,1,0:T(8,128)(2,1)}, bf16[4,32,160]{2,1,0:T(8,128)(2,1)}, bf16[4,32,160]{2,1,0:T(8,128)(2,1)}) custom-call(bf16[3,60,32,160]{3,2,1,0:T(8,128)(2,1)} %bitcast.49, f32[60,160]{1,0:T(8,128)} %depth.3), custom_call_target="tpu_custom_call" | custom-call | tf_op jit(solution)/shard_map/inner/pallas_call | solution.py:748
  4.6 5.2 %all-to-all-start = ((bf16[8,304,256]{2,1,0:T(8,128)(2,1)}), bf16[8,304,256]{2,1,0:T(8,128)(2,1)}, u32[]{:S(2)}, u32[]{:S(2)}) async-start(bf16[8,304,256]{2,1,0:T(8,128)(2,1)} %get-tuple-element.41), calls=%async_computation | async-start | bytes 2490368 | tf_op jit(solution)/shard_map/all_to_all | solution.py:719
  9.8 2.2 %collective-permute-start = (bf16[4,32,160]{2,1,0:T(8,128)(2,1)}, bf16[4,32,160]{2,1,0:T(8,128)(2,1)S(1)}, u32[]{:S(2)}, u32[]{:S(2)}) collective-permute-start(bf16[4,32,160]{2,1,0:T(8,128)(2,1)} %get-tuple-element.43), channel_id=1, source_target_pairs={{0,1},{2,3},{1,0},{3,2},{4,5},{6,7},{5,4},{7,6},{8,9},{10,11},{9,8... | collective-permute-start | bytes 122888 | tf_op jit(solution)/shard_map/ppermute | solution.py:693
  12.0 2.5 %collective-permute-start.1 = (bf16[4,32,160]{2,1,0:T(8,128)(2,1)}, bf16[4,32,160]{2,1,0:T(8,128)(2,1)S(1)}, u32[]{:S(2)}, u32[]{:S(2)}) collective-permute-start(bf16[4,32,160]{2,1,0:T(8,128)(2,1)} %get-tuple-element.44), channel_id=1, source_target_pairs={{1,2},{3,0},{2,1},{0,3},{5,6},{7,4},{6,5},{4,7},{9,10},{11,8},{10,... | collective-permute-start | bytes 122888 | tf_op jit(solution)/shard_map/ppermute | solution.py:693
  15.8 2.7 %collective-permute-done.1.second_swap = bf16[4,32,160]{2,1,0:T(8,128)(2,1)S(1)} collective-permute-done((bf16[4,32,160]{2,1,0:T(8,128)(2,1)}, bf16[4,32,160]{2,1,0:T(8,128)(2,1)S(1)}, u32[]{:S(2)}, u32[]{:S(2)}) %collective-permute-start.1) | collective-permute-done | bytes 40992 | tf_op jit(solution)/shard_map/ppermute | solution.py:693
  21.4 1.9 %collective-permute-start.3 = (bf16[2,152,256]{2,1,0:T(8,128)(2,1)S(1)}, bf16[2,152,256]{2,1,0:T(8,128)(2,1)S(1)}, u32[]{:S(2)}, u32[]{:S(2)}) collective-permute-start(bf16[2,152,256]{2,1,0:T(8,128)(2,1)S(1)} %pad_maximum_fusion), channel_id=1, source_target_pairs={{0,8},{4,12},{8,0},{12,4},{16,24},{20,28},{24,16},{28,20},{1,9},{5... | collective-permute-start | bytes 466952 | tf_op jit(solution)/shard_map/ppermute | solution.py:711
  25.2 2.7 %all-to-all-done.got = bf16[8,304,256]{2,1,0:T(8,128)(2,1)} async-done(((bf16[8,304,256]{2,1,0:T(8,128)(2,1)}), bf16[8,304,256]{2,1,0:T(8,128)(2,1)}, u32[]{:S(2)}, u32[]{:S(2)}) %all-to-all-start) | async-done | bytes 1245216 | tf_op jit(solution)/shard_map/all_to_all | solution.py:719
  27.9 5.0 %spread.1 = (bf16[8,304,256]{2,1,0:T(8,128)(2,1)S(1)}, f32[2,2,512,128]{3,2,1,0:T(8,128)S(1)}) custom-call(s32[2,512]{1,0:T(2,128)S(1)} %get-tuple-element.77.cells, bf16[8,304,256]{2,1,0:T(8,128)(2,1)} %all-to-all-done.got), custom_call_target="tpu_custom_call" | custom-call | flops 1 | bytes 8388608 | tf_op jit(solution)/shard_map/spread/pallas_call | solution.py:808
  34.0 4.0 %observe.1 = (bf16[8,152,256]{2,1,0:T(8,128)(2,1)S(1)}, f32[2,136,256]{2,1,0:T(8,128)S(1)}, bf16[136,256]{1,0:T(8,128)(2,1)S(1)}, bf16[136,256]{1,0:T(8,128)(2,1)S(1)}) custom-call(s32[2,640]{1,0:T(2,128)S(1)} %pad.4.cells, s32[2,640]{1,0:T(2,128)S(1)} %fusion.3.outer, f32[2,512]{1,0:T(2,128)S(1)} %fusion.12.weight, f32[2,512]{1,0:T(2,128)S(1)} %bitcast.52, ...), custom_call_target="tpu_custom_call" | custom-call | tf_op jit(solution)/shard_map/observe/pallas_call | solution.py:821
  38.1 2.1 %collective-permute-start.6 = (bf16[136,256]{1,0:T(8,128)(2,1)S(1)}, bf16[136,256]{1,0:T(8,128)(2,1)S(1)}, u32[]{:S(2)}, u32[]{:S(2)}) collective-permute-start(bf16[136,256]{1,0:T(8,128)(2,1)S(1)} %get-tuple-element.48), channel_id=1, source_target_pairs={{0,1},{2,3},{1,0},{3,2},{4,5},{6,7},{5,4},{7,6},{8,9},{10,11},{9,8... | collective-permute-start | bytes 208904 | tf_op jit(solution)/shard_map/ppermute | solution.py:693
  40.2 2.5 %collective-permute-start.7 = (bf16[136,256]{1,0:T(8,128)(2,1)S(1)}, bf16[136,256]{1,0:T(8,128)(2,1)S(1)}, u32[]{:S(2)}, u32[]{:S(2)}) collective-permute-start(bf16[136,256]{1,0:T(8,128)(2,1)S(1)} %get-tuple-element.49), channel_id=1, source_target_pairs={{1,2},{3,0},{2,1},{0,3},{5,6},{7,4},{6,5},{4,7},{9,10},{11,8},{10,... | collective-permute-start | bytes 208904 | tf_op jit(solution)/shard_map/ppermute | solution.py:693
  42.7 3.6 %collective-permute-done.7.second_swap = bf16[136,256]{1,0:T(8,128)(2,1)S(1)} collective-permute-done((bf16[136,256]{1,0:T(8,128)(2,1)S(1)}, bf16[136,256]{1,0:T(8,128)(2,1)S(1)}, u32[]{:S(2)}, u32[]{:S(2)}) %collective-permute-start.7) | collective-permute-done | bytes 69664 | tf_op jit(solution)/shard_map/ppermute | solution.py:693
  47.2 1.9 %collective-permute-start.8 = (bf16[2,136,256]{2,1,0:T(8,128)(2,1)S(1)}, bf16[2,136,256]{2,1,0:T(8,128)(2,1)S(1)}, u32[]{:S(2)}, u32[]{:S(2)}) collective-permute-start(bf16[2,136,256]{2,1,0:T(8,128)(2,1)S(1)} %get-tuple-element.51), channel_id=1, source_target_pairs={{0,4},{8,12},{16,20},{24,28},{4,0},{12,8},{20,16},{28,24},{1,5},{9... | collective-permute-start | bytes 417800 | tf_op jit(solution)/shard_map/ppermute | solution.py:693
  50.1 6.1 %analyse.1 = (bf16[240,256]{1,0:T(8,128)(2,1)S(1)}, bf16[240,256]{1,0:T(8,128)(2,1)S(1)}, bf16[240,256]{1,0:T(8,128)(2,1)S(1)}, bf16[240,256]{1,0:T(8,128)(2,1)S...) custom-call(f32[2,136,256]{2,1,0:T(8,128)S(1)} %get-tuple-element.50, ...), custom_call_target="tpu_custom_call" | custom-call | tf_op jit(solution)/shard_map/analyse/pallas_call | solution.py:861
  56.2 2.1 %collective-permute-start.10 = (bf16[240,256]{1,0:T(8,128)(2,1)S(1)}, bf16[240,256]{1,0:T(8,128)(2,1)S(1)}, u32[]{:S(2)}, u32[]{:S(2)}) collective-permute-start(bf16[240,256]{1,0:T(8,128)(2,1)S(1)} %get-tuple-element.57), channel_id=1, source_target_pairs={{0,4},{4,0},{8,12},{12,8},{16,20},{20,16},{24,28},{28,24},{1,5},{5... | collective-permute-start | bytes 368648 | tf_op jit(solution)/shard_map/ppermute | solution.py:711
  58.3 2.5 %collective-permute-start.18 = (bf16[240,256]{1,0:T(8,128)(2,1)S(1)}, bf16[240,256]{1,0:T(8,128)(2,1)S(1)}, u32[]{:S(2)}, u32[]{:S(2)}) collective-permute-start(bf16[240,256]{1,0:T(8,128)(2,1)S(1)} %get-tuple-element.69), channel_id=1, source_target_pairs={{0,24},{4,28},{8,16},{12,20},{16,8},{20,12},{24,0},{28,4},{1,25},{... | collective-permute-start | bytes 368648 | tf_op jit(solution)/shard_map/ppermute | solution.py:711
  60.8 1.6 %collective-permute-start.19 = (bf16[240,256]{1,0:T(8,128)(2,1)S(1)}, bf16[240,256]{1,0:T(8,128)(2,1)S(1)}, u32[]{:S(2)}, u32[]{:S(2)}) collective-permute-start(bf16[240,256]{1,0:T(8,128)(2,1)S(1)} %get-tuple-element.70), channel_id=1, source_target_pairs={{0,8},{4,12},{8,0},{12,4},{16,24},{20,28},{24,16},{28,20},{1,9},{5... | collective-permute-start | bytes 368648 | tf_op jit(solution)/shard_map/ppermute | solution.py:711
  63.5 2.1 %collective-permute-start.22 = (bf16[240,256]{1,0:T(8,128)(2,1)S(1)}, bf16[240,256]{1,0:T(8,128)(2,1)S(1)}, u32[]{:S(2)}, u32[]{:S(2)}) collective-permute-start(bf16[240,256]{1,0:T(8,128)(2,1)S(1)} %get-tuple-element.74), channel_id=1, source_target_pairs={{0,12},{4,8},{8,4},{12,0},{16,28},{20,24},{24,20},{28,16},{1,13},{... | collective-permute-start | bytes 368648 | tf_op jit(solution)/shard_map/ppermute | solution.py:711
  66.8 1.8 %second.1 = (bf16[216,256]{1,0:T(8,128)(2,1)S(1)}, bf16[216,256]{1,0:T(8,128)(2,1)S(1)}, bf16[216,256]{1,0:T(8,128)(2,1)S(1)}, bf16[216,256]{1,0:T(8,128)(2,1)S(...) custom-call(bf16[2,256,256]{2,1,0:T(8,128)(2,1)S(1)} %get-tuple-elem, ...), custom_call_target="tpu_custom_call" | custom-call | flops 1 | bytes 6291456 | tf_op jit(solution)/shard_map/second/pallas_call | solution.py:871
  73.6 1.6 %collective-permute-start.14 = (bf16[216,256]{1,0:T(8,128)(2,1)S(1)}, bf16[216,256]{1,0:T(8,128)(2,1)S(1)}, u32[]{:S(2)}, u32[]{:S(2)}) collective-permute-start(bf16[216,256]{1,0:T(8,128)(2,1)S(1)} %get-tuple-element.64), channel_id=1, source_target_pairs={{0,28},{4,24},{8,20},{12,16},{16,12},{20,8},{24,4},{28,0},{1,29},{... | collective-permute-start | bytes 331784 | tf_op jit(solution)/shard_map/ppermute | solution.py:711
  76.1 3.2 %collective-permute-done.12.refs_1_ = bf16[216,256]{1,0:T(8,128)(2,1)S(1)} collective-permute-done((bf16[216,256]{1,0:T(8,128)(2,1)S(1)}, bf16[216,256]{1,0:T(8,128)(2,1)S(1)}, u32[]{:S(2)}, u32[]{:S(2)}) %collective-permute-start.12) | collective-permute-done | bytes 110624 | tf_op jit(solution)/shard_map/ppermute | solution.py:711
  79.3 1.6 %first_return.1.refs_8_ = bf16[3,60,32,160]{3,2,1,0:T(8,128)(2,1)} custom-call(bf16[240,256]{1,0:T(8,128)(2,1)S(1)} %collective-permute-done.18.refs_0_, bf16[240,256]{1,0:T(8,128)(2,1)S(1)} %collective-permute-done.19.refs_1_, bf16[240,256]{1,0:T(8,128)(2,1)S(1)} %collective-permute-done.20.refs_2_, bf16[240,256]{1,0:T(8,128)(2,1)S(1)} %collective-permute-done.21.refs_3_, ...), custom_call_target="tpu_custom_call" | custom-call | flops 1 | bytes 4194304 | tf_op jit(solution)/shard_map/first_return/pallas_call | solution.py:881
  81.0 2.2 %collective-permute-done.16.refs_5_ = bf16[216,256]{1,0:T(8,128)(2,1)S(1)} collective-permute-done((bf16[216,256]{1,0:T(8,128)(2,1)S(1)}, bf16[216,256]{1,0:T(8,128)(2,1)S(1)}, u32[]{:S(2)}, u32[]{:S(2)}) %collective-permute-start.16) | collective-permute-done | bytes 110624 | tf_op jit(solution)/shard_map/ppermute | solution.py:711
  84.0 1.6 %second_return.1 = bf16[3,60,32,160]{3,2,1,0:T(8,128)(2,1)} custom-call(bf16[216,256]{1,0:T(8,128)(2,1)S(1)} %collective-permute-done.11.refs_0_, bf16[216,256]{1,0:T(8,128)(2,1)S(1)} %collective-permute-done.12.refs_1_, bf16[216,256]{1,0:T(8,128)(2,1)S(1)} %collective-permute-done.13.refs_2_, ...), custom_call_target="tpu_custom_call", output_to_operand_aliasing={{}: (8, {})} | custom-call | tf_op jit(solution)/shard_map/second_return/pallas_call | solution.py:895
  (64 shorter events, 18.0 us)
Async XLA Ops:
  4.6 23.3 %all-to-all-start = ((bf16[8,304,256]{2,1,0:T(8,128)(2,1)}), bf16[8,304,256]{2,1,0:T(8,128)(2,1)}, u32[]{:S(2)}, u32[]{:S(2)}) async-start(bf16[8,304,256]{2,1,0:T(8,128)(2,1)} %get-tuple-element.41), calls=%async_computation | async-start | bytes 2490368 | tf_op jit(solution)/shard_map/all_to_all | solution.py:719
  9.8 5.9 %collective-permute-start = (bf16[4,32,160]{2,1,0:T(8,128)(2,1)}, bf16[4,32,160]{2,1,0:T(8,128)(2,1)S(1)}, u32[]{:S(2)}, u32[]{:S(2)}) collective-permute-start(bf16[4,32,160]{2,1,0:T(8,128)(2,1)} %get-tuple-element.43), channel_id=1, source_target_pairs={{0,1},{2,3},{1,0},{3,2},{4,5},{6,7},{5,4},{7,6},{8,9},{10,11},{9,8... | collective-permute-start | bytes 122888 | tf_op jit(solution)/shard_map/ppermute | solution.py:693
  12.0 6.4 %collective-permute-start.1 = (bf16[4,32,160]{2,1,0:T(8,128)(2,1)}, bf16[4,32,160]{2,1,0:T(8,128)(2,1)S(1)}, u32[]{:S(2)}, u32[]{:S(2)}) collective-permute-start(bf16[4,32,160]{2,1,0:T(8,128)(2,1)} %get-tuple-element.44), channel_id=1, source_target_pairs={{1,2},{3,0},{2,1},{0,3},{5,6},{7,4},{6,5},{4,7},{9,10},{11,8},{10,... | collective-permute-start | bytes 122888 | tf_op jit(solution)/shard_map/ppermute | solution.py:693
  21.4 11.6 %collective-permute-start.3 = (bf16[2,152,256]{2,1,0:T(8,128)(2,1)S(1)}, bf16[2,152,256]{2,1,0:T(8,128)(2,1)S(1)}, u32[]{:S(2)}, u32[]{:S(2)}) collective-permute-start(bf16[2,152,256]{2,1,0:T(8,128)(2,1)S(1)} %pad_maximum_fusion), channel_id=1, source_target_pairs={{0,8},{4,12},{8,0},{12,4},{16,24},{20,28},{24,16},{28,20},{1,9},{5... | collective-permute-start | bytes 466952 | tf_op jit(solution)/shard_map/ppermute | solution.py:711
  23.3 9.7 %collective-permute-start.4 = (bf16[2,152,256]{2,1,0:T(8,128)(2,1)S(1)}, bf16[2,152,256]{2,1,0:T(8,128)(2,1)S(1)}, u32[]{:S(2)}, u32[]{:S(2)}) collective-permute-start(bf16[2,152,256]{2,1,0:T(8,128)(2,1)S(1)} %pad_maximum_fusion.1), channel_id=1, source_target_pairs={{0,16},{4,20},{8,24},{12,28},{16,0},{20,4},{24,8},{28,12},{1,17},{... | collective-permute-start | bytes 466952 | tf_op jit(solution)/shard_map/ppermute | solution.py:711
  24.9 9.1 %collective-permute-start.5 = (bf16[2,152,256]{2,1,0:T(8,128)(2,1)S(1)}, bf16[2,152,256]{2,1,0:T(8,128)(2,1)S(1)}, u32[]{:S(2)}, u32[]{:S(2)}) collective-permute-start(bf16[2,152,256]{2,1,0:T(8,128)(2,1)S(1)} %pad_maximum_fusion.2), channel_id=1, source_target_pairs={{0,24},{4,28},{8,16},{12,20},{16,8},{20,12},{24,0},{28,4},{1,25},{... | collective-permute-start | bytes 466952 | tf_op jit(solution)/shard_map/ppermute | solution.py:711
  38.1 4.6 %collective-permute-start.6 = (bf16[136,256]{1,0:T(8,128)(2,1)S(1)}, bf16[136,256]{1,0:T(8,128)(2,1)S(1)}, u32[]{:S(2)}, u32[]{:S(2)}) collective-permute-start(bf16[136,256]{1,0:T(8,128)(2,1)S(1)} %get-tuple-element.48), channel_id=1, source_target_pairs={{0,1},{2,3},{1,0},{3,2},{4,5},{6,7},{5,4},{7,6},{8,9},{10,11},{9,8... | collective-permute-start | bytes 208904 | tf_op jit(solution)/shard_map/ppermute | solution.py:693
  40.2 6.1 %collective-permute-start.7 = (bf16[136,256]{1,0:T(8,128)(2,1)S(1)}, bf16[136,256]{1,0:T(8,128)(2,1)S(1)}, u32[]{:S(2)}, u32[]{:S(2)}) collective-permute-start(bf16[136,256]{1,0:T(8,128)(2,1)S(1)} %get-tuple-element.49), channel_id=1, source_target_pairs={{1,2},{3,0},{2,1},{0,3},{5,6},{7,4},{6,5},{4,7},{9,10},{11,8},{10,... | collective-permute-start | bytes 208904 | tf_op jit(solution)/shard_map/ppermute | solution.py:693
  46.4 3.4 %collective-permute-start.9 = (bf16[2,136,256]{2,1,0:T(8,128)(2,1)S(1)}, bf16[2,136,256]{2,1,0:T(8,128)(2,1)S(1)}, u32[]{:S(2)}, u32[]{:S(2)}) collective-permute-start(bf16[2,136,256]{2,1,0:T(8,128)(2,1)S(1)} %get-tuple-element.51), channel_id=1, source_target_pairs={{4,8},{12,16},{20,24},{8,4},{16,12},{24,20},{5,9},{13,17},{21,25},... | collective-permute-start | bytes 417800 | tf_op jit(solution)/shard_map/ppermute | solution.py:693
  47.2 2.9 %collective-permute-start.8 = (bf16[2,136,256]{2,1,0:T(8,128)(2,1)S(1)}, bf16[2,136,256]{2,1,0:T(8,128)(2,1)S(1)}, u32[]{:S(2)}, u32[]{:S(2)}) collective-permute-start(bf16[2,136,256]{2,1,0:T(8,128)(2,1)S(1)} %get-tuple-element.51), channel_id=1, source_target_pairs={{0,4},{8,12},{16,20},{24,28},{4,0},{12,8},{20,16},{28,24},{1,5},{9... | collective-permute-start | bytes 417800 | tf_op jit(solution)/shard_map/ppermute | solution.py:693
  56.2 7.3 %collective-permute-start.10 = (bf16[240,256]{1,0:T(8,128)(2,1)S(1)}, bf16[240,256]{1,0:T(8,128)(2,1)S(1)}, u32[]{:S(2)}, u32[]{:S(2)}) collective-permute-start(bf16[240,256]{1,0:T(8,128)(2,1)S(1)} %get-tuple-element.57), channel_id=1, source_target_pairs={{0,4},{4,0},{8,12},{12,8},{16,20},{20,16},{24,28},{28,24},{1,5},{5... | collective-permute-start | bytes 368648 | tf_op jit(solution)/shard_map/ppermute | solution.py:711
  58.3 7.3 %collective-permute-start.18 = (bf16[240,256]{1,0:T(8,128)(2,1)S(1)}, bf16[240,256]{1,0:T(8,128)(2,1)S(1)}, u32[]{:S(2)}, u32[]{:S(2)}) collective-permute-start(bf16[240,256]{1,0:T(8,128)(2,1)S(1)} %get-tuple-element.69), channel_id=1, source_target_pairs={{0,24},{4,28},{8,16},{12,20},{16,8},{20,12},{24,0},{28,4},{1,25},{... | collective-permute-start | bytes 368648 | tf_op jit(solution)/shard_map/ppermute | solution.py:711
  60.8 8.4 %collective-permute-start.19 = (bf16[240,256]{1,0:T(8,128)(2,1)S(1)}, bf16[240,256]{1,0:T(8,128)(2,1)S(1)}, u32[]{:S(2)}, u32[]{:S(2)}) collective-permute-start(bf16[240,256]{1,0:T(8,128)(2,1)S(1)} %get-tuple-element.70), channel_id=1, source_target_pairs={{0,8},{4,12},{8,0},{12,4},{16,24},{20,28},{24,16},{28,20},{1,9},{5... | collective-permute-start | bytes 368648 | tf_op jit(solution)/shard_map/ppermute | solution.py:711
  62.4 8.2 %collective-permute-start.20 = (bf16[240,256]{1,0:T(8,128)(2,1)S(1)}, bf16[240,256]{1,0:T(8,128)(2,1)S(1)}, u32[]{:S(2)}, u32[]{:S(2)}) collective-permute-start(bf16[240,256]{1,0:T(8,128)(2,1)S(1)} %get-tuple-element.71), channel_id=1, source_target_pairs={{0,16},{4,20},{8,24},{12,28},{16,0},{20,4},{24,8},{28,12},{1,17},{... | collective-permute-start | bytes 368648 | tf_op jit(solution)/shard_map/ppermute | solution.py:711
  62.4 9.0 %collective-permute-start.21 = (bf16[240,256]{1,0:T(8,128)(2,1)S(1)}, bf16[240,256]{1,0:T(8,128)(2,1)S(1)}, u32[]{:S(2)}, u32[]{:S(2)}) collective-permute-start(bf16[240,256]{1,0:T(8,128)(2,1)S(1)} %get-tuple-element.72), channel_id=1, source_target_pairs={{0,28},{4,24},{8,20},{12,16},{16,12},{20,8},{24,4},{28,0},{1,29},{... | collective-permute-start | bytes 368648 | tf_op jit(solution)/shard_map/ppermute | solution.py:711
  63.5 10.1 %collective-permute-start.22 = (bf16[240,256]{1,0:T(8,128)(2,1)S(1)}, bf16[240,256]{1,0:T(8,128)(2,1)S(1)}, u32[]{:S(2)}, u32[]{:S(2)}) collective-permute-start(bf16[240,256]{1,0:T(8,128)(2,1)S(1)} %get-tuple-element.74), channel_id=1, source_target_pairs={{0,12},{4,8},{8,4},{12,0},{16,28},{20,24},{24,20},{28,16},{1,13},{... | collective-permute-start | bytes 368648 | tf_op jit(solution)/shard_map/ppermute | solution.py:711
  65.6 9.6 %collective-permute-start.23 = (bf16[240,256]{1,0:T(8,128)(2,1)S(1)}, bf16[240,256]{1,0:T(8,128)(2,1)S(1)}, u32[]{:S(2)}, u32[]{:S(2)}) collective-permute-start(bf16[240,256]{1,0:T(8,128)(2,1)S(1)} %get-tuple-element.75), channel_id=1, source_target_pairs={{0,20},{4,16},{8,28},{12,24},{16,4},{20,0},{24,12},{28,8},{1,21},{... | collective-permute-start | bytes 368648 | tf_op jit(solution)/shard_map/ppermute | solution.py:711
  69.2 6.9 %collective-permute-start.11 = (bf16[216,256]{1,0:T(8,128)(2,1)S(1)}, bf16[216,256]{1,0:T(8,128)(2,1)S(1)}, u32[]{:S(2)}, u32[]{:S(2)}) collective-permute-start(bf16[216,256]{1,0:T(8,128)(2,1)S(1)} %get-tuple-element.61), channel_id=1, source_target_pairs={{0,24},{4,28},{8,16},{12,20},{16,8},{20,12},{24,0},{28,4},{1,25},{... | collective-permute-start | bytes 331784 | tf_op jit(solution)/shard_map/ppermute | solution.py:711
  70.6 8.7 %collective-permute-start.12 = (bf16[216,256]{1,0:T(8,128)(2,1)S(1)}, bf16[216,256]{1,0:T(8,128)(2,1)S(1)}, u32[]{:S(2)}, u32[]{:S(2)}) collective-permute-start(bf16[216,256]{1,0:T(8,128)(2,1)S(1)} %get-tuple-element.62), channel_id=1, source_target_pairs={{0,8},{4,12},{8,0},{12,4},{16,24},{20,28},{24,16},{28,20},{1,9},{5... | collective-permute-start | bytes 331784 | tf_op jit(solution)/shard_map/ppermute | solution.py:711
  71.4 9.5 %collective-permute-start.13 = (bf16[216,256]{1,0:T(8,128)(2,1)S(1)}, bf16[216,256]{1,0:T(8,128)(2,1)S(1)}, u32[]{:S(2)}, u32[]{:S(2)}) collective-permute-start(bf16[216,256]{1,0:T(8,128)(2,1)S(1)} %get-tuple-element.63), channel_id=1, source_target_pairs={{0,16},{4,20},{8,24},{12,28},{16,0},{20,4},{24,8},{28,12},{1,17},{... | collective-permute-start | bytes 331784 | tf_op jit(solution)/shard_map/ppermute | solution.py:711
  73.6 7.3 %collective-permute-start.14 = (bf16[216,256]{1,0:T(8,128)(2,1)S(1)}, bf16[216,256]{1,0:T(8,128)(2,1)S(1)}, u32[]{:S(2)}, u32[]{:S(2)}) collective-permute-start(bf16[216,256]{1,0:T(8,128)(2,1)S(1)} %get-tuple-element.64), channel_id=1, source_target_pairs={{0,28},{4,24},{8,20},{12,16},{16,12},{20,8},{24,4},{28,0},{1,29},{... | collective-permute-start | bytes 331784 | tf_op jit(solution)/shard_map/ppermute | solution.py:711
  75.2 5.7 %collective-permute-start.15 = (bf16[216,256]{1,0:T(8,128)(2,1)S(1)}, bf16[216,256]{1,0:T(8,128)(2,1)S(1)}, u32[]{:S(2)}, u32[]{:S(2)}) collective-permute-start(bf16[216,256]{1,0:T(8,128)(2,1)S(1)} %get-tuple-element.65), channel_id=1, source_target_pairs={{0,4},{4,0},{8,12},{12,8},{16,20},{20,16},{24,28},{28,24},{1,5},{5... | collective-permute-start | bytes 331784 | tf_op jit(solution)/shard_map/ppermute | solution.py:711
  76.1 7.1 %collective-permute-start.16 = (bf16[216,256]{1,0:T(8,128)(2,1)S(1)}, bf16[216,256]{1,0:T(8,128)(2,1)S(1)}, u32[]{:S(2)}, u32[]{:S(2)}) collective-permute-start(bf16[216,256]{1,0:T(8,128)(2,1)S(1)} %get-tuple-element.66), channel_id=1, source_target_pairs={{0,12},{4,8},{8,4},{12,0},{16,28},{20,24},{24,20},{28,16},{1,13},{... | collective-permute-start | bytes 331784 | tf_op jit(solution)/shard_map/ppermute | solution.py:711
  79.3 4.7 %collective-permute-start.17 = (bf16[216,256]{1,0:T(8,128)(2,1)S(1)}, bf16[216,256]{1,0:T(8,128)(2,1)S(1)}, u32[]{:S(2)}, u32[]{:S(2)}) collective-permute-start(bf16[216,256]{1,0:T(8,128)(2,1)S(1)} %get-tuple-element.67), channel_id=1, source_target_pairs={{0,20},{4,16},{8,28},{12,24},{16,4},{20,0},{24,12},{28,8},{1,21},{... | collective-permute-start | bytes 331784 | tf_op jit(solution)/shard_map/ppermute | solution.py:711
  (7 other events, 86.2 us)

commit v16 on v15

--- a/solution.py
+++ b/solution.py
@@ -486,17 +486,22 @@
         spread_block(joined, held, wide, start, lane)
     slots = first.shape[2]
     seen[:, :, 0:slots, :] = first[...]
-    for t in range(2):
-
-        def pick(index, carry):
-            for k in range(8):
-                slot = outer[t, index * 8 + k]
+
+    def pick(index, carry):
+        picked = []
+        for k in range(4):
+            for t in range(2):
+                slot = outer[t, index * 4 + k]
                 row = cells[t, slot] - 8 * INNER
-                for h in range(2):
-                    seen[t, h, pl.ds(slot, 1), :] = wide[h, pl.ds(row, 1), :]
-            return carry
-
-        lax.fori_loop(0, (outer[t, slots + LANES - 1] + 7) // 8, pick, 0)
+                picked.append((t, slot, [wide[h, pl.ds(row, 1), :] for h in range(2)]))
+        for t, slot, halves in picked:
+            for h in range(2):
+                seen[t, h, pl.ds(slot, 1), :] = halves[h]
+        return carry
+
+    last = slots + LANES - 1
+    most = jnp.maximum(outer[0, last], outer[1, last])
+    lax.fori_loop(0, (most + 3) // 4, pick, 0)
     eye = identity(256, BF16)
     for t in range(2):
         values = jnp.concatenate([seen[t, h, 0:slots] for h in range(2)], axis=1).astype(BF16)
@@ -673,15 +678,20 @@
     block = dot_nt(eye, turned[10].astype(BF16)).astype(BF16).reshape(shape)
     planes[2, 24:28] = block[0:4]
     copies = []
+
+    def leave(v, at, to, count):
+        source, target = planes.at[v, pl.ds(at, count)], out.at[v, pl.ds(to, count)]
+        copies.append(pltpu.make_async_copy(source, target, sent.at[len(copies)]))
+        copies[-1].start()
+
+    for v in range(3):
+        leave(v, 24, 56, 4)
     for v in range(3):
         for index in range(3):
             at = 8 * index
             block = take_group(wide, turned, eye, group_of(v, index), shape, 12)
             planes[v, at : at + 8] = block
-        for k, (at, to, count) in enumerate(((0, 0, 24), (24, 56, 4))):
-            source, target = planes.at[v, pl.ds(at, count)], out.at[v, pl.ds(to, count)]
-            copies.append(pltpu.make_async_copy(source, target, sent.at[2 * v + k]))
-            copies[-1].start()
+            leave(v, at, at, 8)
     for copy in copies:
         copy.wait()
 
@@ -901,7 +911,7 @@
             pltpu.VMEM((8, SECOND, 256), F32),
             pltpu.VMEM((11, latitudes, 256), F32),
             pltpu.VMEM((3, 28, members, latitudes), BF16),
-            pltpu.SemaphoreType.DMA((6,)),
+            pltpu.SemaphoreType.DMA((12,)),
         ],
         input_output_aliases={8: 0},
         compiler_params=params(20),

time: 86.1 us -> 86.7 us (level)
  no operation moved by 1% of the time
where the time goes in v16:
time: 86.7 us; the launch traced here: 86.5 us
  starting transfers between devices  36.6 us (42%)
  Pallas kernels  27.3 us (31%)
  waiting for transfers between devices  20.7 us (24%)
  other arithmetic  1.44 us (2%)
    ppermute x18, starting transfers between devices, across(): return lax.ppermute(value, 'mem', [(i, i ^ difference) for i in range(8)])  19.2 us
    ppermute x6, starting transfers between devices, swapped_pairs(): moved.append(lax.ppermute(value, axis, both))  12.2 us
    ppermute x18, waiting for transfers between devices, across(): return lax.ppermute(value, 'mem', [(i, i ^ difference) for i in range(8)])  11.4 us
    ppermute x6, waiting for transfers between devices, swapped_pairs(): moved.append(lax.ppermute(value, axis, both))  6.61 us
    pallas_call x1, Pallas kernels, on_device_fast(): pl.pallas_call(analyse_kernel, out_shape=(jax.ShapeDtypeStruct((FIRST, 25...  6.05 us
    all_to_all x1, starting transfers between devices, swap(): return lax.all_to_all(value, 'mem', split_axis=0, concat_axis=0, tiled=True)  5.19 us
    pallas_call x1, Pallas kernels, on_device_fast(): pl.pallas_call(spread_kernel, out_shape=(jax.ShapeDtypeStruct((8, INNER,...  5.04 us
    pallas_call x1, Pallas kernels, on_device_fast(): pl.pallas_call(observe_kernel, out_shape=(jax.ShapeDtypeStruct((8, OUTER,...  4.65 us
  transfers between devices with their start and end apart: 25, of which 13 were waited for; matrix products, arithmetic and copies ran while one was open for 2% of the time, Pallas kernels for 12%

profile of v16, /device:TPU:0, one launch (start us, length us, event | category | flops | bytes accessed | tf_op | source)
XLA Modules:
  0.0 86.5 jit_solution(11470925400298827858)
XLA Ops:
  0.0 4.6 %inner.1 = (bf16[8,304,256]{2,1,0:T(8,128)(2,1)}, bf16[4,32,160]{2,1,0:T(8,128)(2,1)}, bf16[4,32,160]{2,1,0:T(8,128)(2,1)}) custom-call(bf16[3,60,32,160]{3,2,1,0:T(8,128)(2,1)} %bitcast.49, f32[60,160]{1,0:T(8,128)} %depth.3), custom_call_target="tpu_custom_call" | custom-call | tf_op jit(solution)/shard_map/inner/pallas_call | solution.py:758
  4.6 5.2 %all-to-all-start = ((bf16[8,304,256]{2,1,0:T(8,128)(2,1)}), bf16[8,304,256]{2,1,0:T(8,128)(2,1)}, u32[]{:S(2)}, u32[]{:S(2)}) async-start(bf16[8,304,256]{2,1,0:T(8,128)(2,1)} %get-tuple-element.41), calls=%async_computation | async-start | bytes 2490368 | tf_op jit(solution)/shard_map/all_to_all | solution.py:729
  9.8 2.2 %collective-permute-start = (bf16[4,32,160]{2,1,0:T(8,128)(2,1)}, bf16[4,32,160]{2,1,0:T(8,128)(2,1)S(1)}, u32[]{:S(2)}, u32[]{:S(2)}) collective-permute-start(bf16[4,32,160]{2,1,0:T(8,128)(2,1)} %get-tuple-element.43), channel_id=1, source_target_pairs={{0,1},{2,3},{1,0},{3,2},{4,5},{6,7},{5,4},{7,6},{8,9},{10,11},{9,8... | collective-permute-start | bytes 122888 | tf_op jit(solution)/shard_map/ppermute | solution.py:703
  12.0 2.5 %collective-permute-start.1 = (bf16[4,32,160]{2,1,0:T(8,128)(2,1)}, bf16[4,32,160]{2,1,0:T(8,128)(2,1)S(1)}, u32[]{:S(2)}, u32[]{:S(2)}) collective-permute-start(bf16[4,32,160]{2,1,0:T(8,128)(2,1)} %get-tuple-element.44), channel_id=1, source_target_pairs={{1,2},{3,0},{2,1},{0,3},{5,6},{7,4},{6,5},{4,7},{9,10},{11,8},{10,... | collective-permute-start | bytes 122888 | tf_op jit(solution)/shard_map/ppermute | solution.py:703
  15.8 2.7 %collective-permute-done.1.second_swap = bf16[4,32,160]{2,1,0:T(8,128)(2,1)S(1)} collective-permute-done((bf16[4,32,160]{2,1,0:T(8,128)(2,1)}, bf16[4,32,160]{2,1,0:T(8,128)(2,1)S(1)}, u32[]{:S(2)}, u32[]{:S(2)}) %collective-permute-start.1) | collective-permute-done | bytes 40992 | tf_op jit(solution)/shard_map/ppermute | solution.py:703
  21.4 1.9 %collective-permute-start.3 = (bf16[2,152,256]{2,1,0:T(8,128)(2,1)S(1)}, bf16[2,152,256]{2,1,0:T(8,128)(2,1)S(1)}, u32[]{:S(2)}, u32[]{:S(2)}) collective-permute-start(bf16[2,152,256]{2,1,0:T(8,128)(2,1)S(1)} %pad_maximum_fusion), channel_id=1, source_target_pairs={{0,8},{4,12},{8,0},{12,4},{16,24},{20,28},{24,16},{28,20},{1,9},{5... | collective-permute-start | bytes 466952 | tf_op jit(solution)/shard_map/ppermute | solution.py:721
  25.2 2.7 %all-to-all-done.got = bf16[8,304,256]{2,1,0:T(8,128)(2,1)} async-done(((bf16[8,304,256]{2,1,0:T(8,128)(2,1)}), bf16[8,304,256]{2,1,0:T(8,128)(2,1)}, u32[]{:S(2)}, u32[]{:S(2)}) %all-to-all-start) | async-done | bytes 1245216 | tf_op jit(solution)/shard_map/all_to_all | solution.py:729
  27.9 5.0 %spread.1 = (bf16[8,304,256]{2,1,0:T(8,128)(2,1)S(1)}, f32[2,2,512,128]{3,2,1,0:T(8,128)S(1)}) custom-call(s32[2,512]{1,0:T(2,128)S(1)} %get-tuple-element.77.cells, bf16[8,304,256]{2,1,0:T(8,128)(2,1)} %all-to-all-done.got), custom_call_target="tpu_custom_call" | custom-call | flops 1 | bytes 8388608 | tf_op jit(solution)/shard_map/spread/pallas_call | solution.py:818
  34.0 4.7 %observe.1 = (bf16[8,152,256]{2,1,0:T(8,128)(2,1)S(1)}, f32[2,136,256]{2,1,0:T(8,128)S(1)}, bf16[136,256]{1,0:T(8,128)(2,1)S(1)}, bf16[136,256]{1,0:T(8,128)(2,1)S(1)}) custom-call(s32[2,640]{1,0:T(2,128)S(1)} %pad.4.cells, s32[2,640]{1,0:T(2,128)S(1)} %fusion.3.outer, f32[2,512]{1,0:T(2,128)S(1)} %fusion.12.weight, f32[2,512]{1,0:T(2,128)S(1)} %bitcast.52, ...), custom_call_target="tpu_custom_call" | custom-call | tf_op jit(solution)/shard_map/observe/pallas_call | solution.py:831
  38.7 2.1 %collective-permute-start.6 = (bf16[136,256]{1,0:T(8,128)(2,1)S(1)}, bf16[136,256]{1,0:T(8,128)(2,1)S(1)}, u32[]{:S(2)}, u32[]{:S(2)}) collective-permute-start(bf16[136,256]{1,0:T(8,128)(2,1)S(1)} %get-tuple-element.48), channel_id=1, source_target_pairs={{0,1},{2,3},{1,0},{3,2},{4,5},{6,7},{5,4},{7,6},{8,9},{10,11},{9,8... | collective-permute-start | bytes 208904 | tf_op jit(solution)/shard_map/ppermute | solution.py:703
  40.8 2.5 %collective-permute-start.7 = (bf16[136,256]{1,0:T(8,128)(2,1)S(1)}, bf16[136,256]{1,0:T(8,128)(2,1)S(1)}, u32[]{:S(2)}, u32[]{:S(2)}) collective-permute-start(bf16[136,256]{1,0:T(8,128)(2,1)S(1)} %get-tuple-element.49), channel_id=1, source_target_pairs={{1,2},{3,0},{2,1},{0,3},{5,6},{7,4},{6,5},{4,7},{9,10},{11,8},{10,... | collective-permute-start | bytes 208904 | tf_op jit(solution)/shard_map/ppermute | solution.py:703
  43.3 3.6 %collective-permute-done.7.second_swap = bf16[136,256]{1,0:T(8,128)(2,1)S(1)} collective-permute-done((bf16[136,256]{1,0:T(8,128)(2,1)S(1)}, bf16[136,256]{1,0:T(8,128)(2,1)S(1)}, u32[]{:S(2)}, u32[]{:S(2)}) %collective-permute-start.7) | collective-permute-done | bytes 69664 | tf_op jit(solution)/shard_map/ppermute | solution.py:703
  47.8 2.1 %collective-permute-start.8 = (bf16[2,136,256]{2,1,0:T(8,128)(2,1)S(1)}, bf16[2,136,256]{2,1,0:T(8,128)(2,1)S(1)}, u32[]{:S(2)}, u32[]{:S(2)}) collective-permute-start(bf16[2,136,256]{2,1,0:T(8,128)(2,1)S(1)} %get-tuple-element.51), channel_id=1, source_target_pairs={{0,4},{8,12},{16,20},{24,28},{4,0},{12,8},{20,16},{28,24},{1,5},{9... | collective-permute-start | bytes 417800 | tf_op jit(solution)/shard_map/ppermute | solution.py:703
  50.9 6.1 %analyse.1 = (bf16[240,256]{1,0:T(8,128)(2,1)S(1)}, bf16[240,256]{1,0:T(8,128)(2,1)S(1)}, bf16[240,256]{1,0:T(8,128)(2,1)S(1)}, bf16[240,256]{1,0:T(8,128)(2,1)S...) custom-call(f32[2,136,256]{2,1,0:T(8,128)S(1)} %get-tuple-element.50, ...), custom_call_target="tpu_custom_call" | custom-call | tf_op jit(solution)/shard_map/analyse/pallas_call | solution.py:871
  57.0 2.1 %collective-permute-start.10 = (bf16[240,256]{1,0:T(8,128)(2,1)S(1)}, bf16[240,256]{1,0:T(8,128)(2,1)S(1)}, u32[]{:S(2)}, u32[]{:S(2)}) collective-permute-start(bf16[240,256]{1,0:T(8,128)(2,1)S(1)} %get-tuple-element.57), channel_id=1, source_target_pairs={{0,4},{4,0},{8,12},{12,8},{16,20},{20,16},{24,28},{28,24},{1,5},{5... | collective-permute-start | bytes 368648 | tf_op jit(solution)/shard_map/ppermute | solution.py:721
  59.1 2.5 %collective-permute-start.18 = (bf16[240,256]{1,0:T(8,128)(2,1)S(1)}, bf16[240,256]{1,0:T(8,128)(2,1)S(1)}, u32[]{:S(2)}, u32[]{:S(2)}) collective-permute-start(bf16[240,256]{1,0:T(8,128)(2,1)S(1)} %get-tuple-element.69), channel_id=1, source_target_pairs={{0,24},{4,28},{8,16},{12,20},{16,8},{20,12},{24,0},{28,4},{1,25},{... | collective-permute-start | bytes 368648 | tf_op jit(solution)/shard_map/ppermute | solution.py:721
  61.6 1.6 %collective-permute-start.19 = (bf16[240,256]{1,0:T(8,128)(2,1)S(1)}, bf16[240,256]{1,0:T(8,128)(2,1)S(1)}, u32[]{:S(2)}, u32[]{:S(2)}) collective-permute-start(bf16[240,256]{1,0:T(8,128)(2,1)S(1)} %get-tuple-element.70), channel_id=1, source_target_pairs={{0,8},{4,12},{8,0},{12,4},{16,24},{20,28},{24,16},{28,20},{1,9},{5... | collective-permute-start | bytes 368648 | tf_op jit(solution)/shard_map/ppermute | solution.py:721
  64.3 2.1 %collective-permute-start.22 = (bf16[240,256]{1,0:T(8,128)(2,1)S(1)}, bf16[240,256]{1,0:T(8,128)(2,1)S(1)}, u32[]{:S(2)}, u32[]{:S(2)}) collective-permute-start(bf16[240,256]{1,0:T(8,128)(2,1)S(1)} %get-tuple-element.74), channel_id=1, source_target_pairs={{0,12},{4,8},{8,4},{12,0},{16,28},{20,24},{24,20},{28,16},{1,13},{... | collective-permute-start | bytes 368648 | tf_op jit(solution)/shard_map/ppermute | solution.py:721
  67.6 1.8 %second.1 = (bf16[216,256]{1,0:T(8,128)(2,1)S(1)}, bf16[216,256]{1,0:T(8,128)(2,1)S(1)}, bf16[216,256]{1,0:T(8,128)(2,1)S(1)}, bf16[216,256]{1,0:T(8,128)(2,1)S(...) custom-call(bf16[2,256,256]{2,1,0:T(8,128)(2,1)S(1)} %get-tuple-elem, ...), custom_call_target="tpu_custom_call" | custom-call | flops 1 | bytes 6291456 | tf_op jit(solution)/shard_map/second/pallas_call | solution.py:881
  74.4 1.6 %collective-permute-start.14 = (bf16[216,256]{1,0:T(8,128)(2,1)S(1)}, bf16[216,256]{1,0:T(8,128)(2,1)S(1)}, u32[]{:S(2)}, u32[]{:S(2)}) collective-permute-start(bf16[216,256]{1,0:T(8,128)(2,1)S(1)} %get-tuple-element.64), channel_id=1, source_target_pairs={{0,28},{4,24},{8,20},{12,16},{16,12},{20,8},{24,4},{28,0},{1,29},{... | collective-permute-start | bytes 331784 | tf_op jit(solution)/shard_map/ppermute | solution.py:721
  76.8 3.2 %collective-permute-done.12.refs_1_ = bf16[216,256]{1,0:T(8,128)(2,1)S(1)} collective-permute-done((bf16[216,256]{1,0:T(8,128)(2,1)S(1)}, bf16[216,256]{1,0:T(8,128)(2,1)S(1)}, u32[]{:S(2)}, u32[]{:S(2)}) %collective-permute-start.12) | collective-permute-done | bytes 110624 | tf_op jit(solution)/shard_map/ppermute | solution.py:721
  80.1 1.6 %first_return.1.refs_8_ = bf16[3,60,32,160]{3,2,1,0:T(8,128)(2,1)} custom-call(bf16[240,256]{1,0:T(8,128)(2,1)S(1)} %collective-permute-done.18.refs_0_, bf16[240,256]{1,0:T(8,128)(2,1)S(1)} %collective-permute-done.19.refs_1_, bf16[240,256]{1,0:T(8,128)(2,1)S(1)} %collective-permute-done.20.refs_2_, bf16[240,256]{1,0:T(8,128)(2,1)S(1)} %collective-permute-done.21.refs_3_, ...), custom_call_target="tpu_custom_call" | custom-call | flops 1 | bytes 4194304 | tf_op jit(solution)/shard_map/first_return/pallas_call | solution.py:891
  81.7 2.2 %collective-permute-done.16.refs_5_ = bf16[216,256]{1,0:T(8,128)(2,1)S(1)} collective-permute-done((bf16[216,256]{1,0:T(8,128)(2,1)S(1)}, bf16[216,256]{1,0:T(8,128)(2,1)S(1)}, u32[]{:S(2)}, u32[]{:S(2)}) %collective-permute-start.16) | collective-permute-done | bytes 110624 | tf_op jit(solution)/shard_map/ppermute | solution.py:721
  84.8 1.6 %second_return.1 = bf16[3,60,32,160]{3,2,1,0:T(8,128)(2,1)} custom-call(bf16[216,256]{1,0:T(8,128)(2,1)S(1)} %collective-permute-done.11.refs_0_, bf16[216,256]{1,0:T(8,128)(2,1)S(1)} %collective-permute-done.12.refs_1_, bf16[216,256]{1,0:T(8,128)(2,1)S(1)} %collective-permute-done.13.refs_2_, ...), custom_call_target="tpu_custom_call", output_to_operand_aliasing={{}: (8, {})} | custom-call | tf_op jit(solution)/shard_map/second_return/pallas_call | solution.py:905
  (64 shorter events, 18.0 us)
Async XLA Ops:
  4.6 23.3 %all-to-all-start = ((bf16[8,304,256]{2,1,0:T(8,128)(2,1)}), bf16[8,304,256]{2,1,0:T(8,128)(2,1)}, u32[]{:S(2)}, u32[]{:S(2)}) async-start(bf16[8,304,256]{2,1,0:T(8,128)(2,1)} %get-tuple-element.41), calls=%async_computation | async-start | bytes 2490368 | tf_op jit(solution)/shard_map/all_to_all | solution.py:729
  9.8 5.9 %collective-permute-start = (bf16[4,32,160]{2,1,0:T(8,128)(2,1)}, bf16[4,32,160]{2,1,0:T(8,128)(2,1)S(1)}, u32[]{:S(2)}, u32[]{:S(2)}) collective-permute-start(bf16[4,32,160]{2,1,0:T(8,128)(2,1)} %get-tuple-element.43), channel_id=1, source_target_pairs={{0,1},{2,3},{1,0},{3,2},{4,5},{6,7},{5,4},{7,6},{8,9},{10,11},{9,8... | collective-permute-start | bytes 122888 | tf_op jit(solution)/shard_map/ppermute | solution.py:703
  12.0 6.4 %collective-permute-start.1 = (bf16[4,32,160]{2,1,0:T(8,128)(2,1)}, bf16[4,32,160]{2,1,0:T(8,128)(2,1)S(1)}, u32[]{:S(2)}, u32[]{:S(2)}) collective-permute-start(bf16[4,32,160]{2,1,0:T(8,128)(2,1)} %get-tuple-element.44), channel_id=1, source_target_pairs={{1,2},{3,0},{2,1},{0,3},{5,6},{7,4},{6,5},{4,7},{9,10},{11,8},{10,... | collective-permute-start | bytes 122888 | tf_op jit(solution)/shard_map/ppermute | solution.py:703
  21.4 11.6 %collective-permute-start.3 = (bf16[2,152,256]{2,1,0:T(8,128)(2,1)S(1)}, bf16[2,152,256]{2,1,0:T(8,128)(2,1)S(1)}, u32[]{:S(2)}, u32[]{:S(2)}) collective-permute-start(bf16[2,152,256]{2,1,0:T(8,128)(2,1)S(1)} %pad_maximum_fusion), channel_id=1, source_target_pairs={{0,8},{4,12},{8,0},{12,4},{16,24},{20,28},{24,16},{28,20},{1,9},{5... | collective-permute-start | bytes 466952 | tf_op jit(solution)/shard_map/ppermute | solution.py:721
  23.3 9.7 %collective-permute-start.4 = (bf16[2,152,256]{2,1,0:T(8,128)(2,1)S(1)}, bf16[2,152,256]{2,1,0:T(8,128)(2,1)S(1)}, u32[]{:S(2)}, u32[]{:S(2)}) collective-permute-start(bf16[2,152,256]{2,1,0:T(8,128)(2,1)S(1)} %pad_maximum_fusion.1), channel_id=1, source_target_pairs={{0,16},{4,20},{8,24},{12,28},{16,0},{20,4},{24,8},{28,12},{1,17},{... | collective-permute-start | bytes 466952 | tf_op jit(solution)/shard_map/ppermute | solution.py:721
  24.9 9.1 %collective-permute-start.5 = (bf16[2,152,256]{2,1,0:T(8,128)(2,1)S(1)}, bf16[2,152,256]{2,1,0:T(8,128)(2,1)S(1)}, u32[]{:S(2)}, u32[]{:S(2)}) collective-permute-start(bf16[2,152,256]{2,1,0:T(8,128)(2,1)S(1)} %pad_maximum_fusion.2), channel_id=1, source_target_pairs={{0,24},{4,28},{8,16},{12,20},{16,8},{20,12},{24,0},{28,4},{1,25},{... | collective-permute-start | bytes 466952 | tf_op jit(solution)/shard_map/ppermute | solution.py:721
  38.7 4.6 %collective-permute-start.6 = (bf16[136,256]{1,0:T(8,128)(2,1)S(1)}, bf16[136,256]{1,0:T(8,128)(2,1)S(1)}, u32[]{:S(2)}, u32[]{:S(2)}) collective-permute-start(bf16[136,256]{1,0:T(8,128)(2,1)S(1)} %get-tuple-element.48), channel_id=1, source_target_pairs={{0,1},{2,3},{1,0},{3,2},{4,5},{6,7},{5,4},{7,6},{8,9},{10,11},{9,8... | collective-permute-start | bytes 208904 | tf_op jit(solution)/shard_map/ppermute | solution.py:703
  40.8 6.1 %collective-permute-start.7 = (bf16[136,256]{1,0:T(8,128)(2,1)S(1)}, bf16[136,256]{1,0:T(8,128)(2,1)S(1)}, u32[]{:S(2)}, u32[]{:S(2)}) collective-permute-start(bf16[136,256]{1,0:T(8,128)(2,1)S(1)} %get-tuple-element.49), channel_id=1, source_target_pairs={{1,2},{3,0},{2,1},{0,3},{5,6},{7,4},{6,5},{4,7},{9,10},{11,8},{10,... | collective-permute-start | bytes 208904 | tf_op jit(solution)/shard_map/ppermute | solution.py:703
  46.9 3.6 %collective-permute-start.9 = (bf16[2,136,256]{2,1,0:T(8,128)(2,1)S(1)}, bf16[2,136,256]{2,1,0:T(8,128)(2,1)S(1)}, u32[]{:S(2)}, u32[]{:S(2)}) collective-permute-start(bf16[2,136,256]{2,1,0:T(8,128)(2,1)S(1)} %get-tuple-element.51), channel_id=1, source_target_pairs={{4,8},{12,16},{20,24},{8,4},{16,12},{24,20},{5,9},{13,17},{21,25},... | collective-permute-start | bytes 417800 | tf_op jit(solution)/shard_map/ppermute | solution.py:703
  47.8 3.1 %collective-permute-start.8 = (bf16[2,136,256]{2,1,0:T(8,128)(2,1)S(1)}, bf16[2,136,256]{2,1,0:T(8,128)(2,1)S(1)}, u32[]{:S(2)}, u32[]{:S(2)}) collective-permute-start(bf16[2,136,256]{2,1,0:T(8,128)(2,1)S(1)} %get-tuple-element.51), channel_id=1, source_target_pairs={{0,4},{8,12},{16,20},{24,28},{4,0},{12,8},{20,16},{28,24},{1,5},{9... | collective-permute-start | bytes 417800 | tf_op jit(solution)/shard_map/ppermute | solution.py:703
  57.0 7.3 %collective-permute-start.10 = (bf16[240,256]{1,0:T(8,128)(2,1)S(1)}, bf16[240,256]{1,0:T(8,128)(2,1)S(1)}, u32[]{:S(2)}, u32[]{:S(2)}) collective-permute-start(bf16[240,256]{1,0:T(8,128)(2,1)S(1)} %get-tuple-element.57), channel_id=1, source_target_pairs={{0,4},{4,0},{8,12},{12,8},{16,20},{20,16},{24,28},{28,24},{1,5},{5... | collective-permute-start | bytes 368648 | tf_op jit(solution)/shard_map/ppermute | solution.py:721
  59.1 7.3 %collective-permute-start.18 = (bf16[240,256]{1,0:T(8,128)(2,1)S(1)}, bf16[240,256]{1,0:T(8,128)(2,1)S(1)}, u32[]{:S(2)}, u32[]{:S(2)}) collective-permute-start(bf16[240,256]{1,0:T(8,128)(2,1)S(1)} %get-tuple-element.69), channel_id=1, source_target_pairs={{0,24},{4,28},{8,16},{12,20},{16,8},{20,12},{24,0},{28,4},{1,25},{... | collective-permute-start | bytes 368648 | tf_op jit(solution)/shard_map/ppermute | solution.py:721
  61.6 8.4 %collective-permute-start.19 = (bf16[240,256]{1,0:T(8,128)(2,1)S(1)}, bf16[240,256]{1,0:T(8,128)(2,1)S(1)}, u32[]{:S(2)}, u32[]{:S(2)}) collective-permute-start(bf16[240,256]{1,0:T(8,128)(2,1)S(1)} %get-tuple-element.70), channel_id=1, source_target_pairs={{0,8},{4,12},{8,0},{12,4},{16,24},{20,28},{24,16},{28,20},{1,9},{5... | collective-permute-start | bytes 368648 | tf_op jit(solution)/shard_map/ppermute | solution.py:721
  63.2 8.2 %collective-permute-start.20 = (bf16[240,256]{1,0:T(8,128)(2,1)S(1)}, bf16[240,256]{1,0:T(8,128)(2,1)S(1)}, u32[]{:S(2)}, u32[]{:S(2)}) collective-permute-start(bf16[240,256]{1,0:T(8,128)(2,1)S(1)} %get-tuple-element.71), channel_id=1, source_target_pairs={{0,16},{4,20},{8,24},{12,28},{16,0},{20,4},{24,8},{28,12},{1,17},{... | collective-permute-start | bytes 368648 | tf_op jit(solution)/shard_map/ppermute | solution.py:721
  63.2 9.0 %collective-permute-start.21 = (bf16[240,256]{1,0:T(8,128)(2,1)S(1)}, bf16[240,256]{1,0:T(8,128)(2,1)S(1)}, u32[]{:S(2)}, u32[]{:S(2)}) collective-permute-start(bf16[240,256]{1,0:T(8,128)(2,1)S(1)} %get-tuple-element.72), channel_id=1, source_target_pairs={{0,28},{4,24},{8,20},{12,16},{16,12},{20,8},{24,4},{28,0},{1,29},{... | collective-permute-start | bytes 368648 | tf_op jit(solution)/shard_map/ppermute | solution.py:721
  64.3 10.1 %collective-permute-start.22 = (bf16[240,256]{1,0:T(8,128)(2,1)S(1)}, bf16[240,256]{1,0:T(8,128)(2,1)S(1)}, u32[]{:S(2)}, u32[]{:S(2)}) collective-permute-start(bf16[240,256]{1,0:T(8,128)(2,1)S(1)} %get-tuple-element.74), channel_id=1, source_target_pairs={{0,12},{4,8},{8,4},{12,0},{16,28},{20,24},{24,20},{28,16},{1,13},{... | collective-permute-start | bytes 368648 | tf_op jit(solution)/shard_map/ppermute | solution.py:721
  66.4 9.6 %collective-permute-start.23 = (bf16[240,256]{1,0:T(8,128)(2,1)S(1)}, bf16[240,256]{1,0:T(8,128)(2,1)S(1)}, u32[]{:S(2)}, u32[]{:S(2)}) collective-permute-start(bf16[240,256]{1,0:T(8,128)(2,1)S(1)} %get-tuple-element.75), channel_id=1, source_target_pairs={{0,20},{4,16},{8,28},{12,24},{16,4},{20,0},{24,12},{28,8},{1,21},{... | collective-permute-start | bytes 368648 | tf_op jit(solution)/shard_map/ppermute | solution.py:721
  70.0 6.9 %collective-permute-start.11 = (bf16[216,256]{1,0:T(8,128)(2,1)S(1)}, bf16[216,256]{1,0:T(8,128)(2,1)S(1)}, u32[]{:S(2)}, u32[]{:S(2)}) collective-permute-start(bf16[216,256]{1,0:T(8,128)(2,1)S(1)} %get-tuple-element.61), channel_id=1, source_target_pairs={{0,24},{4,28},{8,16},{12,20},{16,8},{20,12},{24,0},{28,4},{1,25},{... | collective-permute-start | bytes 331784 | tf_op jit(solution)/shard_map/ppermute | solution.py:721
  71.4 8.7 %collective-permute-start.12 = (bf16[216,256]{1,0:T(8,128)(2,1)S(1)}, bf16[216,256]{1,0:T(8,128)(2,1)S(1)}, u32[]{:S(2)}, u32[]{:S(2)}) collective-permute-start(bf16[216,256]{1,0:T(8,128)(2,1)S(1)} %get-tuple-element.62), channel_id=1, source_target_pairs={{0,8},{4,12},{8,0},{12,4},{16,24},{20,28},{24,16},{28,20},{1,9},{5... | collective-permute-start | bytes 331784 | tf_op jit(solution)/shard_map/ppermute | solution.py:721
  72.2 9.5 %collective-permute-start.13 = (bf16[216,256]{1,0:T(8,128)(2,1)S(1)}, bf16[216,256]{1,0:T(8,128)(2,1)S(1)}, u32[]{:S(2)}, u32[]{:S(2)}) collective-permute-start(bf16[216,256]{1,0:T(8,128)(2,1)S(1)} %get-tuple-element.63), channel_id=1, source_target_pairs={{0,16},{4,20},{8,24},{12,28},{16,0},{20,4},{24,8},{28,12},{1,17},{... | collective-permute-start | bytes 331784 | tf_op jit(solution)/shard_map/ppermute | solution.py:721
  74.4 7.3 %collective-permute-start.14 = (bf16[216,256]{1,0:T(8,128)(2,1)S(1)}, bf16[216,256]{1,0:T(8,128)(2,1)S(1)}, u32[]{:S(2)}, u32[]{:S(2)}) collective-permute-start(bf16[216,256]{1,0:T(8,128)(2,1)S(1)} %get-tuple-element.64), channel_id=1, source_target_pairs={{0,28},{4,24},{8,20},{12,16},{16,12},{20,8},{24,4},{28,0},{1,29},{... | collective-permute-start | bytes 331784 | tf_op jit(solution)/shard_map/ppermute | solution.py:721
  76.0 5.7 %collective-permute-start.15 = (bf16[216,256]{1,0:T(8,128)(2,1)S(1)}, bf16[216,256]{1,0:T(8,128)(2,1)S(1)}, u32[]{:S(2)}, u32[]{:S(2)}) collective-permute-start(bf16[216,256]{1,0:T(8,128)(2,1)S(1)} %get-tuple-element.65), channel_id=1, source_target_pairs={{0,4},{4,0},{8,12},{12,8},{16,20},{20,16},{24,28},{28,24},{1,5},{5... | collective-permute-start | bytes 331784 | tf_op jit(solution)/shard_map/ppermute | solution.py:721
  76.8 7.1 %collective-permute-start.16 = (bf16[216,256]{1,0:T(8,128)(2,1)S(1)}, bf16[216,256]{1,0:T(8,128)(2,1)S(1)}, u32[]{:S(2)}, u32[]{:S(2)}) collective-permute-start(bf16[216,256]{1,0:T(8,128)(2,1)S(1)} %get-tuple-element.66), channel_id=1, source_target_pairs={{0,12},{4,8},{8,4},{12,0},{16,28},{20,24},{24,20},{28,16},{1,13},{... | collective-permute-start | bytes 331784 | tf_op jit(solution)/shard_map/ppermute | solution.py:721
  80.1 4.7 %collective-permute-start.17 = (bf16[216,256]{1,0:T(8,128)(2,1)S(1)}, bf16[216,256]{1,0:T(8,128)(2,1)S(1)}, u32[]{:S(2)}, u32[]{:S(2)}) collective-permute-start(bf16[216,256]{1,0:T(8,128)(2,1)S(1)} %get-tuple-element.67), channel_id=1, source_target_pairs={{0,20},{4,16},{8,28},{12,24},{16,4},{20,0},{24,12},{28,8},{1,21},{... | collective-permute-start | bytes 331784 | tf_op jit(solution)/shard_map/ppermute | solution.py:721
  (7 other events, 86.2 us)

commit v17 on v15

--- a/solution.py
+++ b/solution.py
@@ -673,15 +673,20 @@
     block = dot_nt(eye, turned[10].astype(BF16)).astype(BF16).reshape(shape)
     planes[2, 24:28] = block[0:4]
     copies = []
+
+    def leave(v, at, to, count):
+        source, target = planes.at[v, pl.ds(at, count)], out.at[v, pl.ds(to, count)]
+        copies.append(pltpu.make_async_copy(source, target, sent.at[len(copies)]))
+        copies[-1].start()
+
+    for v in range(3):
+        leave(v, 24, 56, 4)
     for v in range(3):
         for index in range(3):
             at = 8 * index
             block = take_group(wide, turned, eye, group_of(v, index), shape, 12)
             planes[v, at : at + 8] = block
-        for k, (at, to, count) in enumerate(((0, 0, 24), (24, 56, 4))):
-            source, target = planes.at[v, pl.ds(at, count)], out.at[v, pl.ds(to, count)]
-            copies.append(pltpu.make_async_copy(source, target, sent.at[2 * v + k]))
-            copies[-1].start()
+            leave(v, at, at, 8)
     for copy in copies:
         copy.wait()
 
@@ -901,7 +906,7 @@
             pltpu.VMEM((8, SECOND, 256), F32),
             pltpu.VMEM((11, latitudes, 256), F32),
             pltpu.VMEM((3, 28, members, latitudes), BF16),
-            pltpu.SemaphoreType.DMA((6,)),
+            pltpu.SemaphoreType.DMA((12,)),
         ],
         input_output_aliases={8: 0},
         compiler_params=params(20),

time: 86.1 us -> 86.1 us (level)
  no operation moved by 1% of the time
where the time goes in v17:
time: 86.1 us; the launch traced here: 85.9 us
  starting transfers between devices  36 us (42%)
  Pallas kernels  26.8 us (31%)
  waiting for transfers between devices  21.3 us (25%)
  other arithmetic  1.44 us (2%)
    ppermute x18, starting transfers between devices, across(): return lax.ppermute(value, 'mem', [(i, i ^ difference) for i in range(8)])  18.9 us
    ppermute x6, starting transfers between devices, swapped_pairs(): moved.append(lax.ppermute(value, axis, both))  11.9 us
    ppermute x18, waiting for transfers between devices, across(): return lax.ppermute(value, 'mem', [(i, i ^ difference) for i in range(8)])  11.8 us
    ppermute x6, waiting for transfers between devices, swapped_pairs(): moved.append(lax.ppermute(value, axis, both))  6.77 us
    pallas_call x1, Pallas kernels, on_device_fast(): pl.pallas_call(analyse_kernel, out_shape=(jax.ShapeDtypeStruct((FIRST, 25...  6.06 us
    all_to_all x1, starting transfers between devices, swap(): return lax.all_to_all(value, 'mem', split_axis=0, concat_axis=0, tiled=True)  5.19 us
    pallas_call x1, Pallas kernels, on_device_fast(): pl.pallas_call(spread_kernel, out_shape=(jax.ShapeDtypeStruct((8, INNER,...  5.04 us
    pallas_call x1, Pallas kernels, on_device_fast(): pl.pallas_call(inner_kernel, out_shape=(jax.ShapeDtypeStruct((8, INNER, 2...  4.63 us
  transfers between devices with their start and end apart: 25, of which 13 were waited for; matrix products, arithmetic and copies ran while one was open for 2% of the time, Pallas kernels for 12%

profile of v17, /device:TPU:0, one launch (start us, length us, event | category | flops | bytes accessed | tf_op | source)
XLA Modules:
  0.0 85.9 jit_solution(12372648309010953694)
XLA Ops:
  0.0 4.6 %inner.1 = (bf16[8,304,256]{2,1,0:T(8,128)(2,1)}, bf16[4,32,160]{2,1,0:T(8,128)(2,1)}, bf16[4,32,160]{2,1,0:T(8,128)(2,1)}) custom-call(bf16[3,60,32,160]{3,2,1,0:T(8,128)(2,1)} %bitcast.49, f32[60,160]{1,0:T(8,128)} %depth.3), custom_call_target="tpu_custom_call" | custom-call | tf_op jit(solution)/shard_map/inner/pallas_call | solution.py:753
  4.6 5.2 %all-to-all-start = ((bf16[8,304,256]{2,1,0:T(8,128)(2,1)}), bf16[8,304,256]{2,1,0:T(8,128)(2,1)}, u32[]{:S(2)}, u32[]{:S(2)}) async-start(bf16[8,304,256]{2,1,0:T(8,128)(2,1)} %get-tuple-element.41), calls=%async_computation | async-start | bytes 2490368 | tf_op jit(solution)/shard_map/all_to_all | solution.py:724
  9.8 2.2 %collective-permute-start = (bf16[4,32,160]{2,1,0:T(8,128)(2,1)}, bf16[4,32,160]{2,1,0:T(8,128)(2,1)S(1)}, u32[]{:S(2)}, u32[]{:S(2)}) collective-permute-start(bf16[4,32,160]{2,1,0:T(8,128)(2,1)} %get-tuple-element.43), channel_id=1, source_target_pairs={{0,1},{2,3},{1,0},{3,2},{4,5},{6,7},{5,4},{7,6},{8,9},{10,11},{9,8... | collective-permute-start | bytes 122888 | tf_op jit(solution)/shard_map/ppermute | solution.py:698
  12.0 2.5 %collective-permute-start.1 = (bf16[4,32,160]{2,1,0:T(8,128)(2,1)}, bf16[4,32,160]{2,1,0:T(8,128)(2,1)S(1)}, u32[]{:S(2)}, u32[]{:S(2)}) collective-permute-start(bf16[4,32,160]{2,1,0:T(8,128)(2,1)} %get-tuple-element.44), channel_id=1, source_target_pairs={{1,2},{3,0},{2,1},{0,3},{5,6},{7,4},{6,5},{4,7},{9,10},{11,8},{10,... | collective-permute-start | bytes 122888 | tf_op jit(solution)/shard_map/ppermute | solution.py:698
  15.8 2.7 %collective-permute-done.1.second_swap = bf16[4,32,160]{2,1,0:T(8,128)(2,1)S(1)} collective-permute-done((bf16[4,32,160]{2,1,0:T(8,128)(2,1)}, bf16[4,32,160]{2,1,0:T(8,128)(2,1)S(1)}, u32[]{:S(2)}, u32[]{:S(2)}) %collective-permute-start.1) | collective-permute-done | bytes 40992 | tf_op jit(solution)/shard_map/ppermute | solution.py:698
  21.4 1.9 %collective-permute-start.3 = (bf16[2,152,256]{2,1,0:T(8,128)(2,1)S(1)}, bf16[2,152,256]{2,1,0:T(8,128)(2,1)S(1)}, u32[]{:S(2)}, u32[]{:S(2)}) collective-permute-start(bf16[2,152,256]{2,1,0:T(8,128)(2,1)S(1)} %pad_maximum_fusion), channel_id=1, source_target_pairs={{0,8},{4,12},{8,0},{12,4},{16,24},{20,28},{24,16},{28,20},{1,9},{5... | collective-permute-start | bytes 466952 | tf_op jit(solution)/shard_map/ppermute | solution.py:716
  23.3 1.6 %collective-permute-start.4 = (bf16[2,152,256]{2,1,0:T(8,128)(2,1)S(1)}, bf16[2,152,256]{2,1,0:T(8,128)(2,1)S(1)}, u32[]{:S(2)}, u32[]{:S(2)}) collective-permute-start(bf16[2,152,256]{2,1,0:T(8,128)(2,1)S(1)} %pad_maximum_fusion.1), channel_id=1, source_target_pairs={{0,16},{4,20},{8,24},{12,28},{16,0},{20,4},{24,8},{28,12},{1,17},{... | collective-permute-start | bytes 466952 | tf_op jit(solution)/shard_map/ppermute | solution.py:716
  25.2 2.7 %all-to-all-done.got = bf16[8,304,256]{2,1,0:T(8,128)(2,1)} async-done(((bf16[8,304,256]{2,1,0:T(8,128)(2,1)}), bf16[8,304,256]{2,1,0:T(8,128)(2,1)}, u32[]{:S(2)}, u32[]{:S(2)}) %all-to-all-start) | async-done | bytes 1245216 | tf_op jit(solution)/shard_map/all_to_all | solution.py:724
  27.9 5.0 %spread.1 = (bf16[8,304,256]{2,1,0:T(8,128)(2,1)S(1)}, f32[2,2,512,128]{3,2,1,0:T(8,128)S(1)}) custom-call(s32[2,512]{1,0:T(2,128)S(1)} %get-tuple-element.77.cells, bf16[8,304,256]{2,1,0:T(8,128)(2,1)} %all-to-all-done.got), custom_call_target="tpu_custom_call" | custom-call | flops 1 | bytes 8388608 | tf_op jit(solution)/shard_map/spread/pallas_call | solution.py:813
  34.0 4.1 %observe.1 = (bf16[8,152,256]{2,1,0:T(8,128)(2,1)S(1)}, f32[2,136,256]{2,1,0:T(8,128)S(1)}, bf16[136,256]{1,0:T(8,128)(2,1)S(1)}, bf16[136,256]{1,0:T(8,128)(2,1)S(1)}) custom-call(s32[2,640]{1,0:T(2,128)S(1)} %pad.4.cells, s32[2,640]{1,0:T(2,128)S(1)} %fusion.3.outer, f32[2,512]{1,0:T(2,128)S(1)} %fusion.12.weight, f32[2,512]{1,0:T(2,128)S(1)} %bitcast.52, ...), custom_call_target="tpu_custom_call" | custom-call | tf_op jit(solution)/shard_map/observe/pallas_call | solution.py:826
  38.1 2.0 %collective-permute-start.6 = (bf16[136,256]{1,0:T(8,128)(2,1)S(1)}, bf16[136,256]{1,0:T(8,128)(2,1)S(1)}, u32[]{:S(2)}, u32[]{:S(2)}) collective-permute-start(bf16[136,256]{1,0:T(8,128)(2,1)S(1)} %get-tuple-element.48), channel_id=1, source_target_pairs={{0,1},{2,3},{1,0},{3,2},{4,5},{6,7},{5,4},{7,6},{8,9},{10,11},{9,8... | collective-permute-start | bytes 208904 | tf_op jit(solution)/shard_map/ppermute | solution.py:698
  40.1 2.5 %collective-permute-start.7 = (bf16[136,256]{1,0:T(8,128)(2,1)S(1)}, bf16[136,256]{1,0:T(8,128)(2,1)S(1)}, u32[]{:S(2)}, u32[]{:S(2)}) collective-permute-start(bf16[136,256]{1,0:T(8,128)(2,1)S(1)} %get-tuple-element.49), channel_id=1, source_target_pairs={{1,2},{3,0},{2,1},{0,3},{5,6},{7,4},{6,5},{4,7},{9,10},{11,8},{10,... | collective-permute-start | bytes 208904 | tf_op jit(solution)/shard_map/ppermute | solution.py:698
  42.7 3.8 %collective-permute-done.7.second_swap = bf16[136,256]{1,0:T(8,128)(2,1)S(1)} collective-permute-done((bf16[136,256]{1,0:T(8,128)(2,1)S(1)}, bf16[136,256]{1,0:T(8,128)(2,1)S(1)}, u32[]{:S(2)}, u32[]{:S(2)}) %collective-permute-start.7) | collective-permute-done | bytes 69664 | tf_op jit(solution)/shard_map/ppermute | solution.py:698
  47.3 1.9 %collective-permute-start.8 = (bf16[2,136,256]{2,1,0:T(8,128)(2,1)S(1)}, bf16[2,136,256]{2,1,0:T(8,128)(2,1)S(1)}, u32[]{:S(2)}, u32[]{:S(2)}) collective-permute-start(bf16[2,136,256]{2,1,0:T(8,128)(2,1)S(1)} %get-tuple-element.51), channel_id=1, source_target_pairs={{0,4},{8,12},{16,20},{24,28},{4,0},{12,8},{20,16},{28,24},{1,5},{9... | collective-permute-start | bytes 417800 | tf_op jit(solution)/shard_map/ppermute | solution.py:698
  50.2 6.1 %analyse.1 = (bf16[240,256]{1,0:T(8,128)(2,1)S(1)}, bf16[240,256]{1,0:T(8,128)(2,1)S(1)}, bf16[240,256]{1,0:T(8,128)(2,1)S(1)}, bf16[240,256]{1,0:T(8,128)(2,1)S...) custom-call(f32[2,136,256]{2,1,0:T(8,128)S(1)} %get-tuple-element.50, ...), custom_call_target="tpu_custom_call" | custom-call | tf_op jit(solution)/shard_map/analyse/pallas_call | solution.py:866
  56.3 2.4 %collective-permute-start.10 = (bf16[240,256]{1,0:T(8,128)(2,1)S(1)}, bf16[240,256]{1,0:T(8,128)(2,1)S(1)}, u32[]{:S(2)}, u32[]{:S(2)}) collective-permute-start(bf16[240,256]{1,0:T(8,128)(2,1)S(1)} %get-tuple-element.57), channel_id=1, source_target_pairs={{0,4},{4,0},{8,12},{12,8},{16,20},{20,16},{24,28},{28,24},{1,5},{5... | collective-permute-start | bytes 368648 | tf_op jit(solution)/shard_map/ppermute | solution.py:716
  58.7 2.3 %collective-permute-start.18 = (bf16[240,256]{1,0:T(8,128)(2,1)S(1)}, bf16[240,256]{1,0:T(8,128)(2,1)S(1)}, u32[]{:S(2)}, u32[]{:S(2)}) collective-permute-start(bf16[240,256]{1,0:T(8,128)(2,1)S(1)} %get-tuple-element.69), channel_id=1, source_target_pairs={{0,24},{4,28},{8,16},{12,20},{16,8},{20,12},{24,0},{28,4},{1,25},{... | collective-permute-start | bytes 368648 | tf_op jit(solution)/shard_map/ppermute | solution.py:716
  60.9 1.6 %collective-permute-start.19 = (bf16[240,256]{1,0:T(8,128)(2,1)S(1)}, bf16[240,256]{1,0:T(8,128)(2,1)S(1)}, u32[]{:S(2)}, u32[]{:S(2)}) collective-permute-start(bf16[240,256]{1,0:T(8,128)(2,1)S(1)} %get-tuple-element.70), channel_id=1, source_target_pairs={{0,8},{4,12},{8,0},{12,4},{16,24},{20,28},{24,16},{28,20},{1,9},{5... | collective-permute-start | bytes 368648 | tf_op jit(solution)/shard_map/ppermute | solution.py:716
  63.6 2.1 %collective-permute-start.22 = (bf16[240,256]{1,0:T(8,128)(2,1)S(1)}, bf16[240,256]{1,0:T(8,128)(2,1)S(1)}, u32[]{:S(2)}, u32[]{:S(2)}) collective-permute-start(bf16[240,256]{1,0:T(8,128)(2,1)S(1)} %get-tuple-element.74), channel_id=1, source_target_pairs={{0,12},{4,8},{8,4},{12,0},{16,28},{20,24},{24,20},{28,16},{1,13},{... | collective-permute-start | bytes 368648 | tf_op jit(solution)/shard_map/ppermute | solution.py:716
  67.0 1.8 %second.1 = (bf16[216,256]{1,0:T(8,128)(2,1)S(1)}, bf16[216,256]{1,0:T(8,128)(2,1)S(1)}, bf16[216,256]{1,0:T(8,128)(2,1)S(1)}, bf16[216,256]{1,0:T(8,128)(2,1)S(...) custom-call(bf16[2,256,256]{2,1,0:T(8,128)(2,1)S(1)} %get-tuple-elem, ...), custom_call_target="tpu_custom_call" | custom-call | flops 1 | bytes 6291456 | tf_op jit(solution)/shard_map/second/pallas_call | solution.py:876
  76.3 3.2 %collective-permute-done.12.refs_1_ = bf16[216,256]{1,0:T(8,128)(2,1)S(1)} collective-permute-done((bf16[216,256]{1,0:T(8,128)(2,1)S(1)}, bf16[216,256]{1,0:T(8,128)(2,1)S(1)}, u32[]{:S(2)}, u32[]{:S(2)}) %collective-permute-start.12) | collective-permute-done | bytes 110624 | tf_op jit(solution)/shard_map/ppermute | solution.py:716
  79.4 1.6 %first_return.1.refs_8_ = bf16[3,60,32,160]{3,2,1,0:T(8,128)(2,1)} custom-call(bf16[240,256]{1,0:T(8,128)(2,1)S(1)} %collective-permute-done.18.refs_0_, bf16[240,256]{1,0:T(8,128)(2,1)S(1)} %collective-permute-done.19.refs_1_, bf16[240,256]{1,0:T(8,128)(2,1)S(1)} %collective-permute-done.20.refs_2_, bf16[240,256]{1,0:T(8,128)(2,1)S(1)} %collective-permute-done.21.refs_3_, ...), custom_call_target="tpu_custom_call" | custom-call | flops 1 | bytes 4194304 | tf_op jit(solution)/shard_map/first_return/pallas_call | solution.py:886
  81.1 2.2 %collective-permute-done.16.refs_5_ = bf16[216,256]{1,0:T(8,128)(2,1)S(1)} collective-permute-done((bf16[216,256]{1,0:T(8,128)(2,1)S(1)}, bf16[216,256]{1,0:T(8,128)(2,1)S(1)}, u32[]{:S(2)}, u32[]{:S(2)}) %collective-permute-start.16) | collective-permute-done | bytes 110624 | tf_op jit(solution)/shard_map/ppermute | solution.py:716
  84.2 1.6 %second_return.1 = bf16[3,60,32,160]{3,2,1,0:T(8,128)(2,1)} custom-call(bf16[216,256]{1,0:T(8,128)(2,1)S(1)} %collective-permute-done.11.refs_0_, bf16[216,256]{1,0:T(8,128)(2,1)S(1)} %collective-permute-done.12.refs_1_, bf16[216,256]{1,0:T(8,128)(2,1)S(1)} %collective-permute-done.13.refs_2_, ...), custom_call_target="tpu_custom_call", output_to_operand_aliasing={{}: (8, {})} | custom-call | tf_op jit(solution)/shard_map/second_return/pallas_call | solution.py:900
  (64 shorter events, 18.1 us)
Async XLA Ops:
  4.6 23.3 %all-to-all-start = ((bf16[8,304,256]{2,1,0:T(8,128)(2,1)}), bf16[8,304,256]{2,1,0:T(8,128)(2,1)}, u32[]{:S(2)}, u32[]{:S(2)}) async-start(bf16[8,304,256]{2,1,0:T(8,128)(2,1)} %get-tuple-element.41), calls=%async_computation | async-start | bytes 2490368 | tf_op jit(solution)/shard_map/all_to_all | solution.py:724
  9.8 5.9 %collective-permute-start = (bf16[4,32,160]{2,1,0:T(8,128)(2,1)}, bf16[4,32,160]{2,1,0:T(8,128)(2,1)S(1)}, u32[]{:S(2)}, u32[]{:S(2)}) collective-permute-start(bf16[4,32,160]{2,1,0:T(8,128)(2,1)} %get-tuple-element.43), channel_id=1, source_target_pairs={{0,1},{2,3},{1,0},{3,2},{4,5},{6,7},{5,4},{7,6},{8,9},{10,11},{9,8... | collective-permute-start | bytes 122888 | tf_op jit(solution)/shard_map/ppermute | solution.py:698
  12.0 6.4 %collective-permute-start.1 = (bf16[4,32,160]{2,1,0:T(8,128)(2,1)}, bf16[4,32,160]{2,1,0:T(8,128)(2,1)S(1)}, u32[]{:S(2)}, u32[]{:S(2)}) collective-permute-start(bf16[4,32,160]{2,1,0:T(8,128)(2,1)} %get-tuple-element.44), channel_id=1, source_target_pairs={{1,2},{3,0},{2,1},{0,3},{5,6},{7,4},{6,5},{4,7},{9,10},{11,8},{10,... | collective-permute-start | bytes 122888 | tf_op jit(solution)/shard_map/ppermute | solution.py:698
  21.4 11.6 %collective-permute-start.3 = (bf16[2,152,256]{2,1,0:T(8,128)(2,1)S(1)}, bf16[2,152,256]{2,1,0:T(8,128)(2,1)S(1)}, u32[]{:S(2)}, u32[]{:S(2)}) collective-permute-start(bf16[2,152,256]{2,1,0:T(8,128)(2,1)S(1)} %pad_maximum_fusion), channel_id=1, source_target_pairs={{0,8},{4,12},{8,0},{12,4},{16,24},{20,28},{24,16},{28,20},{1,9},{5... | collective-permute-start | bytes 466952 | tf_op jit(solution)/shard_map/ppermute | solution.py:716
  23.3 9.7 %collective-permute-start.4 = (bf16[2,152,256]{2,1,0:T(8,128)(2,1)S(1)}, bf16[2,152,256]{2,1,0:T(8,128)(2,1)S(1)}, u32[]{:S(2)}, u32[]{:S(2)}) collective-permute-start(bf16[2,152,256]{2,1,0:T(8,128)(2,1)S(1)} %pad_maximum_fusion.1), channel_id=1, source_target_pairs={{0,16},{4,20},{8,24},{12,28},{16,0},{20,4},{24,8},{28,12},{1,17},{... | collective-permute-start | bytes 466952 | tf_op jit(solution)/shard_map/ppermute | solution.py:716
  24.9 9.1 %collective-permute-start.5 = (bf16[2,152,256]{2,1,0:T(8,128)(2,1)S(1)}, bf16[2,152,256]{2,1,0:T(8,128)(2,1)S(1)}, u32[]{:S(2)}, u32[]{:S(2)}) collective-permute-start(bf16[2,152,256]{2,1,0:T(8,128)(2,1)S(1)} %pad_maximum_fusion.2), channel_id=1, source_target_pairs={{0,24},{4,28},{8,16},{12,20},{16,8},{20,12},{24,0},{28,4},{1,25},{... | collective-permute-start | bytes 466952 | tf_op jit(solution)/shard_map/ppermute | solution.py:716
  38.1 4.5 %collective-permute-start.6 = (bf16[136,256]{1,0:T(8,128)(2,1)S(1)}, bf16[136,256]{1,0:T(8,128)(2,1)S(1)}, u32[]{:S(2)}, u32[]{:S(2)}) collective-permute-start(bf16[136,256]{1,0:T(8,128)(2,1)S(1)} %get-tuple-element.48), channel_id=1, source_target_pairs={{0,1},{2,3},{1,0},{3,2},{4,5},{6,7},{5,4},{7,6},{8,9},{10,11},{9,8... | collective-permute-start | bytes 208904 | tf_op jit(solution)/shard_map/ppermute | solution.py:698
  40.1 6.3 %collective-permute-start.7 = (bf16[136,256]{1,0:T(8,128)(2,1)S(1)}, bf16[136,256]{1,0:T(8,128)(2,1)S(1)}, u32[]{:S(2)}, u32[]{:S(2)}) collective-permute-start(bf16[136,256]{1,0:T(8,128)(2,1)S(1)} %get-tuple-element.49), channel_id=1, source_target_pairs={{1,2},{3,0},{2,1},{0,3},{5,6},{7,4},{6,5},{4,7},{9,10},{11,8},{10,... | collective-permute-start | bytes 208904 | tf_op jit(solution)/shard_map/ppermute | solution.py:698
  46.5 3.4 %collective-permute-start.9 = (bf16[2,136,256]{2,1,0:T(8,128)(2,1)S(1)}, bf16[2,136,256]{2,1,0:T(8,128)(2,1)S(1)}, u32[]{:S(2)}, u32[]{:S(2)}) collective-permute-start(bf16[2,136,256]{2,1,0:T(8,128)(2,1)S(1)} %get-tuple-element.51), channel_id=1, source_target_pairs={{4,8},{12,16},{20,24},{8,4},{16,12},{24,20},{5,9},{13,17},{21,25},... | collective-permute-start | bytes 417800 | tf_op jit(solution)/shard_map/ppermute | solution.py:698
  47.3 2.9 %collective-permute-start.8 = (bf16[2,136,256]{2,1,0:T(8,128)(2,1)S(1)}, bf16[2,136,256]{2,1,0:T(8,128)(2,1)S(1)}, u32[]{:S(2)}, u32[]{:S(2)}) collective-permute-start(bf16[2,136,256]{2,1,0:T(8,128)(2,1)S(1)} %get-tuple-element.51), channel_id=1, source_target_pairs={{0,4},{8,12},{16,20},{24,28},{4,0},{12,8},{20,16},{28,24},{1,5},{9... | collective-permute-start | bytes 417800 | tf_op jit(solution)/shard_map/ppermute | solution.py:698
  56.3 7.4 %collective-permute-start.10 = (bf16[240,256]{1,0:T(8,128)(2,1)S(1)}, bf16[240,256]{1,0:T(8,128)(2,1)S(1)}, u32[]{:S(2)}, u32[]{:S(2)}) collective-permute-start(bf16[240,256]{1,0:T(8,128)(2,1)S(1)} %get-tuple-element.57), channel_id=1, source_target_pairs={{0,4},{4,0},{8,12},{12,8},{16,20},{20,16},{24,28},{28,24},{1,5},{5... | collective-permute-start | bytes 368648 | tf_op jit(solution)/shard_map/ppermute | solution.py:716
  58.7 7.1 %collective-permute-start.18 = (bf16[240,256]{1,0:T(8,128)(2,1)S(1)}, bf16[240,256]{1,0:T(8,128)(2,1)S(1)}, u32[]{:S(2)}, u32[]{:S(2)}) collective-permute-start(bf16[240,256]{1,0:T(8,128)(2,1)S(1)} %get-tuple-element.69), channel_id=1, source_target_pairs={{0,24},{4,28},{8,16},{12,20},{16,8},{20,12},{24,0},{28,4},{1,25},{... | collective-permute-start | bytes 368648 | tf_op jit(solution)/shard_map/ppermute | solution.py:716
  60.9 8.4 %collective-permute-start.19 = (bf16[240,256]{1,0:T(8,128)(2,1)S(1)}, bf16[240,256]{1,0:T(8,128)(2,1)S(1)}, u32[]{:S(2)}, u32[]{:S(2)}) collective-permute-start(bf16[240,256]{1,0:T(8,128)(2,1)S(1)} %get-tuple-element.70), channel_id=1, source_target_pairs={{0,8},{4,12},{8,0},{12,4},{16,24},{20,28},{24,16},{28,20},{1,9},{5... | collective-permute-start | bytes 368648 | tf_op jit(solution)/shard_map/ppermute | solution.py:716
  62.6 8.5 %collective-permute-start.20 = (bf16[240,256]{1,0:T(8,128)(2,1)S(1)}, bf16[240,256]{1,0:T(8,128)(2,1)S(1)}, u32[]{:S(2)}, u32[]{:S(2)}) collective-permute-start(bf16[240,256]{1,0:T(8,128)(2,1)S(1)} %get-tuple-element.71), channel_id=1, source_target_pairs={{0,16},{4,20},{8,24},{12,28},{16,0},{20,4},{24,8},{28,12},{1,17},{... | collective-permute-start | bytes 368648 | tf_op jit(solution)/shard_map/ppermute | solution.py:716
  62.6 9.0 %collective-permute-start.21 = (bf16[240,256]{1,0:T(8,128)(2,1)S(1)}, bf16[240,256]{1,0:T(8,128)(2,1)S(1)}, u32[]{:S(2)}, u32[]{:S(2)}) collective-permute-start(bf16[240,256]{1,0:T(8,128)(2,1)S(1)} %get-tuple-element.72), channel_id=1, source_target_pairs={{0,28},{4,24},{8,20},{12,16},{16,12},{20,8},{24,4},{28,0},{1,29},{... | collective-permute-start | bytes 368648 | tf_op jit(solution)/shard_map/ppermute | solution.py:716
  63.6 10.1 %collective-permute-start.22 = (bf16[240,256]{1,0:T(8,128)(2,1)S(1)}, bf16[240,256]{1,0:T(8,128)(2,1)S(1)}, u32[]{:S(2)}, u32[]{:S(2)}) collective-permute-start(bf16[240,256]{1,0:T(8,128)(2,1)S(1)} %get-tuple-element.74), channel_id=1, source_target_pairs={{0,12},{4,8},{8,4},{12,0},{16,28},{20,24},{24,20},{28,16},{1,13},{... | collective-permute-start | bytes 368648 | tf_op jit(solution)/shard_map/ppermute | solution.py:716
  65.8 9.4 %collective-permute-start.23 = (bf16[240,256]{1,0:T(8,128)(2,1)S(1)}, bf16[240,256]{1,0:T(8,128)(2,1)S(1)}, u32[]{:S(2)}, u32[]{:S(2)}) collective-permute-start(bf16[240,256]{1,0:T(8,128)(2,1)S(1)} %get-tuple-element.75), channel_id=1, source_target_pairs={{0,20},{4,16},{8,28},{12,24},{16,4},{20,0},{24,12},{28,8},{1,21},{... | collective-permute-start | bytes 368648 | tf_op jit(solution)/shard_map/ppermute | solution.py:716
  69.3 6.9 %collective-permute-start.11 = (bf16[216,256]{1,0:T(8,128)(2,1)S(1)}, bf16[216,256]{1,0:T(8,128)(2,1)S(1)}, u32[]{:S(2)}, u32[]{:S(2)}) collective-permute-start(bf16[216,256]{1,0:T(8,128)(2,1)S(1)} %get-tuple-element.61), channel_id=1, source_target_pairs={{0,24},{4,28},{8,16},{12,20},{16,8},{20,12},{24,0},{28,4},{1,25},{... | collective-permute-start | bytes 331784 | tf_op jit(solution)/shard_map/ppermute | solution.py:716
  71.0 8.4 %collective-permute-start.12 = (bf16[216,256]{1,0:T(8,128)(2,1)S(1)}, bf16[216,256]{1,0:T(8,128)(2,1)S(1)}, u32[]{:S(2)}, u32[]{:S(2)}) collective-permute-start(bf16[216,256]{1,0:T(8,128)(2,1)S(1)} %get-tuple-element.62), channel_id=1, source_target_pairs={{0,8},{4,12},{8,0},{12,4},{16,24},{20,28},{24,16},{28,20},{1,9},{5... | collective-permute-start | bytes 331784 | tf_op jit(solution)/shard_map/ppermute | solution.py:716
  71.6 9.5 %collective-permute-start.13 = (bf16[216,256]{1,0:T(8,128)(2,1)S(1)}, bf16[216,256]{1,0:T(8,128)(2,1)S(1)}, u32[]{:S(2)}, u32[]{:S(2)}) collective-permute-start(bf16[216,256]{1,0:T(8,128)(2,1)S(1)} %get-tuple-element.63), channel_id=1, source_target_pairs={{0,16},{4,20},{8,24},{12,28},{16,0},{20,4},{24,8},{28,12},{1,17},{... | collective-permute-start | bytes 331784 | tf_op jit(solution)/shard_map/ppermute | solution.py:716
  73.7 7.3 %collective-permute-start.14 = (bf16[216,256]{1,0:T(8,128)(2,1)S(1)}, bf16[216,256]{1,0:T(8,128)(2,1)S(1)}, u32[]{:S(2)}, u32[]{:S(2)}) collective-permute-start(bf16[216,256]{1,0:T(8,128)(2,1)S(1)} %get-tuple-element.64), channel_id=1, source_target_pairs={{0,28},{4,24},{8,20},{12,16},{16,12},{20,8},{24,4},{28,0},{1,29},{... | collective-permute-start | bytes 331784 | tf_op jit(solution)/shard_map/ppermute | solution.py:716
  75.2 5.9 %collective-permute-start.15 = (bf16[216,256]{1,0:T(8,128)(2,1)S(1)}, bf16[216,256]{1,0:T(8,128)(2,1)S(1)}, u32[]{:S(2)}, u32[]{:S(2)}) collective-permute-start(bf16[216,256]{1,0:T(8,128)(2,1)S(1)} %get-tuple-element.65), channel_id=1, source_target_pairs={{0,4},{4,0},{8,12},{12,8},{16,20},{20,16},{24,28},{28,24},{1,5},{5... | collective-permute-start | bytes 331784 | tf_op jit(solution)/shard_map/ppermute | solution.py:716
  76.2 7.1 %collective-permute-start.16 = (bf16[216,256]{1,0:T(8,128)(2,1)S(1)}, bf16[216,256]{1,0:T(8,128)(2,1)S(1)}, u32[]{:S(2)}, u32[]{:S(2)}) collective-permute-start(bf16[216,256]{1,0:T(8,128)(2,1)S(1)} %get-tuple-element.66), channel_id=1, source_target_pairs={{0,12},{4,8},{8,4},{12,0},{16,28},{20,24},{24,20},{28,16},{1,13},{... | collective-permute-start | bytes 331784 | tf_op jit(solution)/shard_map/ppermute | solution.py:716
  79.4 4.7 %collective-permute-start.17 = (bf16[216,256]{1,0:T(8,128)(2,1)S(1)}, bf16[216,256]{1,0:T(8,128)(2,1)S(1)}, u32[]{:S(2)}, u32[]{:S(2)}) collective-permute-start(bf16[216,256]{1,0:T(8,128)(2,1)S(1)} %get-tuple-element.67), channel_id=1, source_target_pairs={{0,20},{4,16},{8,28},{12,24},{16,4},{20,0},{24,12},{28,8},{1,21},{... | collective-permute-start | bytes 331784 | tf_op jit(solution)/shard_map/ppermute | solution.py:716
  (7 other events, 86.2 us)

commit v18 on v17

--- a/solution.py
+++ b/solution.py
@@ -604,15 +604,19 @@
             continue
         parts = [split(inverse) for inverse in inverses]
         products = [dot_nn(left_3(part), right) for part, right in zip(parts, rights)]
-        middles = [left_3(split(1.5 * eye - 0.5 * product)) for product in products]
+        middle_parts = [split(1.5 * eye - 0.5 * product) for product in products]
+        middles = [left_3(part) for part in middle_parts]
         if sweep < SWEEPS - 1:
             roots = [dot_nn(middle, right) for middle, right in zip(middles, rights)]
+        else:
+            pulls = [dot_nn(left_3(split(pull)), right_3(part)) for pull, part in zip(pulls, parts)]
+            rights = [right_3(part) for part in middle_parts]
+            pulls = [dot_nn(left_3(split(pull)), right) for pull, right in zip(pulls, rights)]
         inverses = [dot_nn(middle, right_3(part)) for middle, part in zip(middles, parts)]
     maps = []
     for t in range(2):
         right = right_3(split(inverses[t]))
-        half_pull = dot_nn(left_3(split(pulls[t])), right)
-        shift = dot_nn(left_3(split(half_pull)), right) / norms[t]
+        shift = dot_nn(left_3(split(pulls[t])), right) / norms[t]
         scale = math.sqrt(size - 1) / jnp.sqrt(norms[t])
         ordered[t] = (inverses[t] * scale + shift[0:1]).astype(BF16).reshape(8, 32, size)
     me = lax.axis_index("mem")

time: 86.1 us -> 86.2 us (level)
  no operation moved by 1% of the time
where the time goes in v18:
time: 86.2 us; the launch traced here: 86 us
  starting transfers between devices  36.2 us (42%)
  Pallas kernels  26.9 us (31%)
  waiting for transfers between devices  21.1 us (24%)
  other arithmetic  1.44 us (2%)
    ppermute x18, starting transfers between devices, across(): return lax.ppermute(value, 'mem', [(i, i ^ difference) for i in range(8)])  19 us
    ppermute x6, starting transfers between devices, swapped_pairs(): moved.append(lax.ppermute(value, axis, both))  12 us
    ppermute x18, waiting for transfers between devices, across(): return lax.ppermute(value, 'mem', [(i, i ^ difference) for i in range(8)])  11.6 us
    ppermute x6, waiting for transfers between devices, swapped_pairs(): moved.append(lax.ppermute(value, axis, both))  6.77 us
    pallas_call x1, Pallas kernels, on_device_fast(): pl.pallas_call(analyse_kernel, out_shape=(jax.ShapeDtypeStruct((FIRST, 25...  6.21 us
    all_to_all x1, starting transfers between devices, swap(): return lax.all_to_all(value, 'mem', split_axis=0, concat_axis=0, tiled=True)  5.19 us
    pallas_call x1, Pallas kernels, on_device_fast(): pl.pallas_call(spread_kernel, out_shape=(jax.ShapeDtypeStruct((8, INNER,...  5.04 us
    pallas_call x1, Pallas kernels, on_device_fast(): pl.pallas_call(inner_kernel, out_shape=(jax.ShapeDtypeStruct((8, INNER, 2...  4.63 us
  transfers between devices with their start and end apart: 25, of which 13 were waited for; matrix products, arithmetic and copies ran while one was open for 2% of the time, Pallas kernels for 12%

profile of v18, /device:TPU:0, one launch (start us, length us, event | category | flops | bytes accessed | tf_op | source)
XLA Modules:
  0.0 86.0 jit_solution(14007097062438300465)
XLA Ops:
  0.0 4.6 %inner.1 = (bf16[8,304,256]{2,1,0:T(8,128)(2,1)}, bf16[4,32,160]{2,1,0:T(8,128)(2,1)}, bf16[4,32,160]{2,1,0:T(8,128)(2,1)}) custom-call(bf16[3,60,32,160]{3,2,1,0:T(8,128)(2,1)} %bitcast.49, f32[60,160]{1,0:T(8,128)} %depth.3), custom_call_target="tpu_custom_call" | custom-call | tf_op jit(solution)/shard_map/inner/pallas_call | solution.py:757
  4.6 5.2 %all-to-all-start = ((bf16[8,304,256]{2,1,0:T(8,128)(2,1)}), bf16[8,304,256]{2,1,0:T(8,128)(2,1)}, u32[]{:S(2)}, u32[]{:S(2)}) async-start(bf16[8,304,256]{2,1,0:T(8,128)(2,1)} %get-tuple-element.41), calls=%async_computation | async-start | bytes 2490368 | tf_op jit(solution)/shard_map/all_to_all | solution.py:728
  9.8 2.2 %collective-permute-start = (bf16[4,32,160]{2,1,0:T(8,128)(2,1)}, bf16[4,32,160]{2,1,0:T(8,128)(2,1)S(1)}, u32[]{:S(2)}, u32[]{:S(2)}) collective-permute-start(bf16[4,32,160]{2,1,0:T(8,128)(2,1)} %get-tuple-element.43), channel_id=1, source_target_pairs={{0,1},{2,3},{1,0},{3,2},{4,5},{6,7},{5,4},{7,6},{8,9},{10,11},{9,8... | collective-permute-start | bytes 122888 | tf_op jit(solution)/shard_map/ppermute | solution.py:702
  12.0 2.5 %collective-permute-start.1 = (bf16[4,32,160]{2,1,0:T(8,128)(2,1)}, bf16[4,32,160]{2,1,0:T(8,128)(2,1)S(1)}, u32[]{:S(2)}, u32[]{:S(2)}) collective-permute-start(bf16[4,32,160]{2,1,0:T(8,128)(2,1)} %get-tuple-element.44), channel_id=1, source_target_pairs={{1,2},{3,0},{2,1},{0,3},{5,6},{7,4},{6,5},{4,7},{9,10},{11,8},{10,... | collective-permute-start | bytes 122888 | tf_op jit(solution)/shard_map/ppermute | solution.py:702
  15.8 2.7 %collective-permute-done.1.second_swap = bf16[4,32,160]{2,1,0:T(8,128)(2,1)S(1)} collective-permute-done((bf16[4,32,160]{2,1,0:T(8,128)(2,1)}, bf16[4,32,160]{2,1,0:T(8,128)(2,1)S(1)}, u32[]{:S(2)}, u32[]{:S(2)}) %collective-permute-start.1) | collective-permute-done | bytes 40992 | tf_op jit(solution)/shard_map/ppermute | solution.py:702
  21.4 1.9 %collective-permute-start.3 = (bf16[2,152,256]{2,1,0:T(8,128)(2,1)S(1)}, bf16[2,152,256]{2,1,0:T(8,128)(2,1)S(1)}, u32[]{:S(2)}, u32[]{:S(2)}) collective-permute-start(bf16[2,152,256]{2,1,0:T(8,128)(2,1)S(1)} %pad_maximum_fusion), channel_id=1, source_target_pairs={{0,8},{4,12},{8,0},{12,4},{16,24},{20,28},{24,16},{28,20},{1,9},{5... | collective-permute-start | bytes 466952 | tf_op jit(solution)/shard_map/ppermute | solution.py:720
  23.3 1.6 %collective-permute-start.4 = (bf16[2,152,256]{2,1,0:T(8,128)(2,1)S(1)}, bf16[2,152,256]{2,1,0:T(8,128)(2,1)S(1)}, u32[]{:S(2)}, u32[]{:S(2)}) collective-permute-start(bf16[2,152,256]{2,1,0:T(8,128)(2,1)S(1)} %pad_maximum_fusion.1), channel_id=1, source_target_pairs={{0,16},{4,20},{8,24},{12,28},{16,0},{20,4},{24,8},{28,12},{1,17},{... | collective-permute-start | bytes 466952 | tf_op jit(solution)/shard_map/ppermute | solution.py:720
  25.2 2.7 %all-to-all-done.got = bf16[8,304,256]{2,1,0:T(8,128)(2,1)} async-done(((bf16[8,304,256]{2,1,0:T(8,128)(2,1)}), bf16[8,304,256]{2,1,0:T(8,128)(2,1)}, u32[]{:S(2)}, u32[]{:S(2)}) %all-to-all-start) | async-done | bytes 1245216 | tf_op jit(solution)/shard_map/all_to_all | solution.py:728
  27.9 5.0 %spread.1 = (bf16[8,304,256]{2,1,0:T(8,128)(2,1)S(1)}, f32[2,2,512,128]{3,2,1,0:T(8,128)S(1)}) custom-call(s32[2,512]{1,0:T(2,128)S(1)} %get-tuple-element.77.cells, bf16[8,304,256]{2,1,0:T(8,128)(2,1)} %all-to-all-done.got), custom_call_target="tpu_custom_call" | custom-call | flops 1 | bytes 8388608 | tf_op jit(solution)/shard_map/spread/pallas_call | solution.py:817
  34.0 4.0 %observe.1 = (bf16[8,152,256]{2,1,0:T(8,128)(2,1)S(1)}, f32[2,136,256]{2,1,0:T(8,128)S(1)}, bf16[136,256]{1,0:T(8,128)(2,1)S(1)}, bf16[136,256]{1,0:T(8,128)(2,1)S(1)}) custom-call(s32[2,640]{1,0:T(2,128)S(1)} %pad.4.cells, s32[2,640]{1,0:T(2,128)S(1)} %fusion.3.outer, f32[2,512]{1,0:T(2,128)S(1)} %fusion.12.weight, f32[2,512]{1,0:T(2,128)S(1)} %bitcast.52, ...), custom_call_target="tpu_custom_call" | custom-call | tf_op jit(solution)/shard_map/observe/pallas_call | solution.py:830
  38.1 2.2 %collective-permute-start.6 = (bf16[136,256]{1,0:T(8,128)(2,1)S(1)}, bf16[136,256]{1,0:T(8,128)(2,1)S(1)}, u32[]{:S(2)}, u32[]{:S(2)}) collective-permute-start(bf16[136,256]{1,0:T(8,128)(2,1)S(1)} %get-tuple-element.48), channel_id=1, source_target_pairs={{0,1},{2,3},{1,0},{3,2},{4,5},{6,7},{5,4},{7,6},{8,9},{10,11},{9,8... | collective-permute-start | bytes 208904 | tf_op jit(solution)/shard_map/ppermute | solution.py:702
  40.2 2.4 %collective-permute-start.7 = (bf16[136,256]{1,0:T(8,128)(2,1)S(1)}, bf16[136,256]{1,0:T(8,128)(2,1)S(1)}, u32[]{:S(2)}, u32[]{:S(2)}) collective-permute-start(bf16[136,256]{1,0:T(8,128)(2,1)S(1)} %get-tuple-element.49), channel_id=1, source_target_pairs={{1,2},{3,0},{2,1},{0,3},{5,6},{7,4},{6,5},{4,7},{9,10},{11,8},{10,... | collective-permute-start | bytes 208904 | tf_op jit(solution)/shard_map/ppermute | solution.py:702
  42.6 3.8 %collective-permute-done.7.second_swap = bf16[136,256]{1,0:T(8,128)(2,1)S(1)} collective-permute-done((bf16[136,256]{1,0:T(8,128)(2,1)S(1)}, bf16[136,256]{1,0:T(8,128)(2,1)S(1)}, u32[]{:S(2)}, u32[]{:S(2)}) %collective-permute-start.7) | collective-permute-done | bytes 69664 | tf_op jit(solution)/shard_map/ppermute | solution.py:702
  47.3 2.0 %collective-permute-start.8 = (bf16[2,136,256]{2,1,0:T(8,128)(2,1)S(1)}, bf16[2,136,256]{2,1,0:T(8,128)(2,1)S(1)}, u32[]{:S(2)}, u32[]{:S(2)}) collective-permute-start(bf16[2,136,256]{2,1,0:T(8,128)(2,1)S(1)} %get-tuple-element.51), channel_id=1, source_target_pairs={{0,4},{8,12},{16,20},{24,28},{4,0},{12,8},{20,16},{28,24},{1,5},{9... | collective-permute-start | bytes 417800 | tf_op jit(solution)/shard_map/ppermute | solution.py:702
  50.2 6.2 %analyse.1 = (bf16[240,256]{1,0:T(8,128)(2,1)S(1)}, bf16[240,256]{1,0:T(8,128)(2,1)S(1)}, bf16[240,256]{1,0:T(8,128)(2,1)S(1)}, bf16[240,256]{1,0:T(8,128)(2,1)S...) custom-call(f32[2,136,256]{2,1,0:T(8,128)S(1)} %get-tuple-element.50, ...), custom_call_target="tpu_custom_call" | custom-call | tf_op jit(solution)/shard_map/analyse/pallas_call | solution.py:870
  56.4 2.2 %collective-permute-start.10 = (bf16[240,256]{1,0:T(8,128)(2,1)S(1)}, bf16[240,256]{1,0:T(8,128)(2,1)S(1)}, u32[]{:S(2)}, u32[]{:S(2)}) collective-permute-start(bf16[240,256]{1,0:T(8,128)(2,1)S(1)} %get-tuple-element.57), channel_id=1, source_target_pairs={{0,4},{4,0},{8,12},{12,8},{16,20},{20,16},{24,28},{28,24},{1,5},{5... | collective-permute-start | bytes 368648 | tf_op jit(solution)/shard_map/ppermute | solution.py:720
  58.7 2.4 %collective-permute-start.18 = (bf16[240,256]{1,0:T(8,128)(2,1)S(1)}, bf16[240,256]{1,0:T(8,128)(2,1)S(1)}, u32[]{:S(2)}, u32[]{:S(2)}) collective-permute-start(bf16[240,256]{1,0:T(8,128)(2,1)S(1)} %get-tuple-element.69), channel_id=1, source_target_pairs={{0,24},{4,28},{8,16},{12,20},{16,8},{20,12},{24,0},{28,4},{1,25},{... | collective-permute-start | bytes 368648 | tf_op jit(solution)/shard_map/ppermute | solution.py:720
  61.1 1.6 %collective-permute-start.19 = (bf16[240,256]{1,0:T(8,128)(2,1)S(1)}, bf16[240,256]{1,0:T(8,128)(2,1)S(1)}, u32[]{:S(2)}, u32[]{:S(2)}) collective-permute-start(bf16[240,256]{1,0:T(8,128)(2,1)S(1)} %get-tuple-element.70), channel_id=1, source_target_pairs={{0,8},{4,12},{8,0},{12,4},{16,24},{20,28},{24,16},{28,20},{1,9},{5... | collective-permute-start | bytes 368648 | tf_op jit(solution)/shard_map/ppermute | solution.py:720
  63.8 2.1 %collective-permute-start.22 = (bf16[240,256]{1,0:T(8,128)(2,1)S(1)}, bf16[240,256]{1,0:T(8,128)(2,1)S(1)}, u32[]{:S(2)}, u32[]{:S(2)}) collective-permute-start(bf16[240,256]{1,0:T(8,128)(2,1)S(1)} %get-tuple-element.74), channel_id=1, source_target_pairs={{0,12},{4,8},{8,4},{12,0},{16,28},{20,24},{24,20},{28,16},{1,13},{... | collective-permute-start | bytes 368648 | tf_op jit(solution)/shard_map/ppermute | solution.py:720
  67.1 1.8 %second.1 = (bf16[216,256]{1,0:T(8,128)(2,1)S(1)}, bf16[216,256]{1,0:T(8,128)(2,1)S(1)}, bf16[216,256]{1,0:T(8,128)(2,1)S(1)}, bf16[216,256]{1,0:T(8,128)(2,1)S(...) custom-call(bf16[2,256,256]{2,1,0:T(8,128)(2,1)S(1)} %get-tuple-elem, ...), custom_call_target="tpu_custom_call" | custom-call | flops 1 | bytes 6291456 | tf_op jit(solution)/shard_map/second/pallas_call | solution.py:880
  76.3 3.2 %collective-permute-done.12.refs_1_ = bf16[216,256]{1,0:T(8,128)(2,1)S(1)} collective-permute-done((bf16[216,256]{1,0:T(8,128)(2,1)S(1)}, bf16[216,256]{1,0:T(8,128)(2,1)S(1)}, u32[]{:S(2)}, u32[]{:S(2)}) %collective-permute-start.12) | collective-permute-done | bytes 110624 | tf_op jit(solution)/shard_map/ppermute | solution.py:720
  79.5 1.6 %first_return.1.refs_8_ = bf16[3,60,32,160]{3,2,1,0:T(8,128)(2,1)} custom-call(bf16[240,256]{1,0:T(8,128)(2,1)S(1)} %collective-permute-done.18.refs_0_, bf16[240,256]{1,0:T(8,128)(2,1)S(1)} %collective-permute-done.19.refs_1_, bf16[240,256]{1,0:T(8,128)(2,1)S(1)} %collective-permute-done.20.refs_2_, bf16[240,256]{1,0:T(8,128)(2,1)S(1)} %collective-permute-done.21.refs_3_, ...), custom_call_target="tpu_custom_call" | custom-call | flops 1 | bytes 4194304 | tf_op jit(solution)/shard_map/first_return/pallas_call | solution.py:890
  81.2 2.2 %collective-permute-done.16.refs_5_ = bf16[216,256]{1,0:T(8,128)(2,1)S(1)} collective-permute-done((bf16[216,256]{1,0:T(8,128)(2,1)S(1)}, bf16[216,256]{1,0:T(8,128)(2,1)S(1)}, u32[]{:S(2)}, u32[]{:S(2)}) %collective-permute-start.16) | collective-permute-done | bytes 110624 | tf_op jit(solution)/shard_map/ppermute | solution.py:720
  84.3 1.6 %second_return.1 = bf16[3,60,32,160]{3,2,1,0:T(8,128)(2,1)} custom-call(bf16[216,256]{1,0:T(8,128)(2,1)S(1)} %collective-permute-done.11.refs_0_, bf16[216,256]{1,0:T(8,128)(2,1)S(1)} %collective-permute-done.12.refs_1_, bf16[216,256]{1,0:T(8,128)(2,1)S(1)} %collective-permute-done.13.refs_2_, ...), custom_call_target="tpu_custom_call", output_to_operand_aliasing={{}: (8, {})} | custom-call | tf_op jit(solution)/shard_map/second_return/pallas_call | solution.py:904
  (64 shorter events, 18.0 us)
Async XLA Ops:
  4.6 23.3 %all-to-all-start = ((bf16[8,304,256]{2,1,0:T(8,128)(2,1)}), bf16[8,304,256]{2,1,0:T(8,128)(2,1)}, u32[]{:S(2)}, u32[]{:S(2)}) async-start(bf16[8,304,256]{2,1,0:T(8,128)(2,1)} %get-tuple-element.41), calls=%async_computation | async-start | bytes 2490368 | tf_op jit(solution)/shard_map/all_to_all | solution.py:728
  9.8 5.9 %collective-permute-start = (bf16[4,32,160]{2,1,0:T(8,128)(2,1)}, bf16[4,32,160]{2,1,0:T(8,128)(2,1)S(1)}, u32[]{:S(2)}, u32[]{:S(2)}) collective-permute-start(bf16[4,32,160]{2,1,0:T(8,128)(2,1)} %get-tuple-element.43), channel_id=1, source_target_pairs={{0,1},{2,3},{1,0},{3,2},{4,5},{6,7},{5,4},{7,6},{8,9},{10,11},{9,8... | collective-permute-start | bytes 122888 | tf_op jit(solution)/shard_map/ppermute | solution.py:702
  12.0 6.4 %collective-permute-start.1 = (bf16[4,32,160]{2,1,0:T(8,128)(2,1)}, bf16[4,32,160]{2,1,0:T(8,128)(2,1)S(1)}, u32[]{:S(2)}, u32[]{:S(2)}) collective-permute-start(bf16[4,32,160]{2,1,0:T(8,128)(2,1)} %get-tuple-element.44), channel_id=1, source_target_pairs={{1,2},{3,0},{2,1},{0,3},{5,6},{7,4},{6,5},{4,7},{9,10},{11,8},{10,... | collective-permute-start | bytes 122888 | tf_op jit(solution)/shard_map/ppermute | solution.py:702
  21.4 11.6 %collective-permute-start.3 = (bf16[2,152,256]{2,1,0:T(8,128)(2,1)S(1)}, bf16[2,152,256]{2,1,0:T(8,128)(2,1)S(1)}, u32[]{:S(2)}, u32[]{:S(2)}) collective-permute-start(bf16[2,152,256]{2,1,0:T(8,128)(2,1)S(1)} %pad_maximum_fusion), channel_id=1, source_target_pairs={{0,8},{4,12},{8,0},{12,4},{16,24},{20,28},{24,16},{28,20},{1,9},{5... | collective-permute-start | bytes 466952 | tf_op jit(solution)/shard_map/ppermute | solution.py:720
  23.3 9.7 %collective-permute-start.4 = (bf16[2,152,256]{2,1,0:T(8,128)(2,1)S(1)}, bf16[2,152,256]{2,1,0:T(8,128)(2,1)S(1)}, u32[]{:S(2)}, u32[]{:S(2)}) collective-permute-start(bf16[2,152,256]{2,1,0:T(8,128)(2,1)S(1)} %pad_maximum_fusion.1), channel_id=1, source_target_pairs={{0,16},{4,20},{8,24},{12,28},{16,0},{20,4},{24,8},{28,12},{1,17},{... | collective-permute-start | bytes 466952 | tf_op jit(solution)/shard_map/ppermute | solution.py:720
  24.9 9.1 %collective-permute-start.5 = (bf16[2,152,256]{2,1,0:T(8,128)(2,1)S(1)}, bf16[2,152,256]{2,1,0:T(8,128)(2,1)S(1)}, u32[]{:S(2)}, u32[]{:S(2)}) collective-permute-start(bf16[2,152,256]{2,1,0:T(8,128)(2,1)S(1)} %pad_maximum_fusion.2), channel_id=1, source_target_pairs={{0,24},{4,28},{8,16},{12,20},{16,8},{20,12},{24,0},{28,4},{1,25},{... | collective-permute-start | bytes 466952 | tf_op jit(solution)/shard_map/ppermute | solution.py:720
  38.1 4.5 %collective-permute-start.6 = (bf16[136,256]{1,0:T(8,128)(2,1)S(1)}, bf16[136,256]{1,0:T(8,128)(2,1)S(1)}, u32[]{:S(2)}, u32[]{:S(2)}) collective-permute-start(bf16[136,256]{1,0:T(8,128)(2,1)S(1)} %get-tuple-element.48), channel_id=1, source_target_pairs={{0,1},{2,3},{1,0},{3,2},{4,5},{6,7},{5,4},{7,6},{8,9},{10,11},{9,8... | collective-permute-start | bytes 208904 | tf_op jit(solution)/shard_map/ppermute | solution.py:702
  40.2 6.1 %collective-permute-start.7 = (bf16[136,256]{1,0:T(8,128)(2,1)S(1)}, bf16[136,256]{1,0:T(8,128)(2,1)S(1)}, u32[]{:S(2)}, u32[]{:S(2)}) collective-permute-start(bf16[136,256]{1,0:T(8,128)(2,1)S(1)} %get-tuple-element.49), channel_id=1, source_target_pairs={{1,2},{3,0},{2,1},{0,3},{5,6},{7,4},{6,5},{4,7},{9,10},{11,8},{10,... | collective-permute-start | bytes 208904 | tf_op jit(solution)/shard_map/ppermute | solution.py:702
  46.4 3.5 %collective-permute-start.9 = (bf16[2,136,256]{2,1,0:T(8,128)(2,1)S(1)}, bf16[2,136,256]{2,1,0:T(8,128)(2,1)S(1)}, u32[]{:S(2)}, u32[]{:S(2)}) collective-permute-start(bf16[2,136,256]{2,1,0:T(8,128)(2,1)S(1)} %get-tuple-element.51), channel_id=1, source_target_pairs={{4,8},{12,16},{20,24},{8,4},{16,12},{24,20},{5,9},{13,17},{21,25},... | collective-permute-start | bytes 417800 | tf_op jit(solution)/shard_map/ppermute | solution.py:702
  47.3 3.0 %collective-permute-start.8 = (bf16[2,136,256]{2,1,0:T(8,128)(2,1)S(1)}, bf16[2,136,256]{2,1,0:T(8,128)(2,1)S(1)}, u32[]{:S(2)}, u32[]{:S(2)}) collective-permute-start(bf16[2,136,256]{2,1,0:T(8,128)(2,1)S(1)} %get-tuple-element.51), channel_id=1, source_target_pairs={{0,4},{8,12},{16,20},{24,28},{4,0},{12,8},{20,16},{28,24},{1,5},{9... | collective-permute-start | bytes 417800 | tf_op jit(solution)/shard_map/ppermute | solution.py:702
  56.4 7.3 %collective-permute-start.10 = (bf16[240,256]{1,0:T(8,128)(2,1)S(1)}, bf16[240,256]{1,0:T(8,128)(2,1)S(1)}, u32[]{:S(2)}, u32[]{:S(2)}) collective-permute-start(bf16[240,256]{1,0:T(8,128)(2,1)S(1)} %get-tuple-element.57), channel_id=1, source_target_pairs={{0,4},{4,0},{8,12},{12,8},{16,20},{20,16},{24,28},{28,24},{1,5},{5... | collective-permute-start | bytes 368648 | tf_op jit(solution)/shard_map/ppermute | solution.py:720
  58.7 7.2 %collective-permute-start.18 = (bf16[240,256]{1,0:T(8,128)(2,1)S(1)}, bf16[240,256]{1,0:T(8,128)(2,1)S(1)}, u32[]{:S(2)}, u32[]{:S(2)}) collective-permute-start(bf16[240,256]{1,0:T(8,128)(2,1)S(1)} %get-tuple-element.69), channel_id=1, source_target_pairs={{0,24},{4,28},{8,16},{12,20},{16,8},{20,12},{24,0},{28,4},{1,25},{... | collective-permute-start | bytes 368648 | tf_op jit(solution)/shard_map/ppermute | solution.py:720
  61.1 8.4 %collective-permute-start.19 = (bf16[240,256]{1,0:T(8,128)(2,1)S(1)}, bf16[240,256]{1,0:T(8,128)(2,1)S(1)}, u32[]{:S(2)}, u32[]{:S(2)}) collective-permute-start(bf16[240,256]{1,0:T(8,128)(2,1)S(1)} %get-tuple-element.70), channel_id=1, source_target_pairs={{0,8},{4,12},{8,0},{12,4},{16,24},{20,28},{24,16},{28,20},{1,9},{5... | collective-permute-start | bytes 368648 | tf_op jit(solution)/shard_map/ppermute | solution.py:720
  62.7 8.3 %collective-permute-start.20 = (bf16[240,256]{1,0:T(8,128)(2,1)S(1)}, bf16[240,256]{1,0:T(8,128)(2,1)S(1)}, u32[]{:S(2)}, u32[]{:S(2)}) collective-permute-start(bf16[240,256]{1,0:T(8,128)(2,1)S(1)} %get-tuple-element.71), channel_id=1, source_target_pairs={{0,16},{4,20},{8,24},{12,28},{16,0},{20,4},{24,8},{28,12},{1,17},{... | collective-permute-start | bytes 368648 | tf_op jit(solution)/shard_map/ppermute | solution.py:720
  62.7 9.0 %collective-permute-start.21 = (bf16[240,256]{1,0:T(8,128)(2,1)S(1)}, bf16[240,256]{1,0:T(8,128)(2,1)S(1)}, u32[]{:S(2)}, u32[]{:S(2)}) collective-permute-start(bf16[240,256]{1,0:T(8,128)(2,1)S(1)} %get-tuple-element.72), channel_id=1, source_target_pairs={{0,28},{4,24},{8,20},{12,16},{16,12},{20,8},{24,4},{28,0},{1,29},{... | collective-permute-start | bytes 368648 | tf_op jit(solution)/shard_map/ppermute | solution.py:720
  63.8 10.1 %collective-permute-start.22 = (bf16[240,256]{1,0:T(8,128)(2,1)S(1)}, bf16[240,256]{1,0:T(8,128)(2,1)S(1)}, u32[]{:S(2)}, u32[]{:S(2)}) collective-permute-start(bf16[240,256]{1,0:T(8,128)(2,1)S(1)} %get-tuple-element.74), channel_id=1, source_target_pairs={{0,12},{4,8},{8,4},{12,0},{16,28},{20,24},{24,20},{28,16},{1,13},{... | collective-permute-start | bytes 368648 | tf_op jit(solution)/shard_map/ppermute | solution.py:720
  65.9 9.5 %collective-permute-start.23 = (bf16[240,256]{1,0:T(8,128)(2,1)S(1)}, bf16[240,256]{1,0:T(8,128)(2,1)S(1)}, u32[]{:S(2)}, u32[]{:S(2)}) collective-permute-start(bf16[240,256]{1,0:T(8,128)(2,1)S(1)} %get-tuple-element.75), channel_id=1, source_target_pairs={{0,20},{4,16},{8,28},{12,24},{16,4},{20,0},{24,12},{28,8},{1,21},{... | collective-permute-start | bytes 368648 | tf_op jit(solution)/shard_map/ppermute | solution.py:720
  69.5 6.9 %collective-permute-start.11 = (bf16[216,256]{1,0:T(8,128)(2,1)S(1)}, bf16[216,256]{1,0:T(8,128)(2,1)S(1)}, u32[]{:S(2)}, u32[]{:S(2)}) collective-permute-start(bf16[216,256]{1,0:T(8,128)(2,1)S(1)} %get-tuple-element.61), channel_id=1, source_target_pairs={{0,24},{4,28},{8,16},{12,20},{16,8},{20,12},{24,0},{28,4},{1,25},{... | collective-permute-start | bytes 331784 | tf_op jit(solution)/shard_map/ppermute | solution.py:720
  71.0 8.5 %collective-permute-start.12 = (bf16[216,256]{1,0:T(8,128)(2,1)S(1)}, bf16[216,256]{1,0:T(8,128)(2,1)S(1)}, u32[]{:S(2)}, u32[]{:S(2)}) collective-permute-start(bf16[216,256]{1,0:T(8,128)(2,1)S(1)} %get-tuple-element.62), channel_id=1, source_target_pairs={{0,8},{4,12},{8,0},{12,4},{16,24},{20,28},{24,16},{28,20},{1,9},{5... | collective-permute-start | bytes 331784 | tf_op jit(solution)/shard_map/ppermute | solution.py:720
  71.7 9.5 %collective-permute-start.13 = (bf16[216,256]{1,0:T(8,128)(2,1)S(1)}, bf16[216,256]{1,0:T(8,128)(2,1)S(1)}, u32[]{:S(2)}, u32[]{:S(2)}) collective-permute-start(bf16[216,256]{1,0:T(8,128)(2,1)S(1)} %get-tuple-element.63), channel_id=1, source_target_pairs={{0,16},{4,20},{8,24},{12,28},{16,0},{20,4},{24,8},{28,12},{1,17},{... | collective-permute-start | bytes 331784 | tf_op jit(solution)/shard_map/ppermute | solution.py:720
  73.9 7.3 %collective-permute-start.14 = (bf16[216,256]{1,0:T(8,128)(2,1)S(1)}, bf16[216,256]{1,0:T(8,128)(2,1)S(1)}, u32[]{:S(2)}, u32[]{:S(2)}) collective-permute-start(bf16[216,256]{1,0:T(8,128)(2,1)S(1)} %get-tuple-element.64), channel_id=1, source_target_pairs={{0,28},{4,24},{8,20},{12,16},{16,12},{20,8},{24,4},{28,0},{1,29},{... | collective-permute-start | bytes 331784 | tf_op jit(solution)/shard_map/ppermute | solution.py:720
  75.4 5.8 %collective-permute-start.15 = (bf16[216,256]{1,0:T(8,128)(2,1)S(1)}, bf16[216,256]{1,0:T(8,128)(2,1)S(1)}, u32[]{:S(2)}, u32[]{:S(2)}) collective-permute-start(bf16[216,256]{1,0:T(8,128)(2,1)S(1)} %get-tuple-element.65), channel_id=1, source_target_pairs={{0,4},{4,0},{8,12},{12,8},{16,20},{20,16},{24,28},{28,24},{1,5},{5... | collective-permute-start | bytes 331784 | tf_op jit(solution)/shard_map/ppermute | solution.py:720
  76.3 7.1 %collective-permute-start.16 = (bf16[216,256]{1,0:T(8,128)(2,1)S(1)}, bf16[216,256]{1,0:T(8,128)(2,1)S(1)}, u32[]{:S(2)}, u32[]{:S(2)}) collective-permute-start(bf16[216,256]{1,0:T(8,128)(2,1)S(1)} %get-tuple-element.66), channel_id=1, source_target_pairs={{0,12},{4,8},{8,4},{12,0},{16,28},{20,24},{24,20},{28,16},{1,13},{... | collective-permute-start | bytes 331784 | tf_op jit(solution)/shard_map/ppermute | solution.py:720
  79.5 4.7 %collective-permute-start.17 = (bf16[216,256]{1,0:T(8,128)(2,1)S(1)}, bf16[216,256]{1,0:T(8,128)(2,1)S(1)}, u32[]{:S(2)}, u32[]{:S(2)}) collective-permute-start(bf16[216,256]{1,0:T(8,128)(2,1)S(1)} %get-tuple-element.67), channel_id=1, source_target_pairs={{0,20},{4,16},{8,28},{12,24},{16,4},{20,0},{24,12},{28,8},{1,21},{... | collective-permute-start | bytes 331784 | tf_op jit(solution)/shard_map/ppermute | solution.py:720
  (7 other events, 86.2 us)
